TPU v7x, 32 devices: a whole 2x2x4 slice. The times are simulated.
32 devices in a mesh: ctx: 8 (over z, core), shard: 4 (over y, x).
Axes of the slice: x: 2, y: 2, z: 4, core: 2. Of those that a mesh axis runs over, the one named last changes fastest.
Arguments:
- tokens: bfloat16 [4, 2048, 2048], P('shard', 'ctx'), may hold values from -6 to 6
- doc_ids: int32 [4, 2048], P('shard', 'ctx'), may hold values from 0 to 7, never falling along the last dimension, each value on 1 to 1024 neighbouring positions
- routes: int32 [4, 2048, 8], P('shard', 'ctx'), may hold values from 0 to 15, all different within a row; in each aligned block of 256 rows (0 to 255, 256 to 511, ..., all dimensions but the last counted through in order) at most 256 rows name the same one
- attn_gain: bfloat16 [2048], P(('ctx', 'shard')), may hold values from 0.099609375 to 1.8984375
- w_query: bfloat16 [2048, 2048], P(('ctx', 'shard')), may hold values from -0.125 to 0.125
- w_key: bfloat16 [2048, 2048], P(('ctx', 'shard')), may hold values from -0.125 to 0.125
- w_value: bfloat16 [2048, 2048], P(('ctx', 'shard')), may hold values from -0.125 to 0.125
- query_gain: bfloat16 [2048], P(('ctx', 'shard')), may hold values from 0.7 to 3.8, as said below
- key_gain: bfloat16 [2048], P(('ctx', 'shard')), may hold values from 0.099609375 to 1.8984375
- w_out: bfloat16 [2048, 2048], P(('ctx', 'shard')), may hold values from -3 to 3
- ffn_gain: bfloat16 [2048], P(('ctx', 'shard')), may hold values from 0.099609375 to 1.8984375
- w_router: bfloat16 [2048, 16], P(('ctx', 'shard')), may hold values from -0.0625 to 0.0625
- w_gate: bfloat16 [16, 2048, 1024], P('shard', 'ctx'), may hold values from -0.125 to 0.125
- w_up: bfloat16 [16, 2048, 1024], P('shard', 'ctx'), may hold values from -0.125 to 0.125
- w_down: bfloat16 [16, 1024, 2048], P('shard', None, 'ctx'), may hold values from -1 to 1
- clip_threshold: float32 [], replicated, may hold values from 0.1 to 1
- cotangent: bfloat16 [4, 2048, 2048], P('shard', 'ctx'), may hold values from -6 to 6
Outputs:
- output: bfloat16 [4, 2048, 2048], P('shard', 'ctx')
- input_grad: float32 [4, 2048, 2048], P('shard', 'ctx')
- attn_gain_grad: float32 [2048], P(('ctx', 'shard'))
- w_query_grad: float32 [2048, 2048], P(('ctx', 'shard'))
- w_key_grad: float32 [2048, 2048], P(('ctx', 'shard'))
- w_value_grad: float32 [2048, 2048], P(('ctx', 'shard'))
- query_gain_grad: float32 [2048], P(('ctx', 'shard'))
- key_gain_grad: float32 [2048], P(('ctx', 'shard'))
- w_out_grad: float32 [2048, 2048], P(('ctx', 'shard'))
- ffn_gain_grad: float32 [2048], P(('ctx', 'shard'))
- w_router_grad: float32 [2048, 16], P(('ctx', 'shard'))
- w_gate_grad: float32 [16, 2048, 1024], P('shard', 'ctx')
- w_up_grad: float32 [16, 2048, 1024], P('shard', 'ctx')
- w_down_grad: float32 [16, 1024, 2048], P('shard', None, 'ctx')
- query_clipped: bfloat16 [2048, 2048], P(('ctx', 'shard'))
- key_clipped: bfloat16 [2048, 2048], P(('ctx', 'shard'))
- clip_factors: float32 [16], replicated
Inputs may be any that keep to these rules, and one draw needn't show every extreme that they name: `routes`: each token names 8 different experts. In each aligned block of 256 tokens of a sequence (the tokens of one device) no expert is named more than 256 times, and in some blocks one is named exactly 256 times. `doc_ids`: document numbers never fall along a sequence; a document has at most 1024 tokens, and in each sequence one has exactly that many. `query_gain`: Positive.
All inputs are finite; a program needn't handle non-finite values.
Results may differ from a plain program's by a relative error of at most 0.02.
The roundings to bfloat16 on the way count: a program that leaves them out, or rounds other values in their place, can miss the bound.
Values may be sent and summed in bfloat16 or wider, within the bound.
A program may use at most 384 MiB of HBM per device.

v0:
```python
import jax
import jax.numpy as jnp
from jax import lax
from jax.sharding import PartitionSpec as P

HEADS = 16
HEAD = 128


norm_eps = 1e-06
rope_base = 10000.0


def rms_scale(values, gain_vec):
    inverse = lax.rsqrt(jnp.mean(values * values, axis=-1, keepdims=True) + norm_eps)
    return values * inverse * gain_vec


def rotary(values, positions, head_count):
    row_count, model_width = values.shape
    half_size = model_width // head_count // 2
    inverse_freq = rope_base ** (-jnp.arange(half_size).astype(jnp.float32) / half_size)
    angles = positions.astype(jnp.float32)[:, None] * inverse_freq[None, :]
    cosine = jnp.cos(angles)[:, None, :]
    sine_vals = jnp.sin(angles)[:, None, :]
    paired = values.reshape(row_count, head_count, 2, half_size)
    first_half = paired[:, :, 0, :]
    second_half = paired[:, :, 1, :]
    turned = jnp.stack(
        [
            first_half * cosine - second_half * sine_vals,
            second_half * cosine + first_half * sine_vals,
        ],
        axis=2,
    )
    return turned.reshape(row_count, model_width)


def contract_rows(left_op, right_op):
    return lax.dot_general(
        left_op, right_op, (((0,), (0,)), ((), ())), preferred_element_type=jnp.float32
    )


def contract_cols(left_op, right_op):
    return lax.dot_general(
        left_op, right_op, (((1,), (1,)), ((), ())), preferred_element_type=jnp.float32
    )


def attend_forward(queries, keys_all, values_all, same_doc):
    row_count, model_width = queries.shape

    def one_head(head_idx):
        col_start = head_idx * HEAD
        query_h = lax.dynamic_slice_in_dim(queries, col_start, HEAD, 1)
        key_h = lax.dynamic_slice_in_dim(keys_all, col_start, HEAD, 1)
        value_h = lax.dynamic_slice_in_dim(values_all, col_start, HEAD, 1)
        scores = HEAD ** (-0.5) * contract_cols(query_h, key_h)
        masked = jnp.where(same_doc, scores, -1e30)
        row_top = jnp.max(masked, axis=1, keepdims=True)
        weights = jnp.exp(masked - row_top)
        row_total = jnp.sum(weights, axis=1, keepdims=True)
        prob_vals = (weights / row_total).astype(jnp.bfloat16)
        mixed_h = jnp.dot(prob_vals, value_h, preferred_element_type=jnp.float32)
        return (mixed_h, row_top[:, 0] + jnp.log(row_total[:, 0]), jnp.max(row_top))

    mixed_heads, log_total, head_peaks = lax.map(one_head, jnp.arange(HEADS))
    return (mixed_heads.transpose(1, 0, 2).reshape(row_count, model_width), log_total, head_peaks)


def attend_backward(queries, keys_all, values_all, same_doc, log_total, grad_mixed):
    row_count, model_width = queries.shape
    key_count = keys_all.shape[0]

    def one_head(carried, head_idx):
        grad_q, grad_k, grad_v = carried
        col_start = head_idx * HEAD
        query_h = lax.dynamic_slice_in_dim(queries, col_start, HEAD, 1)
        key_h = lax.dynamic_slice_in_dim(keys_all, col_start, HEAD, 1)
        value_h = lax.dynamic_slice_in_dim(values_all, col_start, HEAD, 1)
        grad_h = lax.dynamic_slice_in_dim(grad_mixed, col_start, HEAD, 1)
        scores = HEAD ** (-0.5) * contract_cols(query_h, key_h)
        prob_vals = jnp.where(same_doc, jnp.exp(scores - log_total[head_idx][:, None]), 0.0)
        grad_p = contract_cols(grad_h, value_h)
        inner_sum = jnp.sum(prob_vals * grad_p, axis=1, keepdims=True)
        grad_s = (prob_vals * (grad_p - inner_sum)).astype(jnp.bfloat16)
        grad_q = lax.dynamic_update_slice_in_dim(
            grad_q,
            HEAD ** (-0.5) * jnp.dot(grad_s, key_h, preferred_element_type=jnp.float32),
            col_start,
            1,
        )
        grad_k = lax.dynamic_update_slice_in_dim(
            grad_k, HEAD ** (-0.5) * contract_rows(grad_s, query_h), col_start, 1
        )
        grad_v = lax.dynamic_update_slice_in_dim(
            grad_v, contract_rows(prob_vals.astype(jnp.bfloat16), grad_h), col_start, 1
        )
        return ((grad_q, grad_k, grad_v), None)

    start_vals = (
        jnp.zeros((row_count, model_width), jnp.float32),
        jnp.zeros((key_count, model_width), jnp.float32),
        jnp.zeros((key_count, model_width), jnp.float32),
    )
    (grad_q, grad_k, grad_v), _ = lax.scan(one_head, start_vals, jnp.arange(HEADS))
    return (grad_q, grad_k, grad_v)


def per_device(
    tokens,
    doc_ids,
    routes,
    attn_gain,
    w_query,
    w_key,
    w_value,
    query_gain,
    key_gain,
    w_out,
    ffn_gain,
    w_router,
    w_gate,
    w_up,
    w_down,
    clip_threshold,
    cotangent,
):
    inputs = tokens[0].astype(jnp.float32)
    row_count, model_width = inputs.shape
    route_rows = routes[0]
    top_count = route_rows.shape[1]
    shard_count = lax.axis_size("shard")
    local_experts = w_gate.shape[0]
    expert_count = local_experts * shard_count
    capacity = 2 * row_count * top_count // expert_count
    slots_all = expert_count * capacity
    gathered = (
        lax.all_gather(attn_gain, ("ctx", "shard"), axis=0, tiled=True),
        lax.all_gather(w_query, ("ctx", "shard"), axis=0, tiled=True),
        lax.all_gather(w_key, ("ctx", "shard"), axis=0, tiled=True),
        lax.all_gather(w_value, ("ctx", "shard"), axis=0, tiled=True),
        lax.all_gather(query_gain, ("ctx", "shard"), axis=0, tiled=True),
        lax.all_gather(key_gain, ("ctx", "shard"), axis=0, tiled=True),
        lax.all_gather(w_out, ("ctx", "shard"), axis=0, tiled=True),
        lax.all_gather(ffn_gain, ("ctx", "shard"), axis=0, tiled=True),
        lax.all_gather(w_router, ("ctx", "shard"), axis=0, tiled=True),
    )
    gain_attn, query_w, key_w, value_w, gain_query, gain_key, out_w, gain_ffn, router_w = gathered
    doc_all = lax.all_gather(doc_ids, "ctx", axis=1, tiled=True)[0]
    same_doc = doc_ids[0][:, None] == doc_all[None, :]
    positions = lax.axis_index("ctx") * row_count + jnp.arange(row_count)
    normed_one, norm_one_back = jax.vjp(rms_scale, inputs, gain_attn.astype(jnp.float32))
    hidden_one = normed_one.astype(jnp.bfloat16)
    query_lin = jnp.dot(hidden_one, query_w, preferred_element_type=jnp.float32)
    key_lin = jnp.dot(hidden_one, key_w, preferred_element_type=jnp.float32)
    value_b = jnp.dot(hidden_one, value_w, preferred_element_type=jnp.float32).astype(jnp.bfloat16)

    def prepare(query_in, key_in, query_g, key_g):
        return (
            rotary(rms_scale(query_in, query_g), positions, HEADS),
            rotary(rms_scale(key_in, key_g), positions, HEADS),
        )

    (query_rot, key_rot), prepare_back = jax.vjp(
        prepare, query_lin, key_lin, gain_query.astype(jnp.float32), gain_key.astype(jnp.float32)
    )
    query_b = query_rot.astype(jnp.bfloat16)
    key_b = key_rot.astype(jnp.bfloat16)
    keys_all, values_all = (
        lax.all_gather(key_b, "ctx", axis=0, tiled=True),
        lax.all_gather(value_b, "ctx", axis=0, tiled=True),
    )
    mixed_heads, log_total, head_peaks = attend_forward(query_b, keys_all, values_all, same_doc)
    peak_all = lax.pmax(head_peaks, ("ctx", "shard"))
    mixed_b = mixed_heads.astype(jnp.bfloat16)
    after_attn = inputs + jnp.dot(mixed_b, out_w, preferred_element_type=jnp.float32)
    normed_two, norm_two_back = jax.vjp(rms_scale, after_attn, gain_ffn.astype(jnp.float32))
    hidden_two = normed_two.astype(jnp.bfloat16)
    logits = jnp.dot(hidden_two, router_w, preferred_element_type=jnp.float32)
    chosen = (route_rows[:, :, None] == jnp.arange(expert_count)[None, None, :]).astype(jnp.float32)

    def gating(logit_in):
        logit_top = jnp.max(logit_in, axis=1, keepdims=True)
        logit_exp = jnp.exp(logit_in - logit_top)
        router_probs = logit_exp / jnp.sum(logit_exp, axis=1, keepdims=True)
        selected = jnp.sum(router_probs[:, None, :] * chosen, axis=2)
        return selected / jnp.sum(selected, axis=1, keepdims=True)

    gate_vals, gating_back = jax.vjp(gating, logits)
    flat_routes = route_rows.reshape(-1)
    route_hits = (flat_routes[:, None] == jnp.arange(expert_count)[None, :]).astype(jnp.int32)
    slot_in = jnp.sum((jnp.cumsum(route_hits, axis=0) - 1) * route_hits, axis=1)
    placed = (
        flat_routes % local_experts * (shard_count * capacity)
        + flat_routes // local_experts * capacity
        + slot_in
    )
    source = (
        jnp.full((slots_all,), row_count * top_count, jnp.int32)
        .at[placed]
        .set(jnp.arange(row_count * top_count))
    )
    pad_row = jnp.zeros((1, model_width), jnp.bfloat16)
    send_in = jnp.concatenate([hidden_two, pad_row], axis=0)[source // top_count].reshape(
        local_experts, shard_count * capacity, model_width
    )
    received = lax.all_to_all(send_in, "shard", split_axis=1, concat_axis=1, tiled=True)
    gate_all, up_all, down_all = (
        lax.all_gather(w_gate, "ctx", axis=1, tiled=True),
        lax.all_gather(w_up, "ctx", axis=1, tiled=True),
        lax.all_gather(w_down, "ctx", axis=2, tiled=True),
    )
    gate_h = jnp.einsum("lrd,ldf->lrf", received, gate_all, preferred_element_type=jnp.float32)
    up_h = jnp.einsum("lrd,ldf->lrf", received, up_all, preferred_element_type=jnp.float32)
    sig_gate = jax.nn.sigmoid(gate_h)
    silu_h = gate_h * sig_gate
    act_b = (silu_h * up_h).astype(jnp.bfloat16)
    expert_out = jnp.einsum(
        "lrf,lfd->lrd", act_b, down_all, preferred_element_type=jnp.float32
    ).astype(jnp.bfloat16)
    returned = lax.all_to_all(expert_out, "shard", split_axis=1, concat_axis=1, tiled=True)
    picked_f = (
        returned.reshape(slots_all, model_width)[placed]
        .reshape(row_count, top_count, model_width)
        .astype(jnp.float32)
    )
    moe_sum = jnp.sum(gate_vals[:, :, None] * picked_f, axis=1)
    output = (after_attn + moe_sum).astype(jnp.bfloat16)
    grad_out = cotangent[0].astype(jnp.float32)
    grad_gates = jnp.sum(grad_out[:, None, :] * picked_f, axis=2)
    grad_logits = gating_back(grad_gates)[0].astype(jnp.bfloat16)
    grad_router = contract_rows(hidden_two, grad_logits)
    grad_hidden = contract_cols(grad_logits, router_w)
    grad_y = (
        (gate_vals[:, :, None] * grad_out[:, None, :])
        .astype(jnp.bfloat16)
        .reshape(row_count * top_count, model_width)
    )
    send_grad = jnp.concatenate([grad_y, pad_row], axis=0)[source].reshape(
        local_experts, shard_count * capacity, model_width
    )
    grad_expert_out = lax.all_to_all(send_grad, "shard", split_axis=1, concat_axis=1, tiled=True)
    gate_back_w, up_back_w, down_back_w = (
        lax.all_gather(w_gate, "ctx", axis=1, tiled=True),
        lax.all_gather(w_up, "ctx", axis=1, tiled=True),
        lax.all_gather(w_down, "ctx", axis=2, tiled=True),
    )
    grad_act = jnp.einsum(
        "lrd,lfd->lrf", grad_expert_out, down_back_w, preferred_element_type=jnp.float32
    )
    grad_gate_h = (grad_act * up_h * sig_gate * (1.0 + gate_h * (1.0 - sig_gate))).astype(
        jnp.bfloat16
    )
    grad_up_h = (grad_act * silu_h).astype(jnp.bfloat16)
    grad_down_w = jnp.einsum(
        "lrf,lrd->lfd", act_b, grad_expert_out, preferred_element_type=jnp.float32
    )
    grad_gate_w = jnp.einsum(
        "lrd,lrf->ldf", received, grad_gate_h, preferred_element_type=jnp.float32
    )
    grad_up_w = jnp.einsum("lrd,lrf->ldf", received, grad_up_h, preferred_element_type=jnp.float32)
    grad_in = (
        jnp.einsum("lrf,ldf->lrd", grad_gate_h, gate_back_w, preferred_element_type=jnp.float32)
        + jnp.einsum("lrf,ldf->lrd", grad_up_h, up_back_w, preferred_element_type=jnp.float32)
    ).astype(jnp.bfloat16)
    grad_back = lax.all_to_all(grad_in, "shard", split_axis=1, concat_axis=1, tiled=True)
    grad_hidden = grad_hidden + jnp.sum(
        grad_back.reshape(slots_all, model_width)[placed]
        .reshape(row_count, top_count, model_width)
        .astype(jnp.float32),
        axis=1,
    )
    expert_grads = (
        lax.psum_scatter(
            grad_gate_w.astype(jnp.bfloat16), "ctx", scatter_dimension=1, tiled=True
        ).astype(jnp.float32),
        lax.psum_scatter(
            grad_up_w.astype(jnp.bfloat16), "ctx", scatter_dimension=1, tiled=True
        ).astype(jnp.float32),
        lax.psum_scatter(
            grad_down_w.astype(jnp.bfloat16), "ctx", scatter_dimension=2, tiled=True
        ).astype(jnp.float32),
    )
    grad_after, grad_gain_ffn = norm_two_back(grad_hidden)
    grad_after = grad_out + grad_after
    grad_attn = grad_after.astype(jnp.bfloat16)
    grad_out_w = contract_rows(mixed_b, grad_attn)
    grad_mixed = contract_cols(grad_attn, out_w).astype(jnp.bfloat16)
    keys_back, values_back = (
        lax.all_gather(key_b, "ctx", axis=0, tiled=True),
        lax.all_gather(value_b, "ctx", axis=0, tiled=True),
    )
    grad_query_rot, grad_keys_all, grad_values_all = attend_backward(
        query_b, keys_back, values_back, same_doc, log_total, grad_mixed
    )
    grad_key_rot, grad_value = (
        lax.psum_scatter(
            grad_keys_all.astype(jnp.bfloat16), "ctx", scatter_dimension=0, tiled=True
        ).astype(jnp.float32),
        lax.psum_scatter(
            grad_values_all.astype(jnp.bfloat16), "ctx", scatter_dimension=0, tiled=True
        ).astype(jnp.float32),
    )
    grad_value_b = grad_value.astype(jnp.bfloat16)
    grad_query_lin, grad_key_lin, grad_gain_query, grad_gain_key = prepare_back(
        (grad_query_rot, grad_key_rot)
    )
    grad_query_b = grad_query_lin.astype(jnp.bfloat16)
    grad_key_b = grad_key_lin.astype(jnp.bfloat16)
    grad_query_w = contract_rows(hidden_one, grad_query_b)
    grad_key_w = contract_rows(hidden_one, grad_key_b)
    grad_value_w = contract_rows(hidden_one, grad_value_b)
    grad_hidden_one = (
        contract_cols(grad_query_b, query_w)
        + contract_cols(grad_key_b, key_w)
        + contract_cols(grad_value_b, value_w)
    )
    grad_inputs, grad_gain_attn = norm_one_back(grad_hidden_one)
    grad_inputs = grad_after + grad_inputs
    weight_grads = (
        lax.psum_scatter(grad_gain_attn, ("ctx", "shard"), scatter_dimension=0, tiled=True),
        lax.psum_scatter(grad_query_w, ("ctx", "shard"), scatter_dimension=0, tiled=True),
        lax.psum_scatter(grad_key_w, ("ctx", "shard"), scatter_dimension=0, tiled=True),
        lax.psum_scatter(grad_value_w, ("ctx", "shard"), scatter_dimension=0, tiled=True),
        lax.psum_scatter(grad_gain_query, ("ctx", "shard"), scatter_dimension=0, tiled=True),
        lax.psum_scatter(grad_gain_key, ("ctx", "shard"), scatter_dimension=0, tiled=True),
        lax.psum_scatter(grad_out_w, ("ctx", "shard"), scatter_dimension=0, tiled=True),
        lax.psum_scatter(grad_gain_ffn, ("ctx", "shard"), scatter_dimension=0, tiled=True),
        lax.psum_scatter(grad_router, ("ctx", "shard"), scatter_dimension=0, tiled=True),
    )
    factors = jnp.sqrt(clip_threshold / jnp.maximum(peak_all, clip_threshold))
    col_scale = jnp.repeat(factors, HEAD)
    query_clipped = (w_query.astype(jnp.float32) * col_scale[None, :]).astype(jnp.bfloat16)
    key_clipped = (w_key.astype(jnp.float32) * col_scale[None, :]).astype(jnp.bfloat16)
    return (
        output[None],
        grad_inputs[None],
        weight_grads[0],
        weight_grads[1],
        weight_grads[2],
        weight_grads[3],
        weight_grads[4],
        weight_grads[5],
        weight_grads[6],
        weight_grads[7],
        weight_grads[8],
        expert_grads[0],
        expert_grads[1],
        expert_grads[2],
        query_clipped,
        key_clipped,
        factors,
    )


def solution(mesh):
    return jax.shard_map(
        per_device,
        mesh=mesh,
        in_specs=(
            P("shard", "ctx", None),
            P("shard", "ctx"),
            P("shard", "ctx", None),
            P(("ctx", "shard")),
            P(("ctx", "shard"), None),
            P(("ctx", "shard"), None),
            P(("ctx", "shard"), None),
            P(("ctx", "shard")),
            P(("ctx", "shard")),
            P(("ctx", "shard"), None),
            P(("ctx", "shard")),
            P(("ctx", "shard"), None),
            P("shard", "ctx", None),
            P("shard", "ctx", None),
            P("shard", None, "ctx"),
            P(),
            P("shard", "ctx", None),
        ),
        out_specs=(
            P("shard", "ctx", None),
            P("shard", "ctx", None),
            P(("ctx", "shard")),
            P(("ctx", "shard"), None),
            P(("ctx", "shard"), None),
            P(("ctx", "shard"), None),
            P(("ctx", "shard")),
            P(("ctx", "shard")),
            P(("ctx", "shard"), None),
            P(("ctx", "shard")),
            P(("ctx", "shard"), None),
            P("shard", "ctx", None),
            P("shard", "ctx", None),
            P("shard", None, "ctx"),
            P(("ctx", "shard"), None),
            P(("ctx", "shard"), None),
            P(),
        ),
        check_vma=False,
    )
```

profile of v0, /device:TPU:0, one launch (start us, length us, event | category | flops | bytes accessed | tf_op | source)
XLA Modules:
  0.0 4251.4 jit_solution(11157558998414011357)
XLA Ops:
  12.9 42.6 %all-reduce.15 = (bf16[2048]{0:T(1024)(128)(2,1)S(1)}, bf16[2048]{0:T(1024)(128)(2,1)S(1)}, bf16[2048]{0:T(1024)(128)(2,1)S(1)}, bf16[2048]{0:T(1024)(128)(2,1)S(1)}) all-reduce(bf16[2048]{0:T(1024)(128)(2,1)S(1)} %dynamic-update-slice, bf16[2048]{0:T(1024)(128)(2,1)S(1)} %dynamic-update-slice.1, ...), channel_id=1, replica_groups=mesh['ctx'=8,'shard'=4] {'ctx','shard'}, use_global_device_ids=true, to_apply=%add.6 | all-reduce | flops 8192 | bytes 32768
  102.5 67.9 %all-gather.13.cloned.1.call-done = bf16[2048,2048]{1,0:T(8,128)(2,1)} async-done(((bf16[64,2048]{1,0:T(8,128)(2,1)}), bf16[2048,2048]{1,0:T(8,128)(2,1)}) %all-gather.13.cloned.1.call-update) | async-done | bytes 8388624 | tf_op jit(solution)/shard_map/all_gather | solution.py:142
  186.3 63.1 %all-gather.17.cloned.1.call-done = bf16[2048,2048]{1,0:T(8,128)(2,1)} async-done(((bf16[64,2048]{1,0:T(8,128)(2,1)}), bf16[2048,2048]{1,0:T(8,128)(2,1)}) %all-gather.17.cloned.1.call-update) | async-done | bytes 8388624 | tf_op jit(solution)/shard_map/all_gather | solution.py:143
  285.9 46.7 %all-gather.15.cloned.1.call-done = bf16[2048,2048]{0,1:T(8,128)(2,1)} async-done(((bf16[256,2048]{0,1:T(8,128)(2,1)}), bf16[2048,2048]{0,1:T(8,128)(2,1)}) %all-gather.15.cloned.1.call-update) | async-done | bytes 8388624 | tf_op jit(solution)/shard_map/all_gather | solution.py:172
  345.1 69.9 %all-gather.19.cloned.1.call-done = bf16[2048,2048]{1,0:T(8,128)(2,1)} async-done(((bf16[256,2048]{1,0:T(8,128)(2,1)}), bf16[2048,2048]{1,0:T(8,128)(2,1)}) %all-gather.19.cloned.1.call-update) | async-done | bytes 8388624 | tf_op jit(solution)/shard_map/all_gather | solution.py:173
  415.0 135.4 %while.30 = (s32[]{:T(128)}, bf16[16,256,128]{1,2,0:T(8,128)(2,1)}, f32[16,256]{1,0:T(8,128)}, f32[16]{0:T(128)S(1)}, s32[16]{0:T(128)S(1)}, /*index=5*/bf16[256...) while((s32[]{:T(128)}, bf16[16,256,128]{1,2,0:T(8,128)(2,1)}, ...), condition=%wide.region_7.8_spmd.clone, body=%wide.region_3.7_spmd.clone.sunk | while | flops 273678080 | bytes 7557847 | solution.py:68
  608.1 243.0 %all-gather = bf16[32,64,16]{1,2,0:T(8,128)(2,1)S(1)} all-gather(bf16[1,64,16]{1,2,0:T(8,128)(2,1)S(1)} %bitcast.171), channel_id=1, replica_groups=mesh['ctx'=8,'shard'=4] {'ctx','shard'}, dimensions={0}, use_global_device_ids=true | all-gather | bytes 67584 | tf_op jit(solution)/shard_map/all_gather | solution.py:148
  868.3 35.8 gather_fusion.2
  1014.6 97.3 %all-to-all-done.2 = bf16[4,1024,2048]{2,0,1:T(4,128)(2,1)} async-done(((bf16[4,1024,2048]{2,0,1:T(4,128)(2,1)}), bf16[4,1024,2048]{2,0,1:T(4,128)(2,1)}, u32[]{:S(2)}, u32[]{:S(2)}) %all-to-all-start.2) | async-done | bytes 16777248 | tf_op jit(solution)/shard_map/all_to_all | solution.py:244
  1111.9 52.4 %multiply_convert_fusion.1 = (bf16[4,1024,1024]{2,1,0:T(8,128)(2,1)}, bf16[4,1024,1024]{2,1,0:T(8,128)(2,1)}, bf16[4,1024,1024]{2,1,0:T(8,128)(2,1)}) fusion(f32[4,1024,1024]{2,1,0:T(8,128)} %fusion.90, f32[4,1024,1024]{2,1,0:T(8,128)} %fusion.91, bf16[4,1024,2048]{2,1,0:T(8,128)(2,1)} %all-gather.27.cloned.1.call-done, ...), kind=kOutput, calls=%fused_computation.55 | convolution fusion | flops 17242783744 | bytes 92274688 | tf_op jit(solution)/shard_map/lrd,lfd->lrf/dot_general | solution.py:250
  1300.2 102.2 %all-to-all-done.1 = bf16[4,1024,2048]{2,0,1:T(4,128)(2,1)} async-done(((bf16[4,1024,2048]{2,0,1:T(4,128)(2,1)}), bf16[4,1024,2048]{2,0,1:T(4,128)(2,1)}, u32[]{:S(2)}, u32[]{:S(2)}) %all-to-all-start.1) | async-done | bytes 16777248 | tf_op jit(solution)/shard_map/all_to_all | solution.py:223
  1462.8 128.3 %all-to-all-done.3 = bf16[4,1024,2048]{2,0,1:T(4,128)(2,1)} async-done(((bf16[4,1024,2048]{2,0,1:T(4,128)(2,1)}), bf16[4,1024,2048]{2,0,1:T(4,128)(2,1)}, u32[]{:S(2)}, u32[]{:S(2)}) %all-to-all-start.3) | async-done | bytes 16777248 | tf_op jit(solution)/shard_map/all_to_all | solution.py:268
  1665.1 308.7 %while.31 = (s32[]{:T(128)}, f32[256,2048]{0,1:T(8,128)}, bf16[2048,2048]{0,1:T(8,128)(2,1)}, bf16[2048,2048]{1,0:T(8,128)(2,1)}, s32[16]{0:T(128)S(1)}, /*index...) while((s32[]{:T(128)}, f32[256,2048]{0,1:T(8,128)}, ...), condition=%wide.region_28.29_spmd.clone, body=%wide.region_26.28_spmd.clone.sunk | while | flops 676888320 | bytes 38683972 | solution.py:107
  1976.7 86.6 %fusion.38 = bf16[4,1024,2048]{2,1,0:T(8,128)(2,1)} fusion(bf16[4,1024,1024]{2,1,0:T(8,128)(2,1)} %get-tuple-element.347, bf16[4,1024,2048]{2,0,1:T(4,128)(2,1)} %all-to-all-done.2), kind=kOutput, calls=%fused_computation.67 | convolution fusion | flops 17188257792 | bytes 41943040 | tf_op jit(solution)/shard_map/lrf,lrd->lfd/dot_general | solution.py:257
  2173.1 45.9 %pmax.7 = f32[16]{0:T(128)S(1)} all-reduce(f32[16]{0:T(128)S(1)} %copy-done.85), channel_id=1, replica_groups=mesh['ctx'=8,'shard'=4] {'ctx','shard'}, use_global_device_ids=true, to_apply=%region_50.51 | all-reduce | flops 16 | bytes 128 | tf_op jit(solution)/shard_map/pmax | solution.py:176
  2220.9 72.9 %reduce-scatter.31.cloned.1.call-done = f32[64,16]{1,0:T(8,128)} async-done(((f32[2048,16]{1,0:T(8,128)}), f32[64,16]{1,0:T(8,128)}) %reduce-scatter.31.cloned.1.call-update) | async-done | bytes 4112
  2312.3 38.9 all-reduce.14
  2357.1 104.7 %reduce-scatter.29.cloned.1.call-done = bf16[4,1024,256]{2,1,0:T(8,128)(2,1)} async-done(((bf16[4,1024,2048]{2,1,0:T(8,128)(2,1)}), bf16[4,1024,256]{2,1,0:T(8,128)(2,1)}) %reduce-scatter.29.cloned.1.call-update) | async-done | bytes 2097168 | tf_op jit(solution)/shard_map/reduce_scatter | solution.py:282
  2465.8 165.0 %reduce-scatter.25.cloned.1.call-done = bf16[4,256,1024]{2,1,0:T(8,128)(2,1)} async-done(((bf16[4,2048,1024]{2,1,0:T(8,128)(2,1)}), bf16[4,256,1024]{2,1,0:T(8,128)(2,1)}) %reduce-scatter.25.cloned.1.call-update) | async-done | bytes 2097168 | tf_op jit(solution)/shard_map/reduce_scatter | solution.py:276
  2634.9 164.9 %reduce-scatter.27.cloned.1.call-done = bf16[4,256,1024]{2,1,0:T(8,128)(2,1)} async-done(((bf16[4,2048,1024]{2,1,0:T(8,128)(2,1)}), bf16[4,256,1024]{2,1,0:T(8,128)(2,1)}) %reduce-scatter.27.cloned.1.call-update) | async-done | bytes 2097168 | tf_op jit(solution)/shard_map/reduce_scatter | solution.py:279
  2803.8 354.7 %reduce-scatter.23.cloned.1.call-done = f32[64,2048]{1,0:T(8,128)} async-done(((f32[2048,2048]{1,0:T(8,128)}), f32[64,2048]{1,0:T(8,128)}) %reduce-scatter.23.cloned.1.call-update) | async-done | bytes 524304 | tf_op jit(solution)/shard_map/reduce_scatter | solution.py:329
  3158.5 361.9 %reduce-scatter.19.cloned.1.call-done = f32[64,2048]{1,0:T(8,128)} async-done(((f32[2048,2048]{1,0:T(8,128)}), f32[64,2048]{1,0:T(8,128)}) %reduce-scatter.19.cloned.1.call-update) | async-done | bytes 524304 | tf_op jit(solution)/shard_map/reduce_scatter | solution.py:325
  3520.4 362.0 %reduce-scatter.17.cloned.1.call-done = f32[64,2048]{1,0:T(8,128)} async-done(((f32[2048,2048]{1,0:T(8,128)}), f32[64,2048]{1,0:T(8,128)}) %reduce-scatter.17.cloned.1.call-update) | async-done | bytes 524304 | tf_op jit(solution)/shard_map/reduce_scatter | solution.py:324
  3882.4 362.0 %reduce-scatter.21.cloned.1.call-done = f32[64,2048]{1,0:T(8,128)} async-done(((f32[2048,2048]{1,0:T(8,128)}), f32[64,2048]{1,0:T(8,128)}) %reduce-scatter.21.cloned.1.call-update) | async-done | bytes 524304 | tf_op jit(solution)/shard_map/reduce_scatter | solution.py:326
  (733 shorter events, 1112.8 us)
Async XLA Ops:
  7.2 84.1 %all-gather.11.cloned.1.call-start = ((), (), s32[]{:S(2)}) async-start(), calls=%async_computation.14 | async-start | bytes 8650752 | tf_op jit(solution)/shard_map/all_gather | solution.py:141
  7.9 162.5 %all-gather.13.cloned.1.call-start = ((), (), s32[]{:S(2)}) async-start(), calls=%async_computation.15 | async-start | bytes 8650752 | tf_op jit(solution)/shard_map/all_gather | solution.py:142
  8.7 240.8 %all-gather.17.cloned.1.call-start = ((), (), s32[]{:S(2)}) async-start(), calls=%async_computation.17 | async-start | bytes 8650752 | tf_op jit(solution)/shard_map/all_gather | solution.py:143
  9.4 323.3 %all-gather.15.cloned.1.call-start = ((), (), s32[]{:S(2)}) async-start(), calls=%async_computation.16 | async-start | bytes 9437184 | tf_op jit(solution)/shard_map/all_gather | solution.py:172
  186.3 228.7 %all-gather.19.cloned.1.call-start = ((), (), s32[]{:S(2)}) async-start(), calls=%async_computation.18 | async-start | bytes 9437184 | tf_op jit(solution)/shard_map/all_gather | solution.py:173
  256.2 294.1 %all-gather.21.cloned.1.call-start = ((), (), s32[]{:S(2)}) async-start(), calls=%async_computation.19 | async-start | bytes 8650752 | tf_op jit(solution)/shard_map/all_gather | solution.py:146
  256.8 703.3 %all-gather.23.cloned.1.call-start = ((), (), s32[]{:S(2)}) async-start(), calls=%async_computation.20 | async-start | bytes 18874368 | tf_op jit(solution)/shard_map/all_gather | solution.py:211
  257.6 729.8 %all-gather.25.cloned.1.call-start = ((), (), s32[]{:S(2)}) async-start(), calls=%async_computation.21 | async-start | bytes 18874368 | tf_op jit(solution)/shard_map/all_gather | solution.py:212
  258.3 756.2 %all-gather.27.cloned.1.call-start = ((), (), s32[]{:S(2)}) async-start(), calls=%async_computation.22 | async-start | bytes 18874368 | tf_op jit(solution)/shard_map/all_gather | solution.py:213
  556.8 296.0 %copy-start.16 = (bf16[256,2048]{1,0:T(8,128)(2,1)}, bf16[256,2048]{1,0:T(8,128)(2,1)S(1)}, u32[]{:S(2)}) copy-start(bf16[256,2048]{1,0:T(8,128)(2,1)S(1)} %multiply_convert_fusion.4) | copy-start | bytes 3145732
  601.0 325.4 %all-to-all-start = ((bf16[4,1024,2048]{2,0,1:T(4,128)(2,1)}), bf16[4,1024,2048]{2,0,1:T(4,128)(2,1)}, u32[]{:S(2)}, u32[]{:S(2)}) async-start(bf16[4,1024,2048]{2,0,1:T(4,128)(2,1)} %copy.135), calls=%async_computation | async-start | bytes 33554432 | tf_op jit(solution)/shard_map/all_to_all | solution.py:209
  926.3 185.6 %all-to-all-start.2 = ((bf16[4,1024,2048]{2,0,1:T(4,128)(2,1)}), bf16[4,1024,2048]{2,0,1:T(4,128)(2,1)}, u32[]{:S(2)}, u32[]{:S(2)}) async-start(bf16[4,1024,2048]{2,0,1:T(4,128)(2,1)} %copy.143), calls=%async_computation.2 | async-start | bytes 33554432 | tf_op jit(solution)/shard_map/all_to_all | solution.py:244
  1213.5 188.9 %all-to-all-start.1 = ((bf16[4,1024,2048]{2,0,1:T(4,128)(2,1)}), bf16[4,1024,2048]{2,0,1:T(4,128)(2,1)}, u32[]{:S(2)}, u32[]{:S(2)}) async-start(bf16[4,1024,2048]{2,0,1:T(4,128)(2,1)} %copy.138), calls=%async_computation.1 | async-start | bytes 33554432 | tf_op jit(solution)/shard_map/all_to_all | solution.py:223
  1402.4 188.7 %all-to-all-start.3 = ((bf16[4,1024,2048]{2,0,1:T(4,128)(2,1)}), bf16[4,1024,2048]{2,0,1:T(4,128)(2,1)}, u32[]{:S(2)}, u32[]{:S(2)}) async-start(bf16[4,1024,2048]{2,0,1:T(4,128)(2,1)} %copy.145), calls=%async_computation.3 | async-start | bytes 33554432 | tf_op jit(solution)/shard_map/all_to_all | solution.py:268
  1409.4 715.6 %reduce-scatter.13.cloned.1.call-start = ((), (), s32[]{:S(2)}) async-start(), calls=%async_computation.23 | async-start | bytes 9437184 | tf_op jit(solution)/shard_map/reduce_scatter | solution.py:299
  1973.9 189.0 %reduce-scatter.15.cloned.1.call-start = ((), (), s32[]{:S(2)}) async-start(), calls=%async_computation.24 | async-start | bytes 9437184 | tf_op jit(solution)/shard_map/reduce_scatter | solution.py:302
  1974.6 319.2 %reduce-scatter.31.cloned.1.call-start = ((), (), s32[]{:S(2)}) async-start(), calls=%async_computation.32 | async-start | bytes 1081344
  1976.7 485.1 %reduce-scatter.29.cloned.1.call-start = ((), (), s32[]{:S(2)}) async-start(), calls=%async_computation.31 | async-start | bytes 18874368 | tf_op jit(solution)/shard_map/reduce_scatter | solution.py:282
  2063.4 567.4 %reduce-scatter.25.cloned.1.call-start = ((), (), s32[]{:S(2)}) async-start(), calls=%async_computation.29 | async-start | bytes 18874368 | tf_op jit(solution)/shard_map/reduce_scatter | solution.py:276
  2089.1 710.7 %reduce-scatter.27.cloned.1.call-start = ((), (), s32[]{:S(2)}) async-start(), calls=%async_computation.30 | async-start | bytes 18874368 | tf_op jit(solution)/shard_map/reduce_scatter | solution.py:279
  2114.8 1043.8 %reduce-scatter.23.cloned.1.call-start = ((), (), s32[]{:S(2)}) async-start(), calls=%async_computation.28 | async-start | bytes 17301504 | tf_op jit(solution)/shard_map/reduce_scatter | solution.py:329
  2124.8 1395.6 %reduce-scatter.19.cloned.1.call-start = ((), (), s32[]{:S(2)}) async-start(), calls=%async_computation.26 | async-start | bytes 17301504 | tf_op jit(solution)/shard_map/reduce_scatter | solution.py:325
  2146.5 1735.9 %reduce-scatter.17.cloned.1.call-start = ((), (), s32[]{:S(2)}) async-start(), calls=%async_computation.25 | async-start | bytes 17301504 | tf_op jit(solution)/shard_map/reduce_scatter | solution.py:324
  2162.8 2081.6 %reduce-scatter.21.cloned.1.call-start = ((), (), s32[]{:S(2)}) async-start(), calls=%async_computation.27 | async-start | bytes 17301504 | tf_op jit(solution)/shard_map/reduce_scatter | solution.py:326
  (119 other events, 2167.2 us)
Sparse Core Ops, SparseCore 0:
  10.9 80.3 all-gather.10
  94.2 76.1 all-gather.12
  173.3 76.1 all-gather.16
  251.5 81.1 all-gather.14
  334.7 80.2 all-gather.18
  417.7 76.0 all-gather.20
  495.4 149.8 all-gather.22
  646.9 149.2 all-gather.24
  797.8 150.3 all-gather.26
  1974.0 94.1 reduce-scatter.12
  2070.4 87.9 reduce-scatter.14
  2160.5 133.2 reduce-scatter.30
  2296.3 165.4 reduce-scatter.28
  2464.1 166.6 reduce-scatter.24
  2633.1 166.6 reduce-scatter.26
  2802.6 355.9 reduce-scatter.22
  3161.4 359.0 reduce-scatter.18
  3523.3 359.1 reduce-scatter.16
  3885.4 359.0 reduce-scatter.20
where the time goes:
time: 4270 us; the launch traced here: 4250 us
  waiting for transfers between devices  2560 us (60%)
  matrix products  624 us (15%)
  local copies, waits for them, and re-layouts  485 us (11%)
  blocking collectives  381 us (9%)
  other arithmetic  98.9 us (2%)
  loops' own time  53.2 us (1%)
    reduce_scatter x1, waiting for transfers between devices, per_device(): lax.psum_scatter(grad_value_w, ('ctx', 'shard'), scatter_dimension=0, til...  362 us
    reduce_scatter x1, waiting for transfers between devices, per_device(): lax.psum_scatter(grad_query_w, ('ctx', 'shard'), scatter_dimension=0, til...  362 us
    reduce_scatter x1, waiting for transfers between devices, per_device(): lax.psum_scatter(grad_key_w, ('ctx', 'shard'), scatter_dimension=0, tiled...  362 us
    reduce_scatter x1, waiting for transfers between devices, per_device(): lax.psum_scatter(grad_out_w, ('ctx', 'shard'), scatter_dimension=0, tiled...  355 us
    all_gather x1, blocking collectives, per_device(): lax.all_gather(w_router, ('ctx', 'shard'), axis=0, tiled=True)  243 us
    reduce_scatter x1, waiting for transfers between devices, per_device(): lax.psum_scatter(grad_gate_w.astype(jnp.bfloat16), 'ctx', scatter_dimensi...  165 us
    reduce_scatter x1, waiting for transfers between devices, per_device(): lax.psum_scatter(grad_up_w.astype(jnp.bfloat16), 'ctx', scatter_dimension...  165 us
    all_to_all x1, waiting for transfers between devices, per_device(): lax.all_to_all(grad_in, 'shard', split_axis=1, concat_axis=1, tiled=True)  128 us
  transfers between devices with their start and end apart: 23, of which 16 were waited for; matrix products, arithmetic and copies ran while one was open for 18% of the time, Pallas kernels for 0%

commit v1 on v0

v1 whole, which is shorter than its diff:
```python
import functools

import jax
import jax.numpy as jnp
from jax import lax
from jax.experimental import pallas as pl
from jax.experimental.pallas import tpu as pltpu
from jax.sharding import PartitionSpec as P

HEADS = 16
HEAD = 128
SCALE = HEAD ** (-0.5)
Q_BLOCK = 256
LANES = 128
EXPERT_GROUP = 2

norm_eps = 1e-06
rope_base = 10000.0
f32 = jnp.float32
bf16 = jnp.bfloat16


def dot(a, b):
    return jnp.dot(a, b, preferred_element_type=f32)


def contract_rows(a, b):
    return lax.dot_general(a, b, (((0,), (0,)), ((), ())), preferred_element_type=f32)


def contract_cols(a, b):
    return lax.dot_general(a, b, (((1,), (1,)), ((), ())), preferred_element_type=f32)


def inverse_rms(values):
    return lax.rsqrt(jnp.mean(values * values, axis=-1, keepdims=True) + norm_eps)


def rope_tables(count):
    half = HEAD // 2
    freq = rope_base ** (-jnp.arange(half).astype(f32) / half)
    angles = jnp.arange(count).astype(f32)[:, None] * freq[None, :]
    return jnp.cos(angles), jnp.sin(angles)


def rotate(values, cosine, sine):
    parts = []
    for col in range(0, values.shape[1], HEAD):
        a = values[:, col : col + HEAD // 2]
        b = values[:, col + HEAD // 2 : col + HEAD]
        parts += [a * cosine - b * sine, b * cosine + a * sine]
    return jnp.concatenate(parts, axis=1)


def attend_forward_kernel(q_ref, k_ref, v_ref, doc_q_ref, doc_k_ref, o_ref, lse_ref, peak_ref):
    s = SCALE * contract_cols(q_ref[...], k_ref[...])
    s = jnp.where(doc_q_ref[...] == doc_k_ref[...], s, -1e30)
    top = jnp.max(s, axis=1, keepdims=True)
    e = jnp.exp(s - top)
    total = jnp.sum(e, axis=1, keepdims=True)
    p = (e * (1.0 / total)).astype(bf16)
    o_ref[...] = dot(p, v_ref[...]).astype(bf16)
    lse_ref[0] = top + jnp.log(total)
    peak = jnp.broadcast_to(jnp.max(top, axis=0, keepdims=True), peak_ref.shape[1:])

    @pl.when(pl.program_id(1) == 0)
    def _():
        peak_ref[0] = peak

    @pl.when(pl.program_id(1) > 0)
    def _():
        peak_ref[0] = jnp.maximum(peak_ref[0], peak)


def attend_backward_kernel(
    q_ref, k_ref, v_ref, doc_q_ref, doc_k_ref, lse_ref, do_ref, dq_ref, dk_ref, dv_ref
):
    q, k, v, do = q_ref[...], k_ref[...], v_ref[...], do_ref[...]
    s = SCALE * contract_cols(q, k)
    p = jnp.where(doc_q_ref[...] == doc_k_ref[...], jnp.exp(s - lse_ref[0]), 0.0)
    dp = contract_cols(do, v)
    inner = jnp.sum(p * dp, axis=1, keepdims=True)
    ds = (p * (dp - inner)).astype(bf16)
    dq_ref[...] = SCALE * dot(ds, k)
    dk = SCALE * contract_rows(ds, q)
    dv = contract_rows(p.astype(bf16), do)

    @pl.when(pl.program_id(1) == 0)
    def _():
        dk_ref[...] = dk
        dv_ref[...] = dv

    @pl.when(pl.program_id(1) > 0)
    def _():
        dk_ref[...] += dk
        dv_ref[...] += dv


def attend_specs(count):
    block = pl.BlockSpec((Q_BLOCK, HEAD), lambda h, i: (i, h))
    whole = pl.BlockSpec((count, HEAD), lambda h, i: (0, h))
    doc_q = pl.BlockSpec((Q_BLOCK, 1), lambda h, i: (i, 0))
    doc_k = pl.BlockSpec((1, count), lambda h, i: (0, 0))
    lse = pl.BlockSpec((1, Q_BLOCK, 1), lambda h, i: (h, i, 0))
    return block, whole, doc_q, doc_k, lse


def attend_forward(q, k, v, docs):
    count, width = q.shape
    heads = width // HEAD
    block, whole, doc_q, doc_k, lse = attend_specs(count)
    return pl.pallas_call(
        attend_forward_kernel,
        grid=(heads, count // Q_BLOCK),
        in_specs=[block, whole, whole, doc_q, doc_k],
        out_specs=[block, lse, pl.BlockSpec((1, 8, 128), lambda h, i: (h, 0, 0))],
        out_shape=[
            jax.ShapeDtypeStruct((count, width), bf16),
            jax.ShapeDtypeStruct((heads, count, 1), f32),
            jax.ShapeDtypeStruct((heads, 8, 128), f32),
        ],
        compiler_params=pltpu.CompilerParams(vmem_limit_bytes=48 << 20),
        cost_estimate=pl.CostEstimate(
            flops=4 * count * count * width,
            transcendentals=heads * count * count,
            bytes_accessed=8 * count * width,
        ),
    )(q, k, v, docs[:, None], docs[None, :])


def attend_backward(q, k, v, docs, log_total, grad):
    count, width = q.shape
    heads = width // HEAD
    block, whole, doc_q, doc_k, lse = attend_specs(count)
    return pl.pallas_call(
        attend_backward_kernel,
        grid=(heads, count // Q_BLOCK),
        in_specs=[block, whole, whole, doc_q, doc_k, lse, block],
        out_specs=[block, whole, whole],
        out_shape=[jax.ShapeDtypeStruct((count, width), f32)] * 3,
        compiler_params=pltpu.CompilerParams(vmem_limit_bytes=56 << 20),
        cost_estimate=pl.CostEstimate(
            flops=10 * count * count * width,
            transcendentals=heads * count * count,
            bytes_accessed=20 * count * width,
        ),
    )(q, k, v, docs[:, None], docs[None, :], log_total, grad)


MESH = pl.DeviceIdType.MESH
ANY = pl.BlockSpec(memory_space=pl.ANY)
VMEM = pl.BlockSpec(memory_space=pltpu.VMEM)


def greet(axis, peers):
    barrier = pltpu.get_barrier_semaphore()
    for there, peer in peers:

        @pl.when(there)
        def _():
            pl.semaphore_signal(barrier, inc=1, device_id={axis: peer}, device_id_type=MESH)

    pl.semaphore_wait(barrier, sum(there.astype(jnp.int32) for there, _ in peers))


def ring_peers(axis):
    n, me = lax.axis_size(axis), lax.axis_index(axis)
    return [lax.rem(me + k, n) for k in range(n)], [lax.rem(me + n - k, n) for k in range(n)]


def greet_ring(axis):
    barrier = pltpu.get_barrier_semaphore()
    to, _ = ring_peers(axis)
    for peer in to[1:]:
        pl.semaphore_signal(barrier, inc=1, device_id={axis: peer}, device_id_type=MESH)
    pl.semaphore_wait(barrier, len(to) - 1)


def exchange_kernel(axis, count, *refs):
    ins, outs = refs[:count], refs[count : 2 * count]
    own_sem, send, recv = refs[2 * count :]
    me = lax.axis_index(axis)
    to, source = ring_peers(axis)
    greet_ring(axis)
    copies = []
    for k in range(1, len(to)):
        for i in range(count):
            copies.append(
                pltpu.make_async_remote_copy(
                    src_ref=ins[i].at[to[k]],
                    dst_ref=outs[i].at[me],
                    send_sem=send.at[i, k],
                    recv_sem=recv.at[i, k],
                    device_id={axis: to[k]},
                    device_id_type=MESH,
                )
            )
            copies[-1].start()
    own = [
        pltpu.make_async_copy(ins[i].at[me], outs[i].at[me], own_sem.at[i]) for i in range(count)
    ]
    for copy in own:
        copy.start()
    for copy in own:
        copy.wait()
    for k in range(1, len(to)):
        for i in range(count):
            pltpu.make_async_remote_copy(
                src_ref=ins[i].at[to[k]],
                dst_ref=outs[i].at[source[k]],
                send_sem=send.at[i, k],
                recv_sem=recv.at[i, k],
                device_id={axis: to[k]},
                device_id_type=MESH,
            ).wait()


def gather_kernel(axis, count, *refs):
    ins, outs = refs[:count], refs[count : 2 * count]
    own_sem, send, recv = refs[2 * count :]
    me = lax.axis_index(axis)
    to, source = ring_peers(axis)
    greet_ring(axis)
    for i in range(count):
        for k in range(1, len(to)):
            pltpu.make_async_remote_copy(
                src_ref=ins[i],
                dst_ref=outs[i].at[me],
                send_sem=send.at[i, k],
                recv_sem=recv.at[i, k],
                device_id={axis: to[k]},
                device_id_type=MESH,
            ).start()
    own = [pltpu.make_async_copy(ins[i], outs[i].at[me], own_sem.at[i]) for i in range(count)]
    for copy in own:
        copy.start()
    for copy in own:
        copy.wait()
    for i in range(count):
        for k in range(1, len(to)):
            pltpu.make_async_remote_copy(
                src_ref=ins[i],
                dst_ref=outs[i].at[source[k]],
                send_sem=send.at[i, k],
                recv_sem=recv.at[i, k],
                device_id={axis: to[k]},
                device_id_type=MESH,
            ).wait()


def reduce_kernel(axis, count, *refs):
    ins, outs, bufs = refs[:count], refs[count : 2 * count], refs[2 * count : 3 * count]
    send, recv = refs[3 * count :]
    me = lax.axis_index(axis)
    to, _ = ring_peers(axis)
    greet_ring(axis)

    def copy(i, k):
        return pltpu.make_async_remote_copy(
            src_ref=ins[i].at[to[k]],
            dst_ref=bufs[i].at[k - 1],
            send_sem=send.at[i, k],
            recv_sem=recv.at[i, k],
            device_id={axis: to[k]},
            device_id_type=MESH,
        )

    for i in range(count):
        for k in range(1, len(to)):
            copy(i, k).start()
    for i in range(count):
        for k in range(1, len(to)):
            copy(i, k).wait_recv()
        rows = outs[i].shape[0]
        step = 8 if rows % 32 else 32

        @pl.loop(0, rows // step)
        def _(j):
            at = pl.ds(pl.multiple_of(j * step, step), step)
            total = ins[i][me, at].astype(f32)
            for k in range(1, len(to)):
                total = total + bufs[i][k - 1, at].astype(f32)
            outs[i][at] = total

    for i in range(count):
        for k in range(1, len(to)):
            copy(i, k).wait_send()


def many_sum_kernel(axis, x_ref, o_ref, buf, send, recv):
    me = lax.axis_index(axis)
    to, source = ring_peers(axis)
    greet_ring(axis)

    def copy(k):
        return pltpu.make_async_remote_copy(
            src_ref=x_ref,
            dst_ref=buf.at[k - 1],
            send_sem=send.at[k],
            recv_sem=recv.at[k],
            device_id={axis: to[k]},
            device_id_type=MESH,
        )

    for k in range(1, len(to)):
        copy(k).start()
    total = x_ref[...]
    for k in range(1, len(to)):
        copy(k).wait_recv()
        total = total + buf[k - 1]
    o_ref[...] = total
    for k in range(1, len(to)):
        copy(k).wait_send()


def line_gather_kernel(chunks, x_ref, o_ref, own_sem, send_r, send_l, send_p, recv_r, recv_l, recv_p):
    n, me = lax.axis_size("ctx") // 2, lax.axis_index("ctx")
    place, core = lax.div(me, 2), lax.rem(me, 2)
    partner = me + 1 - 2 * core
    not_first, not_last = place > 0, place < n - 1
    rows = x_ref.shape[0] // chunks
    greet("ctx", [(place >= 0, partner), (not_last, me + 2), (not_first, me - 2)])
    own = pltpu.make_async_copy(x_ref, o_ref.at[me], own_sem)
    own.start()

    def copy(block, k, c, target, send, recv):
        part = pl.ds(c * rows, rows)
        return pltpu.make_async_remote_copy(
            src_ref=x_ref.at[part] if k == 0 else o_ref.at[block, part],
            dst_ref=o_ref.at[block, part],
            send_sem=send,
            recv_sem=recv,
            device_id={"ctx": target},
            device_id_type=MESH,
        )

    def right(k, c):
        return copy(me - 2 * k, k, c, me + 2, send_r.at[k, c], recv_r.at[k, c])

    def left(k, c):
        return copy(me + 2 * k, k, c, me - 2, send_l.at[k, c], recv_l.at[k, c])

    def across(k, c, sign):
        i = k if sign < 0 else n - 1 + k
        return copy(me + sign * 2 * k, k, c, partner, send_p.at[i, c], recv_p.at[i, c])

    def arrived(block, c, recv):
        part = pl.ds(c * rows, rows)
        pltpu.make_async_remote_copy(
            src_ref=x_ref.at[part],
            dst_ref=o_ref.at[block, part],
            send_sem=own_sem,
            recv_sem=recv,
            device_id={"ctx": partner},
            device_id_type=MESH,
        ).wait_recv()

    for k in range(n):
        for c in range(chunks):

            @pl.when(place >= k)
            def _():
                if k:
                    arrived(me - 2 * k, c, recv_r.at[k - 1, c])

                @pl.when(not_last)
                def _():
                    right(k, c).start()

                across(k, c, -1).start()

            @pl.when(place + k <= n - 1)
            def _():
                if k:
                    arrived(me + 2 * k, c, recv_l.at[k - 1, c])

                @pl.when(not_first)
                def _():
                    left(k, c).start()

                if k:
                    across(k, c, 1).start()

    own.wait()
    for k in range(n):
        for c in range(chunks):

            @pl.when(place >= k)
            def _():
                @pl.when(not_last)
                def _():
                    right(k, c).wait_send()

                across(k, c, -1).wait_send()
                arrived(partner - 2 * k, c, recv_p.at[k, c])

            @pl.when(place + k <= n - 1)
            def _():
                @pl.when(not_first)
                def _():
                    left(k, c).wait_send()

                if k:
                    across(k, c, 1).wait_send()
                    arrived(partner + 2 * k, c, recv_p.at[n - 1 + k, c])


def line_reduce_kernel(
    chunks, x_ref, o_ref, pair, from_left, from_right, out, send_p, recv_p, send_s, recv_r, recv_l
):
    n, me = lax.axis_size("ctx") // 2, lax.axis_index("ctx")
    place, core = lax.div(me, 2), lax.rem(me, 2)
    partner = me + 1 - 2 * core
    not_first, not_last = place > 0, place < n - 1
    rows = x_ref.shape[1] // chunks
    greet("ctx", [(place >= 0, partner), (not_last, me + 2), (not_first, me - 2)])
    order = []
    for j in range(n):
        order += [p for p in (n - 1 - j, j) if p not in order]

    def at(c):
        return pl.ds(c * rows, rows)

    def across(p, c):
        return pltpu.make_async_remote_copy(
            src_ref=x_ref.at[2 * p + 1 - core, at(c)],
            dst_ref=pair.at[p, at(c)],
            send_sem=send_p.at[p, c],
            recv_sem=recv_p.at[p, c],
            device_id={"ctx": partner},
            device_id_type=MESH,
        )

    def right(p, c):
        return pltpu.make_async_remote_copy(
            src_ref=out.at[p, at(c)],
            dst_ref=from_left.at[p, at(c)],
            send_sem=send_s.at[p, c],
            recv_sem=recv_r.at[p, c],
            device_id={"ctx": me + 2},
            device_id_type=MESH,
        )

    def left(p, c):
        return pltpu.make_async_remote_copy(
            src_ref=out.at[p, at(c)],
            dst_ref=from_right.at[p, at(c)],
            send_sem=send_s.at[p, c],
            recv_sem=recv_l.at[p, c],
            device_id={"ctx": me - 2},
            device_id_type=MESH,
        )

    for p in order:
        for c in range(chunks):
            across(p, c).start()
    for p in order:
        for c in range(chunks):
            across(p, c).wait_recv()

            @pl.when(place < p)
            def _():
                total = x_ref[2 * p + core, at(c)].astype(f32) + pair[p, at(c)].astype(f32)

                @pl.when(not_first)
                def _():
                    right(p, c).wait_recv()
                    out[p, at(c)] = (total + from_left[p, at(c)].astype(f32)).astype(bf16)

                @pl.when(place == 0)
                def _():
                    out[p, at(c)] = total.astype(bf16)

                right(p, c).start()

            @pl.when(place > p)
            def _():
                total = x_ref[2 * p + core, at(c)].astype(f32) + pair[p, at(c)].astype(f32)

                @pl.when(not_last)
                def _():
                    left(p, c).wait_recv()
                    out[p, at(c)] = (total + from_right[p, at(c)].astype(f32)).astype(bf16)

                @pl.when(place == n - 1)
                def _():
                    out[p, at(c)] = total.astype(bf16)

                left(p, c).start()

    for p in range(n):
        for c in range(chunks):

            @pl.when(place == p)
            def _():
                o_ref[at(c)] = x_ref[2 * p + core, at(c)].astype(f32) + pair[p, at(c)].astype(f32)
                if p > 0:
                    right(p, c).wait_recv()
                    o_ref[at(c)] += from_left[p, at(c)].astype(f32)
                if p < n - 1:
                    left(p, c).wait_recv()
                    o_ref[at(c)] += from_right[p, at(c)].astype(f32)

    for p in range(n):
        for c in range(chunks):
            across(p, c).wait_send()

            @pl.when(place < p)
            def _():
                right(p, c).wait_send()

            @pl.when(place > p)
            def _():
                left(p, c).wait_send()


def remote_params(collective_id, megabytes=None):
    limit = None if megabytes is None else megabytes << 20
    return pltpu.CompilerParams(
        collective_id=collective_id, has_side_effects=True, vmem_limit_bytes=limit
    )


def direct_call(kernel, axis, collective_id, arrays, shapes):
    count = len(arrays)
    n = lax.axis_size(axis)
    sem = pltpu.SemaphoreType.DMA
    return pl.pallas_call(
        functools.partial(kernel, axis, count),
        out_shape=[jax.ShapeDtypeStruct(s, a.dtype) for s, a in zip(shapes, arrays)],
        in_specs=[ANY] * count,
        out_specs=[ANY] * count,
        scratch_shapes=[sem((count,)), sem((count, n)), sem((count, n))],
        compiler_params=remote_params(collective_id, 8),
    )(*arrays)


def exchange(axis, collective_id, *arrays):
    return direct_call(exchange_kernel, axis, collective_id, arrays, [a.shape for a in arrays])


def gather(axis, collective_id, *arrays):
    n = lax.axis_size(axis)
    return direct_call(gather_kernel, axis, collective_id, arrays, [(n, *a.shape) for a in arrays])


def reduce(axis, collective_id, *arrays):
    count, n = len(arrays), lax.axis_size(axis)
    sem = pltpu.SemaphoreType.DMA
    return pl.pallas_call(
        functools.partial(reduce_kernel, axis, count),
        out_shape=[jax.ShapeDtypeStruct(a.shape[1:], f32) for a in arrays],
        in_specs=[VMEM] * count,
        out_specs=[VMEM] * count,
        scratch_shapes=[pltpu.VMEM((n - 1, *a.shape[1:]), a.dtype) for a in arrays]
        + [sem((count, n)), sem((count, n))],
        compiler_params=remote_params(collective_id, 48),
    )(*arrays)


def many_sum(axis, collective_id, x):
    n = lax.axis_size(axis)
    sem = pltpu.SemaphoreType.DMA
    return pl.pallas_call(
        functools.partial(many_sum_kernel, axis),
        out_shape=jax.ShapeDtypeStruct(x.shape, x.dtype),
        in_specs=[VMEM],
        out_specs=VMEM,
        scratch_shapes=[pltpu.VMEM((n - 1, *x.shape), x.dtype), sem((n,)), sem((n,))],
        compiler_params=remote_params(collective_id, 8),
    )(x)


LINE_CHUNKS = 4


def line_gather(collective_id, x):
    n_ctx = lax.axis_size("ctx")
    n = n_ctx // 2
    sem = pltpu.SemaphoreType.DMA
    return pl.pallas_call(
        functools.partial(line_gather_kernel, LINE_CHUNKS),
        out_shape=jax.ShapeDtypeStruct((n_ctx, *x.shape), x.dtype),
        in_specs=[ANY],
        out_specs=ANY,
        scratch_shapes=[
            sem,
            sem((n, LINE_CHUNKS)),
            sem((n, LINE_CHUNKS)),
            sem((2 * n - 1, LINE_CHUNKS)),
            sem((n, LINE_CHUNKS)),
            sem((n, LINE_CHUNKS)),
            sem((2 * n - 1, LINE_CHUNKS)),
        ],
        compiler_params=remote_params(collective_id, 8),
    )(x)


def line_reduce(collective_id, x):
    n_ctx, rows, width = x.shape
    n = n_ctx // 2
    sem = pltpu.SemaphoreType.DMA
    return pl.pallas_call(
        functools.partial(line_reduce_kernel, LINE_CHUNKS),
        out_shape=jax.ShapeDtypeStruct((rows, width), f32),
        in_specs=[VMEM],
        out_specs=VMEM,
        scratch_shapes=[pltpu.VMEM((n, rows, width), bf16)] * 4 + [sem((n, LINE_CHUNKS))] * 5,
        compiler_params=remote_params(collective_id, 40),
    )(x)


def per_device(
    tokens,
    doc_ids,
    routes,
    attn_gain,
    w_query,
    w_key,
    w_value,
    query_gain,
    key_gain,
    w_out,
    ffn_gain,
    w_router,
    w_gate,
    w_up,
    w_down,
    clip_threshold,
    cotangent,
):
    both = ("ctx", "shard")
    n_ctx, n_shard = lax.axis_size("ctx"), lax.axis_size("shard")
    ctx, shard = lax.axis_index("ctx"), lax.axis_index("shard")
    x_own = tokens[0]
    rows, width = x_own.shape
    part = w_query.shape[0]
    cols = width // n_ctx
    heads = cols // HEAD
    count = rows * n_ctx
    local = w_gate.shape[0]
    experts = local * n_shard

    top = routes.shape[2]
    spare = jnp.zeros((part, LANES - 4 - experts - rows // part * (1 + top)), bf16)
    small = jnp.concatenate(
        [
            jnp.stack([attn_gain, query_gain, key_gain, ffn_gain], axis=1),
            w_router,
            doc_ids.reshape(part, rows // part).astype(bf16),
            routes.reshape(part, rows // part * top).astype(bf16),
            spare,
        ],
        axis=1,
    )
    packed = jnp.concatenate(
        [
            jnp.stack([w_query, w_key, w_value], axis=1)
            .reshape(part, 3, n_ctx, cols)
            .transpose(2, 0, 1, 3)
            .reshape(n_ctx, part, 3 * cols),
            jnp.broadcast_to(small[None], (n_ctx, part, LANES)),
        ],
        axis=2,
    )
    (packed,) = exchange("ctx", 1, packed)
    grad_own = cotangent[0]
    packed, out_w_own, grad_all = gather("shard", 2, packed, w_out, grad_own)
    packed = packed.transpose(1, 0, 2, 3)
    weights = packed[..., : 3 * cols].reshape(width, 3 * cols)
    small_all = packed[..., 3 * cols :]
    out_w_own = out_w_own.reshape(cols, width)
    grad_all = grad_all.reshape(n_shard * rows, width)
    gains = small_all[..., : 4 + experts].reshape(width, 4 + experts)
    gain_attn, gain_query, gain_key, gain_ffn = (gains[:, i].astype(f32) for i in range(4))
    router_w = gains[:, 4:]
    gain_query = lax.dynamic_slice_in_dim(gain_query, ctx * cols, cols)
    gain_key = lax.dynamic_slice_in_dim(gain_key, ctx * cols, cols)
    tail = small_all[..., 4 + experts :].astype(jnp.int32)
    docs = lax.dynamic_index_in_dim(tail[..., : rows // part], shard, 1, False).reshape(count)
    routes_all = lax.dynamic_index_in_dim(
        tail[..., rows // part : rows // part * (1 + top)], ctx, 0, False
    ).reshape(n_shard * rows, top)
    x_all = line_gather(3, x_own).reshape(count, width)
    w_gate, w_up, w_down, x_all = lax.optimization_barrier((w_gate, w_up, w_down, x_all))
    groups = [slice(g, g + EXPERT_GROUP) for g in range(0, local, EXPERT_GROUP)]
    wide_w, down_w = [], []
    for g in groups:
        both_own = jnp.concatenate([w_gate[g], w_up[g]], axis=2)
        wide_w.append(lax.all_gather(both_own, "ctx", axis=1, tiled=True))
        down_w.append(lax.all_gather(w_down[g], "ctx", axis=2, tiled=True))

    x_wide = x_all.astype(f32)
    inverse_one = inverse_rms(x_wide)
    hidden_one = (x_wide * inverse_one * gain_attn).astype(bf16)
    linear = dot(hidden_one, weights)
    query_lin, key_lin = linear[:, :cols], linear[:, cols : 2 * cols]
    value = linear[:, 2 * cols :].astype(bf16)
    squares = jnp.stack(
        [jnp.sum(query_lin * query_lin, axis=1), jnp.sum(key_lin * key_lin, axis=1)]
    )
    squares = many_sum("ctx", 4, squares)
    inverse_qk = lax.rsqrt(squares / width + norm_eps)
    inverse_q, inverse_k = inverse_qk[0][:, None], inverse_qk[1][:, None]
    cosine, sine = rope_tables(count)
    query_n, key_n = query_lin * inverse_q, key_lin * inverse_k
    query = rotate(query_n * gain_query, cosine, sine).astype(bf16)
    key = rotate(key_n * gain_key, cosine, sine).astype(bf16)
    mixed, log_total, peaks = attend_forward(query, key, value, docs)
    x_f = x_own.astype(f32)
    mixed_out = dot(mixed, out_w_own).astype(bf16).reshape(n_ctx, rows, width)
    after = x_f + line_reduce(5, mixed_out)
    inverse_two = inverse_rms(after)
    normed_two = after * inverse_two
    hidden_two = (normed_two * gain_ffn).astype(bf16)

    hidden_all, peaks = gather("shard", 6, hidden_two, peaks)
    hidden_all = hidden_all.reshape(n_shard * rows, width)
    peaks = jnp.max(peaks, axis=0)[:, 0, 0]
    logits = dot(hidden_all, router_w)
    named = jnp.any(routes_all[:, :, None] == jnp.arange(experts)[None, None, :], axis=1)
    probs = jax.nn.softmax(logits, axis=1)
    selected = jnp.where(named, probs, 0.0)
    selected_sum = jnp.sum(selected, axis=1, keepdims=True)
    gates = selected / selected_sum
    gates_own = lax.dynamic_slice_in_dim(gates, shard * local, local, 1)
    named_own = lax.dynamic_slice_in_dim(named, shard * local, local, 1)
    grad_wide = grad_all.astype(f32)
    moe_part = jnp.zeros(grad_all.shape, f32)
    back_part = jnp.zeros(grad_all.shape, f32)
    grad_gates, grad_wide_w, grad_down_w = [], [], []
    for e in range(local):
        group, member = divmod(e, EXPERT_GROUP)
        wide, down = wide_w[group][member], down_w[group][member]
        gate_col = gates_own[:, e : e + 1]
        hidden = dot(hidden_all, wide)
        ff = hidden.shape[1] // 2
        gate_h, up_h = hidden[:, :ff], hidden[:, ff:]
        sig = jax.nn.sigmoid(gate_h)
        silu = gate_h * sig
        act = (silu * up_h).astype(bf16)
        result = dot(act, down).astype(bf16).astype(f32)
        moe_part = moe_part + gate_col * result
        grad_gates.append(
            jnp.where(named_own[:, e], jnp.sum(grad_wide * result, axis=1), 0.0)
        )
        grad_y = (gate_col * grad_wide).astype(bf16)
        grad_act = contract_cols(grad_y, down)
        grad_h = jnp.concatenate(
            [grad_act * up_h * sig * (1.0 + gate_h * (1.0 - sig)), grad_act * silu], axis=1
        ).astype(bf16)
        back_part = back_part + contract_cols(grad_h, wide).astype(bf16).astype(f32)
        grad_down_w.append(contract_rows(act, grad_y).astype(bf16))
        grad_wide_w.append(contract_rows(hidden_all, grad_h).astype(bf16))
    wide_grads = [
        lax.psum_scatter(jnp.stack(grad_wide_w[g]), "ctx", scatter_dimension=1, tiled=True)
        for g in groups
    ]
    down_grads = [
        lax.psum_scatter(jnp.stack(grad_down_w[g]), "ctx", scatter_dimension=2, tiled=True)
        for g in groups
    ]
    (back_sum,) = reduce("shard", 7, back_part.astype(bf16).reshape(n_shard, rows, width))
    grad_gates = lax.all_to_all(
        jnp.stack(grad_gates, axis=1), "shard", split_axis=0, concat_axis=1, tiled=True
    )

    def own_rows(u):
        return lax.dynamic_slice_in_dim(u, shard * rows, rows, 0)

    gates_t, probs_t, named_t, sum_t = map(own_rows, (gates, probs, named, selected_sum))
    grad_selected = (
        grad_gates - jnp.sum(gates_t * grad_gates, axis=1, keepdims=True)
    ) / sum_t
    grad_probs = jnp.where(named_t, grad_selected, 0.0)
    grad_logits = (
        probs_t * (grad_probs - jnp.sum(probs_t * grad_probs, axis=1, keepdims=True))
    ).astype(bf16)
    grad_router = contract_rows(hidden_two, grad_logits)
    grad_hidden = back_sum + contract_cols(grad_logits, router_w)
    grad_gain_ffn = jnp.sum(grad_hidden * normed_two, axis=0)
    scaled_two = grad_hidden * gain_ffn
    grad_after = grad_own.astype(f32) + inverse_two * (
        scaled_two - normed_two * jnp.mean(scaled_two * normed_two, axis=1, keepdims=True)
    )

    grad_attn = line_gather(3, grad_after.astype(bf16)).reshape(count, width)
    grad_mixed = contract_cols(grad_attn, out_w_own).astype(bf16)
    grad_out_w = contract_rows(mixed, grad_attn)
    grad_query_rot, grad_key_rot, grad_value = attend_backward(
        query, key, value, docs, log_total, grad_mixed
    )
    grad_query_n = rotate(grad_query_rot, cosine, -sine)
    grad_key_n = rotate(grad_key_rot, cosine, -sine)
    grad_gain_query = jnp.sum(grad_query_n * query_n, axis=0)
    grad_gain_key = jnp.sum(grad_key_n * key_n, axis=0)
    scaled_q, scaled_k = grad_query_n * gain_query, grad_key_n * gain_key
    peak_row = lax.dynamic_update_slice_in_dim(jnp.zeros((count,), f32), peaks, ctx * heads, 0)
    inner = jnp.stack(
        [jnp.sum(scaled_q * query_n, axis=1), jnp.sum(scaled_k * key_n, axis=1), peak_row]
    )
    inner = many_sum("ctx", 8, inner)
    peak_all = inner[2, :HEADS]
    inner = inner / width
    grad_linear = jnp.concatenate(
        [
            inverse_q * (scaled_q - query_n * inner[0][:, None]),
            inverse_k * (scaled_k - key_n * inner[1][:, None]),
            grad_value,
        ],
        axis=1,
    ).astype(bf16)
    grad_weights = contract_rows(hidden_one, grad_linear)
    hidden_part = contract_cols(grad_linear, weights)
    grad_gain_attn = jnp.sum(hidden_part * (x_wide * inverse_one), axis=0)
    grad_small = jnp.concatenate(
        [jnp.stack([grad_gain_attn, grad_gain_ffn], axis=1), grad_router], axis=1
    )
    grad_small = jnp.pad(grad_small, ((0, 0), (0, LANES - 2 - experts)))
    grad_weights = (
        jnp.concatenate([grad_weights, grad_small], axis=1)
        .astype(bf16)
        .reshape(n_ctx, n_shard, part, 3 * cols + LANES)
        .transpose(1, 0, 2, 3)
        .reshape(n_shard, n_ctx * part, 3 * cols + LANES)
    )
    grad_gain_qk = jnp.pad(
        jnp.stack([grad_gain_query, grad_gain_key], axis=1), ((0, 0), (0, LANES - 2))
    )
    grad_out_w = (
        jnp.concatenate([grad_out_w, grad_gain_qk], axis=1)
        .astype(bf16)
        .reshape(n_shard, part, width + LANES)
    )
    moe_part = moe_part.astype(bf16).reshape(n_shard, rows, width)
    grad_weights, grad_out_w, moe_sum = reduce("shard", 9, grad_weights, grad_out_w, moe_part)
    output = (after + moe_sum).astype(bf16)
    grad_weights = grad_weights.reshape(n_ctx, part, 3 * cols + LANES)
    (grad_weights,) = exchange("ctx", 10, grad_weights)
    grad_small = jnp.sum(grad_weights[..., 3 * cols :], axis=0)
    grad_weights = (
        grad_weights[..., : 3 * cols]
        .reshape(n_ctx, part, 3, cols)
        .transpose(2, 1, 0, 3)
        .reshape(3, part, width)
    )
    grad_hidden_one = line_reduce(5, hidden_part.astype(bf16).reshape(n_ctx, rows, width))
    inverse_own = inverse_rms(x_f)
    normed_own = x_f * inverse_own
    scaled_one = grad_hidden_one * gain_attn
    grad_inputs = grad_after + inverse_own * (
        scaled_one - normed_own * jnp.mean(scaled_one * normed_own, axis=1, keepdims=True)
    )

    wide_grads = jnp.concatenate(wide_grads, axis=0)
    factors = jnp.sqrt(clip_threshold / jnp.maximum(peak_all, clip_threshold))
    col_scale = jnp.repeat(factors, HEAD)
    query_clipped = (w_query.astype(f32) * col_scale[None, :]).astype(bf16)
    key_clipped = (w_key.astype(f32) * col_scale[None, :]).astype(bf16)
    return (
        output[None],
        grad_inputs[None],
        grad_small[:, 0],
        grad_weights[0],
        grad_weights[1],
        grad_weights[2],
        grad_out_w[:, width],
        grad_out_w[:, width + 1],
        grad_out_w[:, :width],
        grad_small[:, 1],
        grad_small[:, 2 : 2 + experts],
        wide_grads[..., :ff].astype(f32),
        wide_grads[..., ff:].astype(f32),
        jnp.concatenate(down_grads, axis=0).astype(f32),
        query_clipped,
        key_clipped,
        factors,
    )


def solution(mesh):
    both = ("ctx", "shard")
    return jax.shard_map(
        per_device,
        mesh=mesh,
        in_specs=(
            P("shard", "ctx", None),
            P("shard", "ctx"),
            P("shard", "ctx", None),
            P(both),
            P(both, None),
            P(both, None),
            P(both, None),
            P(both),
            P(both),
            P(both, None),
            P(both),
            P(both, None),
            P("shard", "ctx", None),
            P("shard", "ctx", None),
            P("shard", None, "ctx"),
            P(),
            P("shard", "ctx", None),
        ),
        out_specs=(
            P("shard", "ctx", None),
            P("shard", "ctx", None),
            P(both),
            P(both, None),
            P(both, None),
            P(both, None),
            P(both),
            P(both),
            P(both, None),
            P(both),
            P(both, None),
            P("shard", "ctx", None),
            P("shard", "ctx", None),
            P("shard", None, "ctx"),
            P(both, None),
            P(both, None),
            P(),
        ),
        check_vma=False,
    )
```

time: 4270 us -> 1590 us (0.37)
  waiting for transfers between devices: 2560 us -> 23.9 us
  Pallas kernels: 0 us -> 1010 us
  local copies, waits for them, and re-layouts: 485 us -> 75.3 us
  blocking collectives: 381 us -> 0 us
  matrix products: 624 us -> 325 us
  loops' own time: 53.2 us -> 0 us
    reduce_scatter x9 -> x4, waiting for transfers between devices: 1880 us -> 0.02 us  [the longest x2 0.01 us: per_device(): lax.psum_scatter(jnp.stack(grad_down_w[g]), 'ctx', scatter_dimension=2, t...]
    pallas_call x0 -> x14, Pallas kernels: none -> 1010 us  [the longest x2 278 us: line_reduce(): pl.pallas_call(functools.partial(line_reduce_kernel, LINE_CHUNKS), out_sh...]
    all_to_all x4 -> x1, waiting for transfers between devices: 328 us -> 0.01 us  [per_device(): lax.all_to_all(jnp.stack(grad_gates, axis=1), 'shard', split_axis=0, conc...]
    dot_general x135 -> x33, matrix products: 623 us -> 325 us  [the longest x11 118 us: contract_cols(): lax.dot_general(a, b, (((1,), (1,)), ((), ())), preferred_element_type=f32)]
    all_gather x9 -> x4, waiting for transfers between devices: 282 us -> 23.2 us  [the longest x2 23.2 us: per_device(): down_w.append(lax.all_gather(w_down[g], 'ctx', axis=2, tiled=True))]
    all_gather x2 -> x0, blocking collectives: 254 us -> none  [the longest x1 243 us: per_device(): lax.all_gather(w_router, ('ctx', 'shard'), axis=0, tiled=True)]
    dynamic_update_slice x96 -> x1, local copies, waits for them, and re-layouts: 111 us -> 0.16 us  [per_device(): lax.dynamic_update_slice_in_dim(jnp.zeros((count,), f32), peaks, ctx * he...]
    gather x4 -> x0, local copies, waits for them, and re-layouts: 106 us -> none  [the longest x1 35.8 us: per_device(): jnp.concatenate([grad_y, pad_row], axis=0)[source]]
  transfers between devices with their start and end apart: 23 -> 9, of which waited for: 16 -> 1; matrix products, arithmetic and copies ran while one was open for 18% -> 26% of each run, Pallas kernels for 0% -> 60%
where the time goes in v1:
time: 1590 us; the launch traced here: 1570 us
  Pallas kernels  1010 us (64%)
  matrix products  325 us (20%)
  other arithmetic  111 us (7%)
  local copies, waits for them, and re-layouts  75.3 us (5%)
  waiting for transfers between devices  23.9 us (2%)
  between operations  17.1 us (1%)
    pallas_call x2, Pallas kernels, line_reduce(): pl.pallas_call(functools.partial(line_reduce_kernel, LINE_CHUNKS), out_sh...  278 us
    pallas_call x2, Pallas kernels, line_gather(): pl.pallas_call(functools.partial(line_gather_kernel, LINE_CHUNKS), out_sh...  259 us
    pallas_call x4, Pallas kernels, direct_call(): pl.pallas_call(functools.partial(kernel, axis, count), out_shape=[jax.Sha...  228 us
    pallas_call x2, Pallas kernels, reduce(): pl.pallas_call(functools.partial(reduce_kernel, axis, count), out_shape=[...  155 us
    dot_general x11, matrix products, contract_cols(): lax.dot_general(a, b, (((1,), (1,)), ((), ())), preferred_element_type=f32)  118 us
    dot_general x11, matrix products, dot(): return jnp.dot(a, b, preferred_element_type=f32)  113 us
    dot_general x11, matrix products, contract_rows(): lax.dot_general(a, b, (((0,), (0,)), ((), ())), preferred_element_type=f32)  93.8 us
    pallas_call x1, Pallas kernels, attend_backward(): pl.pallas_call(attend_backward_kernel, grid=(heads, count // Q_BLOCK), in...  37.6 us
  transfers between devices with their start and end apart: 9, of which 1 were waited for; matrix products, arithmetic and copies ran while one was open for 26% of the time, Pallas kernels for 60%

profile of v1, /device:TPU:0, one launch (start us, length us, event | category | flops | bytes accessed | tf_op | source)
XLA Modules:
  0.0 1570.1 jit_solution(15042075282219332516)
XLA Ops:
  8.5 74.8 %shard_map.296 = bf16[8,256,2048]{2,1,0:T(8,128)(2,1)S(1)} custom-call(bf16[256,2048]{1,0:T(8,128)(2,1)S(1)} %bitcast.238), custom_call_target="tpu_custom_call" | custom-call | tf_op jit(solution)/shard_map/pallas_call | solution.py:581
  99.9 33.0 %shard_map.297.refs_0_ = bf16[8,64,896]{2,1,0:T(8,128)(2,1)S(1)} custom-call(bf16[8,64,896]{2,1,0:T(8,128)(2,1)S(1)} %pad_maximum_fusion.27.refs_0_), custom_call_target="tpu_custom_call" | custom-call | tf_op jit(solution)/shard_map/pallas_call | solution.py:528
  132.9 99.9 %shard_map.298 = (bf16[4,8,64,896]{3,2,1,0:T(8,128)(2,1)S(1)}, bf16[4,64,2048]{2,1,0:T(8,128)(2,1)S(1)}, bf16[4,256,2048]{2,1,0:T(8,128)(2,1)S(1)}) custom-call(bf16[8,64,896]{2,1,0:T(8,128)(2,1)S(1)} %shard_map.297.refs_0_, bf16[64,2048]{1,0:T(8,128)(2,1)S(1)} %copy-done.31, bf16[256,2048]{1,0:T(8,128)(2,1)S(1)} %bitcast.239), custom_call_target="tpu_custom_call" | custom-call | tf_op jit(solution)/shard_map/pallas_call | solution.py:528
  265.4 21.3 %shard_map.299 = f32[2,2048]{1,0:T(2,128)S(1)} custom-call(f32[2,2048]{1,0:T(2,128)S(1)} %pad_maximum_fusion.30.x_ref), custom_call_target="tpu_custom_call" | custom-call | tf_op jit(solution)/shard_map/pallas_call | solution.py:564
  297.2 23.5 %shard_map.300 = (bf16[2048,256]{1,0:T(8,128)(2,1)S(1)}, f32[2,2048,1]{2,1,0:T(8,128)}, f32[2,8,128]{2,1,0:T(8,128)S(1)}) custom-call(bf16[2048,256]{1,0:T(8,128)(2,1)S(1)} %pad_maximum_fusion.25.q_ref, bf16[2048,256]{1,0:T(8,128)(2,1)S(1)} %pad_maximum_fusion.26.k_ref, bf16[2048,256]{1,0:T(8,128)(2,1)S(1)} %slice.496.v_ref, ...), custom_call_target="tpu_custom_call" | custom-call | flops 4294967296 | bytes 4194304 | tf_op jit(solution)/shard_map/pallas_call | solution.py:112
  323.1 138.2 %shard_map.301 = f32[256,2048]{1,0:T(8,128)S(1)} custom-call(bf16[8,256,2048]{2,1,0:T(8,128)(2,1)S(1)} %bitcast.231), custom_call_target="tpu_custom_call" | custom-call | tf_op jit(solution)/shard_map/pallas_call | solution.py:603
  466.0 39.9 %shard_map.302 = (bf16[4,256,2048]{2,1,0:T(8,128)(2,1)S(1)}, f32[4,2,8,128]{3,2,1,0:T(8,128)S(1)}) custom-call(bf16[256,2048]{1,0:T(8,128)(2,1)S(1)} %multiply_convert_fusion.14.refs_0_, f32[2,8,128]{2,1,0:T(8,128)S(1)} %get-tuple-element.40.refs_1_), custom_call_target="tpu_custom_call" | custom-call | tf_op jit(solution)/shard_map/pallas_call | solution.py:528
  520.7 14.8 fusion.28
  555.4 14.0 fusion.26
  586.8 16.0 %fusion.24 = f32[1024,2048]{0,1:T(8,128)} fusion(bf16[1024,2048]{1,0:T(8,128)(2,1)} %bitcast.245, bf16[2,2048,2048]{2,1,0:T(8,128)(2,1)} %all-gather.7.cloned.1.call-done), kind=kOutput, calls=%fused_computation.56 | convolution fusion | flops 8589934592 | bytes 20971520 | tf_op jit(solution)/shard_map/dot_general | solution.py:24
  602.8 13.5 fusion.22
  616.4 23.2 %all-gather.5.cloned.1.call-done = bf16[2,1024,2048]{2,1,0:T(8,128)(2,1)} async-done(((bf16[2,1024,256]{2,1,0:T(8,128)(2,1)}), bf16[2,1024,2048]{2,1,0:T(8,128)(2,1)}) %all-gather.5.cloned.1.call-update) | async-done | bytes 8388624 | tf_op jit(solution)/shard_map/all_gather | solution.py:691
  668.3 22.6 %fusion.5 = (f32[1024]{0:T(1024)S(1)}, f32[1024]{0:T(1024)S(1)}, f32[1024]{0:T(1024)S(1)}, f32[1024]{0:T(1024)S(1)}, bf16[1024,2048]{1,0:T(8,128)(2,1)}, /*index...) fusion(bf16[4,256,2048]{2,1,0:T(8,128)(2,1)} %copy-done.19, ...), kind=kOutput, calls=%fused_computation.17 | convolution fusion | flops 4357877760 | bytes 44072960 | tf_op jit(solution)/shard_map/dot_general | solution.py:24
  730.8 12.6 convert_bitcast_fusion.2
  810.7 14.7 fusion.25
  825.5 12.8 fusion.23
  838.2 13.7 fusion.21
  851.9 16.5 %add_convert_fusion = bf16[1024,2048]{1,0:T(8,128)(2,1)} fusion(bf16[1024,2048]{1,0:T(8,128)(2,1)} %fusion.25, bf16[1024,2048]{1,0:T(8,128)(2,1)} %fusion.23, bf16[1024,2048]{1,0:T(8,128)(2,1)} %fusion.21, bf16[2,2048,2048]{2,1,0:T(8,128)(2,1)} %all-gather.11.cloned.1.call-done, bf16[1024,1024]{0,1:T(8,128)(2,1)} %get-tuple-element.136, ...), kind=kOutput, calls=%fused_computation.51 | convolution fusion | flops 8617197568 | bytes 29360128 | tf_op jit(solution)/shard_map/dot_general | solution.py:32
  868.4 51.5 %shard_map.303 = f32[256,2048]{1,0:T(8,128)S(1)} custom-call(bf16[4,256,2048]{2,1,0:T(8,128)(2,1)} %bitcast.264), custom_call_target="tpu_custom_call" | custom-call | tf_op jit(solution)/shard_map/pallas_call | solution.py:550
  925.5 184.1 %shard_map.304 = bf16[8,256,2048]{2,1,0:T(8,128)(2,1)S(1)} custom-call(bf16[256,2048]{1,0:T(8,128)(2,1)S(1)} %fusion.128.x_ref), custom_call_target="tpu_custom_call" | custom-call | tf_op jit(solution)/shard_map/pallas_call | solution.py:581
  1114.4 37.6 %shard_map.305 = (f32[2048,256]{1,0:T(8,128)}, f32[2048,256]{1,0:T(8,128)}, f32[2048,256]{1,0:T(8,128)}) custom-call(bf16[2048,256]{1,0:T(8,128)(2,1)} %copy-done.22, bf16[2048,256]{1,0:T(8,128)(2,1)} %copy-done.23, bf16[2048,256]{1,0:T(8,128)(2,1)} %copy-done.25, s32[2048,1]{1,0:T(8,128)} %copy-done.24, s32[1,2048]{1,0:T(1,128)} %copy-done.32, ...), custom_call_target="tpu_custom_call" | custom-call | flops 10737418240 | bytes 10485760 | tf_op jit(solution)/shard_map/pallas_call | solution.py:135
  1198.1 140.2 %shard_map.308 = f32[256,2048]{1,0:T(8,128)S(1)} custom-call(bf16[8,256,2048]{2,1,0:T(8,128)(2,1)S(1)} %bitcast.240), custom_call_target="tpu_custom_call" | custom-call | tf_op jit(solution)/shard_map/pallas_call | solution.py:603
  1358.8 103.4 %shard_map.307 = (f32[512,896]{1,0:T(8,128)S(1)}, f32[64,2176]{1,0:T(8,128)S(1)}, f32[256,2048]{1,0:T(8,128)S(1)}) custom-call(bf16[4,512,896]{2,1,0:T(8,128)(2,1)} %bitcast.261, bf16[4,64,2176]{2,1,0:T(8,128)(2,1)S(1)} %pad_maximum_fusion.24.refs_1_, bf16[4,256,2048]{2,1,0:T(8,128)(2,1)} %bitcast.265), custom_call_target="tpu_custom_call" | custom-call | tf_op jit(solution)/shard_map/pallas_call | solution.py:550
  1463.5 54.8 %shard_map.309 = f32[8,64,896]{2,1,0:T(8,128)S(1)} custom-call(f32[8,64,896]{2,1,0:T(8,128)S(1)} %bitcast.256), custom_call_target="tpu_custom_call" | custom-call | tf_op jit(solution)/shard_map/pallas_call | solution.py:528
  (410 shorter events, 376.4 us)
Async XLA Ops:
  7.2 513.5 %all-gather.11.cloned.1.call-start = ((), (), s32[]{:S(2)}) async-start(), calls=%async_computation.8 | async-start | bytes 18874368 | tf_op jit(solution)/shard_map/all_gather | solution.py:690
  8.5 78.1 %copy-start.42 = (bf16[4,256,1024]{2,1,0:T(8,128)(2,1)S(1)}, bf16[4,256,1024]{2,1,0:T(8,128)(2,1)}, u32[]{:S(2)}) copy-start(bf16[4,256,1024]{2,1,0:T(8,128)(2,1)} %param.29) | copy-start | bytes 6291460
  8.5 78.1 %copy-start.43 = (bf16[4,256,1024]{2,1,0:T(8,128)(2,1)S(1)}, bf16[4,256,1024]{2,1,0:T(8,128)(2,1)}, u32[]{:S(2)}) copy-start(bf16[4,256,1024]{2,1,0:T(8,128)(2,1)} %param.30) | copy-start | bytes 6291460
  88.8 446.7 %all-gather.9.cloned.1.call-start = ((), (), s32[]{:S(2)}) async-start(), calls=%async_computation.7 | async-start | bytes 9437184 | tf_op jit(solution)/shard_map/all_gather | solution.py:691
  91.9 494.9 %all-gather.7.cloned.1.call-start = ((), (), s32[]{:S(2)}) async-start(), calls=%async_computation.6 | async-start | bytes 18874368 | tf_op jit(solution)/shard_map/all_gather | solution.py:690
  93.5 546.0 %all-gather.5.cloned.1.call-start = ((), (), s32[]{:S(2)}) async-start(), calls=%async_computation.5 | async-start | bytes 9437184 | tf_op jit(solution)/shard_map/all_gather | solution.py:691
  94.1 1451.7 %reduce-scatter.11.cloned.1.call-start = ((), (), s32[]{:S(2)}) async-start(), calls=%async_computation.12 | async-start | bytes 9437184 | tf_op jit(solution)/shard_map/reduce_scatter | solution.py:760
  238.3 51.9 %copy-start.65 = (f32[2048]{0:T(1024)}, f32[2048]{0:T(1024)S(1)}, u32[]{:S(2)}) copy-start(f32[2048]{0:T(1024)S(1)} %iota_convert_fusion) | copy-start | bytes 24580
  246.0 260.9 %copy-start.49 = (bf16[2048,20]{0,1:T(8,128)(2,1)}, bf16[2048,20]{0,1:T(8,128)(2,1)S(1)}, u32[]{:S(2)}) copy-start(bf16[2048,20]{0,1:T(8,128)(2,1)S(1)} %reshape.232) | copy-start | bytes 245764
  246.6 219.1 %copy-start.56 = (f32[2048,1]{0,1:T(1,128)}, f32[2048,1]{0,1:T(1,128)S(1)}, u32[]{:S(2)}) copy-start(f32[2048,1]{0,1:T(1,128)S(1)} %get-tuple-element.191) | copy-start | bytes 24580
  323.1 138.2 %copy-start.2 = (bf16[1,256,2048]{2,1,0:T(8,128)(2,1)S(1)}, bf16[1,256,2048]{2,1,0:T(8,128)(2,1)}, u32[]{:S(2)}) copy-start(bf16[1,256,2048]{2,1,0:T(8,128)(2,1)} %param.17) | copy-start | bytes 3145732
  710.8 835.0 %reduce-scatter.9.cloned.1.call-start = ((), (), s32[]{:S(2)}) async-start(), calls=%async_computation.11 | async-start | bytes 9437184 | tf_op jit(solution)/shard_map/reduce_scatter | solution.py:760
  730.7 818.9 %reduce-scatter.5.cloned.1.call-start = ((), (), s32[]{:S(2)}) async-start(), calls=%async_computation.9 | async-start | bytes 18874368 | tf_op jit(solution)/shard_map/reduce_scatter | solution.py:756
  766.5 786.3 %reduce-scatter.7.cloned.1.call-start = ((), (), s32[]{:S(2)}) async-start(), calls=%async_computation.10 | async-start | bytes 18874368 | tf_op jit(solution)/shard_map/reduce_scatter | solution.py:756
  806.8 113.1 %all-to-all-start = ((f32[4,256,4]{1,2,0:T(4,128)}), f32[4,256,4]{1,2,0:T(4,128)S(1)}, u32[]{:S(2)}, u32[]{:S(2)}) async-start(f32[4,256,4]{1,2,0:T(4,128)} %pad_maximum_fusion.31), calls=%async_computation | async-start | bytes 32768 | tf_op jit(solution)/shard_map/all_to_all | solution.py:764
  868.4 52.4 %copy-start.52 = (f32[1024,16]{0,1:T(8,128)S(1)}, f32[1024,16]{0,1:T(8,128)}, u32[]{:S(2)}) copy-start(f32[1024,16]{0,1:T(8,128)} %copy-done.51) | copy-start | bytes 196612
  868.4 52.5 %copy-start.50 = (bf16[2048,20]{0,1:T(8,128)(2,1)S(1)}, bf16[2048,20]{0,1:T(8,128)(2,1)}, u32[]{:S(2)}) copy-start(bf16[2048,20]{0,1:T(8,128)(2,1)} %copy-done.49) | copy-start | bytes 245764
  868.4 52.5 %copy-start.57 = (f32[2048,1]{0,1:T(1,128)S(1)}, f32[2048,1]{0,1:T(1,128)}, u32[]{:S(2)}) copy-start(f32[2048,1]{0,1:T(1,128)} %copy-done.56) | copy-start | bytes 24580
  868.4 52.5 %copy-start.68 = (f32[256]{0:T(256)S(1)}, f32[256]{0:T(256)}, u32[]{:S(2)}) copy-start(f32[256]{0:T(256)} %copy-done.67) | copy-start | bytes 3076
  925.5 184.2 %copy-start.28 = (bf16[4,64,2048]{2,1,0:T(8,128)(2,1)S(1)}, bf16[4,64,2048]{2,1,0:T(8,128)(2,1)}, u32[]{:S(2)}) copy-start(bf16[4,64,2048]{2,1,0:T(8,128)(2,1)} %copy-done.26) | copy-start | bytes 3145732
  1109.7 53.0 %slice-start.2 = ((s8[6291456]{0:T(1024)(128)(4,1)}), s8[4194304]{0:T(1024)(128)(4,1)S(1)}, s32[]{:S(2)}) async-start(s8[6291456]{0:T(1024)(128)(4,1)} %bitcast.259), calls=%async_computation.15 | async-start | bytes 8388608
  1198.1 140.2 %copy-start.7 = (bf16[256,2048]{1,0:T(8,128)(2,1)S(1)}, bf16[256,2048]{1,0:T(8,128)(2,1)}, u32[]{:S(2)}) copy-start(bf16[256,2048]{1,0:T(8,128)(2,1)} %copy-done.6) | copy-start | bytes 3145732
  1198.1 141.0 %copy-start.64 = (f32[2048,1]{0,1:T(1,128)S(1)}, f32[2048,1]{0,1:T(1,128)}, u32[]{:S(2)}) copy-start(f32[2048,1]{0,1:T(1,128)} %copy-done.63) | copy-start | bytes 24580
  1463.5 61.3 %copy-start.29 = (f32[64,2176]{1,0:T(8,128)}, f32[64,2176]{1,0:T(8,128)S(1)}, u32[]{:S(2)}) copy-start(f32[64,2176]{1,0:T(8,128)S(1)} %get-tuple-element.52) | copy-start | bytes 1671172
  (99 other events, 1038.7 us)
Sparse Core Ops, SparseCore 0:
  88.9 170.8 all-gather.10
  261.3 99.1 all-gather.8
  362.2 195.1 all-gather.6
  558.9 80.6 all-gather.4
  711.0 123.1 reduce-scatter.10
  836.3 87.9 reduce-scatter.8
  926.7 228.0 reduce-scatter.4
  1157.1 244.1 reduce-scatter.6

commit v2 on v1

v2 whole, which is shorter than its diff:
```python
import functools

import jax
import jax.numpy as jnp
from jax import lax
from jax.experimental import pallas as pl
from jax.experimental.pallas import tpu as pltpu
from jax.sharding import PartitionSpec as P

HEADS = 16
HEAD = 128
SCALE = HEAD ** (-0.5)
Q_BLOCK = 256
LANES = 128

norm_eps = 1e-06
rope_base = 10000.0
f32 = jnp.float32
bf16 = jnp.bfloat16


def dot(a, b):
    return jnp.dot(a, b, preferred_element_type=f32)


def contract_rows(a, b):
    return lax.dot_general(a, b, (((0,), (0,)), ((), ())), preferred_element_type=f32)


def contract_cols(a, b):
    return lax.dot_general(a, b, (((1,), (1,)), ((), ())), preferred_element_type=f32)


def inverse_rms(values):
    return lax.rsqrt(jnp.mean(values * values, axis=-1, keepdims=True) + norm_eps)


def rope_tables(count):
    half = HEAD // 2
    freq = rope_base ** (-jnp.arange(half).astype(f32) / half)
    angles = jnp.arange(count).astype(f32)[:, None] * freq[None, :]
    return jnp.cos(angles), jnp.sin(angles)


def rotate(values, cosine, sine):
    parts = []
    for col in range(0, values.shape[1], HEAD):
        a = values[:, col : col + HEAD // 2]
        b = values[:, col + HEAD // 2 : col + HEAD]
        parts += [a * cosine - b * sine, b * cosine + a * sine]
    return jnp.concatenate(parts, axis=1)


def attend_forward_kernel(q_ref, k_ref, v_ref, doc_q_ref, doc_k_ref, o_ref, lse_ref, peak_ref):
    s = SCALE * contract_cols(q_ref[...], k_ref[...])
    s = jnp.where(doc_q_ref[...] == doc_k_ref[...], s, -1e30)
    top = jnp.max(s, axis=1, keepdims=True)
    e = jnp.exp(s - top)
    total = jnp.sum(e, axis=1, keepdims=True)
    p = (e * (1.0 / total)).astype(bf16)
    o_ref[...] = dot(p, v_ref[...]).astype(bf16)
    lse_ref[0] = top + jnp.log(total)
    peak = jnp.broadcast_to(jnp.max(top, axis=0, keepdims=True), peak_ref.shape[1:])

    @pl.when(pl.program_id(1) == 0)
    def _():
        peak_ref[0] = peak

    @pl.when(pl.program_id(1) > 0)
    def _():
        peak_ref[0] = jnp.maximum(peak_ref[0], peak)


def attend_backward_kernel(
    q_ref, k_ref, v_ref, doc_q_ref, doc_k_ref, lse_ref, do_ref, dq_ref, dk_ref, dv_ref
):
    q, k, v, do = q_ref[...], k_ref[...], v_ref[...], do_ref[...]
    s = SCALE * contract_cols(q, k)
    p = jnp.where(doc_q_ref[...] == doc_k_ref[...], jnp.exp(s - lse_ref[0]), 0.0)
    dp = contract_cols(do, v)
    inner = jnp.sum(p * dp, axis=1, keepdims=True)
    ds = (p * (dp - inner)).astype(bf16)
    dq_ref[...] = SCALE * dot(ds, k)
    dk = SCALE * contract_rows(ds, q)
    dv = contract_rows(p.astype(bf16), do)

    @pl.when(pl.program_id(1) == 0)
    def _():
        dk_ref[...] = dk
        dv_ref[...] = dv

    @pl.when(pl.program_id(1) > 0)
    def _():
        dk_ref[...] += dk
        dv_ref[...] += dv


def attend_specs(count):
    block = pl.BlockSpec((Q_BLOCK, HEAD), lambda h, i: (i, h))
    whole = pl.BlockSpec((count, HEAD), lambda h, i: (0, h))
    doc_q = pl.BlockSpec((Q_BLOCK, 1), lambda h, i: (i, 0))
    doc_k = pl.BlockSpec((1, count), lambda h, i: (0, 0))
    lse = pl.BlockSpec((1, Q_BLOCK, 1), lambda h, i: (h, i, 0))
    return block, whole, doc_q, doc_k, lse


def attend_forward(q, k, v, docs):
    count, width = q.shape
    heads = width // HEAD
    block, whole, doc_q, doc_k, lse = attend_specs(count)
    return pl.pallas_call(
        attend_forward_kernel,
        grid=(heads, count // Q_BLOCK),
        in_specs=[block, whole, whole, doc_q, doc_k],
        out_specs=[block, lse, pl.BlockSpec((1, 8, 128), lambda h, i: (h, 0, 0))],
        out_shape=[
            jax.ShapeDtypeStruct((count, width), bf16),
            jax.ShapeDtypeStruct((heads, count, 1), f32),
            jax.ShapeDtypeStruct((heads, 8, 128), f32),
        ],
        compiler_params=pltpu.CompilerParams(vmem_limit_bytes=48 << 20),
        cost_estimate=pl.CostEstimate(
            flops=4 * count * count * width,
            transcendentals=heads * count * count,
            bytes_accessed=8 * count * width,
        ),
    )(q, k, v, docs[:, None], docs[None, :])


def attend_backward(q, k, v, docs, log_total, grad):
    count, width = q.shape
    heads = width // HEAD
    block, whole, doc_q, doc_k, lse = attend_specs(count)
    return pl.pallas_call(
        attend_backward_kernel,
        grid=(heads, count // Q_BLOCK),
        in_specs=[block, whole, whole, doc_q, doc_k, lse, block],
        out_specs=[block, whole, whole],
        out_shape=[jax.ShapeDtypeStruct((count, width), f32)] * 3,
        compiler_params=pltpu.CompilerParams(vmem_limit_bytes=56 << 20),
        cost_estimate=pl.CostEstimate(
            flops=10 * count * count * width,
            transcendentals=heads * count * count,
            bytes_accessed=20 * count * width,
        ),
    )(q, k, v, docs[:, None], docs[None, :], log_total, grad)


MESH = pl.DeviceIdType.MESH
ANY = pl.BlockSpec(memory_space=pl.ANY)
VMEM = pl.BlockSpec(memory_space=pltpu.VMEM)


def ring_peers(axis):
    n, me = lax.axis_size(axis), lax.axis_index(axis)
    return [lax.rem(me + k, n) for k in range(n)], [lax.rem(me + n - k, n) for k in range(n)]


class Greeting:
    def __init__(self):
        self.barrier, self.total = pltpu.get_barrier_semaphore(), 0

    def ring(self, axis):
        to, _ = ring_peers(axis)
        for peer in to[1:]:
            pl.semaphore_signal(
                self.barrier, inc=1, device_id={axis: peer}, device_id_type=MESH
            )
        self.total = self.total + len(to) - 1
        return self

    def line(self):
        line = Line()
        for there, peer in (
            (line.place >= 0, line.partner),
            (line.not_last, line.me + 2),
            (line.not_first, line.me - 2),
        ):

            @pl.when(there)
            def _():
                pl.semaphore_signal(
                    self.barrier, inc=1, device_id={"ctx": peer}, device_id_type=MESH
                )

            self.total = self.total + there.astype(jnp.int32)
        return self

    def pair(self):
        pl.semaphore_signal(
            self.barrier, inc=1, device_id={"ctx": Pair().peer}, device_id_type=MESH
        )
        self.total = self.total + 1
        return self

    def wait(self):
        pl.semaphore_wait(self.barrier, self.total)


class Line:
    def __init__(self):
        self.n, self.me = lax.axis_size("ctx") // 2, lax.axis_index("ctx")
        self.place, self.core = lax.div(self.me, 2), lax.rem(self.me, 2)
        self.partner = self.me + 1 - 2 * self.core
        self.not_first, self.not_last = self.place > 0, self.place < self.n - 1


class Direct:
    def __init__(self, axis, source, target, send, recv):
        self.axis, self.source, self.target = axis, source, target
        self.send, self.recv = send, recv
        self.me = lax.axis_index(axis)
        self.to, self.origin = ring_peers(axis)

    def copy(self, k, sender):
        return pltpu.make_async_remote_copy(
            src_ref=self.source(self.to[k]),
            dst_ref=self.target(sender, k),
            send_sem=self.send.at[k],
            recv_sem=self.recv.at[k],
            device_id={self.axis: self.to[k]},
            device_id_type=MESH,
        )

    def start(self):
        for k in range(1, len(self.to)):
            self.copy(k, self.me).start()

    def wait_recv(self):
        for k in range(1, len(self.to)):
            self.copy(k, self.origin[k]).wait_recv()

    def wait_send(self):
        for k in range(1, len(self.to)):
            self.copy(k, self.me).wait_send()


class LineGather:
    def __init__(self, pieces, own_sem, send_r, send_l, send_p, recv_r, recv_l, recv_p):
        self.line, self.pieces, self.own_sem = Line(), pieces, own_sem
        self.send_r, self.send_l, self.send_p = send_r, send_l, send_p
        self.recv_r, self.recv_l, self.recv_p = recv_r, recv_l, recv_p

    def own(self, c):
        source, target = self.pieces[c]
        return pltpu.make_async_copy(source, target(self.line.me), self.own_sem.at[c])

    def copy(self, block, k, c, target_device, send, recv):
        source, target = self.pieces[c]
        return pltpu.make_async_remote_copy(
            src_ref=source if k == 0 else target(block),
            dst_ref=target(block),
            send_sem=send,
            recv_sem=recv,
            device_id={"ctx": target_device},
            device_id_type=MESH,
        )

    def right(self, k, c):
        me = self.line.me
        return self.copy(me - 2 * k, k, c, me + 2, self.send_r.at[k, c], self.recv_r.at[k, c])

    def left(self, k, c):
        me = self.line.me
        return self.copy(me + 2 * k, k, c, me - 2, self.send_l.at[k, c], self.recv_l.at[k, c])

    def across(self, k, c, sign):
        line = self.line
        i = k if sign < 0 else line.n - 1 + k
        return self.copy(
            line.me + sign * 2 * k, k, c, line.partner, self.send_p.at[i, c], self.recv_p.at[i, c]
        )

    def arrived(self, block, c, recv):
        source, target = self.pieces[c]
        pltpu.make_async_remote_copy(
            src_ref=source,
            dst_ref=target(block),
            send_sem=recv,
            recv_sem=recv,
            device_id={"ctx": self.line.partner},
            device_id_type=MESH,
        ).wait_recv()

    def start(self):
        for c in range(len(self.pieces)):
            self.own(c).start()

    def hop(self, k):
        line = self.line
        for c in range(len(self.pieces)):

            @pl.when(line.place >= k)
            def _():
                if k:
                    self.arrived(line.me - 2 * k, c, self.recv_r.at[k - 1, c])

                @pl.when(line.not_last)
                def _():
                    self.right(k, c).start()

                self.across(k, c, -1).start()

            @pl.when(line.place + k <= line.n - 1)
            def _():
                if k:
                    self.arrived(line.me + 2 * k, c, self.recv_l.at[k - 1, c])

                @pl.when(line.not_first)
                def _():
                    self.left(k, c).start()

                if k:
                    self.across(k, c, 1).start()

    def finish(self, skip_own=None):
        line = self.line
        for c in range(len(self.pieces)):
            if c != skip_own:
                self.own(c).wait()
        for k in range(line.n):
            for c in range(len(self.pieces)):

                @pl.when(line.place >= k)
                def _():
                    @pl.when(line.not_last)
                    def _():
                        self.right(k, c).wait_send()

                    self.across(k, c, -1).wait_send()
                    self.arrived(line.partner - 2 * k, c, self.recv_p.at[k, c])

                @pl.when(line.place + k <= line.n - 1)
                def _():
                    @pl.when(line.not_first)
                    def _():
                        self.left(k, c).wait_send()

                    if k:
                        self.across(k, c, 1).wait_send()
                        self.arrived(line.partner + 2 * k, c, self.recv_p.at[line.n - 1 + k, c])


def line_gather_scratch(n, pieces):
    sem = pltpu.SemaphoreType.DMA
    one, two = sem((n, pieces)), sem((2 * n - 1, pieces))
    return [sem((pieces,)), one, one, two, one, one, two]


class LineReduce:
    def __init__(
        self, chunks, x, o, pair, from_left, from_right, out, send_p, recv_p, send_s, recv_r, recv_l
    ):
        self.line, self.chunks = Line(), chunks
        self.x, self.o, self.pair, self.out = x, o, pair, out
        self.from_left, self.from_right = from_left, from_right
        self.send_p, self.recv_p, self.send_s = send_p, recv_p, send_s
        self.recv_r, self.recv_l = recv_r, recv_l
        self.order = []
        for j in range(self.line.n):
            self.order += [p for p in (self.line.n - 1 - j, j) if p not in self.order]

    def at(self, c):
        rows = self.x.shape[1] // self.chunks
        return pl.ds(c * rows, rows)

    def across(self, p, c):
        line, at = self.line, self.at(c)
        return pltpu.make_async_remote_copy(
            src_ref=self.x.at[2 * p + 1 - line.core, at],
            dst_ref=self.pair.at[p, at],
            send_sem=self.send_p.at[p, c],
            recv_sem=self.recv_p.at[p, c],
            device_id={"ctx": line.partner},
            device_id_type=MESH,
        )

    def along(self, p, c, step, buffer, recv):
        at = self.at(c)
        return pltpu.make_async_remote_copy(
            src_ref=self.out.at[p, at],
            dst_ref=buffer.at[p, at],
            send_sem=self.send_s.at[p, c],
            recv_sem=recv.at[p, c],
            device_id={"ctx": self.line.me + step},
            device_id_type=MESH,
        )

    def right(self, p, c):
        return self.along(p, c, 2, self.from_left, self.recv_r)

    def left(self, p, c):
        return self.along(p, c, -2, self.from_right, self.recv_l)

    def start(self):
        for p in self.order:
            for c in range(self.chunks):
                self.across(p, c).start()

    def both(self, p, c):
        at = self.at(c)
        return self.x[2 * p + self.line.core, at].astype(f32) + self.pair[p, at].astype(f32)

    def pass_on(self):
        line = self.line
        for p in self.order:
            for c in range(self.chunks):
                at = self.at(c)
                self.across(p, c).wait_recv()

                @pl.when(line.place < p)
                def _():
                    @pl.when(line.not_first)
                    def _():
                        self.right(p, c).wait_recv()
                        total = self.both(p, c) + self.from_left[p, at].astype(f32)
                        self.out[p, at] = total.astype(bf16)

                    @pl.when(line.place == 0)
                    def _():
                        self.out[p, at] = self.both(p, c).astype(bf16)

                    self.right(p, c).start()

                @pl.when(line.place > p)
                def _():
                    @pl.when(line.not_last)
                    def _():
                        self.left(p, c).wait_recv()
                        total = self.both(p, c) + self.from_right[p, at].astype(f32)
                        self.out[p, at] = total.astype(bf16)

                    @pl.when(line.place == line.n - 1)
                    def _():
                        self.out[p, at] = self.both(p, c).astype(bf16)

                    self.left(p, c).start()

    def finish(self):
        line = self.line
        for p in range(line.n):
            for c in range(self.chunks):
                at = self.at(c)

                @pl.when(line.place == p)
                def _():
                    self.o[at] = self.both(p, c)
                    if p > 0:
                        self.right(p, c).wait_recv()
                        self.o[at] += self.from_left[p, at].astype(f32)
                    if p < line.n - 1:
                        self.left(p, c).wait_recv()
                        self.o[at] += self.from_right[p, at].astype(f32)

        for p in range(line.n):
            for c in range(self.chunks):
                self.across(p, c).wait_send()

                @pl.when(line.place < p)
                def _():
                    self.right(p, c).wait_send()

                @pl.when(line.place > p)
                def _():
                    self.left(p, c).wait_send()


def add_up(x, buf, o, me):
    rows = x.shape[1]
    step = 8 if rows % 32 else 32

    @pl.loop(0, rows // step)
    def _(j):
        at = pl.ds(pl.multiple_of(j * step, step), step)
        total = x[me, at].astype(f32)
        for k in range(buf.shape[0]):
            total = total + buf[k, at].astype(f32)
        o[at] = total.astype(o.dtype)


def block_of(ref):
    return lambda device: ref.at[device]


def block_from(ref):
    return lambda device, k: ref.at[device]


def whole_of(ref):
    return lambda device: ref


def buffer_of(ref):
    return lambda device, k: ref.at[k - 1]


def row_pieces(source, target, chunks):
    rows = source.shape[0] // chunks
    return [
        (source.at[pl.ds(c * rows, rows)], lambda b, c=c: target.at[b, pl.ds(c * rows, rows)])
        for c in range(chunks)
    ]


def start_kernel(
    x, w, w_query, w_key, w_value, small, x_all, w_all, packed_mid, packed_all,
    own_sem, ex_send, ex_recv, pk_send, pk_recv, w_send, w_recv, f_send, f_recv,
    *line_sems,
):
    shard, ctx = lax.axis_index("shard"), lax.axis_index("ctx")
    n_ctx = lax.axis_size("ctx")
    cols = w_query.shape[1] // n_ctx
    Greeting().ring("ctx").ring("shard").wait()

    def columns(ref):
        return lambda d: ref.at[:, pl.ds(pl.multiple_of(d * cols, HEAD), cols)]

    def place(i):
        stop = packed_mid.shape[2] if i == 3 else (i + 1) * cols
        return lambda d, k: packed_mid.at[d, :, i * cols : stop]

    sources = [columns(w_query), columns(w_key), columns(w_value), whole_of(small)]
    swaps = [
        Direct("ctx", source, place(i), ex_send.at[i], ex_recv.at[i])
        for i, source in enumerate(sources)
    ]
    spread = Direct(
        "shard", whole_of(packed_mid), lambda d, k: packed_all.at[:, d], pk_send, pk_recv
    )
    pieces = row_pieces(x, x_all, LINE_CHUNKS) + [(w, lambda b: w_all.at[b, shard])]
    line = LineGather(pieces, *line_sems)
    at = line.line
    own = [
        pltpu.make_async_copy(source(ctx), place(i)(ctx, 0), own_sem.at[i])
        for i, source in enumerate(sources)
    ]
    spread_own = pltpu.make_async_copy(packed_mid, packed_all.at[:, shard], own_sem.at[4])
    for swap in swaps:
        swap.start()
    for copy in own:
        copy.start()
    line.start()
    line.hop(0)
    for swap in swaps:
        swap.wait_recv()
    for copy in own:
        copy.wait()
    spread.start()
    spread_own.start()
    for k in range(1, at.n):
        line.hop(k)

    to, origin = ring_peers("shard")

    def row(k, p, sender):
        block = 2 * p + at.core
        return pltpu.make_async_remote_copy(
            src_ref=w_all.at[block, shard],
            dst_ref=w_all.at[block, sender],
            send_sem=w_send.at[k, p],
            recv_sem=w_recv.at[k, p],
            device_id={"shard": to[k]},
            device_id_type=MESH,
        )

    def forward(k, p, core):
        block = w_all.at[2 * p + core, origin[k]]
        return pltpu.make_async_remote_copy(
            src_ref=block,
            dst_ref=block,
            send_sem=f_send.at[k, p],
            recv_sem=f_recv.at[k, p],
            device_id={"ctx": at.partner},
            device_id_type=MESH,
        )

    some = [(k, p) for k in range(1, len(to)) for p in range(at.n)]
    line.own(LINE_CHUNKS).wait()
    for k, p in some:
        row(k, p, shard).start()
    for k, p in some:
        row(k, p, origin[k]).wait_recv()
        forward(k, p, at.core).start()
    line.finish(skip_own=LINE_CHUNKS)
    for k, p in some:
        row(k, p, shard).wait_send()
        forward(k, p, at.core).wait_send()
        forward(k, p, 1 - at.core).wait_recv()
    spread.wait_recv()
    for direct in (*swaps, spread):
        direct.wait_send()
    spread_own.wait()


def exchange_kernel(axis, x, o, own_sem, send, recv):
    me = lax.axis_index(axis)
    Greeting().ring(axis).wait()
    swap = Direct(axis, block_of(x), block_from(o), send, recv)
    swap.start()
    own = pltpu.make_async_copy(x.at[me], o.at[me], own_sem)
    own.start()
    own.wait()
    swap.wait_recv()
    swap.wait_send()


class Pair:
    def __init__(self):
        ctx, half = lax.axis_index("ctx"), lax.axis_size("ctx") // 2
        self.role = lax.div(ctx, half)
        self.peer = ctx + half - 2 * half * self.role

    def copy(self, source, target, send, recv):
        return pltpu.make_async_remote_copy(
            src_ref=source,
            dst_ref=target,
            send_sem=send,
            recv_sem=recv,
            device_id={"ctx": self.peer},
            device_id_type=MESH,
        )


def pair_gather_kernel(x, peaks, o, peaks_all, own_sem, send, recv, pair_send, pair_recv):
    shard, pair = lax.axis_index("shard"), Pair()
    Greeting().ring("shard").pair().wait()
    role = pair.role
    own_rows = Direct(
        "shard", whole_of(x), lambda d, k: o.at[d, role], send.at[0], recv.at[0]
    )
    peer_rows = Direct(
        "shard",
        lambda d: o.at[shard, 1 - role],
        lambda d, k: o.at[d, 1 - role],
        send.at[1],
        recv.at[1],
    )
    tops = Direct("shard", whole_of(peaks), block_from(peaks_all), send.at[2], recv.at[2])
    across = pair.copy(x, o.at[shard, role], pair_send, pair_recv)
    arrive = pair.copy(x, o.at[shard, 1 - role], pair_send, pair_recv)
    across.start()
    own_rows.start()
    tops.start()
    own = [
        pltpu.make_async_copy(x, o.at[shard, role], own_sem.at[0]),
        pltpu.make_async_copy(peaks, peaks_all.at[shard], own_sem.at[1]),
    ]
    for copy in own:
        copy.start()
    arrive.wait_recv()
    peer_rows.start()
    for copy in own:
        copy.wait()
    across.wait_send()
    for direct in (own_rows, peer_rows, tops):
        direct.wait_recv()
        direct.wait_send()


class PairReduce:
    def __init__(self, x, o, buf, part, peer, send, recv, pair_send, pair_recv):
        self.x, self.o, self.buf, self.part, self.peer = x, o, buf, part, peer
        self.pair = Pair()
        theirs, mine = 1 - self.pair.role, self.pair.role
        self.first = Direct(
            "shard",
            lambda d: x.at[d, theirs],
            lambda d, k: buf.at[0, k - 1],
            send.at[0],
            recv.at[0],
        )
        self.second = Direct(
            "shard", lambda d: x.at[d, mine], lambda d, k: buf.at[1, k - 1], send.at[1], recv.at[1]
        )
        self.across = self.pair.copy(part, peer, pair_send, pair_recv)

    def start(self):
        self.first.start()
        self.second.start()

    def add_up(self, half, role, o, more=None):
        x, buf, shard = self.x, self.buf, self.first.me
        rows = x.shape[2]
        step = 8 if rows % 32 else 32

        @pl.loop(0, rows // step)
        def _(j):
            at = pl.ds(pl.multiple_of(j * step, step), step)
            total = x[shard, role, at].astype(f32)
            for k in range(buf.shape[1]):
                total = total + buf[half, k, at].astype(f32)
            if more is not None:
                total = total + more[at].astype(f32)
            o[at] = total.astype(o.dtype)

    def turn(self):
        self.first.wait_recv()
        self.add_up(0, 1 - self.pair.role, self.part)
        self.across.start()

    def finish(self):
        self.second.wait_recv()
        self.across.wait_recv()
        self.add_up(1, self.pair.role, self.o, self.peer)
        self.across.wait_send()
        self.first.wait_send()
        self.second.wait_send()


def pair_reduce_scratch(n_shard, x):
    sem = pltpu.SemaphoreType.DMA
    return [
        pltpu.VMEM((2, n_shard - 1, *x.shape[2:]), x.dtype),
        pltpu.VMEM(x.shape[2:], x.dtype),
        pltpu.VMEM(x.shape[2:], x.dtype),
        sem((2, n_shard)),
        sem((2, n_shard)),
        sem,
        sem,
    ]


def pair_reduce_kernel(count, *refs):
    ins, outs, rest = refs[:count], refs[count : 2 * count], refs[2 * count :]
    Greeting().ring("shard").pair().wait()
    all_of = [PairReduce(ins[i], outs[i], *rest[7 * i : 7 * i + 7]) for i in range(count)]
    for one in all_of:
        one.start()
    for one in all_of:
        one.turn()
    for one in all_of:
        one.finish()


def many_sum_kernel(axis, x, o, buf, send, recv):
    Greeting().ring(axis).wait()
    direct = Direct(axis, whole_of(x), buffer_of(buf), send, recv)
    direct.start()
    direct.wait_recv()
    total = x[...]
    for k in range(buf.shape[0]):
        total = total + buf[k]
    o[...] = total
    direct.wait_send()


def middle_kernel(x, y, x_all, y_sum, *rest):
    Greeting().ring("ctx").ring("shard").wait()
    returns = PairReduce(y, y_sum, *rest[:7])
    line = LineGather(row_pieces(x, x_all, LINE_CHUNKS), *rest[7:])
    returns.start()
    line.start()
    for k in range(line.line.n):
        line.hop(k)
    returns.turn()
    returns.finish()
    line.finish()


def end_kernel(
    x, wide, out, x_sum, wide_all, out_sum, wide_buf, out_buf, wide_sum,
    own_sem, wide_send, wide_recv, out_send, out_recv, swap_send, swap_recv, *line_refs,
):
    ctx = lax.axis_index("ctx")
    Greeting().ring("ctx").ring("shard").wait()
    wides = Direct("shard", block_of(wide), buffer_of(wide_buf), wide_send, wide_recv)
    outs = Direct("shard", block_of(out), buffer_of(out_buf), out_send, out_recv)
    swap = Direct("ctx", block_of(wide_sum), block_from(wide_all), swap_send, swap_recv)
    line = LineReduce(LINE_CHUNKS, x, x_sum, *line_refs)
    line.start()
    wides.start()
    outs.start()
    line.pass_on()
    wides.wait_recv()
    for b in range(lax.axis_size("ctx")):
        rows = wide_sum.shape[1]
        total = wide[wides.me, b * rows : (b + 1) * rows].astype(f32)
        for k in range(wide_buf.shape[0]):
            total = total + wide_buf[k, b * rows : (b + 1) * rows].astype(f32)
        wide_sum[b] = total.astype(bf16)
    swap.start()
    own = pltpu.make_async_copy(wide_sum.at[ctx], wide_all.at[ctx], own_sem)
    own.start()
    outs.wait_recv()
    add_up(out, out_buf, out_sum, outs.me)
    line.finish()
    own.wait()
    swap.wait_recv()
    for direct in (swap, wides, outs):
        direct.wait_send()


def remote_params(collective_id, megabytes):
    return pltpu.CompilerParams(
        collective_id=collective_id, has_side_effects=True, vmem_limit_bytes=megabytes << 20
    )


LINE_CHUNKS = 4


def start_call(collective_id, x, w, w_query, w_key, w_value, small):
    n_ctx, n_shard = lax.axis_size("ctx"), lax.axis_size("shard")
    n = n_ctx // 2
    packed = (w.shape[0], 3 * w.shape[1] // n_ctx + small.shape[1])
    sem = pltpu.SemaphoreType.DMA
    return pl.pallas_call(
        start_kernel,
        out_shape=[
            jax.ShapeDtypeStruct((n_ctx, *x.shape), bf16),
            jax.ShapeDtypeStruct((n_ctx, n_shard, *w.shape), bf16),
            jax.ShapeDtypeStruct((n_ctx, *packed), bf16),
            jax.ShapeDtypeStruct((n_ctx, n_shard, *packed), bf16),
        ],
        in_specs=[ANY] * 6,
        out_specs=[ANY] * 4,
        scratch_shapes=[sem((5,)), sem((4, n_ctx)), sem((4, n_ctx))]
        + [sem((n_shard,))] * 2
        + [sem((n_shard, n))] * 4
        + line_gather_scratch(n, LINE_CHUNKS + 1),
        compiler_params=remote_params(collective_id, 8),
    )(x, w, w_query, w_key, w_value, small)


def exchange(axis, collective_id, x):
    n = lax.axis_size(axis)
    sem = pltpu.SemaphoreType.DMA
    return pl.pallas_call(
        functools.partial(exchange_kernel, axis),
        out_shape=jax.ShapeDtypeStruct(x.shape, x.dtype),
        in_specs=[ANY],
        out_specs=ANY,
        scratch_shapes=[sem, sem((n,)), sem((n,))],
        compiler_params=remote_params(collective_id, 8),
    )(x)


def pair_gather(collective_id, x, peaks):
    n = lax.axis_size("shard")
    sem = pltpu.SemaphoreType.DMA
    return pl.pallas_call(
        pair_gather_kernel,
        out_shape=[
            jax.ShapeDtypeStruct((n, 2, *x.shape), x.dtype),
            jax.ShapeDtypeStruct((n, *peaks.shape), peaks.dtype),
        ],
        in_specs=[ANY] * 2,
        out_specs=[ANY] * 2,
        scratch_shapes=[sem((2,)), sem((3, n)), sem((3, n)), sem, sem],
        compiler_params=remote_params(collective_id, 8),
    )(x, peaks)


def pair_reduce(collective_id, *arrays):
    n = lax.axis_size("shard")
    return pl.pallas_call(
        functools.partial(pair_reduce_kernel, len(arrays)),
        out_shape=[jax.ShapeDtypeStruct(a.shape[2:], f32) for a in arrays],
        in_specs=[VMEM] * len(arrays),
        out_specs=[VMEM] * len(arrays),
        scratch_shapes=sum((pair_reduce_scratch(n, a) for a in arrays), []),
        compiler_params=remote_params(collective_id, 40),
    )(*arrays)


def many_sum(axis, collective_id, x):
    n = lax.axis_size(axis)
    sem = pltpu.SemaphoreType.DMA
    return pl.pallas_call(
        functools.partial(many_sum_kernel, axis),
        out_shape=jax.ShapeDtypeStruct(x.shape, x.dtype),
        in_specs=[VMEM],
        out_specs=VMEM,
        scratch_shapes=[pltpu.VMEM((n - 1, *x.shape), x.dtype), sem((n,)), sem((n,))],
        compiler_params=remote_params(collective_id, 8),
    )(x)


def middle_call(collective_id, x, y):
    n_ctx, n_shard = lax.axis_size("ctx"), lax.axis_size("shard")
    return pl.pallas_call(
        middle_kernel,
        out_shape=[
            jax.ShapeDtypeStruct((n_ctx, *x.shape), x.dtype),
            jax.ShapeDtypeStruct(y.shape[2:], f32),
        ],
        in_specs=[ANY, VMEM],
        out_specs=[ANY, VMEM],
        scratch_shapes=pair_reduce_scratch(n_shard, y)
        + line_gather_scratch(n_ctx // 2, LINE_CHUNKS),
        compiler_params=remote_params(collective_id, 40),
    )(x, y)


def end_call(collective_id, x, wide, out):
    n_ctx, rows, width = x.shape
    n_shard = lax.axis_size("shard")
    n = n_ctx // 2
    wide_rows, wide_cols = wide.shape[1] // n_ctx, wide.shape[2]
    sem = pltpu.SemaphoreType.DMA
    return pl.pallas_call(
        end_kernel,
        out_shape=[
            jax.ShapeDtypeStruct((rows, width), f32),
            jax.ShapeDtypeStruct((n_ctx, wide_rows, wide_cols), bf16),
            jax.ShapeDtypeStruct(out.shape[1:], f32),
        ],
        in_specs=[VMEM] * 3,
        out_specs=[VMEM] * 3,
        scratch_shapes=[
            pltpu.VMEM((n_shard - 1, *wide.shape[1:]), bf16),
            pltpu.VMEM((n_shard - 1, *out.shape[1:]), bf16),
            pltpu.VMEM((n_ctx, wide_rows, wide_cols), bf16),
            sem,
        ]
        + [sem((n_shard,))] * 4
        + [sem((n_ctx,))] * 2
        + [pltpu.VMEM((n, rows, width), bf16)] * 4
        + [sem((n, LINE_CHUNKS))] * 5,
        compiler_params=remote_params(collective_id, 48),
    )(x, wide, out)


def per_device(
    tokens,
    doc_ids,
    routes,
    attn_gain,
    w_query,
    w_key,
    w_value,
    query_gain,
    key_gain,
    w_out,
    ffn_gain,
    w_router,
    w_gate,
    w_up,
    w_down,
    clip_threshold,
    cotangent,
):
    both = ("ctx", "shard")
    n_ctx, n_shard = lax.axis_size("ctx"), lax.axis_size("shard")
    ctx, shard = lax.axis_index("ctx"), lax.axis_index("shard")
    x_own = tokens[0]
    rows, width = x_own.shape
    part = w_query.shape[0]
    cols = width // n_ctx
    heads = cols // HEAD
    count = rows * n_ctx
    local = w_gate.shape[0]
    experts = local * n_shard

    top = routes.shape[2]
    spare = jnp.zeros((part, LANES - 4 - experts - rows // part * (1 + top)), bf16)
    small = jnp.concatenate(
        [
            jnp.stack([attn_gain, query_gain, key_gain, ffn_gain], axis=1),
            w_router,
            doc_ids.reshape(part, rows // part).astype(bf16),
            routes.reshape(part, rows // part * top).astype(bf16),
            spare,
        ],
        axis=1,
    )
    grad_own = cotangent[0]
    x_all, out_w, _, packed = start_call(
        1, x_own, w_out, w_query, w_key, w_value, small
    )
    x_all = x_all.reshape(count, width)
    out_w = out_w.reshape(width, width)
    weights = packed[..., : 3 * cols].reshape(width, 3 * cols)
    small_all = packed[..., 3 * cols :]
    out_w_own = lax.dynamic_slice_in_dim(out_w, ctx * cols, cols, 0)
    gains = small_all[..., : 4 + experts].reshape(width, 4 + experts)
    gain_attn, gain_query, gain_key, gain_ffn = (gains[:, i].astype(f32) for i in range(4))
    router_w = gains[:, 4:]
    gain_query = lax.dynamic_slice_in_dim(gain_query, ctx * cols, cols)
    gain_key = lax.dynamic_slice_in_dim(gain_key, ctx * cols, cols)
    tail = small_all[..., 4 + experts :].astype(jnp.int32)
    docs = lax.dynamic_index_in_dim(tail[..., : rows // part], shard, 1, False).reshape(count)
    span = n_ctx // 2
    role = lax.div(ctx, span)
    routes_all = tail[..., rows // part : rows // part * (1 + top)].reshape(
        n_ctx, n_shard, rows, top
    )
    routes_all = jnp.stack(
        [lax.dynamic_index_in_dim(routes_all, ctx + span * (r - role), 0, False) for r in (0, 1)],
        axis=1,
    ).reshape(2 * n_shard * rows, top)

    def swap(u):
        both = lax.all_gather(
            u, "ctx", axis=0, axis_index_groups=[[i, i + span] for i in range(span)]
        )
        return lax.dynamic_index_in_dim(both, 1 - role, 0, False)

    def in_order(mine, theirs):
        return jnp.where(role == 0, jnp.stack([mine, theirs]), jnp.stack([theirs, mine]))

    half = local // 2
    ff = w_gate.shape[2]
    own_w = jnp.concatenate([w_gate, w_up, w_down.transpose(0, 2, 1)], axis=2)
    keep_w = lax.dynamic_slice_in_dim(own_w, role * half, half, 0)
    give_w = lax.dynamic_slice_in_dim(own_w, (1 - role) * half, half, 0)
    spans = [list(range(r * span, (r + 1) * span)) for r in (0, 1)]
    early = [swap(give_w[e]) for e in range(half)] + [swap(grad_own)]
    x_all, early[0], early[-1] = lax.optimization_barrier((x_all, early[0], early[-1]))
    expert_w = [
        lax.all_gather(
            in_order(keep_w[e], early[e]),
            "ctx",
            axis=1,
            tiled=True,
            axis_index_groups=spans,
        ).reshape(width, 3 * ff)
        for e in range(half)
    ]

    grad_all = lax.all_gather(in_order(grad_own, early[-1]), "shard", axis=0, tiled=False)
    grad_all = grad_all.reshape(2 * n_shard * rows, width)

    x_wide = x_all.astype(f32)
    inverse_one = inverse_rms(x_wide)
    hidden_one = (x_wide * inverse_one * gain_attn).astype(bf16)
    linear = dot(hidden_one, weights)
    query_lin, key_lin = linear[:, :cols], linear[:, cols : 2 * cols]
    value = linear[:, 2 * cols :].astype(bf16)
    squares = jnp.stack(
        [jnp.sum(query_lin * query_lin, axis=1), jnp.sum(key_lin * key_lin, axis=1)]
    )
    squares = many_sum("ctx", 6, squares)
    inverse_qk = lax.rsqrt(squares / width + norm_eps)
    inverse_q, inverse_k = inverse_qk[0][:, None], inverse_qk[1][:, None]
    cosine, sine = rope_tables(count)
    query_n, key_n = query_lin * inverse_q, key_lin * inverse_k
    query = rotate(query_n * gain_query, cosine, sine).astype(bf16)
    key = rotate(key_n * gain_key, cosine, sine).astype(bf16)
    mixed, log_total, peaks = attend_forward(query, key, value, docs)
    x_f = x_own.astype(f32)
    mixed_own = exchange("ctx", 2, mixed.reshape(n_ctx, rows, cols))
    mixed_own = mixed_own.transpose(1, 0, 2).reshape(rows, width)
    after = x_f + dot(mixed_own, out_w)
    inverse_two = inverse_rms(after)
    normed_two = after * inverse_two
    hidden_two = (normed_two * gain_ffn).astype(bf16)

    hidden_all, peaks = pair_gather(3, hidden_two, peaks)
    hidden_all = hidden_all.reshape(2 * n_shard * rows, width)
    peaks = jnp.max(peaks, axis=0)[:, 0, 0]
    logits = dot(hidden_all, router_w)
    named = jnp.any(routes_all[:, :, None] == jnp.arange(experts)[None, None, :], axis=1)
    probs = jax.nn.softmax(logits, axis=1)
    selected = jnp.where(named, probs, 0.0)
    selected_sum = jnp.sum(selected, axis=1, keepdims=True)
    gates = selected / selected_sum
    first = shard * local + role * half
    gates_own = lax.dynamic_slice_in_dim(gates, first, half, 1)
    named_own = lax.dynamic_slice_in_dim(named, first, half, 1)
    grad_wide = grad_all.astype(f32)
    moe_part = jnp.zeros(grad_all.shape, f32)
    back_part = jnp.zeros(grad_all.shape, f32)
    grad_gates, expert_grads = [], []
    for e in range(half):
        wide, down = expert_w[e][:, : 2 * ff], expert_w[e][:, 2 * ff :]
        gate_col = gates_own[:, e : e + 1]
        hidden = dot(hidden_all, wide)
        gate_h, up_h = hidden[:, :ff], hidden[:, ff:]
        sig = jax.nn.sigmoid(gate_h)
        silu = gate_h * sig
        act = (silu * up_h).astype(bf16)
        result = contract_cols(act, down).astype(bf16).astype(f32)
        moe_part = moe_part + gate_col * result
        grad_gates.append(
            jnp.where(named_own[:, e], jnp.sum(grad_wide * result, axis=1), 0.0)
        )
        grad_y = (gate_col * grad_wide).astype(bf16)
        grad_act = dot(grad_y, down)
        grad_h = jnp.concatenate(
            [grad_act * up_h * sig * (1.0 + gate_h * (1.0 - sig)), grad_act * silu], axis=1
        ).astype(bf16)
        back_part = back_part + contract_cols(grad_h, wide).astype(bf16).astype(f32)
        grad_w = [
            contract_rows(hidden_all, grad_h).astype(bf16),
            contract_rows(grad_y, act).astype(bf16),
        ]
        hidden_all, back_part, grad_w = lax.optimization_barrier((hidden_all, back_part, grad_w))
        expert_grads.append(
            [
                lax.psum_scatter(
                    u.reshape(2, width // 2, -1),
                    "ctx",
                    scatter_dimension=1,
                    tiled=True,
                    axis_index_groups=spans,
                )
                for u in grad_w
            ]
        )
    slots = jnp.stack(grad_gates).reshape(half, n_shard, 2, rows).transpose(1, 2, 0, 3)
    grad_gates = lax.dynamic_update_slice_in_dim(
        jnp.zeros((n_shard, 2, experts, rows), f32), slots, first, 2
    )
    back_sum, grad_gates = pair_reduce(
        4, back_part.astype(bf16).reshape(n_shard, 2, rows, width), grad_gates
    )
    grad_gates = grad_gates.T
    def own_rows(u):
        return lax.dynamic_slice_in_dim(u, (2 * shard + role) * rows, rows, 0)

    gates_t, probs_t, named_t, sum_t = map(own_rows, (gates, probs, named, selected_sum))
    grad_selected = (
        grad_gates - jnp.sum(gates_t * grad_gates, axis=1, keepdims=True)
    ) / sum_t
    grad_probs = jnp.where(named_t, grad_selected, 0.0)
    grad_logits = (
        probs_t * (grad_probs - jnp.sum(probs_t * grad_probs, axis=1, keepdims=True))
    ).astype(bf16)
    grad_router = contract_rows(hidden_two, grad_logits)
    grad_hidden = back_sum + contract_cols(grad_logits, router_w)
    grad_gain_ffn = jnp.sum(grad_hidden * normed_two, axis=0)
    scaled_two = grad_hidden * gain_ffn
    grad_after = grad_own.astype(f32) + inverse_two * (
        scaled_two - normed_two * jnp.mean(scaled_two * normed_two, axis=1, keepdims=True)
    )

    moe_part = moe_part.astype(bf16).reshape(n_shard, 2, rows, width)
    grad_attn, moe_sum = middle_call(5, grad_after.astype(bf16), moe_part)
    grad_attn = grad_attn.reshape(count, width)
    output = (after + moe_sum).astype(bf16)
    grad_mixed = contract_cols(grad_attn, out_w_own).astype(bf16)
    grad_out_w = contract_rows(mixed, grad_attn)
    grad_query_rot, grad_key_rot, grad_value = attend_backward(
        query, key, value, docs, log_total, grad_mixed
    )
    grad_query_rot, expert_grads = lax.optimization_barrier((grad_query_rot, expert_grads))
    kept = [[lax.dynamic_index_in_dim(u, role, 0, False) for u in sums] for sums in expert_grads]
    peers = swap(
        jnp.stack(
            [
                jnp.concatenate(
                    [lax.dynamic_index_in_dim(u, 1 - role, 0, False) for u in sums], axis=1
                )
                for sums in expert_grads
            ]
        )
    )
    peers = [(peer[:, : 2 * ff], peer[:, 2 * ff :]) for peer in peers]
    both_halves = [
        in_order(jnp.stack([k[i] for k in kept]), jnp.stack([p[i] for p in peers]))
        .reshape(local, width // n_ctx, -1)
        .astype(f32)
        for i in (0, 1)
    ]
    grad_query_n = rotate(grad_query_rot, cosine, -sine)
    grad_key_n = rotate(grad_key_rot, cosine, -sine)
    grad_gain_query = jnp.sum(grad_query_n * query_n, axis=0)
    grad_gain_key = jnp.sum(grad_key_n * key_n, axis=0)
    scaled_q, scaled_k = grad_query_n * gain_query, grad_key_n * gain_key
    peak_row = lax.dynamic_update_slice_in_dim(jnp.zeros((count,), f32), peaks, ctx * heads, 0)
    inner = jnp.stack(
        [jnp.sum(scaled_q * query_n, axis=1), jnp.sum(scaled_k * key_n, axis=1), peak_row]
    )
    inner = many_sum("ctx", 7, inner)
    peak_all = inner[2, :HEADS]
    inner = inner / width
    grad_linear = jnp.concatenate(
        [
            inverse_q * (scaled_q - query_n * inner[0][:, None]),
            inverse_k * (scaled_k - key_n * inner[1][:, None]),
            grad_value,
        ],
        axis=1,
    ).astype(bf16)
    grad_weights = contract_rows(hidden_one, grad_linear)
    hidden_part = contract_cols(grad_linear, weights)
    grad_gain_attn = jnp.sum(hidden_part * (x_wide * inverse_one), axis=0)
    grad_small = jnp.concatenate(
        [jnp.stack([grad_gain_attn, grad_gain_ffn], axis=1), grad_router], axis=1
    )
    grad_small = jnp.pad(grad_small, ((0, 0), (0, LANES - 2 - experts)))
    grad_weights = (
        jnp.concatenate([grad_weights, grad_small], axis=1)
        .astype(bf16)
        .reshape(n_ctx, n_shard, part, 3 * cols + LANES)
        .transpose(1, 0, 2, 3)
        .reshape(n_shard, n_ctx * part, 3 * cols + LANES)
    )
    grad_gain_qk = jnp.pad(
        jnp.stack([grad_gain_query, grad_gain_key], axis=1), ((0, 0), (0, LANES - 2))
    )
    grad_out_w = (
        jnp.concatenate([grad_out_w, grad_gain_qk], axis=1)
        .astype(bf16)
        .reshape(n_shard, part, width + LANES)
    )
    grad_hidden_one, grad_weights, grad_out_w = end_call(
        8, hidden_part.astype(bf16).reshape(n_ctx, rows, width), grad_weights, grad_out_w
    )
    grad_weights = grad_weights.astype(f32)
    grad_small = jnp.sum(grad_weights[..., 3 * cols :], axis=0)
    grad_weights = (
        grad_weights[..., : 3 * cols]
        .reshape(n_ctx, part, 3, cols)
        .transpose(2, 1, 0, 3)
        .reshape(3, part, width)
    )
    inverse_own = inverse_rms(x_f)
    normed_own = x_f * inverse_own
    scaled_one = grad_hidden_one * gain_attn
    grad_inputs = grad_after + inverse_own * (
        scaled_one - normed_own * jnp.mean(scaled_one * normed_own, axis=1, keepdims=True)
    )

    factors = jnp.sqrt(clip_threshold / jnp.maximum(peak_all, clip_threshold))
    col_scale = jnp.repeat(factors, HEAD)
    query_clipped = (w_query.astype(f32) * col_scale[None, :]).astype(bf16)
    key_clipped = (w_key.astype(f32) * col_scale[None, :]).astype(bf16)
    return (
        output[None],
        grad_inputs[None],
        grad_small[:, 0],
        grad_weights[0],
        grad_weights[1],
        grad_weights[2],
        grad_out_w[:, width],
        grad_out_w[:, width + 1],
        grad_out_w[:, :width],
        grad_small[:, 1],
        grad_small[:, 2 : 2 + experts],
        both_halves[0][..., :ff],
        both_halves[0][..., ff:],
        both_halves[1].transpose(0, 2, 1),
        query_clipped,
        key_clipped,
        factors,
    )


def solution(mesh):
    both = ("ctx", "shard")
    return jax.shard_map(
        per_device,
        mesh=mesh,
        in_specs=(
            P("shard", "ctx", None),
            P("shard", "ctx"),
            P("shard", "ctx", None),
            P(both),
            P(both, None),
            P(both, None),
            P(both, None),
            P(both),
            P(both),
            P(both, None),
            P(both),
            P(both, None),
            P("shard", "ctx", None),
            P("shard", "ctx", None),
            P("shard", None, "ctx"),
            P(),
            P("shard", "ctx", None),
        ),
        out_specs=(
            P("shard", "ctx", None),
            P("shard", "ctx", None),
            P(both),
            P(both, None),
            P(both, None),
            P(both, None),
            P(both),
            P(both),
            P(both, None),
            P(both),
            P(both, None),
            P("shard", "ctx", None),
            P("shard", "ctx", None),
            P("shard", None, "ctx"),
            P(both, None),
            P(both, None),
            P(),
        ),
        check_vma=False,
    )
```

time: 1590 us -> 1440 us (0.906)
  Pallas kernels: 1010 us -> 918 us
  other arithmetic: 111 us -> 85.7 us
  matrix products: 325 us -> 309 us
  local copies, waits for them, and re-layouts: 75.3 us -> 91.2 us
    pallas_call x10 -> x6, Pallas kernels: 920 us -> 778 us  [the longest x1 252 us: start_call(): pl.pallas_call(start_kernel, out_shape=[jax.ShapeDtypeStruct((n_ctx, *x.s...]
    pallas_call x2, Pallas kernels: 32.2 us -> 79.6 us  [many_sum(): pl.pallas_call(functools.partial(many_sum_kernel, axis), out_shape=jax.Sh...]
    another operation x8 -> x11, other arithmetic: 49.9 us -> 20.8 us  [the longest x2 21.1 us: per_device(): jnp.stack(grad_wide_w[g])]
    dot_general x11 -> x7, matrix products: 118 us -> 102 us  [contract_cols(): lax.dot_general(a, b, (((1,), (1,)), ((), ())), preferred_element_type=f32)]
    unnamed x239 -> x194, local copies, waits for them, and re-layouts: 34.7 us -> 30.4 us
    dot_general x11 -> x7, matrix products: 93.8 us -> 92.4 us  [contract_rows(): lax.dot_general(a, b, (((0,), (0,)), ((), ())), preferred_element_type=f32)]
    dot_general x11 -> x7, matrix products: 113 us -> 115 us  [dot(): return jnp.dot(a, b, preferred_element_type=f32)]
  transfers between devices with their start and end apart: 9 -> 11, of which waited for: 1 -> 2; matrix products, arithmetic and copies ran while one was open for 26% -> 31% of each run, Pallas kernels for 60% -> 64%
where the time goes in v2:
time: 1440 us; the launch traced here: 1430 us
  Pallas kernels  918 us (64%)
  matrix products  309 us (21%)
  local copies, waits for them, and re-layouts  91.2 us (6%)
  other arithmetic  85.7 us (6%)
  between operations  16.5 us (1%)
    pallas_call x1, Pallas kernels, start_call(): pl.pallas_call(start_kernel, out_shape=[jax.ShapeDtypeStruct((n_ctx, *x.s...  252 us
    pallas_call x1, Pallas kernels, middle_call(): pl.pallas_call(middle_kernel, out_shape=[jax.ShapeDtypeStruct((n_ctx, *x....  189 us
    pallas_call x1, Pallas kernels, end_call(): pl.pallas_call(end_kernel, out_shape=[jax.ShapeDtypeStruct((rows, width),...  118 us
    dot_general x7, matrix products, dot(): return jnp.dot(a, b, preferred_element_type=f32)  115 us
    dot_general x7, matrix products, contract_cols(): lax.dot_general(a, b, (((1,), (1,)), ((), ())), preferred_element_type=f32)  102 us
    pallas_call x1, Pallas kernels, pair_reduce(): pl.pallas_call(functools.partial(pair_reduce_kernel, len(arrays)), out_sh...  101 us
    pallas_call x1, Pallas kernels, pair_gather(): pl.pallas_call(pair_gather_kernel, out_shape=[jax.ShapeDtypeStruct((n, 2,...  97 us
    dot_general x7, matrix products, contract_rows(): lax.dot_general(a, b, (((0,), (0,)), ((), ())), preferred_element_type=f32)  92.4 us
  transfers between devices with their start and end apart: 11, of which 2 were waited for; matrix products, arithmetic and copies ran while one was open for 31% of the time, Pallas kernels for 64%

profile of v2, /device:TPU:0, one launch (start us, length us, event | category | flops | bytes accessed | tf_op | source)
XLA Modules:
  0.0 1432.0 jit_solution(9218737855085300810)
XLA Ops:
  19.1 251.6 %shard_map.296 = (bf16[8,256,2048]{2,1,0:T(8,128)(2,1)S(1)}, bf16[8,4,64,2048]{3,2,1,0:T(8,128)(2,1)S(1)}, bf16[8,64,896]{2,1,0:T(8,128)(2,1)}, bf16[8,4,64,896]{3,2,1,0:T(8,128)(2,1)S(1)}) custom-call(bf16[256,2048]{1,0:T(8,128)(2,1)S(1)} %bitcast.184, bf16[64,2048]{1,0:T(8,128)(2,1)S(1)} %copy-done.22, bf16[64,2048]{1,0:T(8,128)(2,1)S(1)} %copy-done.17, ...), custom_call_target="tpu_custom_call" | custom-call | tf_op jit(solution)/shard_map/pallas_call | solution.py:807
  343.8 23.0 %shard_map.298 = (bf16[2048,256]{1,0:T(8,128)(2,1)S(1)}, f32[2,2048,1]{2,1,0:T(8,128)}, f32[2,8,128]{2,1,0:T(8,128)S(1)}) custom-call(bf16[2048,256]{1,0:T(8,128)(2,1)S(1)} %pad_maximum_fusion.15.q_ref, bf16[2048,256]{1,0:T(8,128)(2,1)S(1)} %pad_maximum_fusion.16.k_ref, bf16[2048,256]{1,0:T(8,128)(2,1)S(1)} %slice.429.v_ref, ...), custom_call_target="tpu_custom_call" | custom-call | flops 4294967296 | bytes 4194304 | tf_op jit(solution)/shard_map/pallas_call | solution.py:111
  366.8 19.9 %shard_map.299 = bf16[8,256,256]{2,1,0:T(8,128)(2,1)S(1)} custom-call(bf16[8,256,256]{2,1,0:T(8,128)(2,1)S(1)} %bitcast.199), custom_call_target="tpu_custom_call" | custom-call | tf_op jit(solution)/shard_map/pallas_call | solution.py:828
  404.0 97.0 %shard_map.300 = (bf16[4,2,256,2048]{3,2,1,0:T(8,128)(2,1)S(1)}, f32[4,2,8,128]{3,2,1,0:T(8,128)S(1)}) custom-call(bf16[256,2048]{1,0:T(8,128)(2,1)S(1)} %multiply_convert_fusion.8.x, f32[2,8,128]{2,1,0:T(8,128)S(1)} %get-tuple-element.55.peaks), custom_call_target="tpu_custom_call" | custom-call | tf_op jit(solution)/shard_map/pallas_call | solution.py:841
  506.1 10.3 fusion.8
  517.6 24.3 %fusion.17 = f32[2048,2048]{0,1:T(8,128)} fusion(bf16[2048,2048]{1,0:T(8,128)(2,1)} %bitcast.186, bf16[2048,3072]{1,0:T(8,128)(2,1)} %bitcast.277), kind=kOutput, calls=%fused_computation.41 | convolution fusion | flops 17179869184 | bytes 33554432 | tf_op jit(solution)/shard_map/dot_general | solution.py:23
  541.9 22.9 %multiply_convert_fusion.5 = (bf16[2048,1024]{0,1:T(8,128)(2,1)}, bf16[2048,1024]{0,1:T(8,128)(2,1)}, bf16[2048,1024]{0,1:T(8,128)(2,1)}) fusion(f32[2048,2048]{0,1:T(8,128)} %fusion.17, bf16[2048,2048]{1,0:T(8,128)(2,1)} %get-tuple-element.162, bf16[2048,3072]{1,0:T(8,128)(2,1)} %bitcast.278), kind=kOutput, calls=%fused_computation.30 | convolution fusion | flops 8621391872 | bytes 41943040 | tf_op jit(solution)/shard_map/dot_general | solution.py:23
  564.8 14.2 convolution_convert_fusion.5
  579.0 24.1 %convolution_convert_fusion.3 = bf16[2048,2048]{1,0:T(8,128)(2,1)} fusion(bf16[2048,2048]{1,0:T(8,128)(2,1)} %bitcast.187, bf16[2048,1024]{0,1:T(8,128)(2,1)} %get-tuple-element.153, bf16[2048,1024]{0,1:T(8,128)(2,1)} %get-tuple-element.152), kind=kOutput, calls=%fused_computation.36 | convolution fusion | flops 17200840704 | bytes 25165824 | tf_op jit(solution)/shard_map/dot_general | solution.py:27
  603.1 21.8 %convert_convert_fusion = f32[2048,2048]{1,0:T(8,128)} fusion(bf16[2048,3072]{1,0:T(8,128)(2,1)S(1)} %bitcast.282, bf16[2048,1024]{0,1:T(8,128)(2,1)} %get-tuple-element.153, bf16[2048,1024]{0,1:T(8,128)(2,1)} %get-tuple-element.152), kind=kOutput, calls=%fused_computation.28 | convolution fusion | flops 17205035008 | bytes 33554432 | tf_op jit(solution)/shard_map/dot_general | solution.py:31
  632.7 24.5 %fusion.14 = f32[2048,2048]{0,1:T(8,128)} fusion(bf16[2048,2048]{1,0:T(8,128)(2,1)} %bitcast.188, bf16[2048,3072]{1,0:T(8,128)(2,1)} %bitcast.283), kind=kOutput, calls=%fused_computation.38 | convolution fusion | flops 17179869184 | bytes 33554432 | tf_op jit(solution)/shard_map/dot_general | solution.py:23
  657.2 22.7 %multiply_convert_fusion.2 = (bf16[2048,1024]{0,1:T(8,128)(2,1)}, bf16[2048,1024]{0,1:T(8,128)(2,1)}, bf16[2048,1024]{0,1:T(8,128)(2,1)}) fusion(f32[2048,2048]{0,1:T(8,128)} %fusion.14, bf16[2048,2048]{1,0:T(8,128)(2,1)} %get-tuple-element.161, bf16[2048,3072]{1,0:T(8,128)(2,1)} %bitcast.284), kind=kOutput, calls=%fused_computation.24 | convolution fusion | flops 8621391872 | bytes 41943040 | tf_op jit(solution)/shard_map/dot_general | solution.py:23
  679.9 14.7 %convolution_convert_fusion.4 = bf16[2048,1024]{1,0:T(8,128)(2,1)} fusion(bf16[2048,2048]{1,0:T(8,128)(2,1)} %get-tuple-element.161, bf16[2048,1024]{0,1:T(8,128)(2,1)} %get-tuple-element.157), kind=kOutput, calls=%fused_computation.46 | convolution fusion | flops 8592031744 | bytes 16777216 | tf_op jit(solution)/shard_map/dot_general | solution.py:27
  694.6 21.2 %convolution_convert_fusion.2 = bf16[2048,2048]{1,0:T(8,128)(2,1)} fusion(bf16[2048,2048]{1,0:T(8,128)(2,1)} %bitcast.189, bf16[2048,1024]{0,1:T(8,128)(2,1)S(1)} %copy-done.85, bf16[2048,1024]{0,1:T(8,128)(2,1)S(1)} %copy-done.84), kind=kOutput, calls=%fused_computation.35 | convolution fusion | flops 17200840704 | bytes 25165824 | tf_op jit(solution)/shard_map/dot_general | solution.py:27
  715.8 24.9 %convert_add_fusion = bf16[2048,2048]{1,0:T(8,128)(2,1)} fusion(f32[2048,2048]{1,0:T(8,128)} %convert_convert_fusion, bf16[2048,3072]{1,0:T(8,128)(2,1)} %bitcast.285, bf16[2048,1024]{0,1:T(8,128)(2,1)} %get-tuple-element.151, bf16[2048,1024]{0,1:T(8,128)(2,1)S(1)} %copy-done.84), kind=kOutput, calls=%fused_computation.19 | convolution fusion | flops 17213423616 | bytes 41943040 | tf_op jit(solution)/shard_map/dot_general | solution.py:31
  744.9 14.0 convolution_convert_fusion
  758.9 22.3 %fusion.9 = (f32[2048]{0:T(1024)S(1)}, f32[2048]{0:T(1024)S(1)}, bf16[2048,2048]{1,0:T(8,128)(2,1)}) fusion(bf16[4,2,256,2048]{3,2,1,0:T(8,128)(2,1)} %all-gather.13.cloned.1.call-done, bf16[2048,2048]{1,0:T(8,128)(2,1)} %convolution_convert_fusion, f32[2048]{0:T(1024)S(1)} %bitcast.253, f32[2048]{0:T(1024)S(1)} %bitcast.255, ...), kind=kOutput, calls=%fused_computation.17 | convolution fusion | flops 8640262144 | bytes 33587200 | tf_op jit(solution)/shard_map/dot_general | solution.py:31
  784.8 101.3 %shard_map.301 = (f32[256,2048]{1,0:T(8,128)S(1)}, f32[16,256]{1,0:T(8,128)S(1)}) custom-call(bf16[4,2,256,2048]{3,2,1,0:T(8,128)(2,1)S(1)} %bitcast.198, f32[4,2,16,256]{3,2,1,0:T(8,128)S(1)} %fusion.106.refs_1_), custom_call_target="tpu_custom_call" | custom-call | tf_op jit(solution)/shard_map/pallas_call | solution.py:856
  890.1 189.4 %shard_map.302 = (bf16[8,256,2048]{2,1,0:T(8,128)(2,1)S(1)}, f32[256,2048]{1,0:T(8,128)S(1)}) custom-call(bf16[256,2048]{1,0:T(8,128)(2,1)S(1)} %fusion.117.x, bf16[4,2,256,2048]{3,2,1,0:T(8,128)(2,1)} %bitcast.209), custom_call_target="tpu_custom_call" | custom-call | tf_op jit(solution)/shard_map/pallas_call | solution.py:881
  1084.9 37.6 %shard_map.303 = (f32[2048,256]{1,0:T(8,128)}, f32[2048,256]{1,0:T(8,128)}, f32[2048,256]{1,0:T(8,128)}) custom-call(bf16[2048,256]{1,0:T(8,128)(2,1)} %copy-done.14, bf16[2048,256]{1,0:T(8,128)(2,1)} %copy-done.13, bf16[2048,256]{1,0:T(8,128)(2,1)} %copy-done.16, s32[2048,1]{1,0:T(8,128)} %copy-done.15, s32[1,2048]{1,0:T(1,128)} %copy-done.24, ...), custom_call_target="tpu_custom_call" | custom-call | flops 10737418240 | bytes 10485760 | tf_op jit(solution)/shard_map/pallas_call | solution.py:134
  1153.9 73.6 %shard_map.304 = f32[3,2048]{1,0:T(4,128)S(1)} custom-call(f32[3,2048]{1,0:T(4,128)S(1)} %pad_maximum_fusion.18.x), custom_call_target="tpu_custom_call" | custom-call | tf_op jit(solution)/shard_map/pallas_call | solution.py:869
  1233.8 11.6 fusion.3
  1246.2 10.5 convolution_convert_fusion.6
  1259.5 118.5 %shard_map.305 = (f32[256,2048]{1,0:T(8,128)S(1)}, bf16[8,64,896]{2,1,0:T(8,128)(2,1)S(1)}, f32[64,2176]{1,0:T(8,128)S(1)}) custom-call(bf16[8,256,2048]{2,1,0:T(8,128)(2,1)} %bitcast.212, bf16[4,512,896]{2,1,0:T(8,128)(2,1)} %bitcast.208, bf16[4,64,2176]{2,1,0:T(8,128)(2,1)S(1)} %pad_maximum_fusion.14.out), custom_call_target="tpu_custom_call" | custom-call | tf_op jit(solution)/shard_map/pallas_call | solution.py:901
  (363 shorter events, 219.7 us)
Async XLA Ops:
  7.2 271.9 %all-gather.11.cloned.1.call-start = ((), (), s32[]{:S(2)}) async-start(), calls=%async_computation.5 | async-start | bytes 3145728 | tf_op jit(solution)/shard_map/all_gather | solution.py:994
  7.9 272.5 %all-gather.9.cloned.1.call-start = ((), (), s32[]{:S(2)}) async-start(), calls=%async_computation.4 | async-start | bytes 4718592 | tf_op jit(solution)/shard_map/all_gather | solution.py:994
  17.1 381.0 %all-gather.17.cloned.1.call-start = ((), (), s32[]{:S(2)}) async-start(), calls=%async_computation.8 | async-start | bytes 4718592 | tf_op jit(solution)/shard_map/all_gather | solution.py:994
  17.9 265.2 %copy-start.34 = (bf16[1,256,2048]{2,1,0:T(8,128)(2,1)S(1)}, bf16[1,256,2048]{2,1,0:T(8,128)(2,1)}, u32[]{:S(2)}) copy-start(bf16[1,256,2048]{2,1,0:T(8,128)(2,1)} %param.33) | copy-start | bytes 3145732
  17.9 488.2 %all-gather.13.cloned.1.call-start = ((), (), s32[]{:S(2)}) async-start(), calls=%async_computation.6 | async-start | bytes 10485760 | tf_op jit(solution)/shard_map/all_gather | solution.py:1021
  284.8 232.8 %all-gather.15.cloned.1.call-start = ((), (), s32[]{:S(2)}) async-start(), calls=%async_computation.7 | async-start | bytes 15728640 | tf_op jit(solution)/shard_map/all_gather | solution.py:1011
  289.7 343.0 %all-gather.19.cloned.1.call-start = ((), (), s32[]{:S(2)}) async-start(), calls=%async_computation.9 | async-start | bytes 15728640 | tf_op jit(solution)/shard_map/all_gather | solution.py:1011
  290.9 211.2 %copy-start.30 = (bf16[8,4,64,20]{3,2,1,0:T(8,128)(2,1)}, bf16[8,4,64,20]{3,2,1,0:T(8,128)(2,1)S(1)}, u32[]{:S(2)}) copy-start(bf16[8,4,64,20]{3,2,1,0:T(8,128)(2,1)S(1)} %slice.214) | copy-start | bytes 245764
  297.4 46.4 %copy-start.24 = (s32[1,2048]{1,0:T(1,128)}, s32[1,2048]{1,0:T(1,128)S(1)}, u32[]{:S(2)}) copy-start(s32[1,2048]{1,0:T(1,128)S(1)} %broadcast_in_dim_reshape.5.doc_k_ref) | copy-start | bytes 24580
  297.6 46.1 %copy-start.15 = (s32[2048,1]{1,0:T(8,128)}, s32[2048,1]{1,0:T(8,128)S(1)}, u32[]{:S(2)}) copy-start(s32[2048,1]{1,0:T(8,128)S(1)} %broadcast_in_dim_reshape.6.doc_q_ref) | copy-start | bytes 24580
  311.7 92.0 %copy-start.50 = (f32[2048,1]{0,1:T(1,128)}, f32[2048,1]{0,1:T(1,128)S(1)}, u32[]{:S(2)}) copy-start(f32[2048,1]{0,1:T(1,128)S(1)} %copy.210) | copy-start | bytes 24580
  314.5 190.8 %copy-start.48 = (pred[2048,16]{0,1:T(8,128)(4,1)}, pred[2048,16]{0,1:T(8,128)(4,1)S(1)}, u32[]{:S(2)}) copy-start(pred[2048,16]{0,1:T(8,128)(4,1)S(1)} %fusion.99) | copy-start | bytes 98308
  403.7 729.2 %reduce-scatter.7.cloned.1.call-start = ((), (), s32[]{:S(2)}) async-start(), calls=%async_computation.11 | async-start | bytes 5242880 | tf_op jit(solution)/shard_map/reduce_scatter | solution.py:1091
  624.9 508.0 %reduce-scatter.11.cloned.1.call-start = ((), (), s32[]{:S(2)}) async-start(), calls=%async_computation.13 | async-start | bytes 5242880 | tf_op jit(solution)/shard_map/reduce_scatter | solution.py:1091
  740.7 392.1 %reduce-scatter.5.cloned.1.call-start = ((), (), s32[]{:S(2)}) async-start(), calls=%async_computation.10 | async-start | bytes 10485760 | tf_op jit(solution)/shard_map/reduce_scatter | solution.py:1091
  741.4 391.4 %reduce-scatter.9.cloned.1.call-start = ((), (), s32[]{:S(2)}) async-start(), calls=%async_computation.12 | async-start | bytes 10485760 | tf_op jit(solution)/shard_map/reduce_scatter | solution.py:1091
  742.0 664.2 %all-gather.21.cloned.1.call-start = ((), (), s32[]{:S(2)}) async-start(), calls=%async_computation.14 | async-start | bytes 9437184 | tf_op jit(solution)/shard_map/all_gather | solution.py:994
  784.8 102.9 %copy-start.27 = (f32[256,2048]{1,0:T(8,128)S(1)}, f32[256,2048]{1,0:T(8,128)}, u32[]{:S(2)}) copy-start(f32[256,2048]{1,0:T(8,128)} %get-tuple-element.229) | copy-start | bytes 6291460
  784.8 102.9 %copy-start.31 = (bf16[8,4,64,20]{3,2,1,0:T(8,128)(2,1)S(1)}, bf16[8,4,64,20]{3,2,1,0:T(8,128)(2,1)}, u32[]{:S(2)}) copy-start(bf16[8,4,64,20]{3,2,1,0:T(8,128)(2,1)} %copy-done.30) | copy-start | bytes 245764
  784.8 102.9 %copy-start.51 = (f32[2048,1]{0,1:T(1,128)S(1)}, f32[2048,1]{0,1:T(1,128)}, u32[]{:S(2)}) copy-start(f32[2048,1]{0,1:T(1,128)} %copy-done.50) | copy-start | bytes 24580
  784.8 102.9 %copy-start.67 = (f32[256]{0:T(256)S(1)}, f32[256]{0:T(256)}, u32[]{:S(2)}) copy-start(f32[256]{0:T(256)} %copy-done.66) | copy-start | bytes 3076
  889.4 190.0 %copy-start.32 = (f32[256,2048]{1,0:T(8,128)}, f32[256,2048]{1,0:T(8,128)S(1)}, u32[]{:S(2)}) copy-start(f32[256,2048]{1,0:T(8,128)S(1)} %get-tuple-element.232) | copy-start | bytes 6291460
  1084.9 40.3 %copy-start.5 = (bf16[256,2048]{1,0:T(8,128)(2,1)S(1)}, bf16[256,2048]{1,0:T(8,128)(2,1)}, u32[]{:S(2)}) copy-start(bf16[256,2048]{1,0:T(8,128)(2,1)} %copy-done.4) | copy-start | bytes 3145732
  1148.5 85.3 %slice-start = ((s8[8388608]{0:T(1024)(128)(4,1)}), s8[4194304]{0:T(1024)(128)(4,1)S(1)}, s32[]{:S(2)}) async-start(s8[8388608]{0:T(1024)(128)(4,1)} %bitcast.195), calls=%async_computation.15 | async-start | bytes 8388608
  (78 other events, 586.5 us)
Sparse Core Ops, SparseCore 0:
  9.6 90.7 all-gather.10
  102.5 109.6 all-gather.8
  213.7 78.5 all-gather.16
  294.6 86.5 all-gather.12
  383.2 134.3 all-gather.14
  519.0 113.6 all-gather.18
  635.0 44.5 reduce-scatter.6
  740.8 44.5 reduce-scatter.10
  787.8 99.3 reduce-scatter.4
  889.4 165.7 reduce-scatter.8
  1139.9 155.4 all-gather.20

commit v3 on v2

--- a/solution.py
+++ b/solution.py
@@ -349,10 +349,10 @@
 
 class LineReduce:
     def __init__(
-        self, chunks, x, o, pair, from_left, from_right, out, send_p, recv_p, send_s, recv_r, recv_l
+        self, chunks, x, o, pair, from_left, from_right, send_p, recv_p, send_s, recv_r, recv_l
     ):
         self.line, self.chunks = Line(), chunks
-        self.x, self.o, self.pair, self.out = x, o, pair, out
+        self.x, self.o, self.pair, self.out = x, o, pair, pair
         self.from_left, self.from_right = from_left, from_right
         self.send_p, self.recv_p, self.send_s = send_p, recv_p, send_s
         self.recv_r, self.recv_l = recv_r, recv_l
@@ -503,9 +503,9 @@
 
 
 def start_kernel(
-    x, w, w_query, w_key, w_value, small, x_all, w_all, packed_mid, packed_all,
-    own_sem, ex_send, ex_recv, pk_send, pk_recv, w_send, w_recv, f_send, f_recv,
-    *line_sems,
+    x, w, w_query, w_key, w_value, small, cot, x_all, w_all, heads_all, small_all, cot_all,
+    heads_mid, small_mid, own_sem, ex_send, ex_recv, sp_send, sp_recv, w_send, w_recv, f_send,
+    f_recv, *line_sems,
 ):
     shard, ctx = lax.axis_index("shard"), lax.axis_index("ctx")
     n_ctx = lax.axis_size("ctx")
@@ -516,17 +516,24 @@
         return lambda d: ref.at[:, pl.ds(pl.multiple_of(d * cols, HEAD), cols)]
 
     def place(i):
-        stop = packed_mid.shape[2] if i == 3 else (i + 1) * cols
-        return lambda d, k: packed_mid.at[d, :, i * cols : stop]
+        if i == 3:
+            return block_from(small_mid)
+        return lambda d, k: heads_mid.at[d, :, i * cols : (i + 1) * cols]
 
     sources = [columns(w_query), columns(w_key), columns(w_value), whole_of(small)]
     swaps = [
         Direct("ctx", source, place(i), ex_send.at[i], ex_recv.at[i])
         for i, source in enumerate(sources)
     ]
-    spread = Direct(
-        "shard", whole_of(packed_mid), lambda d, k: packed_all.at[:, d], pk_send, pk_recv
-    )
+
+    def by_shard(ref):
+        return lambda d, k: ref.at[:, d]
+
+    spreads = [
+        Direct("shard", whole_of(heads_mid), by_shard(heads_all), sp_send.at[0], sp_recv.at[0]),
+        Direct("shard", whole_of(small_mid), by_shard(small_all), sp_send.at[1], sp_recv.at[1]),
+    ]
+    other = Direct("shard", whole_of(cot), block_from(cot_all), sp_send.at[2], sp_recv.at[2])
     pieces = row_pieces(x, x_all, LINE_CHUNKS) + [(w, lambda b: w_all.at[b, shard])]
     line = LineGather(pieces, *line_sems)
     at = line.line
@@ -534,7 +541,11 @@
         pltpu.make_async_copy(source(ctx), place(i)(ctx, 0), own_sem.at[i])
         for i, source in enumerate(sources)
     ]
-    spread_own = pltpu.make_async_copy(packed_mid, packed_all.at[:, shard], own_sem.at[4])
+    later = [
+        pltpu.make_async_copy(heads_mid, heads_all.at[:, shard], own_sem.at[4]),
+        pltpu.make_async_copy(small_mid, small_all.at[:, shard], own_sem.at[5]),
+        pltpu.make_async_copy(cot, cot_all.at[shard], own_sem.at[6]),
+    ]
     for swap in swaps:
         swap.start()
     for copy in own:
@@ -545,8 +556,8 @@
         swap.wait_recv()
     for copy in own:
         copy.wait()
-    spread.start()
-    spread_own.start()
+    for one in (*spreads, other, *later):
+        one.start()
     for k in range(1, at.n):
         line.hop(k)
 
@@ -586,18 +597,31 @@
         row(k, p, shard).wait_send()
         forward(k, p, at.core).wait_send()
         forward(k, p, 1 - at.core).wait_recv()
-    spread.wait_recv()
-    for direct in (*swaps, spread):
+    for direct in (*spreads, other):
+        direct.wait_recv()
+    for direct in (*swaps, *spreads, other):
         direct.wait_send()
-    spread_own.wait()
-
-
-def exchange_kernel(axis, x, o, own_sem, send, recv):
-    me = lax.axis_index(axis)
-    Greeting().ring(axis).wait()
-    swap = Direct(axis, block_of(x), block_from(o), send, recv)
+    for copy in later:
+        copy.wait()
+
+
+def exchange_kernel(to_rows, x, o, own_sem, send, recv):
+    n, me = lax.axis_size("ctx"), lax.axis_index("ctx")
+    cols, rows = (x.shape[1] // n, x.shape[0]) if to_rows else (x.shape[1], o.shape[0])
+
+    def row_block(ref):
+        return lambda d, k=0: ref.at[pl.ds(pl.multiple_of(d * rows, rows), rows)]
+
+    def column_block(ref):
+        return lambda d, k=0: ref.at[:, pl.ds(pl.multiple_of(d * cols, cols), cols)]
+
+    source, target = (
+        (column_block(x), row_block(o)) if to_rows else (row_block(x), column_block(o))
+    )
+    Greeting().ring("ctx").wait()
+    swap = Direct("ctx", source, target, send, recv)
     swap.start()
-    own = pltpu.make_async_copy(x.at[me], o.at[me], own_sem)
+    own = pltpu.make_async_copy(source(me), target(me), own_sem)
     own.start()
     own.wait()
     swap.wait_recv()
@@ -624,30 +648,24 @@
 def pair_gather_kernel(x, peaks, o, peaks_all, own_sem, send, recv, pair_send, pair_recv):
     shard, pair = lax.axis_index("shard"), Pair()
     Greeting().ring("shard").pair().wait()
-    role = pair.role
     own_rows = Direct(
-        "shard", whole_of(x), lambda d, k: o.at[d, role], send.at[0], recv.at[0]
+        "shard", whole_of(x), lambda d, k: o.at[0, d], send.at[0], recv.at[0]
     )
     peer_rows = Direct(
-        "shard",
-        lambda d: o.at[shard, 1 - role],
-        lambda d, k: o.at[d, 1 - role],
-        send.at[1],
-        recv.at[1],
+        "shard", lambda d: o.at[1, shard], lambda d, k: o.at[1, d], send.at[1], recv.at[1]
     )
     tops = Direct("shard", whole_of(peaks), block_from(peaks_all), send.at[2], recv.at[2])
-    across = pair.copy(x, o.at[shard, role], pair_send, pair_recv)
-    arrive = pair.copy(x, o.at[shard, 1 - role], pair_send, pair_recv)
+    across = pair.copy(x, o.at[1, shard], pair_send, pair_recv)
     across.start()
     own_rows.start()
     tops.start()
     own = [
-        pltpu.make_async_copy(x, o.at[shard, role], own_sem.at[0]),
+        pltpu.make_async_copy(x, o.at[0, shard], own_sem.at[0]),
         pltpu.make_async_copy(peaks, peaks_all.at[shard], own_sem.at[1]),
     ]
     for copy in own:
         copy.start()
-    arrive.wait_recv()
+    across.wait_recv()
     peer_rows.start()
     for copy in own:
         copy.wait()
@@ -661,16 +679,11 @@
     def __init__(self, x, o, buf, part, peer, send, recv, pair_send, pair_recv):
         self.x, self.o, self.buf, self.part, self.peer = x, o, buf, part, peer
         self.pair = Pair()
-        theirs, mine = 1 - self.pair.role, self.pair.role
         self.first = Direct(
-            "shard",
-            lambda d: x.at[d, theirs],
-            lambda d, k: buf.at[0, k - 1],
-            send.at[0],
-            recv.at[0],
+            "shard", lambda d: x.at[1, d], lambda d, k: buf.at[1, k - 1], send.at[1], recv.at[1]
         )
         self.second = Direct(
-            "shard", lambda d: x.at[d, mine], lambda d, k: buf.at[1, k - 1], send.at[1], recv.at[1]
+            "shard", lambda d: x.at[0, d], lambda d, k: buf.at[0, k - 1], send.at[0], recv.at[0]
         )
         self.across = self.pair.copy(part, peer, pair_send, pair_recv)
 
@@ -678,7 +691,7 @@
         self.first.start()
         self.second.start()
 
-    def add_up(self, half, role, o, more=None):
+    def add_up(self, half, o, more=None):
         x, buf, shard = self.x, self.buf, self.first.me
         rows = x.shape[2]
         step = 8 if rows % 32 else 32
@@ -686,7 +699,7 @@
         @pl.loop(0, rows // step)
         def _(j):
             at = pl.ds(pl.multiple_of(j * step, step), step)
-            total = x[shard, role, at].astype(f32)
+            total = x[half, shard, at].astype(f32)
             for k in range(buf.shape[1]):
                 total = total + buf[half, k, at].astype(f32)
             if more is not None:
@@ -695,13 +708,13 @@
 
     def turn(self):
         self.first.wait_recv()
-        self.add_up(0, 1 - self.pair.role, self.part)
+        self.add_up(1, self.part)
         self.across.start()
 
     def finish(self):
         self.second.wait_recv()
         self.across.wait_recv()
-        self.add_up(1, self.pair.role, self.o, self.peer)
+        self.add_up(0, self.o, self.peer)
         self.across.wait_send()
         self.first.wait_send()
         self.second.wait_send()
@@ -744,31 +757,20 @@
     direct.wait_send()
 
 
-def middle_kernel(x, y, x_all, y_sum, *rest):
-    Greeting().ring("ctx").ring("shard").wait()
-    returns = PairReduce(y, y_sum, *rest[:7])
-    line = LineGather(row_pieces(x, x_all, LINE_CHUNKS), *rest[7:])
-    returns.start()
-    line.start()
-    for k in range(line.line.n):
-        line.hop(k)
-    returns.turn()
-    returns.finish()
-    line.finish()
-
-
 def end_kernel(
-    x, wide, out, x_sum, wide_all, out_sum, wide_buf, out_buf, wide_sum,
-    own_sem, wide_send, wide_recv, out_send, out_recv, swap_send, swap_recv, *line_refs,
+    x, wide, out, y, x_sum, wide_all, out_sum, y_sum, wide_buf, out_buf, wide_sum,
+    own_sem, wide_send, wide_recv, out_send, out_recv, swap_send, swap_recv, *rest,
 ):
     ctx = lax.axis_index("ctx")
     Greeting().ring("ctx").ring("shard").wait()
     wides = Direct("shard", block_of(wide), buffer_of(wide_buf), wide_send, wide_recv)
     outs = Direct("shard", block_of(out), buffer_of(out_buf), out_send, out_recv)
     swap = Direct("ctx", block_of(wide_sum), block_from(wide_all), swap_send, swap_recv)
-    line = LineReduce(LINE_CHUNKS, x, x_sum, *line_refs)
+    line = LineReduce(LINE_CHUNKS, x, x_sum, *rest[7:])
+    returns = PairReduce(y, y_sum, *rest[:7])
     line.start()
     wides.start()
+    returns.start()
     outs.start()
     line.pass_on()
     wides.wait_recv()
@@ -781,9 +783,11 @@
     swap.start()
     own = pltpu.make_async_copy(wide_sum.at[ctx], wide_all.at[ctx], own_sem)
     own.start()
+    line.finish()
+    returns.turn()
     outs.wait_recv()
     add_up(out, out_buf, out_sum, outs.me)
-    line.finish()
+    returns.finish()
     own.wait()
     swap.wait_recv()
     for direct in (swap, wides, outs):
@@ -799,35 +803,43 @@
 LINE_CHUNKS = 4
 
 
-def start_call(collective_id, x, w, w_query, w_key, w_value, small):
+def start_call(collective_id, x, w, w_query, w_key, w_value, small, cot):
     n_ctx, n_shard = lax.axis_size("ctx"), lax.axis_size("shard")
     n = n_ctx // 2
-    packed = (w.shape[0], 3 * w.shape[1] // n_ctx + small.shape[1])
+    heads = (w.shape[0], 3 * w.shape[1] // n_ctx)
     sem = pltpu.SemaphoreType.DMA
     return pl.pallas_call(
         start_kernel,
         out_shape=[
             jax.ShapeDtypeStruct((n_ctx, *x.shape), bf16),
             jax.ShapeDtypeStruct((n_ctx, n_shard, *w.shape), bf16),
-            jax.ShapeDtypeStruct((n_ctx, *packed), bf16),
-            jax.ShapeDtypeStruct((n_ctx, n_shard, *packed), bf16),
+            jax.ShapeDtypeStruct((n_ctx, n_shard, *heads), bf16),
+            jax.ShapeDtypeStruct((n_ctx, n_shard, *small.shape), bf16),
+            jax.ShapeDtypeStruct((n_shard, *cot.shape), bf16),
         ],
-        in_specs=[ANY] * 6,
-        out_specs=[ANY] * 4,
-        scratch_shapes=[sem((5,)), sem((4, n_ctx)), sem((4, n_ctx))]
-        + [sem((n_shard,))] * 2
+        in_specs=[ANY] * 7,
+        out_specs=[ANY] * 5,
+        scratch_shapes=[
+            pltpu.VMEM((n_ctx, *heads), bf16),
+            pltpu.VMEM((n_ctx, *small.shape), bf16),
+            sem((7,)),
+            sem((4, n_ctx)),
+            sem((4, n_ctx)),
+        ]
+        + [sem((3, n_shard))] * 2
         + [sem((n_shard, n))] * 4
         + line_gather_scratch(n, LINE_CHUNKS + 1),
         compiler_params=remote_params(collective_id, 8),
-    )(x, w, w_query, w_key, w_value, small)
-
-
-def exchange(axis, collective_id, x):
-    n = lax.axis_size(axis)
+    )(x, w, w_query, w_key, w_value, small, cot)
+
+
+def exchange(collective_id, x, to_rows):
+    n = lax.axis_size("ctx")
+    shape = (x.shape[0] * n, x.shape[1] // n) if to_rows else (x.shape[0] // n, x.shape[1] * n)
     sem = pltpu.SemaphoreType.DMA
     return pl.pallas_call(
-        functools.partial(exchange_kernel, axis),
-        out_shape=jax.ShapeDtypeStruct(x.shape, x.dtype),
+        functools.partial(exchange_kernel, to_rows),
+        out_shape=jax.ShapeDtypeStruct(shape, x.dtype),
         in_specs=[ANY],
         out_specs=ANY,
         scratch_shapes=[sem, sem((n,)), sem((n,))],
@@ -841,7 +853,7 @@
     return pl.pallas_call(
         pair_gather_kernel,
         out_shape=[
-            jax.ShapeDtypeStruct((n, 2, *x.shape), x.dtype),
+            jax.ShapeDtypeStruct((2, n, *x.shape), x.dtype),
             jax.ShapeDtypeStruct((n, *peaks.shape), peaks.dtype),
         ],
         in_specs=[ANY] * 2,
@@ -876,23 +888,7 @@
     )(x)
 
 
-def middle_call(collective_id, x, y):
-    n_ctx, n_shard = lax.axis_size("ctx"), lax.axis_size("shard")
-    return pl.pallas_call(
-        middle_kernel,
-        out_shape=[
-            jax.ShapeDtypeStruct((n_ctx, *x.shape), x.dtype),
-            jax.ShapeDtypeStruct(y.shape[2:], f32),
-        ],
-        in_specs=[ANY, VMEM],
-        out_specs=[ANY, VMEM],
-        scratch_shapes=pair_reduce_scratch(n_shard, y)
-        + line_gather_scratch(n_ctx // 2, LINE_CHUNKS),
-        compiler_params=remote_params(collective_id, 40),
-    )(x, y)
-
-
-def end_call(collective_id, x, wide, out):
+def end_call(collective_id, x, wide, out, y):
     n_ctx, rows, width = x.shape
     n_shard = lax.axis_size("shard")
     n = n_ctx // 2
@@ -904,9 +900,10 @@
             jax.ShapeDtypeStruct((rows, width), f32),
             jax.ShapeDtypeStruct((n_ctx, wide_rows, wide_cols), bf16),
             jax.ShapeDtypeStruct(out.shape[1:], f32),
+            jax.ShapeDtypeStruct(y.shape[2:], f32),
         ],
-        in_specs=[VMEM] * 3,
-        out_specs=[VMEM] * 3,
+        in_specs=[VMEM] * 4,
+        out_specs=[VMEM] * 4,
         scratch_shapes=[
             pltpu.VMEM((n_shard - 1, *wide.shape[1:]), bf16),
             pltpu.VMEM((n_shard - 1, *out.shape[1:]), bf16),
@@ -915,10 +912,11 @@
         ]
         + [sem((n_shard,))] * 4
         + [sem((n_ctx,))] * 2
-        + [pltpu.VMEM((n, rows, width), bf16)] * 4
+        + pair_reduce_scratch(n_shard, y)
+        + [pltpu.VMEM((n, rows, width), bf16)] * 3
         + [sem((n, LINE_CHUNKS))] * 5,
-        compiler_params=remote_params(collective_id, 48),
-    )(x, wide, out)
+        compiler_params=remote_params(collective_id, 56),
+    )(x, wide, out, y)
 
 
 def per_device(
@@ -965,14 +963,12 @@
         axis=1,
     )
     grad_own = cotangent[0]
-    x_all, out_w, _, packed = start_call(
-        1, x_own, w_out, w_query, w_key, w_value, small
+    x_all, out_w, weights, small_all, grad_mine = start_call(
+        1, x_own, w_out, w_query, w_key, w_value, small, grad_own
     )
     x_all = x_all.reshape(count, width)
     out_w = out_w.reshape(width, width)
-    weights = packed[..., : 3 * cols].reshape(width, 3 * cols)
-    small_all = packed[..., 3 * cols :]
-    out_w_own = lax.dynamic_slice_in_dim(out_w, ctx * cols, cols, 0)
+    weights = weights.reshape(width, 3 * cols)
     gains = small_all[..., : 4 + experts].reshape(width, 4 + experts)
     gain_attn, gain_query, gain_key, gain_ffn = (gains[:, i].astype(f32) for i in range(4))
     router_w = gains[:, 4:]
@@ -986,8 +982,10 @@
         n_ctx, n_shard, rows, top
     )
     routes_all = jnp.stack(
-        [lax.dynamic_index_in_dim(routes_all, ctx + span * (r - role), 0, False) for r in (0, 1)],
-        axis=1,
+        [
+            lax.dynamic_index_in_dim(routes_all, ctx, 0, False),
+            lax.dynamic_index_in_dim(routes_all, lax.rem(ctx + span, n_ctx), 0, False),
+        ]
     ).reshape(2 * n_shard * rows, top)
 
     def swap(u):
@@ -1005,8 +1003,12 @@
     keep_w = lax.dynamic_slice_in_dim(own_w, role * half, half, 0)
     give_w = lax.dynamic_slice_in_dim(own_w, (1 - role) * half, half, 0)
     spans = [list(range(r * span, (r + 1) * span)) for r in (0, 1)]
-    early = [swap(give_w[e]) for e in range(half)] + [swap(grad_own)]
-    x_all, early[0], early[-1] = lax.optimization_barrier((x_all, early[0], early[-1]))
+    first_w = swap(give_w[0])
+    x_all, first_w, later_w, later_grad = lax.optimization_barrier(
+        (x_all, first_w, give_w[1:], grad_own)
+    )
+    grad_theirs = swap(later_grad)
+    early = [first_w] + [swap(later_w[e]) for e in range(half - 1)]
     expert_w = [
         lax.all_gather(
             in_order(keep_w[e], early[e]),
@@ -1018,9 +1020,6 @@
         for e in range(half)
     ]
 
-    grad_all = lax.all_gather(in_order(grad_own, early[-1]), "shard", axis=0, tiled=False)
-    grad_all = grad_all.reshape(2 * n_shard * rows, width)
-
     x_wide = x_all.astype(f32)
     inverse_one = inverse_rms(x_wide)
     hidden_one = (x_wide * inverse_one * gain_attn).astype(bf16)
@@ -1038,10 +1037,11 @@
     query = rotate(query_n * gain_query, cosine, sine).astype(bf16)
     key = rotate(key_n * gain_key, cosine, sine).astype(bf16)
     mixed, log_total, peaks = attend_forward(query, key, value, docs)
+    mixed, grad_theirs = lax.optimization_barrier((mixed, grad_theirs))
+    grad_theirs = lax.all_gather(grad_theirs, "shard", axis=0, tiled=True)
+    grad_mine = grad_mine.reshape(n_shard * rows, width)
     x_f = x_own.astype(f32)
-    mixed_own = exchange("ctx", 2, mixed.reshape(n_ctx, rows, cols))
-    mixed_own = mixed_own.transpose(1, 0, 2).reshape(rows, width)
-    after = x_f + dot(mixed_own, out_w)
+    after = x_f + dot(exchange(2, mixed, False), out_w)
     inverse_two = inverse_rms(after)
     normed_two = after * inverse_two
     hidden_two = (normed_two * gain_ffn).astype(bf16)
@@ -1058,9 +1058,18 @@
     first = shard * local + role * half
     gates_own = lax.dynamic_slice_in_dim(gates, first, half, 1)
     named_own = lax.dynamic_slice_in_dim(named, first, half, 1)
-    grad_wide = grad_all.astype(f32)
-    moe_part = jnp.zeros(grad_all.shape, f32)
-    back_part = jnp.zeros(grad_all.shape, f32)
+    moe_part = jnp.zeros(hidden_all.shape, f32)
+    back_part = jnp.zeros(hidden_all.shape, f32)
+
+    def by_half(function, *arrays):
+        split = grad_mine.shape[0]
+        return jnp.concatenate(
+            [
+                function(grad_mine.astype(f32), *(u[:split] for u in arrays)),
+                function(grad_theirs.astype(f32), *(u[split:] for u in arrays)),
+            ]
+        )
+
     grad_gates, expert_grads = [], []
     for e in range(half):
         wide, down = expert_w[e][:, : 2 * ff], expert_w[e][:, 2 * ff :]
@@ -1072,10 +1081,9 @@
         act = (silu * up_h).astype(bf16)
         result = contract_cols(act, down).astype(bf16).astype(f32)
         moe_part = moe_part + gate_col * result
-        grad_gates.append(
-            jnp.where(named_own[:, e], jnp.sum(grad_wide * result, axis=1), 0.0)
-        )
-        grad_y = (gate_col * grad_wide).astype(bf16)
+        along = by_half(lambda d, u: jnp.sum(d * u, axis=1), result)
+        grad_gates.append(jnp.where(named_own[:, e], along, 0.0))
+        grad_y = by_half(lambda d, u: (u * d).astype(bf16), gate_col)
         grad_act = dot(grad_y, down)
         grad_h = jnp.concatenate(
             [grad_act * up_h * sig * (1.0 + gate_h * (1.0 - sig)), grad_act * silu], axis=1
@@ -1098,16 +1106,16 @@
                 for u in grad_w
             ]
         )
-    slots = jnp.stack(grad_gates).reshape(half, n_shard, 2, rows).transpose(1, 2, 0, 3)
+    slots = jnp.stack(grad_gates).reshape(half, 2, n_shard, rows).transpose(1, 2, 0, 3)
     grad_gates = lax.dynamic_update_slice_in_dim(
-        jnp.zeros((n_shard, 2, experts, rows), f32), slots, first, 2
+        jnp.zeros((2, n_shard, experts, rows), f32), slots, first, 2
     )
     back_sum, grad_gates = pair_reduce(
-        4, back_part.astype(bf16).reshape(n_shard, 2, rows, width), grad_gates
+        4, back_part.astype(bf16).reshape(2, n_shard, rows, width), grad_gates
     )
     grad_gates = grad_gates.T
     def own_rows(u):
-        return lax.dynamic_slice_in_dim(u, (2 * shard + role) * rows, rows, 0)
+        return lax.dynamic_slice_in_dim(u, shard * rows, rows, 0)
 
     gates_t, probs_t, named_t, sum_t = map(own_rows, (gates, probs, named, selected_sum))
     grad_selected = (
@@ -1125,16 +1133,15 @@
         scaled_two - normed_two * jnp.mean(scaled_two * normed_two, axis=1, keepdims=True)
     )
 
-    moe_part = moe_part.astype(bf16).reshape(n_shard, 2, rows, width)
-    grad_attn, moe_sum = middle_call(5, grad_after.astype(bf16), moe_part)
-    grad_attn = grad_attn.reshape(count, width)
-    output = (after + moe_sum).astype(bf16)
-    grad_mixed = contract_cols(grad_attn, out_w_own).astype(bf16)
+    grad_attn_own = grad_after.astype(bf16)
+    to_gather, expert_grads = lax.optimization_barrier((grad_attn_own, expert_grads))
+    grad_attn = lax.all_gather(to_gather, "ctx", axis=0, tiled=True)
+    grad_mixed = exchange(5, contract_cols(grad_attn_own, out_w).astype(bf16), True)
+    grad_mixed, expert_grads = lax.optimization_barrier((grad_mixed, expert_grads))
     grad_out_w = contract_rows(mixed, grad_attn)
     grad_query_rot, grad_key_rot, grad_value = attend_backward(
         query, key, value, docs, log_total, grad_mixed
     )
-    grad_query_rot, expert_grads = lax.optimization_barrier((grad_query_rot, expert_grads))
     kept = [[lax.dynamic_index_in_dim(u, role, 0, False) for u in sums] for sums in expert_grads]
     peers = swap(
         jnp.stack(
@@ -1195,9 +1202,14 @@
         .astype(bf16)
         .reshape(n_shard, part, width + LANES)
     )
-    grad_hidden_one, grad_weights, grad_out_w = end_call(
-        8, hidden_part.astype(bf16).reshape(n_ctx, rows, width), grad_weights, grad_out_w
-    )
+    grad_hidden_one, grad_weights, grad_out_w, moe_sum = end_call(
+        8,
+        hidden_part.astype(bf16).reshape(n_ctx, rows, width),
+        grad_weights,
+        grad_out_w,
+        moe_part.astype(bf16).reshape(2, n_shard, rows, width),
+    )
+    output = (after + moe_sum).astype(bf16)
     grad_weights = grad_weights.astype(f32)
     grad_small = jnp.sum(grad_weights[..., 3 * cols :], axis=0)
     grad_weights = (

time: 1440 us -> 1560 us (1.083)
  waiting for transfers between devices: 11.6 us -> 274 us
  Pallas kernels: 918 us -> 761 us
  other arithmetic: 85.7 us -> 105 us
    pallas_call x3, Pallas kernels: 306 us -> 187 us  [the longest x1 128 us: pair_gather(): pl.pallas_call(pair_gather_kernel, out_shape=[jax.ShapeDtypeStruct((2, n,...]
    all_gather x2, waiting for transfers between devices: 8.84 us -> 102 us  [per_device(): lax.all_gather(in_order(keep_w[e], early[e]), 'ctx', axis=1, tiled=True,...]
    all_gather x4, waiting for transfers between devices: 0.04 us -> 62.5 us  [swap(): lax.all_gather(u, 'ctx', axis=0, axis_index_groups=[[i, i + span] for i i...]
    all_gather x1 -> x2, waiting for transfers between devices: 0.02 us -> 61.9 us  [the longest x1 61.9 us: per_device(): grad_attn = lax.all_gather(to_gather, 'ctx', axis=0, tiled=True)]
    reduce_scatter x4, waiting for transfers between devices: 0.02 us -> 45.7 us  [per_device(): lax.psum_scatter(u.reshape(2, width // 2, -1), 'ctx', scatter_dimension=1...]
    pallas_call x1, Pallas kernels: 252 us -> 209 us  [start_call(): pl.pallas_call(start_kernel, out_shape=[jax.ShapeDtypeStruct((n_ctx, *x.s...]
    pallas_call x1, Pallas kernels: 118 us -> 159 us  [end_call(): pl.pallas_call(end_kernel, out_shape=[jax.ShapeDtypeStruct((rows, width),...]
    pallas_call x2, Pallas kernels: 79.6 us -> 44.2 us  [many_sum(): pl.pallas_call(functools.partial(many_sum_kernel, axis), out_shape=jax.Sh...]
  transfers between devices with their start and end apart: 11 -> 12, of which waited for: 2 -> 6; matrix products, arithmetic and copies ran while one was open for 31% -> 27% of each run, Pallas kernels for 64% -> 39%
where the time goes in v3:
time: 1560 us; the launch traced here: 1550 us
  Pallas kernels  761 us (49%)
  matrix products  302 us (19%)
  waiting for transfers between devices  274 us (18%)
  other arithmetic  105 us (7%)
  local copies, waits for them, and re-layouts  91.3 us (6%)
  between operations  17.1 us (1%)
    pallas_call x1, Pallas kernels, start_call(): pl.pallas_call(start_kernel, out_shape=[jax.ShapeDtypeStruct((n_ctx, *x.s...  209 us
    pallas_call x1, Pallas kernels, end_call(): pl.pallas_call(end_kernel, out_shape=[jax.ShapeDtypeStruct((rows, width),...  159 us
    pallas_call x1, Pallas kernels, pair_gather(): pl.pallas_call(pair_gather_kernel, out_shape=[jax.ShapeDtypeStruct((2, n,...  128 us
    dot_general x7, matrix products, dot(): return jnp.dot(a, b, preferred_element_type=f32)  108 us
    dot_general x7, matrix products, contract_cols(): lax.dot_general(a, b, (((1,), (1,)), ((), ())), preferred_element_type=f32)  105 us
    all_gather x2, waiting for transfers between devices, per_device(): lax.all_gather(in_order(keep_w[e], early[e]), 'ctx', axis=1, tiled=True,...  102 us
    pallas_call x1, Pallas kernels, pair_reduce(): pl.pallas_call(functools.partial(pair_reduce_kernel, len(arrays)), out_sh...  101 us
    dot_general x7, matrix products, contract_rows(): lax.dot_general(a, b, (((0,), (0,)), ((), ())), preferred_element_type=f32)  88.9 us
  transfers between devices with their start and end apart: 12, of which 6 were waited for; matrix products, arithmetic and copies ran while one was open for 27% of the time, Pallas kernels for 39%

profile of v3, /device:TPU:0, one launch (start us, length us, event | category | flops | bytes accessed | tf_op | source)
XLA Modules:
  0.0 1550.8 jit_solution(12624485290532635763)
XLA Ops:
  18.8 208.7 %shard_map.296 = (bf16[8,256,2048]{2,1,0:T(8,128)(2,1)S(1)}, bf16[8,4,64,2048]{3,2,1,0:T(8,128)(2,1)S(1)}, bf16[8,4,64,768]{3,2,1,0:T(8,128)(2,1)S(1)}, bf16[8,4...) custom-call(bf16[256,2048]{1,0:T(8,128)(2,1)S(1)} %bitcast.189, bf16[64,2048]{1,0:T(8,128)(2,1)S(1)} %copy-done.23, ...), custom_call_target="tpu_custom_call" | custom-call | tf_op jit(solution)/shard_map/pallas_call | solution.py:811
  263.9 17.4 %shard_map.297 = f32[2,2048]{1,0:T(2,128)S(1)} custom-call(f32[2,2048]{1,0:T(2,128)S(1)} %pad_maximum_fusion.29.x), custom_call_target="tpu_custom_call" | custom-call | tf_op jit(solution)/shard_map/pallas_call | solution.py:881
  291.8 23.1 %shard_map.298 = (bf16[2048,256]{1,0:T(8,128)(2,1)S(1)}, f32[2,2048,1]{2,1,0:T(8,128)}, f32[2,8,128]{2,1,0:T(8,128)S(1)}) custom-call(bf16[2048,256]{1,0:T(8,128)(2,1)S(1)} %pad_maximum_fusion.25.q_ref, bf16[2048,256]{1,0:T(8,128)(2,1)S(1)} %pad_maximum_fusion.26.k_ref, bf16[2048,256]{1,0:T(8,128)(2,1)S(1)} %copy-done.17, s32[2048,1]{1,0:T(8,128)S(1)} %copy-done.16, ...), custom_call_target="tpu_custom_call" | custom-call | flops 4294967296 | bytes 4194304 | tf_op jit(solution)/shard_map/pallas_call | solution.py:111
  335.0 32.9 %shard_map.299 = bf16[256,2048]{1,0:T(8,128)(2,1)S(1)} custom-call(bf16[2048,256]{1,0:T(8,128)(2,1)S(1)} %get-tuple-element.65.x), custom_call_target="tpu_custom_call" | custom-call | tf_op jit(solution)/shard_map/pallas_call | solution.py:840
  375.0 31.3 %all-gather.17.cloned.1.call-done = bf16[2,256,3072]{2,1,0:T(8,128)(2,1)} async-done(((bf16[1,256,3072]{2,1,0:T(8,128)(2,1)}), bf16[2,256,3072]{2,1,0:T(8,128)(2,1)}) %all-gather.17.cloned.1.call-update) | async-done | bytes 3145744 | tf_op jit(solution)/shard_map/all_gather | solution.py:992
  413.4 127.6 %shard_map.300 = (bf16[2,4,256,2048]{3,2,1,0:T(8,128)(2,1)S(1)}, f32[4,2,8,128]{3,2,1,0:T(8,128)S(1)}) custom-call(bf16[256,2048]{1,0:T(8,128)(2,1)S(1)} %multiply_convert_fusion.8.x, f32[2,8,128]{2,1,0:T(8,128)S(1)} %get-tuple-element.68.peaks), custom_call_target="tpu_custom_call" | custom-call | tf_op jit(solution)/shard_map/pallas_call | solution.py:853
  557.0 91.3 %all-gather.15.cloned.1.call-done = bf16[2,1024,3072]{2,1,0:T(8,128)(2,1)} async-done(((bf16[2,256,3072]{2,1,0:T(8,128)(2,1)}), bf16[2,1024,3072]{2,1,0:T(8,128)(2,1)}) %all-gather.15.cloned.1.call-update) | async-done | bytes 12582928 | tf_op jit(solution)/shard_map/all_gather | solution.py:1013
  648.3 24.5 %fusion.19 = f32[2048,2048]{0,1:T(8,128)} fusion(bf16[2048,2048]{1,0:T(8,128)(2,1)} %bitcast.181, bf16[2048,3072]{1,0:T(8,128)(2,1)} %bitcast.271), kind=kOutput, calls=%fused_computation.48 | convolution fusion | flops 17179869184 | bytes 33554432 | tf_op jit(solution)/shard_map/dot_general | solution.py:23
  672.7 20.1 %multiply_convert_fusion.5 = (bf16[2048,1024]{0,1:T(8,128)(2,1)}, bf16[2048,1024]{0,1:T(8,128)(2,1)}, bf16[2048,1024]{0,1:T(8,128)(2,1)}) fusion(f32[2048,2048]{0,1:T(8,128)} %fusion.19, bf16[2048,3072]{1,0:T(8,128)(2,1)} %bitcast.272, bf16[1024,2048]{1,0:T(8,128)(2,1)} %get-tuple-element.197, bf16[1024,2048]{1,0:T(8,128)(2,1)S(1)} %copy-done.49), kind=kOutput, calls=%fused_computation.39 | convolution fusion | flops 8638169088 | bytes 41943040 | tf_op jit(solution)/shard_map/dot_general | solution.py:23
  706.3 22.1 %convolution_convert_fusion.1 = bf16[2048,2048]{1,0:T(8,128)(2,1)} fusion(bf16[2048,2048]{1,0:T(8,128)(2,1)S(1)} %bitcast.185, bf16[2048,1024]{0,1:T(8,128)(2,1)} %get-tuple-element.175, bf16[2048,1024]{0,1:T(8,128)(2,1)} %get-tuple-element.174), kind=kOutput, calls=%fused_computation.43 | convolution fusion | flops 17200840704 | bytes 25165824 | tf_op jit(solution)/shard_map/dot_general | solution.py:27
  728.4 23.8 %convert_convert_fusion.2 = f32[2048,2048]{1,0:T(8,128)} fusion(bf16[2048,3072]{1,0:T(8,128)(2,1)} %bitcast.273, bf16[2048,1024]{0,1:T(8,128)(2,1)} %get-tuple-element.175, bf16[2048,1024]{0,1:T(8,128)(2,1)S(1)} %copy-done.91), kind=kOutput, calls=%fused_computation.37 | convolution fusion | flops 17205035008 | bytes 33554432 | tf_op jit(solution)/shard_map/dot_general | solution.py:31
  763.3 24.5 %fusion.16 = f32[2048,2048]{0,1:T(8,128)} fusion(bf16[2048,2048]{1,0:T(8,128)(2,1)} %bitcast.182, bf16[2048,3072]{1,0:T(8,128)(2,1)} %bitcast.275), kind=kOutput, calls=%fused_computation.45 | convolution fusion | flops 17179869184 | bytes 33554432 | tf_op jit(solution)/shard_map/dot_general | solution.py:23
  787.8 20.1 %multiply_convert_fusion.2 = (bf16[2048,1024]{0,1:T(8,128)(2,1)}, bf16[2048,1024]{0,1:T(8,128)(2,1)}, bf16[2048,1024]{0,1:T(8,128)(2,1)}) fusion(f32[2048,2048]{0,1:T(8,128)} %fusion.16, bf16[2048,3072]{1,0:T(8,128)(2,1)} %bitcast.276, bf16[1024,2048]{1,0:T(8,128)(2,1)} %get-tuple-element.196, bf16[1024,2048]{1,0:T(8,128)(2,1)S(1)} %copy-done.48), kind=kOutput, calls=%fused_computation.33 | convolution fusion | flops 8638169088 | bytes 41943040 | tf_op jit(solution)/shard_map/dot_general | solution.py:23
  821.4 22.0 %convolution_convert_fusion = bf16[2048,2048]{1,0:T(8,128)(2,1)} fusion(bf16[2048,2048]{1,0:T(8,128)(2,1)S(1)} %bitcast.188, bf16[2048,1024]{0,1:T(8,128)(2,1)} %get-tuple-element.173, bf16[2048,1024]{0,1:T(8,128)(2,1)} %get-tuple-element.172), kind=kOutput, calls=%fused_computation.42 | convolution fusion | flops 17200840704 | bytes 25165824 | tf_op jit(solution)/shard_map/dot_general | solution.py:27
  843.5 24.6 %convert_add_fusion = bf16[2048,2048]{1,0:T(8,128)(2,1)} fusion(f32[2048,2048]{1,0:T(8,128)} %convert_convert_fusion.2, bf16[2048,3072]{1,0:T(8,128)(2,1)} %bitcast.277, bf16[2048,1024]{0,1:T(8,128)(2,1)} %get-tuple-element.173, bf16[2048,1024]{0,1:T(8,128)(2,1)S(1)} %copy-done.92), kind=kOutput, calls=%fused_computation.8 | convolution fusion | flops 17213423616 | bytes 41943040 | tf_op jit(solution)/shard_map/dot_general | solution.py:31
  886.9 20.9 %add_convert_fusion = (bf16[2048,2048]{1,0:T(8,128)(2,1)}, f32[2048,2048]{1,0:T(8,128)}) fusion(f32[2048,2048]{1,0:T(8,128)} %convert_convert_fusion.1, f32[2048]{0:T(1024)S(1)} %bitcast.265, f32[2048]{0:T(1024)S(1)} %bitcast.264, bf16[2048,1024]{0,1:T(8,128)(2,1)} %get-tuple-element.178, bf16[2048,3072]{1,0:T(8,128)(2,1)} %bitcast.278), kind=kOutput, calls=%fused_computation.7 | convolution fusion | flops 8615100416 | bytes 50348032 | tf_op jit(solution)/shard_map/dot_general | solution.py:31
  924.4 100.9 %shard_map.301 = (f32[256,2048]{1,0:T(8,128)S(1)}, f32[16,256]{1,0:T(8,128)S(1)}) custom-call(bf16[2,4,256,2048]{3,2,1,0:T(8,128)(2,1)S(1)} %bitcast.198, f32[2,4,16,256]{3,2,1,0:T(8,128)S(1)} %fusion.111.refs_1_), custom_call_target="tpu_custom_call" | custom-call | tf_op jit(solution)/shard_map/pallas_call | solution.py:868
  1036.5 26.9 %shard_map.302.do_ref = bf16[2048,256]{1,0:T(8,128)(2,1)S(1)} custom-call(bf16[256,2048]{1,0:T(8,128)(2,1)S(1)} %convolution_convert_fusion.4.x), custom_call_target="tpu_custom_call" | custom-call | tf_op jit(solution)/shard_map/pallas_call | solution.py:840
  1064.4 45.7 %reduce-scatter.9.cloned.1.call-done = bf16[2,256,2048]{2,1,0:T(8,128)(2,1)} async-done(((bf16[2,1024,2048]{2,1,0:T(8,128)(2,1)}), bf16[2,256,2048]{2,1,0:T(8,128)(2,1)}) %reduce-scatter.9.cloned.1.call-update) | async-done | bytes 2097168 | tf_op jit(solution)/shard_map/reduce_scatter | solution.py:1099
  1119.7 37.7 %shard_map.303 = (f32[2048,256]{1,0:T(8,128)}, f32[2048,256]{1,0:T(8,128)}, f32[2048,256]{1,0:T(8,128)}) custom-call(bf16[2048,256]{1,0:T(8,128)(2,1)} %copy-done.15, bf16[2048,256]{1,0:T(8,128)(2,1)} %copy-done.14, bf16[2048,256]{1,0:T(8,128)(2,1)} %slice.466.v_ref, s32[2048,1]{1,0:T(8,128)} %broadcast_in_dim_reshape.6.doc_q_ref, s32[1,2048]{1,0:T(1,128)} %copy-done.25, ...), custom_call_target="tpu_custom_call" | custom-call | flops 10737418240 | bytes 10485760 | tf_op jit(solution)/shard_map/pallas_call | solution.py:134
  1174.7 26.7 %shard_map.304 = f32[3,2048]{1,0:T(4,128)S(1)} custom-call(f32[3,2048]{1,0:T(4,128)S(1)} %pad_maximum_fusion.28.x), custom_call_target="tpu_custom_call" | custom-call | tf_op jit(solution)/shard_map/pallas_call | solution.py:881
  1238.1 31.2 %all-gather.25.cloned.1.call-done = bf16[4,256,3072]{2,1,0:T(8,128)(2,1)} async-done(((bf16[2,256,3072]{2,1,0:T(8,128)(2,1)}), bf16[4,256,3072]{2,1,0:T(8,128)(2,1)}) %all-gather.25.cloned.1.call-update) | async-done | bytes 6291472 | tf_op jit(solution)/shard_map/all_gather | solution.py:992
  1290.5 61.9 %all-gather.21.cloned.1.call-done = bf16[2048,2048]{1,0:T(8,128)(2,1)} async-done(((bf16[256,2048]{1,0:T(8,128)(2,1)}), bf16[2048,2048]{1,0:T(8,128)(2,1)}) %all-gather.21.cloned.1.call-update) | async-done | bytes 8388624 | tf_op jit(solution)/shard_map/all_gather | solution.py:1138
  1359.3 159.1 %shard_map.305 = (f32[256,2048]{1,0:T(8,128)}, bf16[8,64,896]{2,1,0:T(8,128)(2,1)}, f32[64,2176]{1,0:T(8,128)}, f32[256,2048]{1,0:T(8,128)}) custom-call(bf16[8,256,2048]{2,1,0:T(8,128)(2,1)} %bitcast.208, bf16[4,512,896]{2,1,0:T(8,128)(2,1)} %bitcast.203, bf16[4,64,2176]{2,1,0:T(8,128)(2,1)} %pad_maximum_fusion.24.out, bf16[2,4,256,2048]{3,2,1,0:T(8,128)(2,1)} %bitcast.207), custom_call_target="tpu_custom_call" | custom-call | tf_op jit(solution)/shard_map/pallas_call | solution.py:897
  (381 shorter events, 308.6 us)
Async XLA Ops:
  7.2 236.3 %all-gather.11.cloned.1.call-start = ((), (), s32[]{:S(2)}) async-start(), calls=%async_computation.4 | async-start | bytes 4718592 | tf_op jit(solution)/shard_map/all_gather | solution.py:992
  16.6 299.3 %all-gather.23.cloned.1.call-start = ((), (), s32[]{:S(2)}) async-start(), calls=%async_computation.14 | async-start | bytes 3145728 | tf_op jit(solution)/shard_map/all_gather | solution.py:992
  237.7 303.4 %copy-start = (bf16[8,4,64,128]{3,2,1,0:T(8,128)(2,1)}, bf16[8,4,64,128]{3,2,1,0:T(8,128)(2,1)S(1)}, u32[]{:S(2)}) copy-start(bf16[8,4,64,128]{3,2,1,0:T(8,128)(2,1)S(1)} %get-tuple-element.61) | copy-start | bytes 1572868
  239.2 52.2 %copy-start.25 = (s32[1,2048]{1,0:T(1,128)}, s32[1,2048]{1,0:T(1,128)S(1)}, u32[]{:S(2)}) copy-start(s32[1,2048]{1,0:T(1,128)S(1)} %broadcast_in_dim_reshape.5.doc_k_ref) | copy-start | bytes 24580
  246.2 160.1 %all-gather.17.cloned.1.call-start = ((), (), s32[]{:S(2)}) async-start(), calls=%async_computation.7 | async-start | bytes 4718592 | tf_op jit(solution)/shard_map/all_gather | solution.py:992
  281.4 269.9 %all-gather.13.cloned.1.call-start = ((), (), s32[]{:S(2)}) async-start(), calls=%async_computation.5 | async-start | bytes 5242880 | tf_op jit(solution)/shard_map/all_gather | solution.py:1041
  318.7 329.6 %all-gather.15.cloned.1.call-start = ((), (), s32[]{:S(2)}) async-start(), calls=%async_computation.6 | async-start | bytes 15728640 | tf_op jit(solution)/shard_map/all_gather | solution.py:1013
  323.5 439.9 %all-gather.19.cloned.1.call-start = ((), (), s32[]{:S(2)}) async-start(), calls=%async_computation.8 | async-start | bytes 15728640 | tf_op jit(solution)/shard_map/all_gather | solution.py:1013
  334.8 76.8 %copy-start.62 = (f32[2048,1]{0,1:T(1,128)}, f32[2048,1]{0,1:T(1,128)S(1)}, u32[]{:S(2)}) copy-start(f32[2048,1]{0,1:T(1,128)S(1)} %copy.194) | copy-start | bytes 24580
  335.0 210.8 %copy-start.59 = (pred[2048,16]{0,1:T(8,128)(4,1)}, pred[2048,16]{0,1:T(8,128)(4,1)S(1)}, u32[]{:S(2)}) copy-start(pred[2048,16]{0,1:T(8,128)(4,1)S(1)} %fusion.104) | copy-start | bytes 98308
  411.5 652.8 %reduce-scatter.7.cloned.1.call-start = ((), (), s32[]{:S(2)}) async-start(), calls=%async_computation.10 | async-start | bytes 5242880 | tf_op jit(solution)/shard_map/reduce_scatter | solution.py:1099
  413.4 127.7 %copy-start.9 = (bf16[256,2048]{1,0:T(8,128)(2,1)}, bf16[256,2048]{1,0:T(8,128)(2,1)S(1)}, u32[]{:S(2)}) copy-start(bf16[256,2048]{1,0:T(8,128)(2,1)S(1)} %multiply_convert_fusion.8.x) | copy-start | bytes 3145732
  648.3 58.0 %slice-start = ((s8[8388608]{0:T(1024)(128)(4,1)}), s8[4194304]{0:T(1024)(128)(4,1)S(1)}, s32[]{:S(2)}) async-start(s8[8388608]{0:T(1024)(128)(4,1)} %bitcast.183), calls=%async_computation.16 | async-start | bytes 8388608
  752.3 312.1 %reduce-scatter.11.cloned.1.call-start = ((), (), s32[]{:S(2)}) async-start(), calls=%async_computation.12 | async-start | bytes 5242880 | tf_op jit(solution)/shard_map/reduce_scatter | solution.py:1099
  763.3 58.1 %slice-start.2 = ((s8[8388608]{0:T(1024)(128)(4,1)}), s8[4194304]{0:T(1024)(128)(4,1)S(1)}, s32[]{:S(2)}) async-start(s8[8388608]{0:T(1024)(128)(4,1)} %bitcast.186), calls=%async_computation.18 | async-start | bytes 8388608
  868.1 196.2 %reduce-scatter.5.cloned.1.call-start = ((), (), s32[]{:S(2)}) async-start(), calls=%async_computation.9 | async-start | bytes 10485760 | tf_op jit(solution)/shard_map/reduce_scatter | solution.py:1099
  868.9 241.2 %reduce-scatter.9.cloned.1.call-start = ((), (), s32[]{:S(2)}) async-start(), calls=%async_computation.11 | async-start | bytes 10485760 | tf_op jit(solution)/shard_map/reduce_scatter | solution.py:1099
  869.5 399.9 %all-gather.25.cloned.1.call-start = ((), (), s32[]{:S(2)}) async-start(), calls=%async_computation.15 | async-start | bytes 9437184 | tf_op jit(solution)/shard_map/all_gather | solution.py:992
  924.3 102.6 %copy-start.1 = (bf16[8,4,64,128]{3,2,1,0:T(8,128)(2,1)S(1)}, bf16[8,4,64,128]{3,2,1,0:T(8,128)(2,1)}, u32[]{:S(2)}) copy-start(bf16[8,4,64,128]{3,2,1,0:T(8,128)(2,1)} %copy-done) | copy-start | bytes 1572868
  924.3 102.5 %copy-start.31 = (f32[256,2048]{1,0:T(8,128)S(1)}, f32[256,2048]{1,0:T(8,128)}, u32[]{:S(2)}) copy-start(f32[256,2048]{1,0:T(8,128)} %get-tuple-element.256) | copy-start | bytes 6291460
  924.4 102.5 %copy-start.63 = (f32[2048,1]{0,1:T(1,128)S(1)}, f32[2048,1]{0,1:T(1,128)}, u32[]{:S(2)}) copy-start(f32[2048,1]{0,1:T(1,128)} %copy-done.62) | copy-start | bytes 24580
  924.4 102.5 %copy-start.74 = (f32[256]{0:T(256)S(1)}, f32[256]{0:T(256)}, u32[]{:S(2)}) copy-start(f32[256]{0:T(256)} %copy-done.73) | copy-start | bytes 3076
  1117.0 235.5 %all-gather.21.cloned.1.call-start = ((), (), s32[]{:S(2)}) async-start(), calls=%async_computation.13 | async-start | bytes 9437184 | tf_op jit(solution)/shard_map/all_gather | solution.py:1138
  1286.3 66.2 %copy-start.13 = (bf16[2048,256]{1,0:T(8,128)(2,1)S(1)}, bf16[2048,256]{1,0:T(8,128)(2,1)}, u32[]{:S(2)}) copy-start(bf16[2048,256]{1,0:T(8,128)(2,1)} %copy-done.12) | copy-start | bytes 3145732
  (87 other events, 837.4 us)
Sparse Core Ops, SparseCore 0:
  16.7 122.3 all-gather.10
  246.3 57.2 all-gather.22
  305.2 101.0 all-gather.16
  408.0 127.7 all-gather.12
  537.2 110.9 all-gather.14
  649.7 113.6 all-gather.18
  765.6 44.5 reduce-scatter.6
  868.3 44.4 reduce-scatter.10
  915.1 87.6 reduce-scatter.4
  1005.0 104.9 reduce-scatter.8
  1117.1 152.1 all-gather.24
  1271.4 81.0 all-gather.20

commit v4 on v3

--- a/solution.py
+++ b/solution.py
@@ -989,6 +989,9 @@
     ).reshape(2 * n_shard * rows, top)
 
     def swap(u):
+        return lax.ppermute(u, "ctx", [(i, (i + span) % n_ctx) for i in range(n_ctx)])
+
+    def queued_swap(u):
         both = lax.all_gather(
             u, "ctx", axis=0, axis_index_groups=[[i, i + span] for i in range(span)]
         )
@@ -1008,17 +1011,17 @@
         (x_all, first_w, give_w[1:], grad_own)
     )
     grad_theirs = swap(later_grad)
-    early = [first_w] + [swap(later_w[e]) for e in range(half - 1)]
-    expert_w = [
-        lax.all_gather(
-            in_order(keep_w[e], early[e]),
+    early = [first_w] + [queued_swap(later_w[e]) for e in range(half - 1)]
+    def expert_weights(e, theirs):
+        return lax.all_gather(
+            in_order(keep_w[e], theirs),
             "ctx",
             axis=1,
             tiled=True,
             axis_index_groups=spans,
         ).reshape(width, 3 * ff)
-        for e in range(half)
-    ]
+
+    expert_w = [expert_weights(0, early[0])]
 
     x_wide = x_all.astype(f32)
     inverse_one = inverse_rms(x_wide)
@@ -1037,8 +1040,6 @@
     query = rotate(query_n * gain_query, cosine, sine).astype(bf16)
     key = rotate(key_n * gain_key, cosine, sine).astype(bf16)
     mixed, log_total, peaks = attend_forward(query, key, value, docs)
-    mixed, grad_theirs = lax.optimization_barrier((mixed, grad_theirs))
-    grad_theirs = lax.all_gather(grad_theirs, "shard", axis=0, tiled=True)
     grad_mine = grad_mine.reshape(n_shard * rows, width)
     x_f = x_own.astype(f32)
     after = x_f + dot(exchange(2, mixed, False), out_w)
@@ -1047,6 +1048,11 @@
     hidden_two = (normed_two * gain_ffn).astype(bf16)
 
     hidden_all, peaks = pair_gather(3, hidden_two, peaks)
+    hidden_all, early, grad_theirs = lax.optimization_barrier(
+        (hidden_all, early[1:], grad_theirs)
+    )
+    grad_theirs = lax.all_gather(grad_theirs, "shard", axis=0, tiled=True)
+    expert_w += [expert_weights(e + 1, u) for e, u in enumerate(early)]
     hidden_all = hidden_all.reshape(2 * n_shard * rows, width)
     peaks = jnp.max(peaks, axis=0)[:, 0, 0]
     logits = dot(hidden_all, router_w)
@@ -1061,7 +1067,7 @@
     moe_part = jnp.zeros(hidden_all.shape, f32)
     back_part = jnp.zeros(hidden_all.shape, f32)
 
-    def by_half(function, *arrays):
+    def by_half(grad_theirs, function, *arrays):
         split = grad_mine.shape[0]
         return jnp.concatenate(
             [
@@ -1079,11 +1085,13 @@
         sig = jax.nn.sigmoid(gate_h)
         silu = gate_h * sig
         act = (silu * up_h).astype(bf16)
+        if e == 0:
+            act, grad_theirs = lax.optimization_barrier((act, grad_theirs))
         result = contract_cols(act, down).astype(bf16).astype(f32)
         moe_part = moe_part + gate_col * result
-        along = by_half(lambda d, u: jnp.sum(d * u, axis=1), result)
+        along = by_half(grad_theirs, lambda d, u: jnp.sum(d * u, axis=1), result)
         grad_gates.append(jnp.where(named_own[:, e], along, 0.0))
-        grad_y = by_half(lambda d, u: (u * d).astype(bf16), gate_col)
+        grad_y = by_half(grad_theirs, lambda d, u: (u * d).astype(bf16), gate_col)
         grad_act = dot(grad_y, down)
         grad_h = jnp.concatenate(
             [grad_act * up_h * sig * (1.0 + gate_h * (1.0 - sig)), grad_act * silu], axis=1
@@ -1093,7 +1101,9 @@
             contract_rows(hidden_all, grad_h).astype(bf16),
             contract_rows(grad_y, act).astype(bf16),
         ]
-        hidden_all, back_part, grad_w = lax.optimization_barrier((hidden_all, back_part, grad_w))
+        hidden_all, back_part, grad_w, expert_grads = lax.optimization_barrier(
+            (hidden_all, back_part, grad_w, expert_grads)
+        )
         expert_grads.append(
             [
                 lax.psum_scatter(
@@ -1137,13 +1147,13 @@
     to_gather, expert_grads = lax.optimization_barrier((grad_attn_own, expert_grads))
     grad_attn = lax.all_gather(to_gather, "ctx", axis=0, tiled=True)
     grad_mixed = exchange(5, contract_cols(grad_attn_own, out_w).astype(bf16), True)
-    grad_mixed, expert_grads = lax.optimization_barrier((grad_mixed, expert_grads))
+    grad_attn, expert_grads = lax.optimization_barrier((grad_attn, expert_grads))
     grad_out_w = contract_rows(mixed, grad_attn)
     grad_query_rot, grad_key_rot, grad_value = attend_backward(
         query, key, value, docs, log_total, grad_mixed
     )
     kept = [[lax.dynamic_index_in_dim(u, role, 0, False) for u in sums] for sums in expert_grads]
-    peers = swap(
+    peers = queued_swap(
         jnp.stack(
             [
                 jnp.concatenate(

time: 1560 us -> 1490 us (0.955)
  waiting for transfers between devices: 274 us -> 52.2 us
  Pallas kernels: 761 us -> 900 us
    all_gather x6 -> x4, waiting for transfers between devices: 165 us -> 29.4 us  [the longest x2 29.4 us: expert_weights(): lax.all_gather(in_order(keep_w[e], theirs), 'ctx', axis=1, tiled=True, ax...]
    pallas_call x1, Pallas kernels: 159 us -> 242 us  [end_call(): pl.pallas_call(end_kernel, out_shape=[jax.ShapeDtypeStruct((rows, width),...]
    pallas_call x2, Pallas kernels: 44.2 us -> 108 us  [many_sum(): pl.pallas_call(functools.partial(many_sum_kernel, axis), out_shape=jax.Sh...]
    all_gather x1, waiting for transfers between devices: 61.9 us -> 0.01 us  [per_device(): grad_attn = lax.all_gather(to_gather, 'ctx', axis=0, tiled=True)]
    pallas_call x1, Pallas kernels: 128 us -> 94.3 us  [pair_gather(): pl.pallas_call(pair_gather_kernel, out_shape=[jax.ShapeDtypeStruct((2, n,...]
    reduce_scatter x4, waiting for transfers between devices: 45.7 us -> 20.1 us  [per_device(): lax.psum_scatter(u.reshape(2, width // 2, -1), 'ctx', scatter_dimension=1...]
    unnamed x210 -> x212, local copies, waits for them, and re-layouts: 30.6 us -> 35.5 us
  transfers between devices with their start and end apart: 12 -> 12, of which waited for: 6 -> 3; matrix products, arithmetic and copies ran while one was open for 27% -> 30% of each run, Pallas kernels for 39% -> 61%
where the time goes in v4:
time: 1490 us; the launch traced here: 1480 us
  Pallas kernels  900 us (60%)
  matrix products  302 us (20%)
  other arithmetic  113 us (8%)
  local copies, waits for them, and re-layouts  88.3 us (6%)
  waiting for transfers between devices  52.2 us (4%)
  between operations  16.8 us (1%)
    pallas_call x1, Pallas kernels, end_call(): pl.pallas_call(end_kernel, out_shape=[jax.ShapeDtypeStruct((rows, width),...  242 us
    pallas_call x1, Pallas kernels, start_call(): pl.pallas_call(start_kernel, out_shape=[jax.ShapeDtypeStruct((n_ctx, *x.s...  223 us
    dot_general x7, matrix products, dot(): return jnp.dot(a, b, preferred_element_type=f32)  110 us
    pallas_call x2, Pallas kernels, many_sum(): pl.pallas_call(functools.partial(many_sum_kernel, axis), out_shape=jax.Sh...  108 us
    dot_general x7, matrix products, contract_cols(): lax.dot_general(a, b, (((1,), (1,)), ((), ())), preferred_element_type=f32)  105 us
    pallas_call x1, Pallas kernels, pair_reduce(): pl.pallas_call(functools.partial(pair_reduce_kernel, len(arrays)), out_sh...  99.5 us
    pallas_call x1, Pallas kernels, pair_gather(): pl.pallas_call(pair_gather_kernel, out_shape=[jax.ShapeDtypeStruct((2, n,...  94.3 us
    dot_general x7, matrix products, contract_rows(): lax.dot_general(a, b, (((0,), (0,)), ((), ())), preferred_element_type=f32)  87 us
  transfers between devices with their start and end apart: 12, of which 3 were waited for; matrix products, arithmetic and copies ran while one was open for 30% of the time, Pallas kernels for 61%

profile of v4, /device:TPU:0, one launch (start us, length us, event | category | flops | bytes accessed | tf_op | source)
XLA Modules:
  0.0 1478.3 jit_solution(12359034226522163377)
XLA Ops:
  22.7 223.3 %shard_map.296 = (bf16[8,256,2048]{2,1,0:T(8,128)(2,1)S(1)}, bf16[8,4,64,2048]{3,2,1,0:T(8,128)(2,1)S(1)}, bf16[8,4,64,768]{3,2,1,0:T(8,128)(2,1)S(1)}, bf16[8,4...) custom-call(bf16[256,2048]{1,0:T(8,128)(2,1)S(1)} %bitcast.189, bf16[64,2048]{1,0:T(8,128)(2,1)S(1)} %copy-done.20, ...), custom_call_target="tpu_custom_call" | custom-call | tf_op jit(solution)/shard_map/pallas_call | solution.py:811
  287.4 84.3 %shard_map.297 = f32[2,2048]{1,0:T(2,128)S(1)} custom-call(f32[2,2048]{1,0:T(2,128)S(1)} %pad_maximum_fusion.29.x), custom_call_target="tpu_custom_call" | custom-call | tf_op jit(solution)/shard_map/pallas_call | solution.py:881
  379.7 23.0 %shard_map.298 = (bf16[2048,256]{1,0:T(8,128)(2,1)S(1)}, f32[2,2048,1]{2,1,0:T(8,128)}, f32[2,8,128]{2,1,0:T(8,128)S(1)}) custom-call(bf16[2048,256]{1,0:T(8,128)(2,1)S(1)} %pad_maximum_fusion.25.q_ref, bf16[2048,256]{1,0:T(8,128)(2,1)S(1)} %pad_maximum_fusion.26.k_ref, bf16[2048,256]{1,0:T(8,128)(2,1)S(1)} %slice.466.v_ref, s32[2048,1]{1,0:T(8,128)S(1)} %copy-done.15, ...), custom_call_target="tpu_custom_call" | custom-call | flops 4294967296 | bytes 4194304 | tf_op jit(solution)/shard_map/pallas_call | solution.py:111
  402.7 36.9 %shard_map.299 = bf16[256,2048]{1,0:T(8,128)(2,1)S(1)} custom-call(bf16[2048,256]{1,0:T(8,128)(2,1)S(1)} %get-tuple-element.68.x), custom_call_target="tpu_custom_call" | custom-call | tf_op jit(solution)/shard_map/pallas_call | solution.py:840
  446.9 94.3 %shard_map.300 = (bf16[2,4,256,2048]{3,2,1,0:T(8,128)(2,1)S(1)}, f32[4,2,8,128]{3,2,1,0:T(8,128)S(1)}) custom-call(bf16[256,2048]{1,0:T(8,128)(2,1)S(1)} %multiply_convert_fusion.8.x, f32[2,8,128]{2,1,0:T(8,128)S(1)} %get-tuple-element.71.peaks), custom_call_target="tpu_custom_call" | custom-call | tf_op jit(solution)/shard_map/pallas_call | solution.py:853
  567.7 24.4 %fusion.19 = f32[2048,2048]{0,1:T(8,128)} fusion(bf16[2048,2048]{1,0:T(8,128)(2,1)} %bitcast.181, bf16[2048,3072]{1,0:T(8,128)(2,1)} %bitcast.270), kind=kOutput, calls=%fused_computation.48 | convolution fusion | flops 17179869184 | bytes 33554432 | tf_op jit(solution)/shard_map/dot_general | solution.py:23
  620.6 19.1 %multiply_convert_fusion.4 = (bf16[2048,1024]{0,1:T(8,128)(2,1)}, bf16[2048,1024]{0,1:T(8,128)(2,1)}) fusion(f32[2048,2048]{0,1:T(8,128)} %fusion.19, bf16[2048,3072]{1,0:T(8,128)(2,1)} %bitcast.271, bf16[1024,2048]{1,0:T(8,128)(2,1)} %copy-done.50, bf16[1024,2048]{1,0:T(8,128)(2,1)S(1)} %copy-done.49), kind=kOutput, calls=%fused_computation.38 | convolution fusion | flops 8633974784 | bytes 37748736 | tf_op jit(solution)/shard_map/dot_general | solution.py:23
  639.7 22.3 %convolution_convert_fusion.1 = bf16[2048,2048]{1,0:T(8,128)(2,1)} fusion(bf16[2048,2048]{1,0:T(8,128)(2,1)S(1)} %bitcast.185, bf16[2048,1024]{0,1:T(8,128)(2,1)} %get-tuple-element.185, bf16[2048,1024]{0,1:T(8,128)(2,1)} %get-tuple-element.184), kind=kOutput, calls=%fused_computation.43 | convolution fusion | flops 17200840704 | bytes 25165824 | tf_op jit(solution)/shard_map/dot_general | solution.py:27
  662.0 23.5 %convert_convert_fusion.2 = f32[2048,2048]{1,0:T(8,128)} fusion(bf16[2048,3072]{1,0:T(8,128)(2,1)} %bitcast.272, bf16[2048,1024]{0,1:T(8,128)(2,1)} %get-tuple-element.185, bf16[2048,1024]{0,1:T(8,128)(2,1)S(1)} %copy-done.92), kind=kOutput, calls=%fused_computation.36 | convolution fusion | flops 17205035008 | bytes 33554432 | tf_op jit(solution)/shard_map/dot_general | solution.py:31
  686.1 29.4 %all-gather.14.cloned.1.call-done = bf16[2,1024,3072]{2,1,0:T(8,128)(2,1)} async-done(((bf16[2,256,3072]{2,1,0:T(8,128)(2,1)}), bf16[2,1024,3072]{2,1,0:T(8,128)(2,1)}) %all-gather.14.cloned.1.call-update) | async-done | bytes 12582928 | tf_op jit(solution)/shard_map/all_gather | solution.py:1016
  715.5 24.7 %fusion.16 = f32[2048,2048]{0,1:T(8,128)} fusion(bf16[2048,2048]{1,0:T(8,128)(2,1)} %bitcast.182, bf16[2048,3072]{1,0:T(8,128)(2,1)} %bitcast.274), kind=kOutput, calls=%fused_computation.45 | convolution fusion | flops 17179869184 | bytes 33554432 | tf_op jit(solution)/shard_map/dot_general | solution.py:23
  740.2 20.1 %multiply_convert_fusion.2 = (bf16[2048,1024]{0,1:T(8,128)(2,1)}, bf16[2048,1024]{0,1:T(8,128)(2,1)}, bf16[2048,1024]{0,1:T(8,128)(2,1)}) fusion(f32[2048,2048]{0,1:T(8,128)} %fusion.16, bf16[2048,3072]{1,0:T(8,128)(2,1)} %bitcast.275, bf16[1024,2048]{1,0:T(8,128)(2,1)} %get-tuple-element.205, bf16[1024,2048]{1,0:T(8,128)(2,1)S(1)} %copy-done.48), kind=kOutput, calls=%fused_computation.33 | convolution fusion | flops 8638169088 | bytes 41943040 | tf_op jit(solution)/shard_map/dot_general | solution.py:23
  760.3 13.8 fusion.26
  774.1 22.1 %convolution_convert_fusion = bf16[2048,2048]{1,0:T(8,128)(2,1)} fusion(bf16[2048,2048]{1,0:T(8,128)(2,1)S(1)} %bitcast.188, bf16[2048,1024]{0,1:T(8,128)(2,1)} %get-tuple-element.183, bf16[2048,1024]{0,1:T(8,128)(2,1)} %get-tuple-element.182), kind=kOutput, calls=%fused_computation.42 | convolution fusion | flops 17200840704 | bytes 25165824 | tf_op jit(solution)/shard_map/dot_general | solution.py:27
  796.2 24.9 %convert_add_fusion = bf16[2048,2048]{1,0:T(8,128)(2,1)} fusion(f32[2048,2048]{1,0:T(8,128)} %convert_convert_fusion.2, bf16[2048,3072]{1,0:T(8,128)(2,1)} %bitcast.276, bf16[2048,1024]{0,1:T(8,128)(2,1)} %get-tuple-element.183, bf16[2048,1024]{0,1:T(8,128)(2,1)S(1)} %copy-done.93), kind=kOutput, calls=%fused_computation.8 | convolution fusion | flops 17213423616 | bytes 41943040 | tf_op jit(solution)/shard_map/dot_general | solution.py:31
  821.1 20.1 %reduce-scatter.5.cloned.1.call-done = bf16[2,256,2048]{2,1,0:T(8,128)(2,1)} async-done(((bf16[2,1024,2048]{2,1,0:T(8,128)(2,1)}), bf16[2,256,2048]{2,1,0:T(8,128)(2,1)}) %reduce-scatter.5.cloned.1.call-update) | async-done | bytes 2097168 | tf_op jit(solution)/shard_map/reduce_scatter | solution.py:1109
  843.7 15.6 %convert_convert_fusion.1 = f32[2048,2048]{1,0:T(8,128)} fusion(bf16[2048,1024]{0,1:T(8,128)(2,1)} %multiply_convert_fusion.5, bf16[2048,3072]{1,0:T(8,128)(2,1)} %bitcast.273), kind=kOutput, calls=%fused_computation.30 | convolution fusion | flops 8598323200 | bytes 25165824 | tf_op jit(solution)/shard_map/dot_general | solution.py:31
  859.3 20.6 %add_convert_fusion = (bf16[2048,2048]{1,0:T(8,128)(2,1)}, f32[2048,2048]{1,0:T(8,128)}) fusion(f32[2048,2048]{1,0:T(8,128)} %convert_convert_fusion.1, f32[2048]{0:T(1024)S(1)} %bitcast.264, f32[2048]{0:T(1024)S(1)} %bitcast.263, bf16[2048,1024]{0,1:T(8,128)(2,1)} %get-tuple-element.188, bf16[2048,3072]{1,0:T(8,128)(2,1)} %bitcast.277), kind=kOutput, calls=%fused_computation.7 | convolution fusion | flops 8615100416 | bytes 50348032 | tf_op jit(solution)/shard_map/dot_general | solution.py:31
  879.9 15.8 %fusion.12 = (f32[1024]{0:T(1024)S(1)}, f32[1024]{0:T(1024)S(1)}, f32[1024]{0:T(1024)S(1)}, f32[1024]{0:T(1024)S(1)}) fusion(f32[2048,2048]{1,0:T(8,128)} %get-tuple-element.271, bf16[4,256,2048]{2,1,0:T(8,128)(2,1)} %copy-done.5, bf16[1024,2048]{1,0:T(8,128)(2,1)} %all-gather.12.cloned.1.call-done, f32[2048,2048]{1,0:T(8,128)} %convert_convert_fusion.1), kind=kLoop, calls=%fused_computation.24 | loop fusion | flops 20967424 | bytes 41959424 | tf_op jit(solution)/shard_map/reduce_sum | solution.py:1092
  896.4 99.5 %shard_map.301 = (f32[256,2048]{1,0:T(8,128)S(1)}, f32[16,256]{1,0:T(8,128)S(1)}) custom-call(bf16[2,4,256,2048]{3,2,1,0:T(8,128)(2,1)S(1)} %bitcast.198, f32[2,4,16,256]{3,2,1,0:T(8,128)S(1)} %fusion.111.refs_1_), custom_call_target="tpu_custom_call" | custom-call | tf_op jit(solution)/shard_map/pallas_call | solution.py:868
  1009.9 36.2 %shard_map.302.do_ref = bf16[2048,256]{1,0:T(8,128)(2,1)S(1)} custom-call(bf16[256,2048]{1,0:T(8,128)(2,1)S(1)} %convolution_convert_fusion.4.x), custom_call_target="tpu_custom_call" | custom-call | tf_op jit(solution)/shard_map/pallas_call | solution.py:840
  1047.1 37.5 %shard_map.303 = (f32[2048,256]{1,0:T(8,128)}, f32[2048,256]{1,0:T(8,128)}, f32[2048,256]{1,0:T(8,128)}) custom-call(bf16[2048,256]{1,0:T(8,128)(2,1)} %copy-done.14, bf16[2048,256]{1,0:T(8,128)(2,1)} %copy-done.13, bf16[2048,256]{1,0:T(8,128)(2,1)} %copy-done.16, s32[2048,1]{1,0:T(8,128)} %broadcast_in_dim_reshape.6.doc_q_ref, s32[1,2048]{1,0:T(1,128)} %copy-done.22, ...), custom_call_target="tpu_custom_call" | custom-call | flops 10737418240 | bytes 10485760 | tf_op jit(solution)/shard_map/pallas_call | solution.py:134
  1102.2 23.7 %shard_map.304 = f32[3,2048]{1,0:T(4,128)S(1)} custom-call(f32[3,2048]{1,0:T(4,128)S(1)} %pad_maximum_fusion.28.x), custom_call_target="tpu_custom_call" | custom-call | tf_op jit(solution)/shard_map/pallas_call | solution.py:881
  1180.5 241.8 %shard_map.305 = (f32[256,2048]{1,0:T(8,128)}, bf16[8,64,896]{2,1,0:T(8,128)(2,1)}, f32[64,2176]{1,0:T(8,128)}, f32[256,2048]{1,0:T(8,128)}) custom-call(bf16[8,256,2048]{2,1,0:T(8,128)(2,1)} %bitcast.208, bf16[4,512,896]{2,1,0:T(8,128)(2,1)} %bitcast.203, bf16[4,64,2176]{2,1,0:T(8,128)(2,1)} %pad_maximum_fusion.24.out, bf16[2,4,256,2048]{3,2,1,0:T(8,128)(2,1)} %bitcast.207), custom_call_target="tpu_custom_call" | custom-call | tf_op jit(solution)/shard_map/pallas_call | solution.py:897
  (382 shorter events, 264.8 us)
Async XLA Ops:
  7.2 537.4 %all-gather.8.cloned.1.call-start = ((), (), s32[]{:S(2)}) async-start(), calls=%async_computation.4 | async-start | bytes 4718592 | tf_op jit(solution)/shard_map/all_gather | solution.py:995
  16.6 239.7 %collective-permute-start = (bf16[256,3072]{1,0:T(8,128)(2,1)}, bf16[256,3072]{1,0:T(8,128)(2,1)}, u32[]{:S(2)}, u32[]{:S(2)}) collective-permute-start(bf16[256,3072]{1,0:T(8,128)(2,1)} %get-tuple-element.199), channel_id=1, source_target_pairs={{0,16},{4,20},{8,24},{12,28},{16,0},{20,4},{24,8},{28,12},{1,17},{... | collective-permute-start | bytes 4718600 | tf_op jit(solution)/shard_map/ppermute | solution.py:992
  256.3 296.9 %copy-start = (bf16[8,4,64,128]{3,2,1,0:T(8,128)(2,1)}, bf16[8,4,64,128]{3,2,1,0:T(8,128)(2,1)S(1)}, u32[]{:S(2)}) copy-start(bf16[8,4,64,128]{3,2,1,0:T(8,128)(2,1)S(1)} %get-tuple-element.66) | copy-start | bytes 1572868
  256.3 311.4 %all-gather.10.cloned.1.call-start = ((), (), s32[]{:S(2)}) async-start(), calls=%async_computation.5 | async-start | bytes 15728640 | tf_op jit(solution)/shard_map/all_gather | solution.py:1016
  261.1 341.1 %all-gather.12.cloned.1.call-start = ((), (), s32[]{:S(2)}) async-start(), calls=%async_computation.6 | async-start | bytes 5242880 | tf_op jit(solution)/shard_map/all_gather | solution.py:1054
  262.6 117.0 %copy-start.22 = (s32[1,2048]{1,0:T(1,128)}, s32[1,2048]{1,0:T(1,128)S(1)}, u32[]{:S(2)}) copy-start(s32[1,2048]{1,0:T(1,128)S(1)} %broadcast_in_dim_reshape.5.doc_k_ref) | copy-start | bytes 24580
  267.8 177.9 %copy-start.63 = (f32[2048,1]{0,1:T(1,128)}, f32[2048,1]{0,1:T(1,128)S(1)}, u32[]{:S(2)}) copy-start(f32[2048,1]{0,1:T(1,128)S(1)} %copy.194) | copy-start | bytes 24580
  270.3 101.5 %copy-start.76 = (f32[256,1]{0,1:T(1,128)}, f32[256,1]{0,1:T(1,128)S(1)}, u32[]{:S(2)}) copy-start(f32[256,1]{0,1:T(1,128)S(1)} %copy.193) | copy-start | bytes 3076
  270.4 101.4 %copy-start.78 = (f32[256,1]{0,1:T(1,128)}, f32[256,1]{0,1:T(1,128)S(1)}, u32[]{:S(2)}) copy-start(f32[256,1]{0,1:T(1,128)S(1)} %copy.192) | copy-start | bytes 3076
  270.4 102.1 %copy-start.84 = (f32[64]{0:T(128)}, f32[64]{0:T(128)S(1)}, u32[]{:S(2)}) copy-start(f32[64]{0:T(128)S(1)} %multiply_power_fusion) | copy-start | bytes 772
  270.5 102.1 %copy-start.71 = (f32[2048]{0:T(1024)}, f32[2048]{0:T(1024)S(1)}, u32[]{:S(2)}) copy-start(f32[2048]{0:T(1024)S(1)} %iota_convert_fusion) | copy-start | bytes 24580
  270.5 276.7 %collective-permute-start.1 = (bf16[256,2048]{1,0:T(8,128)(2,1)S(1)}, bf16[256,2048]{1,0:T(8,128)(2,1)}, u32[]{:S(2)}, u32[]{:S(2)}) collective-permute-start(bf16[256,2048]{1,0:T(8,128)(2,1)S(1)} %bitcast.191), channel_id=1, source_target_pairs={{0,16},{4,20},{8,24},{12,28},{16,0},{20,4},{24,8},{28,12},{1,17},{... | collective-permute-start | bytes 3145736 | tf_op jit(solution)/shard_map/ppermute | solution.py:992
  446.9 104.5 %copy-start.8 = (bf16[256,2048]{1,0:T(8,128)(2,1)}, bf16[256,2048]{1,0:T(8,128)(2,1)S(1)}, u32[]{:S(2)}) copy-start(bf16[256,2048]{1,0:T(8,128)(2,1)S(1)} %multiply_convert_fusion.8.x) | copy-start | bytes 3145732
  547.2 168.3 %all-gather.14.cloned.1.call-start = ((), (), s32[]{:S(2)}) async-start(), calls=%async_computation.7 | async-start | bytes 15728640 | tf_op jit(solution)/shard_map/all_gather | solution.py:1016
  561.5 259.6 %reduce-scatter.7.cloned.1.call-start = ((), (), s32[]{:S(2)}) async-start(), calls=%async_computation.9 | async-start | bytes 5242880 | tf_op jit(solution)/shard_map/reduce_scatter | solution.py:1109
  685.5 155.7 %reduce-scatter.5.cloned.1.call-start = ((), (), s32[]{:S(2)}) async-start(), calls=%async_computation.8 | async-start | bytes 10485760 | tf_op jit(solution)/shard_map/reduce_scatter | solution.py:1109
  686.0 316.1 %reduce-scatter.11.cloned.1.call-start = ((), (), s32[]{:S(2)}) async-start(), calls=%async_computation.11 | async-start | bytes 5242880 | tf_op jit(solution)/shard_map/reduce_scatter | solution.py:1109
  841.2 161.0 %reduce-scatter.9.cloned.1.call-start = ((), (), s32[]{:S(2)}) async-start(), calls=%async_computation.10 | async-start | bytes 10485760 | tf_op jit(solution)/shard_map/reduce_scatter | solution.py:1109
  841.9 307.5 %all-gather.16.cloned.1.call-start = ((), (), s32[]{:S(2)}) async-start(), calls=%async_computation.12 | async-start | bytes 9437184 | tf_op jit(solution)/shard_map/all_gather | solution.py:1148
  896.4 101.1 %copy-start.1 = (bf16[8,4,64,128]{3,2,1,0:T(8,128)(2,1)S(1)}, bf16[8,4,64,128]{3,2,1,0:T(8,128)(2,1)}, u32[]{:S(2)}) copy-start(bf16[8,4,64,128]{3,2,1,0:T(8,128)(2,1)} %copy-done) | copy-start | bytes 1572868
  896.4 101.1 %copy-start.29 = (f32[256,2048]{1,0:T(8,128)S(1)}, f32[256,2048]{1,0:T(8,128)}, u32[]{:S(2)}) copy-start(f32[256,2048]{1,0:T(8,128)} %copy-done.28) | copy-start | bytes 6291460
  896.4 101.1 %copy-start.64 = (f32[2048,1]{0,1:T(1,128)S(1)}, f32[2048,1]{0,1:T(1,128)}, u32[]{:S(2)}) copy-start(f32[2048,1]{0,1:T(1,128)} %copy-done.63) | copy-start | bytes 24580
  896.4 101.1 %copy-start.75 = (f32[256]{0:T(256)S(1)}, f32[256]{0:T(256)}, u32[]{:S(2)}) copy-start(f32[256]{0:T(256)} %copy-done.74) | copy-start | bytes 3076
  1002.2 451.0 %all-gather.18.cloned.1.call-start = ((), (), s32[]{:S(2)}) async-start(), calls=%async_computation.13 | async-start | bytes 9437184 | tf_op jit(solution)/shard_map/all_gather | solution.py:995
  (88 other events, 999.9 us)
Sparse Core Ops, SparseCore 0:
  256.4 126.2 all-gather.7
  384.9 150.2 all-gather.9
  547.4 54.7 all-gather.11
  603.6 111.8 all-gather.13
  717.6 44.5 reduce-scatter.6
  764.6 76.5 reduce-scatter.4
  843.5 42.8 reduce-scatter.10
  888.8 91.1 reduce-scatter.8
  1002.3 101.7 all-gather.15
  1158.4 174.6 all-gather.17

commit v5 on v4

--- a/solution.py
+++ b/solution.py
@@ -503,7 +503,7 @@
 
 
 def start_kernel(
-    x, w, w_query, w_key, w_value, small, cot, x_all, w_all, heads_all, small_all, cot_all,
+    x, w, w_query, w_key, w_value, small, x_all, w_all, heads_all, small_all,
     heads_mid, small_mid, own_sem, ex_send, ex_recv, sp_send, sp_recv, w_send, w_recv, f_send,
     f_recv, *line_sems,
 ):
@@ -533,7 +533,6 @@
         Direct("shard", whole_of(heads_mid), by_shard(heads_all), sp_send.at[0], sp_recv.at[0]),
         Direct("shard", whole_of(small_mid), by_shard(small_all), sp_send.at[1], sp_recv.at[1]),
     ]
-    other = Direct("shard", whole_of(cot), block_from(cot_all), sp_send.at[2], sp_recv.at[2])
     pieces = row_pieces(x, x_all, LINE_CHUNKS) + [(w, lambda b: w_all.at[b, shard])]
     line = LineGather(pieces, *line_sems)
     at = line.line
@@ -544,7 +543,6 @@
     later = [
         pltpu.make_async_copy(heads_mid, heads_all.at[:, shard], own_sem.at[4]),
         pltpu.make_async_copy(small_mid, small_all.at[:, shard], own_sem.at[5]),
-        pltpu.make_async_copy(cot, cot_all.at[shard], own_sem.at[6]),
     ]
     for swap in swaps:
         swap.start()
@@ -556,7 +554,7 @@
         swap.wait_recv()
     for copy in own:
         copy.wait()
-    for one in (*spreads, other, *later):
+    for one in (*spreads, *later):
         one.start()
     for k in range(1, at.n):
         line.hop(k)
@@ -597,15 +595,20 @@
         row(k, p, shard).wait_send()
         forward(k, p, at.core).wait_send()
         forward(k, p, 1 - at.core).wait_recv()
-    for direct in (*spreads, other):
+    for direct in spreads:
         direct.wait_recv()
-    for direct in (*swaps, *spreads, other):
+    for direct in (*swaps, *spreads):
         direct.wait_send()
     for copy in later:
         copy.wait()
 
 
-def exchange_kernel(to_rows, x, o, own_sem, send, recv):
+def exchange_kernel(to_rows, *refs):
+    more = len(refs) > 5
+    if more:
+        x, cot, o, cot_all, own_sem, send, recv, cot_send, cot_recv = refs
+    else:
+        x, o, own_sem, send, recv = refs
     n, me = lax.axis_size("ctx"), lax.axis_index("ctx")
     cols, rows = (x.shape[1] // n, x.shape[0]) if to_rows else (x.shape[1], o.shape[0])
 
@@ -618,14 +621,24 @@
     source, target = (
         (column_block(x), row_block(o)) if to_rows else (row_block(x), column_block(o))
     )
-    Greeting().ring("ctx").wait()
-    swap = Direct("ctx", source, target, send, recv)
-    swap.start()
-    own = pltpu.make_async_copy(source(me), target(me), own_sem)
-    own.start()
-    own.wait()
-    swap.wait_recv()
-    swap.wait_send()
+    greeting = Greeting().ring("ctx")
+    if more:
+        greeting.ring("shard")
+    greeting.wait()
+    all_of = [Direct("ctx", source, target, send, recv)]
+    own = [pltpu.make_async_copy(source(me), target(me), own_sem.at[0])]
+    if more:
+        all_of.append(Direct("shard", whole_of(cot), block_from(cot_all), cot_send, cot_recv))
+        own.append(
+            pltpu.make_async_copy(cot, cot_all.at[lax.axis_index("shard")], own_sem.at[1])
+        )
+    for one in (*all_of, *own):
+        one.start()
+    for copy in own:
+        copy.wait()
+    for direct in all_of:
+        direct.wait_recv()
+        direct.wait_send()
 
 
 class Pair:
@@ -803,7 +816,7 @@
 LINE_CHUNKS = 4
 
 
-def start_call(collective_id, x, w, w_query, w_key, w_value, small, cot):
+def start_call(collective_id, x, w, w_query, w_key, w_value, small):
     n_ctx, n_shard = lax.axis_size("ctx"), lax.axis_size("shard")
     n = n_ctx // 2
     heads = (w.shape[0], 3 * w.shape[1] // n_ctx)
@@ -815,36 +828,36 @@
             jax.ShapeDtypeStruct((n_ctx, n_shard, *w.shape), bf16),
             jax.ShapeDtypeStruct((n_ctx, n_shard, *heads), bf16),
             jax.ShapeDtypeStruct((n_ctx, n_shard, *small.shape), bf16),
-            jax.ShapeDtypeStruct((n_shard, *cot.shape), bf16),
         ],
-        in_specs=[ANY] * 7,
-        out_specs=[ANY] * 5,
+        in_specs=[ANY] * 6,
+        out_specs=[ANY] * 4,
         scratch_shapes=[
             pltpu.VMEM((n_ctx, *heads), bf16),
             pltpu.VMEM((n_ctx, *small.shape), bf16),
-            sem((7,)),
+            sem((6,)),
             sem((4, n_ctx)),
             sem((4, n_ctx)),
         ]
-        + [sem((3, n_shard))] * 2
+        + [sem((2, n_shard))] * 2
         + [sem((n_shard, n))] * 4
         + line_gather_scratch(n, LINE_CHUNKS + 1),
         compiler_params=remote_params(collective_id, 8),
-    )(x, w, w_query, w_key, w_value, small, cot)
-
-
-def exchange(collective_id, x, to_rows):
-    n = lax.axis_size("ctx")
+    )(x, w, w_query, w_key, w_value, small)
+
+
+def exchange(collective_id, x, to_rows, *more):
+    n, n_shard = lax.axis_size("ctx"), lax.axis_size("shard")
     shape = (x.shape[0] * n, x.shape[1] // n) if to_rows else (x.shape[0] // n, x.shape[1] * n)
     sem = pltpu.SemaphoreType.DMA
     return pl.pallas_call(
         functools.partial(exchange_kernel, to_rows),
-        out_shape=jax.ShapeDtypeStruct(shape, x.dtype),
-        in_specs=[ANY],
-        out_specs=ANY,
-        scratch_shapes=[sem, sem((n,)), sem((n,))],
+        out_shape=[jax.ShapeDtypeStruct(shape, x.dtype)]
+        + [jax.ShapeDtypeStruct((n_shard, *u.shape), u.dtype) for u in more],
+        in_specs=[ANY] * (1 + len(more)),
+        out_specs=[ANY] * (1 + len(more)),
+        scratch_shapes=[sem((2,)), sem((n,)), sem((n,))] + [sem((n_shard,))] * (2 * len(more)),
         compiler_params=remote_params(collective_id, 8),
-    )(x)
+    )(x, *more)
 
 
 def pair_gather(collective_id, x, peaks):
@@ -963,8 +976,8 @@
         axis=1,
     )
     grad_own = cotangent[0]
-    x_all, out_w, weights, small_all, grad_mine = start_call(
-        1, x_own, w_out, w_query, w_key, w_value, small, grad_own
+    x_all, out_w, weights, small_all = start_call(
+        1, x_own, w_out, w_query, w_key, w_value, small
     )
     x_all = x_all.reshape(count, width)
     out_w = out_w.reshape(width, width)
@@ -1006,12 +1019,11 @@
     keep_w = lax.dynamic_slice_in_dim(own_w, role * half, half, 0)
     give_w = lax.dynamic_slice_in_dim(own_w, (1 - role) * half, half, 0)
     spans = [list(range(r * span, (r + 1) * span)) for r in (0, 1)]
-    first_w = swap(give_w[0])
-    x_all, first_w, later_w, later_grad = lax.optimization_barrier(
-        (x_all, first_w, give_w[1:], grad_own)
-    )
-    grad_theirs = swap(later_grad)
+    grad_theirs = queued_swap(grad_own)
+    first_w = queued_swap(give_w[0])
+    x_all, first_w, later_w = lax.optimization_barrier((x_all, first_w, give_w[1:]))
     early = [first_w] + [queued_swap(later_w[e]) for e in range(half - 1)]
+
     def expert_weights(e, theirs):
         return lax.all_gather(
             in_order(keep_w[e], theirs),
@@ -1040,9 +1052,10 @@
     query = rotate(query_n * gain_query, cosine, sine).astype(bf16)
     key = rotate(key_n * gain_key, cosine, sine).astype(bf16)
     mixed, log_total, peaks = attend_forward(query, key, value, docs)
+    x_f = x_own.astype(f32)
+    mixed_own, grad_mine = exchange(2, mixed, False, grad_own)
     grad_mine = grad_mine.reshape(n_shard * rows, width)
-    x_f = x_own.astype(f32)
-    after = x_f + dot(exchange(2, mixed, False), out_w)
+    after = x_f + dot(mixed_own, out_w)
     inverse_two = inverse_rms(after)
     normed_two = after * inverse_two
     hidden_two = (normed_two * gain_ffn).astype(bf16)
@@ -1144,32 +1157,22 @@
     )
 
     grad_attn_own = grad_after.astype(bf16)
-    to_gather, expert_grads = lax.optimization_barrier((grad_attn_own, expert_grads))
+
+    def give(sums):
+        return jnp.concatenate(
+            [lax.dynamic_index_in_dim(u, 1 - role, 0, False) for u in sums], axis=1
+        )
+
+    peers = [swap(give(sums)) for sums in expert_grads[:-1]]
+    to_gather, grad_attn_own, expert_grads[-1], peers = lax.optimization_barrier(
+        (grad_attn_own, grad_attn_own, expert_grads[-1], peers)
+    )
     grad_attn = lax.all_gather(to_gather, "ctx", axis=0, tiled=True)
-    grad_mixed = exchange(5, contract_cols(grad_attn_own, out_w).astype(bf16), True)
-    grad_attn, expert_grads = lax.optimization_barrier((grad_attn, expert_grads))
+    (grad_mixed,) = exchange(5, contract_cols(grad_attn_own, out_w).astype(bf16), True)
     grad_out_w = contract_rows(mixed, grad_attn)
     grad_query_rot, grad_key_rot, grad_value = attend_backward(
         query, key, value, docs, log_total, grad_mixed
     )
-    kept = [[lax.dynamic_index_in_dim(u, role, 0, False) for u in sums] for sums in expert_grads]
-    peers = queued_swap(
-        jnp.stack(
-            [
-                jnp.concatenate(
-                    [lax.dynamic_index_in_dim(u, 1 - role, 0, False) for u in sums], axis=1
-                )
-                for sums in expert_grads
-            ]
-        )
-    )
-    peers = [(peer[:, : 2 * ff], peer[:, 2 * ff :]) for peer in peers]
-    both_halves = [
-        in_order(jnp.stack([k[i] for k in kept]), jnp.stack([p[i] for p in peers]))
-        .reshape(local, width // n_ctx, -1)
-        .astype(f32)
-        for i in (0, 1)
-    ]
     grad_query_n = rotate(grad_query_rot, cosine, -sine)
     grad_key_n = rotate(grad_key_rot, cosine, -sine)
     grad_gain_query = jnp.sum(grad_query_n * query_n, axis=0)
@@ -1180,6 +1183,16 @@
         [jnp.sum(scaled_q * query_n, axis=1), jnp.sum(scaled_k * key_n, axis=1), peak_row]
     )
     inner = many_sum("ctx", 7, inner)
+    inner, expert_grads[-1] = lax.optimization_barrier((inner, expert_grads[-1]))
+    peers.append(swap(give(expert_grads[-1])))
+    kept = [[lax.dynamic_index_in_dim(u, role, 0, False) for u in sums] for sums in expert_grads]
+    peers = [(peer[:, : 2 * ff], peer[:, 2 * ff :]) for peer in peers]
+    both_halves = [
+        in_order(jnp.stack([k[i] for k in kept]), jnp.stack([p[i] for p in peers]))
+        .reshape(local, width // n_ctx, -1)
+        .astype(f32)
+        for i in (0, 1)
+    ]
     peak_all = inner[2, :HEADS]
     inner = inner / width
     grad_linear = jnp.concatenate(

time: 1490 us -> 1420 us (0.953)
  Pallas kernels: 900 us -> 809 us
  waiting for transfers between devices: 52.2 us -> 75.9 us
    pallas_call x1, Pallas kernels: 242 us -> 160 us  [end_call(): pl.pallas_call(end_kernel, out_shape=[jax.ShapeDtypeStruct((rows, width),...]
    pallas_call x2, Pallas kernels: 108 us -> 42 us  [many_sum(): pl.pallas_call(functools.partial(many_sum_kernel, axis), out_shape=jax.Sh...]
    pallas_call x1, Pallas kernels: 223 us -> 254 us  [start_call(): pl.pallas_call(start_kernel, out_shape=[jax.ShapeDtypeStruct((n_ctx, *x.s...]
    ppermute x2, waiting for transfers between devices: 0.01 us -> 30.2 us  [swap(): lax.ppermute(u, 'ctx', [(i, (i + span) % n_ctx) for i in range(n_ctx)])]
    unnamed x212 -> x194, local copies, waits for them, and re-layouts: 35.5 us -> 33.2 us
  transfers between devices with their start and end apart: 12 -> 13, of which waited for: 3 -> 3; matrix products, arithmetic and copies ran while one was open for 30% -> 31% of each run, Pallas kernels for 61% -> 46%
where the time goes in v5:
time: 1420 us; the launch traced here: 1410 us
  Pallas kernels  809 us (57%)
  matrix products  305 us (21%)
  other arithmetic  109 us (8%)
  local copies, waits for them, and re-layouts  90.4 us (6%)
  waiting for transfers between devices  75.9 us (5%)
  between operations  16.6 us (1%)
    pallas_call x1, Pallas kernels, start_call(): pl.pallas_call(start_kernel, out_shape=[jax.ShapeDtypeStruct((n_ctx, *x.s...  254 us
    pallas_call x1, Pallas kernels, end_call(): pl.pallas_call(end_kernel, out_shape=[jax.ShapeDtypeStruct((rows, width),...  160 us
    pallas_call x1, Pallas kernels, pair_reduce(): pl.pallas_call(functools.partial(pair_reduce_kernel, len(arrays)), out_sh...  112 us
    dot_general x7, matrix products, dot(): return jnp.dot(a, b, preferred_element_type=f32)  111 us
    dot_general x7, matrix products, contract_cols(): lax.dot_general(a, b, (((1,), (1,)), ((), ())), preferred_element_type=f32)  106 us
    pallas_call x1, Pallas kernels, pair_gather(): pl.pallas_call(pair_gather_kernel, out_shape=[jax.ShapeDtypeStruct((2, n,...  93.8 us
    dot_general x7, matrix products, contract_rows(): lax.dot_general(a, b, (((0,), (0,)), ((), ())), preferred_element_type=f32)  88.4 us
    pallas_call x2, Pallas kernels, exchange(): pl.pallas_call(functools.partial(exchange_kernel, to_rows), out_shape=[ja...  87.4 us
  transfers between devices with their start and end apart: 13, of which 3 were waited for; matrix products, arithmetic and copies ran while one was open for 31% of the time, Pallas kernels for 46%

profile of v5, /device:TPU:0, one launch (start us, length us, event | category | flops | bytes accessed | tf_op | source)
XLA Modules:
  0.0 1410.3 jit_solution(7349064107458598233)
XLA Ops:
  18.4 253.5 %shard_map.296 = (bf16[8,256,2048]{2,1,0:T(8,128)(2,1)S(1)}, bf16[8,4,64,2048]{3,2,1,0:T(8,128)(2,1)S(1)}, bf16[8,4,64,768]{3,2,1,0:T(8,128)(2,1)S(1)}, bf16[8,4,64,128]{3,2,1,0:T(8,128)(2,1)S(1)}) custom-call(bf16[256,2048]{1,0:T(8,128)(2,1)S(1)} %bitcast.182, bf16[64,2048]{1,0:T(8,128)(2,1)S(1)} %copy-done.24, bf16[64,2048]{1,0:T(8,128)(2,1)S(1)} %copy-done.20, ...), custom_call_target="tpu_custom_call" | custom-call | tf_op jit(solution)/shard_map/pallas_call | solution.py:824
  311.6 17.3 %shard_map.297 = f32[2,2048]{1,0:T(2,128)S(1)} custom-call(f32[2,2048]{1,0:T(2,128)S(1)} %pad_maximum_fusion.30.x), custom_call_target="tpu_custom_call" | custom-call | tf_op jit(solution)/shard_map/pallas_call | solution.py:894
  337.0 23.0 %shard_map.298 = (bf16[2048,256]{1,0:T(8,128)(2,1)S(1)}, f32[2,2048,1]{2,1,0:T(8,128)}, f32[2,8,128]{2,1,0:T(8,128)S(1)}) custom-call(bf16[2048,256]{1,0:T(8,128)(2,1)S(1)} %pad_maximum_fusion.26.q_ref, bf16[2048,256]{1,0:T(8,128)(2,1)S(1)} %pad_maximum_fusion.27.k_ref, bf16[2048,256]{1,0:T(8,128)(2,1)S(1)} %slice.462.v_ref, ...), custom_call_target="tpu_custom_call" | custom-call | flops 4294967296 | bytes 4194304 | tf_op jit(solution)/shard_map/pallas_call | solution.py:111
  360.0 50.2 %shard_map.299 = (bf16[256,2048]{1,0:T(8,128)(2,1)S(1)}, bf16[4,256,2048]{2,1,0:T(8,128)(2,1)S(1)}) custom-call(bf16[2048,256]{1,0:T(8,128)(2,1)S(1)} %get-tuple-element.66.refs_0_, bf16[256,2048]{1,0:T(8,128)(2,1)S(1)} %bitcast.183), custom_call_target="tpu_custom_call" | custom-call | tf_op jit(solution)/shard_map/pallas_call | solution.py:852
  419.5 93.8 %shard_map.300 = (bf16[2,4,256,2048]{3,2,1,0:T(8,128)(2,1)S(1)}, f32[4,2,8,128]{3,2,1,0:T(8,128)S(1)}) custom-call(bf16[256,2048]{1,0:T(8,128)(2,1)S(1)} %multiply_convert_fusion.8.x, f32[2,8,128]{2,1,0:T(8,128)S(1)} %get-tuple-element.70.peaks), custom_call_target="tpu_custom_call" | custom-call | tf_op jit(solution)/shard_map/pallas_call | solution.py:866
  541.0 24.3 %fusion.19 = f32[2048,2048]{0,1:T(8,128)} fusion(bf16[2048,2048]{1,0:T(8,128)(2,1)} %bitcast.174, bf16[2048,3072]{1,0:T(8,128)(2,1)} %bitcast.264), kind=kOutput, calls=%fused_computation.48 | convolution fusion | flops 17179869184 | bytes 33554432 | tf_op jit(solution)/shard_map/dot_general | solution.py:23
  594.5 19.2 %multiply_convert_fusion.4 = (bf16[2048,1024]{0,1:T(8,128)(2,1)}, bf16[2048,1024]{0,1:T(8,128)(2,1)}) fusion(f32[2048,2048]{0,1:T(8,128)} %fusion.19, bf16[2048,3072]{1,0:T(8,128)(2,1)} %bitcast.265, bf16[1024,2048]{1,0:T(8,128)(2,1)} %get-tuple-element.200, bf16[1024,2048]{1,0:T(8,128)(2,1)} %get-tuple-element.198), kind=kOutput, calls=%fused_computation.38 | convolution fusion | flops 8633974784 | bytes 37748736 | tf_op jit(solution)/shard_map/dot_general | solution.py:23
  613.7 21.9 %convolution_convert_fusion.1 = bf16[2048,2048]{1,0:T(8,128)(2,1)} fusion(bf16[2048,2048]{1,0:T(8,128)(2,1)S(1)} %bitcast.178, bf16[2048,1024]{0,1:T(8,128)(2,1)} %get-tuple-element.181, bf16[2048,1024]{0,1:T(8,128)(2,1)} %get-tuple-element.180), kind=kOutput, calls=%fused_computation.43 | convolution fusion | flops 17200840704 | bytes 25165824 | tf_op jit(solution)/shard_map/dot_general | solution.py:27
  635.6 24.4 %convert_convert_fusion.2 = f32[2048,2048]{1,0:T(8,128)} fusion(bf16[2048,3072]{1,0:T(8,128)(2,1)} %bitcast.266, bf16[2048,1024]{0,1:T(8,128)(2,1)} %get-tuple-element.181, bf16[2048,1024]{0,1:T(8,128)(2,1)} %get-tuple-element.180), kind=kOutput, calls=%fused_computation.36 | convolution fusion | flops 17205035008 | bytes 33554432 | tf_op jit(solution)/shard_map/dot_general | solution.py:31
  660.8 25.0 %all-gather.18.cloned.1.call-done = bf16[2,1024,3072]{2,1,0:T(8,128)(2,1)} async-done(((bf16[2,256,3072]{2,1,0:T(8,128)(2,1)}), bf16[2,1024,3072]{2,1,0:T(8,128)(2,1)}) %all-gather.18.cloned.1.call-update) | async-done | bytes 12582928 | tf_op jit(solution)/shard_map/all_gather | solution.py:1028
  685.8 25.1 %fusion.16 = f32[2048,2048]{0,1:T(8,128)} fusion(bf16[2048,2048]{1,0:T(8,128)(2,1)} %bitcast.175, bf16[2048,3072]{1,0:T(8,128)(2,1)} %bitcast.268), kind=kOutput, calls=%fused_computation.45 | convolution fusion | flops 17179869184 | bytes 33554432 | tf_op jit(solution)/shard_map/dot_general | solution.py:23
  710.9 20.3 %multiply_convert_fusion.2 = (bf16[2048,1024]{0,1:T(8,128)(2,1)}, bf16[2048,1024]{0,1:T(8,128)(2,1)}, bf16[2048,1024]{0,1:T(8,128)(2,1)}) fusion(f32[2048,2048]{0,1:T(8,128)} %fusion.16, bf16[2048,3072]{1,0:T(8,128)(2,1)} %bitcast.269, bf16[1024,2048]{1,0:T(8,128)(2,1)} %get-tuple-element.199, bf16[1024,2048]{1,0:T(8,128)(2,1)} %get-tuple-element.197), kind=kOutput, calls=%fused_computation.33 | convolution fusion | flops 8638169088 | bytes 41943040 | tf_op jit(solution)/shard_map/dot_general | solution.py:23
  745.6 22.0 %convolution_convert_fusion = bf16[2048,2048]{1,0:T(8,128)(2,1)} fusion(bf16[2048,2048]{1,0:T(8,128)(2,1)S(1)} %bitcast.181, bf16[2048,1024]{0,1:T(8,128)(2,1)} %get-tuple-element.179, bf16[2048,1024]{0,1:T(8,128)(2,1)} %get-tuple-element.178), kind=kOutput, calls=%fused_computation.42 | convolution fusion | flops 17200840704 | bytes 25165824 | tf_op jit(solution)/shard_map/dot_general | solution.py:27
  767.6 25.6 %convert_add_fusion = bf16[2048,2048]{1,0:T(8,128)(2,1)} fusion(f32[2048,2048]{1,0:T(8,128)} %convert_convert_fusion.2, bf16[2048,3072]{1,0:T(8,128)(2,1)} %bitcast.270, bf16[2048,1024]{0,1:T(8,128)(2,1)} %get-tuple-element.179, bf16[2048,1024]{0,1:T(8,128)(2,1)} %get-tuple-element.178), kind=kOutput, calls=%fused_computation.8 | convolution fusion | flops 17213423616 | bytes 41943040 | tf_op jit(solution)/shard_map/dot_general | solution.py:31
  793.2 18.6 %reduce-scatter.5.cloned.1.call-done = bf16[2,256,2048]{2,1,0:T(8,128)(2,1)} async-done(((bf16[2,1024,2048]{2,1,0:T(8,128)(2,1)}), bf16[2,256,2048]{2,1,0:T(8,128)(2,1)}) %reduce-scatter.5.cloned.1.call-update) | async-done | bytes 2097168 | tf_op jit(solution)/shard_map/reduce_scatter | solution.py:1122
  815.9 15.4 %convert_convert_fusion.1 = f32[2048,2048]{1,0:T(8,128)} fusion(bf16[2048,1024]{0,1:T(8,128)(2,1)} %multiply_convert_fusion.5, bf16[2048,3072]{1,0:T(8,128)(2,1)} %bitcast.267), kind=kOutput, calls=%fused_computation.30 | convolution fusion | flops 8598323200 | bytes 25165824 | tf_op jit(solution)/shard_map/dot_general | solution.py:31
  831.3 21.0 %add_convert_fusion = (bf16[2048,2048]{1,0:T(8,128)(2,1)}, f32[2048,2048]{1,0:T(8,128)}) fusion(f32[2048,2048]{1,0:T(8,128)} %convert_convert_fusion.1, f32[2048]{0:T(1024)S(1)} %bitcast.258, f32[2048]{0:T(1024)S(1)} %bitcast.257, bf16[2048,1024]{0,1:T(8,128)(2,1)} %get-tuple-element.184, bf16[2048,3072]{1,0:T(8,128)(2,1)} %bitcast.271), kind=kOutput, calls=%fused_computation.7 | convolution fusion | flops 8615100416 | bytes 50348032 | tf_op jit(solution)/shard_map/dot_general | solution.py:31
  852.3 16.5 %fusion.12 = (f32[1024]{0:T(1024)S(1)}, f32[1024]{0:T(1024)S(1)}, f32[1024]{0:T(1024)S(1)}, f32[1024]{0:T(1024)S(1)}) fusion(f32[2048,2048]{1,0:T(8,128)} %get-tuple-element.265, bf16[4,256,2048]{2,1,0:T(8,128)(2,1)} %copy-done.3, bf16[1024,2048]{1,0:T(8,128)(2,1)} %all-gather.16.cloned.1.call-done, f32[2048,2048]{1,0:T(8,128)} %convert_convert_fusion.1), kind=kLoop, calls=%fused_computation.24 | loop fusion | flops 20967424 | bytes 41959424 | tf_op jit(solution)/shard_map/reduce_sum | solution.py:1105
  877.2 111.6 %shard_map.301 = (f32[256,2048]{1,0:T(8,128)S(1)}, f32[16,256]{1,0:T(8,128)S(1)}) custom-call(bf16[2,4,256,2048]{3,2,1,0:T(8,128)(2,1)S(1)} %bitcast.190, f32[2,4,16,256]{3,2,1,0:T(8,128)S(1)} %fusion.111.refs_1_), custom_call_target="tpu_custom_call" | custom-call | tf_op jit(solution)/shard_map/pallas_call | solution.py:881
  1001.3 37.2 %shard_map.302.do_ref = bf16[2048,256]{1,0:T(8,128)(2,1)S(1)} custom-call(bf16[256,2048]{1,0:T(8,128)(2,1)S(1)} %convolution_convert_fusion.4.refs_0_), custom_call_target="tpu_custom_call" | custom-call | tf_op jit(solution)/shard_map/pallas_call | solution.py:852
  1039.5 37.5 %shard_map.303 = (f32[2048,256]{1,0:T(8,128)}, f32[2048,256]{1,0:T(8,128)}, f32[2048,256]{1,0:T(8,128)}) custom-call(bf16[2048,256]{1,0:T(8,128)(2,1)} %copy-done.16, bf16[2048,256]{1,0:T(8,128)(2,1)} %copy-done.15, bf16[2048,256]{1,0:T(8,128)(2,1)} %copy-done.18, s32[2048,1]{1,0:T(8,128)} %copy-done.17, s32[1,2048]{1,0:T(1,128)} %copy-done.26, ...), custom_call_target="tpu_custom_call" | custom-call | flops 10737418240 | bytes 10485760 | tf_op jit(solution)/shard_map/pallas_call | solution.py:134
  1093.2 24.7 %shard_map.304 = f32[3,2048]{1,0:T(4,128)S(1)} custom-call(f32[3,2048]{1,0:T(4,128)S(1)} %pad_maximum_fusion.29.x), custom_call_target="tpu_custom_call" | custom-call | tf_op jit(solution)/shard_map/pallas_call | solution.py:894
  1161.9 30.2 %collective-permute-done.1 = bf16[256,3072]{1,0:T(8,128)(2,1)} collective-permute-done((bf16[256,3072]{1,0:T(8,128)(2,1)}, bf16[256,3072]{1,0:T(8,128)(2,1)}, u32[]{:S(2)}, u32[]{:S(2)}) %collective-permute-start.1) | collective-permute-done | bytes 1572896 | tf_op jit(solution)/shard_map/ppermute | solution.py:1005
  1217.1 159.7 %shard_map.305 = (f32[256,2048]{1,0:T(8,128)}, bf16[8,64,896]{2,1,0:T(8,128)(2,1)}, f32[64,2176]{1,0:T(8,128)}, f32[256,2048]{1,0:T(8,128)}) custom-call(bf16[8,256,2048]{2,1,0:T(8,128)(2,1)} %bitcast.202, bf16[4,512,896]{2,1,0:T(8,128)(2,1)} %bitcast.197, bf16[4,64,2176]{2,1,0:T(8,128)(2,1)} %pad_maximum_fusion.25.out, bf16[2,4,256,2048]{3,2,1,0:T(8,128)(2,1)} %bitcast.201), custom_call_target="tpu_custom_call" | custom-call | tf_op jit(solution)/shard_map/pallas_call | solution.py:910
  (368 shorter events, 275.7 us)
Async XLA Ops:
  7.2 272.9 %all-gather.8.cloned.1.call-start = ((), (), s32[]{:S(2)}) async-start(), calls=%async_computation.4 | async-start | bytes 4718592 | tf_op jit(solution)/shard_map/all_gather | solution.py:1008
  16.4 277.4 %all-gather.12.cloned.1.call-start = ((), (), s32[]{:S(2)}) async-start(), calls=%async_computation.6 | async-start | bytes 3145728 | tf_op jit(solution)/shard_map/all_gather | solution.py:1008
  17.1 500.4 %all-gather.10.cloned.1.call-start = ((), (), s32[]{:S(2)}) async-start(), calls=%async_computation.5 | async-start | bytes 4718592 | tf_op jit(solution)/shard_map/all_gather | solution.py:1008
  280.1 245.9 %copy-start = (bf16[8,4,64,128]{3,2,1,0:T(8,128)(2,1)}, bf16[8,4,64,128]{3,2,1,0:T(8,128)(2,1)S(1)}, u32[]{:S(2)}) copy-start(bf16[8,4,64,128]{3,2,1,0:T(8,128)(2,1)S(1)} %get-tuple-element.64) | copy-start | bytes 1572868
  281.8 259.2 %all-gather.14.cloned.1.call-start = ((), (), s32[]{:S(2)}) async-start(), calls=%async_computation.7 | async-start | bytes 15728640 | tf_op jit(solution)/shard_map/all_gather | solution.py:1028
  285.7 288.4 %all-gather.16.cloned.1.call-start = ((), (), s32[]{:S(2)}) async-start(), calls=%async_computation.8 | async-start | bytes 5242880 | tf_op jit(solution)/shard_map/all_gather | solution.py:1067
  287.2 49.8 %copy-start.26 = (s32[1,2048]{1,0:T(1,128)}, s32[1,2048]{1,0:T(1,128)S(1)}, u32[]{:S(2)}) copy-start(s32[1,2048]{1,0:T(1,128)S(1)} %broadcast_in_dim_reshape.5.doc_k_ref) | copy-start | bytes 24580
  287.4 49.5 %copy-start.17 = (s32[2048,1]{1,0:T(8,128)}, s32[2048,1]{1,0:T(8,128)S(1)}, u32[]{:S(2)}) copy-start(s32[2048,1]{1,0:T(8,128)S(1)} %broadcast_in_dim_reshape.6.doc_q_ref) | copy-start | bytes 24580
  291.1 127.1 %copy-start.53 = (f32[2048,1]{0,1:T(1,128)}, f32[2048,1]{0,1:T(1,128)S(1)}, u32[]{:S(2)}) copy-start(f32[2048,1]{0,1:T(1,128)S(1)} %copy.194) | copy-start | bytes 24580
  360.0 58.1 %copy-start.13 = (bf16[2048,256]{1,0:T(8,128)(2,1)}, bf16[2048,256]{1,0:T(8,128)(2,1)S(1)}, u32[]{:S(2)}) copy-start(bf16[2048,256]{1,0:T(8,128)(2,1)S(1)} %get-tuple-element.66.refs_0_) | copy-start | bytes 3145732
  418.2 101.0 %copy-start.39 = (s32[8,4,64,108]{3,2,1,0:T(8,128)S(1)}, s32[8,4,64,108]{3,2,1,0:T(8,128)}, u32[]{:S(2)}) copy-start(s32[8,4,64,108]{3,2,1,0:T(8,128)} %copy-done.38) | copy-start | bytes 2654212
  519.1 166.7 %all-gather.18.cloned.1.call-start = ((), (), s32[]{:S(2)}) async-start(), calls=%async_computation.9 | async-start | bytes 15728640 | tf_op jit(solution)/shard_map/all_gather | solution.py:1028
  534.8 258.4 %reduce-scatter.7.cloned.1.call-start = ((), (), s32[]{:S(2)}) async-start(), calls=%async_computation.11 | async-start | bytes 5242880 | tf_op jit(solution)/shard_map/reduce_scatter | solution.py:1122
  660.0 151.7 %reduce-scatter.5.cloned.1.call-start = ((), (), s32[]{:S(2)}) async-start(), calls=%async_computation.10 | async-start | bytes 10485760 | tf_op jit(solution)/shard_map/reduce_scatter | solution.py:1122
  660.8 334.4 %reduce-scatter.11.cloned.1.call-start = ((), (), s32[]{:S(2)}) async-start(), calls=%async_computation.13 | async-start | bytes 5242880 | tf_op jit(solution)/shard_map/reduce_scatter | solution.py:1122
  685.8 59.8 %slice-start.2 = ((s8[8388608]{0:T(1024)(128)(4,1)}), s8[4194304]{0:T(1024)(128)(4,1)S(1)}, s32[]{:S(2)}) async-start(s8[8388608]{0:T(1024)(128)(4,1)} %bitcast.179), calls=%async_computation.17 | async-start | bytes 8388608
  811.8 183.4 %reduce-scatter.9.cloned.1.call-start = ((), (), s32[]{:S(2)}) async-start(), calls=%async_computation.12 | async-start | bytes 10485760 | tf_op jit(solution)/shard_map/reduce_scatter | solution.py:1122
  812.4 397.9 %all-gather.20.cloned.1.call-start = ((), (), s32[]{:S(2)}) async-start(), calls=%async_computation.14 | async-start | bytes 9437184 | tf_op jit(solution)/shard_map/all_gather | solution.py:1170
  871.4 123.7 %collective-permute-start = (bf16[256,3072]{1,0:T(8,128)(2,1)}, bf16[256,3072]{1,0:T(8,128)(2,1)}, u32[]{:S(2)}, u32[]{:S(2)}) collective-permute-start(bf16[256,3072]{1,0:T(8,128)(2,1)} %pad_maximum_fusion.21), channel_id=1, source_target_pairs={{0,16},{4,20},{8,24},{12,28},{16,0},{20,4},{24,8},{28,12},{1,17},{... | collective-permute-start | bytes 4718600 | tf_op jit(solution)/shard_map/ppermute | solution.py:1005
  877.2 113.3 %copy-start.1 = (bf16[8,4,64,128]{3,2,1,0:T(8,128)(2,1)S(1)}, bf16[8,4,64,128]{3,2,1,0:T(8,128)(2,1)}, u32[]{:S(2)}) copy-start(bf16[8,4,64,128]{3,2,1,0:T(8,128)(2,1)} %copy-done) | copy-start | bytes 1572868
  877.2 113.3 %copy-start.32 = (f32[256,2048]{1,0:T(8,128)S(1)}, f32[256,2048]{1,0:T(8,128)}, u32[]{:S(2)}) copy-start(f32[256,2048]{1,0:T(8,128)} %copy-done.31) | copy-start | bytes 6291460
  877.2 113.3 %copy-start.54 = (f32[2048,1]{0,1:T(1,128)S(1)}, f32[2048,1]{0,1:T(1,128)}, u32[]{:S(2)}) copy-start(f32[2048,1]{0,1:T(1,128)} %copy-done.53) | copy-start | bytes 24580
  877.2 113.3 %copy-start.65 = (f32[256]{0:T(256)S(1)}, f32[256]{0:T(256)}, u32[]{:S(2)}) copy-start(f32[256]{0:T(256)} %copy-done.64) | copy-start | bytes 3076
  1120.4 71.7 %collective-permute-start.1 = (bf16[256,3072]{1,0:T(8,128)(2,1)}, bf16[256,3072]{1,0:T(8,128)(2,1)}, u32[]{:S(2)}, u32[]{:S(2)}) collective-permute-start(bf16[256,3072]{1,0:T(8,128)(2,1)} %pad_maximum_fusion.22), channel_id=1, source_target_pairs={{0,16},{4,20},{8,24},{12,28},{16,0},{20,4},{24,8},{28,12},{1,17},{... | collective-permute-start | bytes 4718600 | tf_op jit(solution)/shard_map/ppermute | solution.py:1005
  (80 other events, 897.3 us)
Sparse Core Ops, SparseCore 0:
  16.5 122.2 all-gather.7
  140.4 73.4 all-gather.11
  282.0 80.4 all-gather.9
  364.4 140.7 all-gather.13
  519.2 53.2 all-gather.15
  573.9 111.8 all-gather.17
  688.1 44.5 reduce-scatter.6
  735.2 76.4 reduce-scatter.4
  814.1 42.8 reduce-scatter.10
  859.2 133.0 reduce-scatter.8
  995.3 101.8 all-gather.19

commit v6 on v5

--- a/solution.py
+++ b/solution.py
@@ -503,9 +503,9 @@
 
 
 def start_kernel(
-    x, w, w_query, w_key, w_value, small, x_all, w_all, heads_all, small_all,
+    x, w, w_query, w_key, w_value, small, cot, x_all, w_all, heads_all, small_all, cot_peer,
     heads_mid, small_mid, own_sem, ex_send, ex_recv, sp_send, sp_recv, w_send, w_recv, f_send,
-    f_recv, *line_sems,
+    f_recv, pair_send, pair_recv, *line_sems,
 ):
     shard, ctx = lax.axis_index("shard"), lax.axis_index("ctx")
     n_ctx = lax.axis_size("ctx")
@@ -558,6 +558,8 @@
         one.start()
     for k in range(1, at.n):
         line.hop(k)
+    across = Pair().copy(cot, cot_peer, pair_send, pair_recv)
+    across.start()
 
     to, origin = ring_peers("shard")
 
@@ -595,6 +597,7 @@
         row(k, p, shard).wait_send()
         forward(k, p, at.core).wait_send()
         forward(k, p, 1 - at.core).wait_recv()
+    across.wait()
     for direct in spreads:
         direct.wait_recv()
     for direct in (*swaps, *spreads):
@@ -771,21 +774,22 @@
 
 
 def end_kernel(
-    x, wide, out, y, x_sum, wide_all, out_sum, y_sum, wide_buf, out_buf, wide_sum,
-    own_sem, wide_send, wide_recv, out_send, out_recv, swap_send, swap_recv, *rest,
+    x, wide, out, y, x_sum, wide_all, out_sum, y_peer, wide_buf, out_buf, wide_sum,
+    own_sem, wide_send, wide_recv, out_send, out_recv, swap_send, swap_recv, pair_send, pair_recv,
+    *line_refs,
 ):
     ctx = lax.axis_index("ctx")
     Greeting().ring("ctx").ring("shard").wait()
     wides = Direct("shard", block_of(wide), buffer_of(wide_buf), wide_send, wide_recv)
     outs = Direct("shard", block_of(out), buffer_of(out_buf), out_send, out_recv)
     swap = Direct("ctx", block_of(wide_sum), block_from(wide_all), swap_send, swap_recv)
-    line = LineReduce(LINE_CHUNKS, x, x_sum, *rest[7:])
-    returns = PairReduce(y, y_sum, *rest[:7])
+    line = LineReduce(LINE_CHUNKS, x, x_sum, *line_refs)
     line.start()
     wides.start()
-    returns.start()
     outs.start()
     line.pass_on()
+    across = Pair().copy(y, y_peer, pair_send, pair_recv)
+    across.start()
     wides.wait_recv()
     for b in range(lax.axis_size("ctx")):
         rows = wide_sum.shape[1]
@@ -796,12 +800,11 @@
     swap.start()
     own = pltpu.make_async_copy(wide_sum.at[ctx], wide_all.at[ctx], own_sem)
     own.start()
-    line.finish()
-    returns.turn()
     outs.wait_recv()
     add_up(out, out_buf, out_sum, outs.me)
-    returns.finish()
+    line.finish()
     own.wait()
+    across.wait()
     swap.wait_recv()
     for direct in (swap, wides, outs):
         direct.wait_send()
@@ -816,7 +819,7 @@
 LINE_CHUNKS = 4
 
 
-def start_call(collective_id, x, w, w_query, w_key, w_value, small):
+def start_call(collective_id, x, w, w_query, w_key, w_value, small, cot):
     n_ctx, n_shard = lax.axis_size("ctx"), lax.axis_size("shard")
     n = n_ctx // 2
     heads = (w.shape[0], 3 * w.shape[1] // n_ctx)
@@ -828,9 +831,10 @@
             jax.ShapeDtypeStruct((n_ctx, n_shard, *w.shape), bf16),
             jax.ShapeDtypeStruct((n_ctx, n_shard, *heads), bf16),
             jax.ShapeDtypeStruct((n_ctx, n_shard, *small.shape), bf16),
+            jax.ShapeDtypeStruct(cot.shape, bf16),
         ],
-        in_specs=[ANY] * 6,
-        out_specs=[ANY] * 4,
+        in_specs=[ANY] * 7,
+        out_specs=[ANY] * 5,
         scratch_shapes=[
             pltpu.VMEM((n_ctx, *heads), bf16),
             pltpu.VMEM((n_ctx, *small.shape), bf16),
@@ -840,9 +844,10 @@
         ]
         + [sem((2, n_shard))] * 2
         + [sem((n_shard, n))] * 4
+        + [sem, sem]
         + line_gather_scratch(n, LINE_CHUNKS + 1),
         compiler_params=remote_params(collective_id, 8),
-    )(x, w, w_query, w_key, w_value, small)
+    )(x, w, w_query, w_key, w_value, small, cot)
 
 
 def exchange(collective_id, x, to_rows, *more):
@@ -913,10 +918,10 @@
             jax.ShapeDtypeStruct((rows, width), f32),
             jax.ShapeDtypeStruct((n_ctx, wide_rows, wide_cols), bf16),
             jax.ShapeDtypeStruct(out.shape[1:], f32),
-            jax.ShapeDtypeStruct(y.shape[2:], f32),
+            jax.ShapeDtypeStruct(y.shape, y.dtype),
         ],
-        in_specs=[VMEM] * 4,
-        out_specs=[VMEM] * 4,
+        in_specs=[VMEM] * 3 + [ANY],
+        out_specs=[VMEM] * 3 + [ANY],
         scratch_shapes=[
             pltpu.VMEM((n_shard - 1, *wide.shape[1:]), bf16),
             pltpu.VMEM((n_shard - 1, *out.shape[1:]), bf16),
@@ -925,7 +930,7 @@
         ]
         + [sem((n_shard,))] * 4
         + [sem((n_ctx,))] * 2
-        + pair_reduce_scratch(n_shard, y)
+        + [sem, sem]
         + [pltpu.VMEM((n, rows, width), bf16)] * 3
         + [sem((n, LINE_CHUNKS))] * 5,
         compiler_params=remote_params(collective_id, 56),
@@ -976,8 +981,8 @@
         axis=1,
     )
     grad_own = cotangent[0]
-    x_all, out_w, weights, small_all = start_call(
-        1, x_own, w_out, w_query, w_key, w_value, small
+    x_all, out_w, weights, small_all, grad_theirs = start_call(
+        1, x_own, w_out, w_query, w_key, w_value, small, grad_own
     )
     x_all = x_all.reshape(count, width)
     out_w = out_w.reshape(width, width)
@@ -1019,10 +1024,8 @@
     keep_w = lax.dynamic_slice_in_dim(own_w, role * half, half, 0)
     give_w = lax.dynamic_slice_in_dim(own_w, (1 - role) * half, half, 0)
     spans = [list(range(r * span, (r + 1) * span)) for r in (0, 1)]
-    grad_theirs = queued_swap(grad_own)
-    first_w = queued_swap(give_w[0])
-    x_all, first_w, later_w = lax.optimization_barrier((x_all, first_w, give_w[1:]))
-    early = [first_w] + [queued_swap(later_w[e]) for e in range(half - 1)]
+    x_all, give_w = lax.optimization_barrier((x_all, give_w))
+    early = queued_swap(give_w[0])
 
     def expert_weights(e, theirs):
         return lax.all_gather(
@@ -1033,8 +1036,6 @@
             axis_index_groups=spans,
         ).reshape(width, 3 * ff)
 
-    expert_w = [expert_weights(0, early[0])]
-
     x_wide = x_all.astype(f32)
     inverse_one = inverse_rms(x_wide)
     hidden_one = (x_wide * inverse_one * gain_attn).astype(bf16)
@@ -1052,8 +1053,12 @@
     query = rotate(query_n * gain_query, cosine, sine).astype(bf16)
     key = rotate(key_n * gain_key, cosine, sine).astype(bf16)
     mixed, log_total, peaks = attend_forward(query, key, value, docs)
+    mixed, early = lax.optimization_barrier((mixed, early))
+    expert_w = [expert_weights(0, early)]
     x_f = x_own.astype(f32)
     mixed_own, grad_mine = exchange(2, mixed, False, grad_own)
+    mixed_own, give_w = lax.optimization_barrier((mixed_own, give_w))
+    early = [queued_swap(give_w[e]) for e in range(1, half)]
     grad_mine = grad_mine.reshape(n_shard * rows, width)
     after = x_f + dot(mixed_own, out_w)
     inverse_two = inverse_rms(after)
@@ -1061,9 +1066,7 @@
     hidden_two = (normed_two * gain_ffn).astype(bf16)
 
     hidden_all, peaks = pair_gather(3, hidden_two, peaks)
-    hidden_all, early, grad_theirs = lax.optimization_barrier(
-        (hidden_all, early[1:], grad_theirs)
-    )
+    hidden_all, early, grad_theirs = lax.optimization_barrier((hidden_all, early, grad_theirs))
     grad_theirs = lax.all_gather(grad_theirs, "shard", axis=0, tiled=True)
     expert_w += [expert_weights(e + 1, u) for e, u in enumerate(early)]
     hidden_all = hidden_all.reshape(2 * n_shard * rows, width)
@@ -1169,7 +1172,6 @@
     )
     grad_attn = lax.all_gather(to_gather, "ctx", axis=0, tiled=True)
     (grad_mixed,) = exchange(5, contract_cols(grad_attn_own, out_w).astype(bf16), True)
-    grad_out_w = contract_rows(mixed, grad_attn)
     grad_query_rot, grad_key_rot, grad_value = attend_backward(
         query, key, value, docs, log_total, grad_mixed
     )
@@ -1183,16 +1185,18 @@
         [jnp.sum(scaled_q * query_n, axis=1), jnp.sum(scaled_k * key_n, axis=1), peak_row]
     )
     inner = many_sum("ctx", 7, inner)
-    inner, expert_grads[-1] = lax.optimization_barrier((inner, expert_grads[-1]))
+    inner, expert_grads[-1], moe_part, grad_attn = lax.optimization_barrier(
+        (inner, expert_grads[-1], moe_part, grad_attn)
+    )
+    grad_out_w = contract_rows(mixed, grad_attn)
+    moe_sums = lax.psum_scatter(
+        moe_part.astype(bf16).reshape(2, n_shard * rows, width),
+        "shard",
+        scatter_dimension=1,
+        tiled=True,
+    )
     peers.append(swap(give(expert_grads[-1])))
     kept = [[lax.dynamic_index_in_dim(u, role, 0, False) for u in sums] for sums in expert_grads]
-    peers = [(peer[:, : 2 * ff], peer[:, 2 * ff :]) for peer in peers]
-    both_halves = [
-        in_order(jnp.stack([k[i] for k in kept]), jnp.stack([p[i] for p in peers]))
-        .reshape(local, width // n_ctx, -1)
-        .astype(f32)
-        for i in (0, 1)
-    ]
     peak_all = inner[2, :HEADS]
     inner = inner / width
     grad_linear = jnp.concatenate(
@@ -1225,14 +1229,19 @@
         .astype(bf16)
         .reshape(n_shard, part, width + LANES)
     )
-    grad_hidden_one, grad_weights, grad_out_w, moe_sum = end_call(
-        8,
-        hidden_part.astype(bf16).reshape(n_ctx, rows, width),
-        grad_weights,
-        grad_out_w,
-        moe_part.astype(bf16).reshape(2, n_shard, rows, width),
-    )
-    output = (after + moe_sum).astype(bf16)
+    hidden_part = hidden_part.astype(bf16).reshape(n_ctx, rows, width)
+    hidden_part, peers = lax.optimization_barrier((hidden_part, peers))
+    grad_hidden_one, grad_weights, grad_out_w, moe_peer = end_call(
+        8, hidden_part, grad_weights, grad_out_w, moe_sums[1]
+    )
+    output = (after + (moe_sums[0].astype(f32) + moe_peer.astype(f32))).astype(bf16)
+    peers = [(peer[:, : 2 * ff], peer[:, 2 * ff :]) for peer in peers]
+    both_halves = [
+        in_order(jnp.stack([k[i] for k in kept]), jnp.stack([p[i] for p in peers]))
+        .reshape(local, width // n_ctx, -1)
+        .astype(f32)
+        for i in (0, 1)
+    ]
     grad_weights = grad_weights.astype(f32)
     grad_small = jnp.sum(grad_weights[..., 3 * cols :], axis=0)
     grad_weights = (

time: 1420 us -> 1490 us (1.049)
  waiting for transfers between devices: 75.9 us -> 151 us
  local copies, waits for them, and re-layouts: 90.4 us -> 124 us
  Pallas kernels: 809 us -> 777 us
    pallas_call x1, Pallas kernels: 254 us -> 181 us  [start_call(): pl.pallas_call(start_kernel, out_shape=[jax.ShapeDtypeStruct((n_ctx, *x.s...]
    all_gather x2, waiting for transfers between devices: 25 us -> 77.5 us  [expert_weights(): lax.all_gather(in_order(keep_w[e], theirs), 'ctx', axis=1, tiled=True, ax...]
    pallas_call x1, Pallas kernels: 93.8 us -> 145 us  [pair_gather(): pl.pallas_call(pair_gather_kernel, out_shape=[jax.ShapeDtypeStruct((2, n,...]
    all_gather x1, waiting for transfers between devices: 0.01 us -> 23.1 us  [per_device(): grad_theirs = lax.all_gather(grad_theirs, 'shard', axis=0, tiled=True)]
    unnamed x194 -> x220, local copies, waits for them, and re-layouts: 33.2 us -> 47.4 us
  transfers between devices with their start and end apart: 13 -> 13, of which waited for: 3 -> 5; matrix products, arithmetic and copies ran while one was open for 31% -> 30% of each run, Pallas kernels for 46% -> 27%
where the time goes in v6:
time: 1490 us; the launch traced here: 1480 us
  Pallas kernels  777 us (52%)
  matrix products  298 us (20%)
  waiting for transfers between devices  151 us (10%)
  local copies, waits for them, and re-layouts  124 us (8%)
  other arithmetic  107 us (7%)
  between operations  16.6 us (1%)
    pallas_call x1, Pallas kernels, start_call(): pl.pallas_call(start_kernel, out_shape=[jax.ShapeDtypeStruct((n_ctx, *x.s...  181 us
    pallas_call x1, Pallas kernels, end_call(): pl.pallas_call(end_kernel, out_shape=[jax.ShapeDtypeStruct((rows, width),...  148 us
    pallas_call x1, Pallas kernels, pair_gather(): pl.pallas_call(pair_gather_kernel, out_shape=[jax.ShapeDtypeStruct((2, n,...  145 us
    pallas_call x1, Pallas kernels, pair_reduce(): pl.pallas_call(functools.partial(pair_reduce_kernel, len(arrays)), out_sh...  115 us
    dot_general x7, matrix products, dot(): return jnp.dot(a, b, preferred_element_type=f32)  111 us
    dot_general x7, matrix products, contract_cols(): lax.dot_general(a, b, (((1,), (1,)), ((), ())), preferred_element_type=f32)  104 us
    pallas_call x2, Pallas kernels, exchange(): pl.pallas_call(functools.partial(exchange_kernel, to_rows), out_shape=[ja...  87.8 us
    dot_general x7, matrix products, contract_rows(): lax.dot_general(a, b, (((0,), (0,)), ((), ())), preferred_element_type=f32)  83 us
  transfers between devices with their start and end apart: 13, of which 5 were waited for; matrix products, arithmetic and copies ran while one was open for 30% of the time, Pallas kernels for 27%

profile of v6, /device:TPU:0, one launch (start us, length us, event | category | flops | bytes accessed | tf_op | source)
XLA Modules:
  0.0 1478.9 jit_solution(13433665972664653952)
XLA Ops:
  24.2 181.0 %shard_map.296 = (bf16[8,256,2048]{2,1,0:T(8,128)(2,1)S(1)}, bf16[8,4,64,2048]{3,2,1,0:T(8,128)(2,1)S(1)}, bf16[8,4,64,768]{3,2,1,0:T(8,128)(2,1)S(1)}, bf16[8,4...) custom-call(bf16[256,2048]{1,0:T(8,128)(2,1)S(1)} %bitcast.187, bf16[64,2048]{1,0:T(8,128)(2,1)S(1)} %copy-done.22, ...), custom_call_target="tpu_custom_call" | custom-call | tf_op jit(solution)/shard_map/pallas_call | solution.py:827
  271.6 23.0 %shard_map.298 = (bf16[2048,256]{1,0:T(8,128)(2,1)S(1)}, f32[2,2048,1]{2,1,0:T(8,128)}, f32[2,8,128]{2,1,0:T(8,128)S(1)}) custom-call(bf16[2048,256]{1,0:T(8,128)(2,1)S(1)} %pad_maximum_fusion.26.q_ref, bf16[2048,256]{1,0:T(8,128)(2,1)S(1)} %pad_maximum_fusion.27.k_ref, bf16[2048,256]{1,0:T(8,128)(2,1)S(1)} %copy-done.16, s32[2048,1]{1,0:T(8,128)S(1)} %copy-done.15, ...), custom_call_target="tpu_custom_call" | custom-call | flops 4294967296 | bytes 4194304 | tf_op jit(solution)/shard_map/pallas_call | solution.py:111
  300.6 50.1 %shard_map.299 = (bf16[256,2048]{1,0:T(8,128)(2,1)S(1)}, bf16[4,256,2048]{2,1,0:T(8,128)(2,1)S(1)}) custom-call(bf16[2048,256]{1,0:T(8,128)(2,1)S(1)} %copy-done.11, bf16[256,2048]{1,0:T(8,128)(2,1)S(1)} %bitcast.189), custom_call_target="tpu_custom_call" | custom-call | tf_op jit(solution)/shard_map/pallas_call | solution.py:857
  370.6 145.4 %shard_map.300 = (bf16[2,4,256,2048]{3,2,1,0:T(8,128)(2,1)S(1)}, f32[4,2,8,128]{3,2,1,0:T(8,128)S(1)}) custom-call(bf16[256,2048]{1,0:T(8,128)(2,1)S(1)} %multiply_convert_fusion.8.x, f32[2,8,128]{2,1,0:T(8,128)S(1)} %get-tuple-element.82.peaks), custom_call_target="tpu_custom_call" | custom-call | tf_op jit(solution)/shard_map/pallas_call | solution.py:871
  543.8 48.0 %all-gather.11.cloned.1.call-done = bf16[2,1024,3072]{2,1,0:T(8,128)(2,1)} async-done(((bf16[2,256,3072]{2,1,0:T(8,128)(2,1)}), bf16[2,1024,3072]{2,1,0:T(8,128)(2,1)}) %all-gather.11.cloned.1.call-update) | async-done | bytes 12582928 | tf_op jit(solution)/shard_map/all_gather | solution.py:1031
  591.7 24.4 %fusion.19 = f32[2048,2048]{0,1:T(8,128)} fusion(bf16[2048,2048]{1,0:T(8,128)(2,1)} %bitcast.179, bf16[2048,3072]{1,0:T(8,128)(2,1)} %bitcast.274), kind=kOutput, calls=%fused_computation.48 | convolution fusion | flops 17179869184 | bytes 33554432 | tf_op jit(solution)/shard_map/dot_general | solution.py:23
  624.8 23.1 %all-gather.13.cloned.1.call-done = bf16[1024,2048]{1,0:T(8,128)(2,1)} async-done(((bf16[256,2048]{1,0:T(8,128)(2,1)}), bf16[1024,2048]{1,0:T(8,128)(2,1)}) %all-gather.13.cloned.1.call-update) | async-done | bytes 4194320 | tf_op jit(solution)/shard_map/all_gather | solution.py:1070
  666.3 19.2 %multiply_convert_fusion.4 = (bf16[2048,1024]{0,1:T(8,128)(2,1)}, bf16[2048,1024]{0,1:T(8,128)(2,1)}) fusion(f32[2048,2048]{0,1:T(8,128)} %fusion.19, bf16[2048,3072]{1,0:T(8,128)(2,1)} %bitcast.275, bf16[1024,2048]{1,0:T(8,128)(2,1)} %copy-done.60, bf16[1024,2048]{1,0:T(8,128)(2,1)S(1)} %copy-done.59), kind=kOutput, calls=%fused_computation.38 | convolution fusion | flops 8633974784 | bytes 37748736 | tf_op jit(solution)/shard_map/dot_general | solution.py:23
  685.5 22.1 %convolution_convert_fusion.1 = bf16[2048,2048]{1,0:T(8,128)(2,1)} fusion(bf16[2048,2048]{1,0:T(8,128)(2,1)S(1)} %bitcast.183, bf16[2048,1024]{0,1:T(8,128)(2,1)} %get-tuple-element.199, bf16[2048,1024]{0,1:T(8,128)(2,1)} %get-tuple-element.198), kind=kOutput, calls=%fused_computation.43 | convolution fusion | flops 17200840704 | bytes 25165824 | tf_op jit(solution)/shard_map/dot_general | solution.py:27
  707.6 23.2 %convert_convert_fusion.2 = f32[2048,2048]{1,0:T(8,128)} fusion(bf16[2048,3072]{1,0:T(8,128)(2,1)} %bitcast.276, bf16[2048,1024]{0,1:T(8,128)(2,1)} %get-tuple-element.199, bf16[2048,1024]{0,1:T(8,128)(2,1)S(1)} %copy-done.90), kind=kOutput, calls=%fused_computation.36 | convolution fusion | flops 17205035008 | bytes 33554432 | tf_op jit(solution)/shard_map/dot_general | solution.py:31
  731.7 29.5 %all-gather.15.cloned.1.call-done = bf16[2,1024,3072]{2,1,0:T(8,128)(2,1)} async-done(((bf16[2,256,3072]{2,1,0:T(8,128)(2,1)}), bf16[2,1024,3072]{2,1,0:T(8,128)(2,1)}) %all-gather.15.cloned.1.call-update) | async-done | bytes 12582928 | tf_op jit(solution)/shard_map/all_gather | solution.py:1031
  761.2 24.7 %fusion.16 = f32[2048,2048]{0,1:T(8,128)} fusion(bf16[2048,2048]{1,0:T(8,128)(2,1)} %bitcast.180, bf16[2048,3072]{1,0:T(8,128)(2,1)} %bitcast.278), kind=kOutput, calls=%fused_computation.45 | convolution fusion | flops 17179869184 | bytes 33554432 | tf_op jit(solution)/shard_map/dot_general | solution.py:23
  785.9 20.1 %multiply_convert_fusion.2 = (bf16[2048,1024]{0,1:T(8,128)(2,1)}, bf16[2048,1024]{0,1:T(8,128)(2,1)}, bf16[2048,1024]{0,1:T(8,128)(2,1)}) fusion(f32[2048,2048]{0,1:T(8,128)} %fusion.16, bf16[2048,3072]{1,0:T(8,128)(2,1)} %bitcast.279, bf16[1024,2048]{1,0:T(8,128)(2,1)} %get-tuple-element.215, bf16[1024,2048]{1,0:T(8,128)(2,1)S(1)} %copy-done.58), kind=kOutput, calls=%fused_computation.33 | convolution fusion | flops 8638169088 | bytes 41943040 | tf_op jit(solution)/shard_map/dot_general | solution.py:23
  819.8 22.1 %convolution_convert_fusion = bf16[2048,2048]{1,0:T(8,128)(2,1)} fusion(bf16[2048,2048]{1,0:T(8,128)(2,1)S(1)} %bitcast.186, bf16[2048,1024]{0,1:T(8,128)(2,1)} %get-tuple-element.197, bf16[2048,1024]{0,1:T(8,128)(2,1)} %get-tuple-element.196), kind=kOutput, calls=%fused_computation.42 | convolution fusion | flops 17200840704 | bytes 25165824 | tf_op jit(solution)/shard_map/dot_general | solution.py:27
  841.9 25.0 %convert_add_fusion = bf16[2048,2048]{1,0:T(8,128)(2,1)} fusion(f32[2048,2048]{1,0:T(8,128)} %convert_convert_fusion.2, bf16[2048,3072]{1,0:T(8,128)(2,1)} %bitcast.280, bf16[2048,1024]{0,1:T(8,128)(2,1)} %get-tuple-element.197, bf16[2048,1024]{0,1:T(8,128)(2,1)S(1)} %copy-done.91), kind=kOutput, calls=%fused_computation.8 | convolution fusion | flops 17213423616 | bytes 41943040 | tf_op jit(solution)/shard_map/dot_general | solution.py:31
  866.9 20.1 %reduce-scatter.6.cloned.1.call-done = bf16[2,256,2048]{2,1,0:T(8,128)(2,1)} async-done(((bf16[2,1024,2048]{2,1,0:T(8,128)(2,1)}), bf16[2,256,2048]{2,1,0:T(8,128)(2,1)}) %reduce-scatter.6.cloned.1.call-update) | async-done | bytes 2097168 | tf_op jit(solution)/shard_map/reduce_scatter | solution.py:1125
  905.1 20.6 %multiply_add_fusion = (bf16[2048,2048]{1,0:T(8,128)(2,1)}, f32[2048,2048]{1,0:T(8,128)}) fusion(f32[2048,2048]{1,0:T(8,128)} %convert_convert_fusion.1, f32[2048]{0:T(1024)S(1)} %bitcast.268, f32[2048]{0:T(1024)S(1)} %bitcast.267, bf16[2048,1024]{0,1:T(8,128)(2,1)} %get-tuple-element.202, bf16[2048,3072]{1,0:T(8,128)(2,1)} %bitcast.281), kind=kOutput, calls=%fused_computation.7 | convolution fusion | flops 8615100416 | bytes 50348032 | tf_op jit(solution)/shard_map/dot_general | solution.py:31
  925.8 15.8 %fusion.12 = (f32[1024]{0:T(1024)S(1)}, f32[1024]{0:T(1024)S(1)}, f32[1024]{0:T(1024)S(1)}, f32[1024]{0:T(1024)S(1)}) fusion(f32[2048,2048]{1,0:T(8,128)} %get-tuple-element.280, bf16[4,256,2048]{2,1,0:T(8,128)(2,1)} %copy-done.6, bf16[1024,2048]{1,0:T(8,128)(2,1)} %all-gather.13.cloned.1.call-done, f32[2048,2048]{1,0:T(8,128)} %convert_convert_fusion.1), kind=kLoop, calls=%fused_computation.24 | loop fusion | flops 20967424 | bytes 41959424 | tf_op jit(solution)/shard_map/reduce_sum | solution.py:1108
  950.2 114.7 %shard_map.301 = (f32[256,2048]{1,0:T(8,128)S(1)}, f32[16,256]{1,0:T(8,128)S(1)}) custom-call(bf16[2,4,256,2048]{3,2,1,0:T(8,128)(2,1)S(1)} %bitcast.198, f32[2,4,16,256]{3,2,1,0:T(8,128)S(1)} %fusion.113.refs_1_), custom_call_target="tpu_custom_call" | custom-call | tf_op jit(solution)/shard_map/pallas_call | solution.py:886
  1077.6 37.7 %shard_map.302.do_ref = bf16[2048,256]{1,0:T(8,128)(2,1)S(1)} custom-call(bf16[256,2048]{1,0:T(8,128)(2,1)S(1)} %convolution_convert_fusion.4.refs_0_), custom_call_target="tpu_custom_call" | custom-call | tf_op jit(solution)/shard_map/pallas_call | solution.py:857
  1116.3 37.6 %shard_map.303 = (f32[2048,256]{1,0:T(8,128)}, f32[2048,256]{1,0:T(8,128)}, f32[2048,256]{1,0:T(8,128)}) custom-call(bf16[2048,256]{1,0:T(8,128)(2,1)} %copy-done.14, bf16[2048,256]{1,0:T(8,128)(2,1)} %copy-done.13, bf16[2048,256]{1,0:T(8,128)(2,1)} %slice.474.v_ref, s32[2048,1]{1,0:T(8,128)} %broadcast_in_dim_reshape.6.doc_q_ref, s32[1,2048]{1,0:T(1,128)} %copy-done.24, ...), custom_call_target="tpu_custom_call" | custom-call | flops 10737418240 | bytes 10485760 | tf_op jit(solution)/shard_map/pallas_call | solution.py:134
  1166.1 25.2 %shard_map.304 = f32[3,2048]{1,0:T(4,128)S(1)} custom-call(f32[3,2048]{1,0:T(4,128)S(1)} %pad_maximum_fusion.29.x), custom_call_target="tpu_custom_call" | custom-call | tf_op jit(solution)/shard_map/pallas_call | solution.py:899
  1246.7 28.7 %collective-permute-done.1 = bf16[256,3072]{1,0:T(8,128)(2,1)} collective-permute-done((bf16[256,3072]{1,0:T(8,128)(2,1)}, bf16[256,3072]{1,0:T(8,128)(2,1)}, u32[]{:S(2)}, u32[]{:S(2)}) %collective-permute-start.1) | collective-permute-done | bytes 1572896 | tf_op jit(solution)/shard_map/ppermute | solution.py:1010
  1297.2 148.3 %shard_map.305 = (f32[256,2048]{1,0:T(8,128)}, bf16[8,64,896]{2,1,0:T(8,128)(2,1)}, f32[64,2176]{1,0:T(8,128)}, bf16[256,2048]{1,0:T(8,128)(2,1)}) custom-call(bf16[8,256,2048]{2,1,0:T(8,128)(2,1)} %bitcast.208, bf16[4,512,896]{2,1,0:T(8,128)(2,1)} %bitcast.207, bf16[4,64,2176]{2,1,0:T(8,128)(2,1)} %pad_maximum_fusion.25.out, ...), custom_call_target="tpu_custom_call" | custom-call | tf_op jit(solution)/shard_map/pallas_call | solution.py:915
  (399 shorter events, 332.7 us)
Async XLA Ops:
  7.2 289.4 %all-gather.7.cloned.1.call-start = ((), (), s32[]{:S(2)}) async-start(), calls=%async_computation.5 | async-start | bytes 4718592 | tf_op jit(solution)/shard_map/all_gather | solution.py:1013
  24.2 189.2 %copy-start.33 = (bf16[2,256,3072]{2,1,0:T(8,128)(2,1)S(1)}, bf16[2,256,3072]{2,1,0:T(8,128)(2,1)}, u32[]{:S(2)}) copy-start(bf16[2,256,3072]{2,1,0:T(8,128)(2,1)} %constant_dynamic-slice_fusion.15) | copy-start | bytes 9437188
  213.4 316.5 %copy-start = (bf16[8,4,64,128]{3,2,1,0:T(8,128)(2,1)}, bf16[8,4,64,128]{3,2,1,0:T(8,128)(2,1)S(1)}, u32[]{:S(2)}) copy-start(bf16[8,4,64,128]{3,2,1,0:T(8,128)(2,1)S(1)} %get-tuple-element.73) | copy-start | bytes 1572868
  214.8 305.6 %all-gather.9.cloned.1.call-start = ((), (), s32[]{:S(2)}) async-start(), calls=%async_computation.6 | async-start | bytes 4718592 | tf_op jit(solution)/shard_map/all_gather | solution.py:1013
  296.6 57.2 %copy-start.34 = (bf16[2,256,3072]{2,1,0:T(8,128)(2,1)S(1)}, bf16[2,256,3072]{2,1,0:T(8,128)(2,1)}, u32[]{:S(2)}) copy-start(bf16[2,256,3072]{2,1,0:T(8,128)(2,1)} %constant_dynamic-slice_fusion.15) | copy-start | bytes 9437188
  355.0 236.7 %all-gather.11.cloned.1.call-start = ((), (), s32[]{:S(2)}) async-start(), calls=%async_computation.7 | async-start | bytes 15728640 | tf_op jit(solution)/shard_map/all_gather | solution.py:1031
  360.4 287.6 %all-gather.13.cloned.1.call-start = ((), (), s32[]{:S(2)}) async-start(), calls=%async_computation.8 | async-start | bytes 5242880 | tf_op jit(solution)/shard_map/all_gather | solution.py:1070
  369.3 153.7 %copy-start.54 = (s32[8,4,64,108]{3,2,1,0:T(8,128)S(1)}, s32[8,4,64,108]{3,2,1,0:T(8,128)}, u32[]{:S(2)}) copy-start(s32[8,4,64,108]{3,2,1,0:T(8,128)} %slice_convert_fusion.3) | copy-start | bytes 2654212
  523.0 238.2 %all-gather.15.cloned.1.call-start = ((), (), s32[]{:S(2)}) async-start(), calls=%async_computation.9 | async-start | bytes 15728640 | tf_op jit(solution)/shard_map/all_gather | solution.py:1031
  538.0 328.9 %reduce-scatter.8.cloned.1.call-start = ((), (), s32[]{:S(2)}) async-start(), calls=%async_computation.11 | async-start | bytes 5242880 | tf_op jit(solution)/shard_map/reduce_scatter | solution.py:1125
  730.9 156.1 %reduce-scatter.6.cloned.1.call-start = ((), (), s32[]{:S(2)}) async-start(), calls=%async_computation.10 | async-start | bytes 10485760 | tf_op jit(solution)/shard_map/reduce_scatter | solution.py:1125
  731.6 339.4 %reduce-scatter.12.cloned.1.call-start = ((), (), s32[]{:S(2)}) async-start(), calls=%async_computation.13 | async-start | bytes 5242880 | tf_op jit(solution)/shard_map/reduce_scatter | solution.py:1125
  761.2 58.5 %slice-start.2 = ((s8[8388608]{0:T(1024)(128)(4,1)}), s8[4194304]{0:T(1024)(128)(4,1)S(1)}, s32[]{:S(2)}) async-start(s8[8388608]{0:T(1024)(128)(4,1)} %bitcast.184), calls=%async_computation.18 | async-start | bytes 8388608
  887.0 184.0 %reduce-scatter.10.cloned.1.call-start = ((), (), s32[]{:S(2)}) async-start(), calls=%async_computation.12 | async-start | bytes 10485760 | tf_op jit(solution)/shard_map/reduce_scatter | solution.py:1125
  887.8 303.6 %all-gather.17.cloned.1.call-start = ((), (), s32[]{:S(2)}) async-start(), calls=%async_computation.14 | async-start | bytes 9437184 | tf_op jit(solution)/shard_map/all_gather | solution.py:1173
  947.6 123.4 %collective-permute-start = (bf16[256,3072]{1,0:T(8,128)(2,1)}, bf16[256,3072]{1,0:T(8,128)(2,1)}, u32[]{:S(2)}, u32[]{:S(2)}) collective-permute-start(bf16[256,3072]{1,0:T(8,128)(2,1)} %pad_maximum_fusion.21), channel_id=1, source_target_pairs={{0,16},{4,20},{8,24},{12,28},{16,0},{20,4},{24,8},{28,12},{1,17},{... | collective-permute-start | bytes 4718600 | tf_op jit(solution)/shard_map/ppermute | solution.py:1010
  950.1 116.2 %copy-start.1 = (bf16[8,4,64,128]{3,2,1,0:T(8,128)(2,1)S(1)}, bf16[8,4,64,128]{3,2,1,0:T(8,128)(2,1)}, u32[]{:S(2)}) copy-start(bf16[8,4,64,128]{3,2,1,0:T(8,128)(2,1)} %copy-done) | copy-start | bytes 1572868
  950.1 116.2 %copy-start.30 = (f32[256,2048]{1,0:T(8,128)S(1)}, f32[256,2048]{1,0:T(8,128)}, u32[]{:S(2)}) copy-start(f32[256,2048]{1,0:T(8,128)} %copy-done.29) | copy-start | bytes 6291460
  950.1 116.2 %copy-start.69 = (f32[2048,1]{0,1:T(1,128)S(1)}, f32[2048,1]{0,1:T(1,128)}, u32[]{:S(2)}) copy-start(f32[2048,1]{0,1:T(1,128)} %copy-done.68) | copy-start | bytes 24580
  950.2 116.2 %copy-start.80 = (f32[256]{0:T(256)S(1)}, f32[256]{0:T(256)}, u32[]{:S(2)}) copy-start(f32[256]{0:T(256)} %copy-done.79) | copy-start | bytes 3076
  1071.0 223.9 %reduce-scatter.14.cloned.1.call-start = ((), (), s32[]{:S(2)}) async-start(), calls=%async_computation.15 | async-start | bytes 10485760 | tf_op jit(solution)/shard_map/reduce_scatter | solution.py:1192
  1071.4 91.2 %slice-start.8 = ((s8[6291456]{0:T(1024)(128)(4,1)}), s8[4194304]{0:T(1024)(128)(4,1)S(1)}, s32[]{:S(2)}) async-start(s8[6291456]{0:T(1024)(128)(4,1)} %bitcast.203), calls=%async_computation.24 | async-start | bytes 8388608
  1116.3 46.3 %slice-start.9 = ((s8[6291456]{0:T(1024)(128)(4,1)}), s8[2097152]{0:T(1024)(128)(4,1)S(1)}, s32[]{:S(2)}) async-start(s8[6291456]{0:T(1024)(128)(4,1)} %bitcast.203), calls=%async_computation.25 | async-start | bytes 4194304
  1203.8 71.7 %collective-permute-start.1 = (bf16[256,3072]{1,0:T(8,128)(2,1)}, bf16[256,3072]{1,0:T(8,128)(2,1)}, u32[]{:S(2)}, u32[]{:S(2)}) collective-permute-start(bf16[256,3072]{1,0:T(8,128)(2,1)} %pad_maximum_fusion.22), channel_id=1, source_target_pairs={{0,16},{4,20},{8,24},{12,28},{16,0},{20,4},{24,8},{28,12},{1,17},{... | collective-permute-start | bytes 4718600 | tf_op jit(solution)/shard_map/ppermute | solution.py:1010
  (93 other events, 716.8 us)
Sparse Core Ops, SparseCore 0:
  214.9 80.0 all-gather.6
  355.1 123.4 all-gather.8
  480.8 110.8 all-gather.10
  593.4 54.4 all-gather.12
  649.3 111.8 all-gather.14
  763.4 44.5 reduce-scatter.7
  810.5 76.4 reduce-scatter.5
  889.4 42.8 reduce-scatter.11
  934.6 133.0 reduce-scatter.9
  1071.2 102.6 all-gather.16
  1191.5 88.3 reduce-scatter.13

commit v7 on v5

--- a/solution.py
+++ b/solution.py
@@ -186,13 +186,6 @@
             self.total = self.total + there.astype(jnp.int32)
         return self
 
-    def pair(self):
-        pl.semaphore_signal(
-            self.barrier, inc=1, device_id={"ctx": Pair().peer}, device_id_type=MESH
-        )
-        self.total = self.total + 1
-        return self
-
     def wait(self):
         pl.semaphore_wait(self.barrier, self.total)
 
@@ -503,7 +496,7 @@
 
 
 def start_kernel(
-    x, w, w_query, w_key, w_value, small, x_all, w_all, heads_all, small_all,
+    x, w, w_query, w_key, w_value, small, cot, x_all, w_all, heads_all, small_all, cot_all,
     heads_mid, small_mid, own_sem, ex_send, ex_recv, sp_send, sp_recv, w_send, w_recv, f_send,
     f_recv, *line_sems,
 ):
@@ -533,9 +526,10 @@
         Direct("shard", whole_of(heads_mid), by_shard(heads_all), sp_send.at[0], sp_recv.at[0]),
         Direct("shard", whole_of(small_mid), by_shard(small_all), sp_send.at[1], sp_recv.at[1]),
     ]
-    pieces = row_pieces(x, x_all, LINE_CHUNKS) + [(w, lambda b: w_all.at[b, shard])]
-    line = LineGather(pieces, *line_sems)
-    at = line.line
+    other = Direct("shard", whole_of(cot), block_from(cot_all), sp_send.at[2], sp_recv.at[2])
+    rows_w = LineGather([(w, lambda b: w_all.at[b, shard])], *line_sems[:7])
+    rows_x = LineGather(row_pieces(x, x_all, LINE_CHUNKS), *line_sems[7:])
+    at = rows_x.line
     own = [
         pltpu.make_async_copy(source(ctx), place(i)(ctx, 0), own_sem.at[i])
         for i, source in enumerate(sources)
@@ -543,13 +537,17 @@
     later = [
         pltpu.make_async_copy(heads_mid, heads_all.at[:, shard], own_sem.at[4]),
         pltpu.make_async_copy(small_mid, small_all.at[:, shard], own_sem.at[5]),
+        pltpu.make_async_copy(cot, cot_all.at[shard], own_sem.at[6]),
     ]
+    other.start()
     for swap in swaps:
         swap.start()
     for copy in own:
         copy.start()
-    line.start()
-    line.hop(0)
+    rows_w.start()
+    rows_w.hop(0)
+    rows_x.start()
+    rows_x.hop(0)
     for swap in swaps:
         swap.wait_recv()
     for copy in own:
@@ -557,7 +555,7 @@
     for one in (*spreads, *later):
         one.start()
     for k in range(1, at.n):
-        line.hop(k)
+        rows_w.hop(k)
 
     to, origin = ring_peers("shard")
 
@@ -584,20 +582,23 @@
         )
 
     some = [(k, p) for k in range(1, len(to)) for p in range(at.n)]
-    line.own(LINE_CHUNKS).wait()
+    rows_w.own(0).wait()
     for k, p in some:
         row(k, p, shard).start()
+    for k in range(1, at.n):
+        rows_x.hop(k)
     for k, p in some:
         row(k, p, origin[k]).wait_recv()
         forward(k, p, at.core).start()
-    line.finish(skip_own=LINE_CHUNKS)
+    rows_w.finish(skip_own=0)
+    rows_x.finish()
     for k, p in some:
         row(k, p, shard).wait_send()
         forward(k, p, at.core).wait_send()
         forward(k, p, 1 - at.core).wait_recv()
-    for direct in spreads:
+    for direct in (other, *spreads):
         direct.wait_recv()
-    for direct in (*swaps, *spreads):
+    for direct in (other, *swaps, *spreads):
         direct.wait_send()
     for copy in later:
         copy.wait()
@@ -641,121 +642,41 @@
         direct.wait_send()
 
 
-class Pair:
-    def __init__(self):
-        ctx, half = lax.axis_index("ctx"), lax.axis_size("ctx") // 2
-        self.role = lax.div(ctx, half)
-        self.peer = ctx + half - 2 * half * self.role
-
-    def copy(self, source, target, send, recv):
-        return pltpu.make_async_remote_copy(
-            src_ref=source,
-            dst_ref=target,
-            send_sem=send,
-            recv_sem=recv,
-            device_id={"ctx": self.peer},
-            device_id_type=MESH,
-        )
-
-
-def pair_gather_kernel(x, peaks, o, peaks_all, own_sem, send, recv, pair_send, pair_recv):
-    shard, pair = lax.axis_index("shard"), Pair()
-    Greeting().ring("shard").pair().wait()
-    own_rows = Direct(
-        "shard", whole_of(x), lambda d, k: o.at[0, d], send.at[0], recv.at[0]
-    )
-    peer_rows = Direct(
-        "shard", lambda d: o.at[1, shard], lambda d, k: o.at[1, d], send.at[1], recv.at[1]
-    )
-    tops = Direct("shard", whole_of(peaks), block_from(peaks_all), send.at[2], recv.at[2])
-    across = pair.copy(x, o.at[1, shard], pair_send, pair_recv)
-    across.start()
-    own_rows.start()
-    tops.start()
-    own = [
-        pltpu.make_async_copy(x, o.at[0, shard], own_sem.at[0]),
-        pltpu.make_async_copy(peaks, peaks_all.at[shard], own_sem.at[1]),
+def gather_kernel(axis, count, *refs):
+    ins, outs = refs[:count], refs[count : 2 * count]
+    own_sem, send, recv = refs[2 * count :]
+    me = lax.axis_index(axis)
+    Greeting().ring(axis).wait()
+    all_of = [
+        Direct(axis, whole_of(ins[i]), block_from(outs[i]), send.at[i], recv.at[i])
+        for i in range(count)
     ]
+    own = [pltpu.make_async_copy(ins[i], outs[i].at[me], own_sem.at[i]) for i in range(count)]
+    for direct in all_of:
+        direct.start()
     for copy in own:
         copy.start()
-    across.wait_recv()
-    peer_rows.start()
     for copy in own:
         copy.wait()
-    across.wait_send()
-    for direct in (own_rows, peer_rows, tops):
+    for direct in all_of:
         direct.wait_recv()
         direct.wait_send()
 
 
-class PairReduce:
-    def __init__(self, x, o, buf, part, peer, send, recv, pair_send, pair_recv):
-        self.x, self.o, self.buf, self.part, self.peer = x, o, buf, part, peer
-        self.pair = Pair()
-        self.first = Direct(
-            "shard", lambda d: x.at[1, d], lambda d, k: buf.at[1, k - 1], send.at[1], recv.at[1]
-        )
-        self.second = Direct(
-            "shard", lambda d: x.at[0, d], lambda d, k: buf.at[0, k - 1], send.at[0], recv.at[0]
-        )
-        self.across = self.pair.copy(part, peer, pair_send, pair_recv)
-
-    def start(self):
-        self.first.start()
-        self.second.start()
-
-    def add_up(self, half, o, more=None):
-        x, buf, shard = self.x, self.buf, self.first.me
-        rows = x.shape[2]
-        step = 8 if rows % 32 else 32
-
-        @pl.loop(0, rows // step)
-        def _(j):
-            at = pl.ds(pl.multiple_of(j * step, step), step)
-            total = x[half, shard, at].astype(f32)
-            for k in range(buf.shape[1]):
-                total = total + buf[half, k, at].astype(f32)
-            if more is not None:
-                total = total + more[at].astype(f32)
-            o[at] = total.astype(o.dtype)
-
-    def turn(self):
-        self.first.wait_recv()
-        self.add_up(1, self.part)
-        self.across.start()
-
-    def finish(self):
-        self.second.wait_recv()
-        self.across.wait_recv()
-        self.add_up(0, self.o, self.peer)
-        self.across.wait_send()
-        self.first.wait_send()
-        self.second.wait_send()
-
-
-def pair_reduce_scratch(n_shard, x):
-    sem = pltpu.SemaphoreType.DMA
-    return [
-        pltpu.VMEM((2, n_shard - 1, *x.shape[2:]), x.dtype),
-        pltpu.VMEM(x.shape[2:], x.dtype),
-        pltpu.VMEM(x.shape[2:], x.dtype),
-        sem((2, n_shard)),
-        sem((2, n_shard)),
-        sem,
-        sem,
+def reduce_kernel(axis, count, *refs):
+    ins, outs, bufs = refs[:count], refs[count : 2 * count], refs[2 * count : 3 * count]
+    send, recv = refs[3 * count :]
+    Greeting().ring(axis).wait()
+    all_of = [
+        Direct(axis, block_of(ins[i]), buffer_of(bufs[i]), send.at[i], recv.at[i])
+        for i in range(count)
     ]
-
-
-def pair_reduce_kernel(count, *refs):
-    ins, outs, rest = refs[:count], refs[count : 2 * count], refs[2 * count :]
-    Greeting().ring("shard").pair().wait()
-    all_of = [PairReduce(ins[i], outs[i], *rest[7 * i : 7 * i + 7]) for i in range(count)]
-    for one in all_of:
-        one.start()
-    for one in all_of:
-        one.turn()
-    for one in all_of:
-        one.finish()
+    for direct in all_of:
+        direct.start()
+    for i, direct in enumerate(all_of):
+        direct.wait_recv()
+        add_up(ins[i], bufs[i], outs[i], direct.me)
+        direct.wait_send()
 
 
 def many_sum_kernel(axis, x, o, buf, send, recv):
@@ -771,20 +692,21 @@
 
 
 def end_kernel(
-    x, wide, out, y, x_sum, wide_all, out_sum, y_sum, wide_buf, out_buf, wide_sum,
-    own_sem, wide_send, wide_recv, out_send, out_recv, swap_send, swap_recv, *rest,
+    x, wide, out, y, x_sum, wide_all, out_sum, y_sum, wide_buf, out_buf, y_buf, wide_sum,
+    own_sem, wide_send, wide_recv, out_send, out_recv, y_send, y_recv, swap_send, swap_recv,
+    *line_refs,
 ):
     ctx = lax.axis_index("ctx")
     Greeting().ring("ctx").ring("shard").wait()
     wides = Direct("shard", block_of(wide), buffer_of(wide_buf), wide_send, wide_recv)
     outs = Direct("shard", block_of(out), buffer_of(out_buf), out_send, out_recv)
     swap = Direct("ctx", block_of(wide_sum), block_from(wide_all), swap_send, swap_recv)
-    line = LineReduce(LINE_CHUNKS, x, x_sum, *rest[7:])
-    returns = PairReduce(y, y_sum, *rest[:7])
+    line = LineReduce(LINE_CHUNKS, x, x_sum, *line_refs)
+    returns = Direct("shard", block_of(y), buffer_of(y_buf), y_send, y_recv)
     line.start()
     wides.start()
+    outs.start()
     returns.start()
-    outs.start()
     line.pass_on()
     wides.wait_recv()
     for b in range(lax.axis_size("ctx")):
@@ -796,14 +718,14 @@
     swap.start()
     own = pltpu.make_async_copy(wide_sum.at[ctx], wide_all.at[ctx], own_sem)
     own.start()
-    line.finish()
-    returns.turn()
     outs.wait_recv()
     add_up(out, out_buf, out_sum, outs.me)
-    returns.finish()
+    line.finish()
+    returns.wait_recv()
+    add_up(y, y_buf, y_sum, returns.me)
     own.wait()
     swap.wait_recv()
-    for direct in (swap, wides, outs):
+    for direct in (swap, wides, outs, returns):
         direct.wait_send()
 
 
@@ -816,7 +738,7 @@
 LINE_CHUNKS = 4
 
 
-def start_call(collective_id, x, w, w_query, w_key, w_value, small):
+def start_call(collective_id, x, w, w_query, w_key, w_value, small, cot):
     n_ctx, n_shard = lax.axis_size("ctx"), lax.axis_size("shard")
     n = n_ctx // 2
     heads = (w.shape[0], 3 * w.shape[1] // n_ctx)
@@ -828,21 +750,23 @@
             jax.ShapeDtypeStruct((n_ctx, n_shard, *w.shape), bf16),
             jax.ShapeDtypeStruct((n_ctx, n_shard, *heads), bf16),
             jax.ShapeDtypeStruct((n_ctx, n_shard, *small.shape), bf16),
+            jax.ShapeDtypeStruct((n_shard, *cot.shape), bf16),
         ],
-        in_specs=[ANY] * 6,
-        out_specs=[ANY] * 4,
+        in_specs=[ANY] * 7,
+        out_specs=[ANY] * 5,
         scratch_shapes=[
             pltpu.VMEM((n_ctx, *heads), bf16),
             pltpu.VMEM((n_ctx, *small.shape), bf16),
-            sem((6,)),
+            sem((7,)),
             sem((4, n_ctx)),
             sem((4, n_ctx)),
         ]
-        + [sem((2, n_shard))] * 2
+        + [sem((3, n_shard))] * 2
         + [sem((n_shard, n))] * 4
-        + line_gather_scratch(n, LINE_CHUNKS + 1),
+        + line_gather_scratch(n, 1)
+        + line_gather_scratch(n, LINE_CHUNKS),
         compiler_params=remote_params(collective_id, 8),
-    )(x, w, w_query, w_key, w_value, small)
+    )(x, w, w_query, w_key, w_value, small, cot)
 
 
 def exchange(collective_id, x, to_rows, *more):
@@ -860,31 +784,30 @@
     )(x, *more)
 
 
-def pair_gather(collective_id, x, peaks):
-    n = lax.axis_size("shard")
+def gather(axis, collective_id, *arrays):
+    count, n = len(arrays), lax.axis_size(axis)
     sem = pltpu.SemaphoreType.DMA
     return pl.pallas_call(
-        pair_gather_kernel,
-        out_shape=[
-            jax.ShapeDtypeStruct((2, n, *x.shape), x.dtype),
-            jax.ShapeDtypeStruct((n, *peaks.shape), peaks.dtype),
-        ],
-        in_specs=[ANY] * 2,
-        out_specs=[ANY] * 2,
-        scratch_shapes=[sem((2,)), sem((3, n)), sem((3, n)), sem, sem],
+        functools.partial(gather_kernel, axis, count),
+        out_shape=[jax.ShapeDtypeStruct((n, *a.shape), a.dtype) for a in arrays],
+        in_specs=[ANY] * count,
+        out_specs=[ANY] * count,
+        scratch_shapes=[sem((count,)), sem((count, n)), sem((count, n))],
         compiler_params=remote_params(collective_id, 8),
-    )(x, peaks)
-
-
-def pair_reduce(collective_id, *arrays):
-    n = lax.axis_size("shard")
+    )(*arrays)
+
+
+def reduce(axis, collective_id, *arrays):
+    count, n = len(arrays), lax.axis_size(axis)
+    sem = pltpu.SemaphoreType.DMA
     return pl.pallas_call(
-        functools.partial(pair_reduce_kernel, len(arrays)),
-        out_shape=[jax.ShapeDtypeStruct(a.shape[2:], f32) for a in arrays],
-        in_specs=[VMEM] * len(arrays),
-        out_specs=[VMEM] * len(arrays),
-        scratch_shapes=sum((pair_reduce_scratch(n, a) for a in arrays), []),
-        compiler_params=remote_params(collective_id, 40),
+        functools.partial(reduce_kernel, axis, count),
+        out_shape=[jax.ShapeDtypeStruct(a.shape[1:], f32) for a in arrays],
+        in_specs=[VMEM] * count,
+        out_specs=[VMEM] * count,
+        scratch_shapes=[pltpu.VMEM((n - 1, *a.shape[1:]), a.dtype) for a in arrays]
+        + [sem((count, n)), sem((count, n))],
+        compiler_params=remote_params(collective_id, 32),
     )(*arrays)
 
 
@@ -913,19 +836,19 @@
             jax.ShapeDtypeStruct((rows, width), f32),
             jax.ShapeDtypeStruct((n_ctx, wide_rows, wide_cols), bf16),
             jax.ShapeDtypeStruct(out.shape[1:], f32),
-            jax.ShapeDtypeStruct(y.shape[2:], f32),
+            jax.ShapeDtypeStruct(y.shape[1:], f32),
         ],
         in_specs=[VMEM] * 4,
         out_specs=[VMEM] * 4,
         scratch_shapes=[
             pltpu.VMEM((n_shard - 1, *wide.shape[1:]), bf16),
             pltpu.VMEM((n_shard - 1, *out.shape[1:]), bf16),
+            pltpu.VMEM((n_shard - 1, *y.shape[1:]), bf16),
             pltpu.VMEM((n_ctx, wide_rows, wide_cols), bf16),
             sem,
         ]
-        + [sem((n_shard,))] * 4
+        + [sem((n_shard,))] * 6
         + [sem((n_ctx,))] * 2
-        + pair_reduce_scratch(n_shard, y)
         + [pltpu.VMEM((n, rows, width), bf16)] * 3
         + [sem((n, LINE_CHUNKS))] * 5,
         compiler_params=remote_params(collective_id, 56),
@@ -976,8 +899,8 @@
         axis=1,
     )
     grad_own = cotangent[0]
-    x_all, out_w, weights, small_all = start_call(
-        1, x_own, w_out, w_query, w_key, w_value, small
+    x_all, out_w, weights, small_all, grad_all = start_call(
+        1, x_own, w_out, w_query, w_key, w_value, small, grad_own
     )
     x_all = x_all.reshape(count, width)
     out_w = out_w.reshape(width, width)
@@ -989,51 +912,15 @@
     gain_key = lax.dynamic_slice_in_dim(gain_key, ctx * cols, cols)
     tail = small_all[..., 4 + experts :].astype(jnp.int32)
     docs = lax.dynamic_index_in_dim(tail[..., : rows // part], shard, 1, False).reshape(count)
-    span = n_ctx // 2
-    role = lax.div(ctx, span)
-    routes_all = tail[..., rows // part : rows // part * (1 + top)].reshape(
-        n_ctx, n_shard, rows, top
-    )
-    routes_all = jnp.stack(
-        [
-            lax.dynamic_index_in_dim(routes_all, ctx, 0, False),
-            lax.dynamic_index_in_dim(routes_all, lax.rem(ctx + span, n_ctx), 0, False),
-        ]
-    ).reshape(2 * n_shard * rows, top)
-
-    def swap(u):
-        return lax.ppermute(u, "ctx", [(i, (i + span) % n_ctx) for i in range(n_ctx)])
-
-    def queued_swap(u):
-        both = lax.all_gather(
-            u, "ctx", axis=0, axis_index_groups=[[i, i + span] for i in range(span)]
-        )
-        return lax.dynamic_index_in_dim(both, 1 - role, 0, False)
-
-    def in_order(mine, theirs):
-        return jnp.where(role == 0, jnp.stack([mine, theirs]), jnp.stack([theirs, mine]))
-
-    half = local // 2
+    grad_all = grad_all.reshape(n_shard * rows, width)
+    routes_all = lax.dynamic_index_in_dim(
+        tail[..., rows // part : rows // part * (1 + top)], ctx, 0, False
+    ).reshape(n_shard * rows, top)
+
     ff = w_gate.shape[2]
     own_w = jnp.concatenate([w_gate, w_up, w_down.transpose(0, 2, 1)], axis=2)
-    keep_w = lax.dynamic_slice_in_dim(own_w, role * half, half, 0)
-    give_w = lax.dynamic_slice_in_dim(own_w, (1 - role) * half, half, 0)
-    spans = [list(range(r * span, (r + 1) * span)) for r in (0, 1)]
-    grad_theirs = queued_swap(grad_own)
-    first_w = queued_swap(give_w[0])
-    x_all, first_w, later_w = lax.optimization_barrier((x_all, first_w, give_w[1:]))
-    early = [first_w] + [queued_swap(later_w[e]) for e in range(half - 1)]
-
-    def expert_weights(e, theirs):
-        return lax.all_gather(
-            in_order(keep_w[e], theirs),
-            "ctx",
-            axis=1,
-            tiled=True,
-            axis_index_groups=spans,
-        ).reshape(width, 3 * ff)
-
-    expert_w = [expert_weights(0, early[0])]
+    x_all, own_w = lax.optimization_barrier((x_all, own_w))
+    expert_w = [lax.all_gather(own_w[e], "ctx", axis=0, tiled=True) for e in range(local)]
 
     x_wide = x_all.astype(f32)
     inverse_one = inverse_rms(x_wide)
@@ -1053,20 +940,14 @@
     key = rotate(key_n * gain_key, cosine, sine).astype(bf16)
     mixed, log_total, peaks = attend_forward(query, key, value, docs)
     x_f = x_own.astype(f32)
-    mixed_own, grad_mine = exchange(2, mixed, False, grad_own)
-    grad_mine = grad_mine.reshape(n_shard * rows, width)
+    (mixed_own,) = exchange(2, mixed, False)
     after = x_f + dot(mixed_own, out_w)
     inverse_two = inverse_rms(after)
     normed_two = after * inverse_two
     hidden_two = (normed_two * gain_ffn).astype(bf16)
 
-    hidden_all, peaks = pair_gather(3, hidden_two, peaks)
-    hidden_all, early, grad_theirs = lax.optimization_barrier(
-        (hidden_all, early[1:], grad_theirs)
-    )
-    grad_theirs = lax.all_gather(grad_theirs, "shard", axis=0, tiled=True)
-    expert_w += [expert_weights(e + 1, u) for e, u in enumerate(early)]
-    hidden_all = hidden_all.reshape(2 * n_shard * rows, width)
+    hidden_all, peaks = gather("shard", 3, hidden_two, peaks)
+    hidden_all = hidden_all.reshape(n_shard * rows, width)
     peaks = jnp.max(peaks, axis=0)[:, 0, 0]
     logits = dot(hidden_all, router_w)
     named = jnp.any(routes_all[:, :, None] == jnp.arange(experts)[None, None, :], axis=1)
@@ -1074,23 +955,17 @@
     selected = jnp.where(named, probs, 0.0)
     selected_sum = jnp.sum(selected, axis=1, keepdims=True)
     gates = selected / selected_sum
-    first = shard * local + role * half
-    gates_own = lax.dynamic_slice_in_dim(gates, first, half, 1)
-    named_own = lax.dynamic_slice_in_dim(named, first, half, 1)
+    gates_own = lax.dynamic_slice_in_dim(gates, shard * local, local, 1)
+    named_own = lax.dynamic_slice_in_dim(named, shard * local, local, 1)
     moe_part = jnp.zeros(hidden_all.shape, f32)
     back_part = jnp.zeros(hidden_all.shape, f32)
 
-    def by_half(grad_theirs, function, *arrays):
-        split = grad_mine.shape[0]
-        return jnp.concatenate(
-            [
-                function(grad_mine.astype(f32), *(u[:split] for u in arrays)),
-                function(grad_theirs.astype(f32), *(u[split:] for u in arrays)),
-            ]
-        )
+    grad_wide = grad_all.astype(f32)
+    def to_owners(parts):
+        return [lax.psum_scatter(u, "ctx", scatter_dimension=0, tiled=True) for u in parts]
 
     grad_gates, expert_grads = [], []
-    for e in range(half):
+    for e in range(local):
         wide, down = expert_w[e][:, : 2 * ff], expert_w[e][:, 2 * ff :]
         gate_col = gates_own[:, e : e + 1]
         hidden = dot(hidden_all, wide)
@@ -1098,13 +973,11 @@
         sig = jax.nn.sigmoid(gate_h)
         silu = gate_h * sig
         act = (silu * up_h).astype(bf16)
-        if e == 0:
-            act, grad_theirs = lax.optimization_barrier((act, grad_theirs))
         result = contract_cols(act, down).astype(bf16).astype(f32)
         moe_part = moe_part + gate_col * result
-        along = by_half(grad_theirs, lambda d, u: jnp.sum(d * u, axis=1), result)
+        along = jnp.sum(grad_wide * result, axis=1)
         grad_gates.append(jnp.where(named_own[:, e], along, 0.0))
-        grad_y = by_half(grad_theirs, lambda d, u: (u * d).astype(bf16), gate_col)
+        grad_y = (gate_col * grad_wide).astype(bf16)
         grad_act = dot(grad_y, down)
         grad_h = jnp.concatenate(
             [grad_act * up_h * sig * (1.0 + gate_h * (1.0 - sig)), grad_act * silu], axis=1
@@ -1114,29 +987,19 @@
             contract_rows(hidden_all, grad_h).astype(bf16),
             contract_rows(grad_y, act).astype(bf16),
         ]
-        hidden_all, back_part, grad_w, expert_grads = lax.optimization_barrier(
-            (hidden_all, back_part, grad_w, expert_grads)
-        )
-        expert_grads.append(
-            [
-                lax.psum_scatter(
-                    u.reshape(2, width // 2, -1),
-                    "ctx",
-                    scatter_dimension=1,
-                    tiled=True,
-                    axis_index_groups=spans,
-                )
-                for u in grad_w
-            ]
-        )
-    slots = jnp.stack(grad_gates).reshape(half, 2, n_shard, rows).transpose(1, 2, 0, 3)
+        hidden_all, back_part, grad_w = lax.optimization_barrier((hidden_all, back_part, grad_w))
+        expert_grads.append(grad_w)
+    early = local // 2
+    expert_grads[:early] = [to_owners(grad_w) for grad_w in expert_grads[:early]]
+    slots = jnp.stack(grad_gates).reshape(local, n_shard, rows).transpose(1, 0, 2)
     grad_gates = lax.dynamic_update_slice_in_dim(
-        jnp.zeros((2, n_shard, experts, rows), f32), slots, first, 2
-    )
-    back_sum, grad_gates = pair_reduce(
-        4, back_part.astype(bf16).reshape(2, n_shard, rows, width), grad_gates
+        jnp.zeros((n_shard, experts, rows), f32), slots, shard * local, 1
+    )
+    back_sum, grad_gates = reduce(
+        "shard", 4, back_part.astype(bf16).reshape(n_shard, rows, width), grad_gates
     )
     grad_gates = grad_gates.T
+
     def own_rows(u):
         return lax.dynamic_slice_in_dim(u, shard * rows, rows, 0)
 
@@ -1157,19 +1020,11 @@
     )
 
     grad_attn_own = grad_after.astype(bf16)
-
-    def give(sums):
-        return jnp.concatenate(
-            [lax.dynamic_index_in_dim(u, 1 - role, 0, False) for u in sums], axis=1
-        )
-
-    peers = [swap(give(sums)) for sums in expert_grads[:-1]]
-    to_gather, grad_attn_own, expert_grads[-1], peers = lax.optimization_barrier(
-        (grad_attn_own, grad_attn_own, expert_grads[-1], peers)
-    )
+    to_gather, expert_grads[0] = lax.optimization_barrier((grad_attn_own, expert_grads[0]))
     grad_attn = lax.all_gather(to_gather, "ctx", axis=0, tiled=True)
     (grad_mixed,) = exchange(5, contract_cols(grad_attn_own, out_w).astype(bf16), True)
-    grad_out_w = contract_rows(mixed, grad_attn)
+    grad_mixed, late = lax.optimization_barrier((grad_mixed, expert_grads[early:]))
+    expert_grads[early:] = [to_owners(grad_w) for grad_w in late]
     grad_query_rot, grad_key_rot, grad_value = attend_backward(
         query, key, value, docs, log_total, grad_mixed
     )
@@ -1183,16 +1038,7 @@
         [jnp.sum(scaled_q * query_n, axis=1), jnp.sum(scaled_k * key_n, axis=1), peak_row]
     )
     inner = many_sum("ctx", 7, inner)
-    inner, expert_grads[-1] = lax.optimization_barrier((inner, expert_grads[-1]))
-    peers.append(swap(give(expert_grads[-1])))
-    kept = [[lax.dynamic_index_in_dim(u, role, 0, False) for u in sums] for sums in expert_grads]
-    peers = [(peer[:, : 2 * ff], peer[:, 2 * ff :]) for peer in peers]
-    both_halves = [
-        in_order(jnp.stack([k[i] for k in kept]), jnp.stack([p[i] for p in peers]))
-        .reshape(local, width // n_ctx, -1)
-        .astype(f32)
-        for i in (0, 1)
-    ]
+    grad_out_w = contract_rows(mixed, grad_attn)
     peak_all = inner[2, :HEADS]
     inner = inner / width
     grad_linear = jnp.concatenate(
@@ -1225,14 +1071,16 @@
         .astype(bf16)
         .reshape(n_shard, part, width + LANES)
     )
+    hidden_part = hidden_part.astype(bf16).reshape(n_ctx, rows, width)
     grad_hidden_one, grad_weights, grad_out_w, moe_sum = end_call(
         8,
-        hidden_part.astype(bf16).reshape(n_ctx, rows, width),
+        hidden_part,
         grad_weights,
         grad_out_w,
-        moe_part.astype(bf16).reshape(2, n_shard, rows, width),
+        moe_part.astype(bf16).reshape(n_shard, rows, width),
     )
     output = (after + moe_sum).astype(bf16)
+    grad_hidden_one, expert_grads = lax.optimization_barrier((grad_hidden_one, expert_grads))
     grad_weights = grad_weights.astype(f32)
     grad_small = jnp.sum(grad_weights[..., 3 * cols :], axis=0)
     grad_weights = (
@@ -1248,6 +1096,8 @@
         scaled_one - normed_own * jnp.mean(scaled_one * normed_own, axis=1, keepdims=True)
     )
 
+    wide_grads = jnp.stack([u for u, _ in expert_grads])
+    down_grads = jnp.stack([u for _, u in expert_grads])
     factors = jnp.sqrt(clip_threshold / jnp.maximum(peak_all, clip_threshold))
     col_scale = jnp.repeat(factors, HEAD)
     query_clipped = (w_query.astype(f32) * col_scale[None, :]).astype(bf16)
@@ -1264,9 +1114,9 @@
         grad_out_w[:, :width],
         grad_small[:, 1],
         grad_small[:, 2 : 2 + experts],
-        both_halves[0][..., :ff],
-        both_halves[0][..., ff:],
-        both_halves[1].transpose(0, 2, 1),
+        wide_grads[..., :ff].astype(f32),
+        wide_grads[..., ff:].astype(f32),
+        down_grads.transpose(0, 2, 1).astype(f32),
         query_clipped,
         key_clipped,
         factors,

time: 1420 us -> 1480 us (1.042)
  waiting for transfers between devices: 75.9 us -> 374 us
  Pallas kernels: 809 us -> 590 us
  other arithmetic: 109 us -> 81.9 us
  matrix products: 305 us -> 326 us
    reduce_scatter x4 -> x8, waiting for transfers between devices: 18.6 us -> 246 us  [to_owners(): lax.psum_scatter(u, 'ctx', scatter_dimension=0, tiled=True)]
    pallas_call x1, Pallas kernels: 254 us -> 142 us  [start_call(): pl.pallas_call(start_kernel, out_shape=[jax.ShapeDtypeStruct((n_ctx, *x.s...]
    pallas_call x2, Pallas kernels: 205 us -> 99.7 us  [the longest x1 49.9 us: gather(): pl.pallas_call(functools.partial(gather_kernel, axis, count), out_shape=[...]
    all_gather x6 -> x4, waiting for transfers between devices: 25.1 us -> 123 us  [per_device(): lax.all_gather(own_w[e], 'ctx', axis=0, tiled=True)]
    ppermute x2 -> x0, waiting for transfers between devices: 30.2 us -> none  [swap(): lax.ppermute(u, 'ctx', [(i, (i + span) % n_ctx) for i in range(n_ctx)])]
    reduce_sum x1 -> x0, other arithmetic: 16.5 us -> none  [per_device(): along = by_half(grad_theirs, lambda d, u: jnp.sum(d * u, axis=1), result)]
    unnamed x194 -> x238, local copies, waits for them, and re-layouts: 33.2 us -> 49.3 us
    pallas_call x1, Pallas kernels: 160 us -> 175 us  [end_call(): pl.pallas_call(end_kernel, out_shape=[jax.ShapeDtypeStruct((rows, width),...]
  transfers between devices with their start and end apart: 13 -> 13, of which waited for: 3 -> 6; matrix products, arithmetic and copies ran while one was open for 31% -> 27% of each run, Pallas kernels for 46% -> 30%
where the time goes in v7:
time: 1480 us; the launch traced here: 1470 us
  Pallas kernels  590 us (40%)
  waiting for transfers between devices  374 us (25%)
  matrix products  326 us (22%)
  local copies, waits for them, and re-layouts  84.1 us (6%)
  other arithmetic  81.9 us (6%)
  between operations  16.5 us (1%)
    reduce_scatter x8, waiting for transfers between devices, to_owners(): lax.psum_scatter(u, 'ctx', scatter_dimension=0, tiled=True)  246 us
    pallas_call x1, Pallas kernels, end_call(): pl.pallas_call(end_kernel, out_shape=[jax.ShapeDtypeStruct((rows, width),...  175 us
    pallas_call x1, Pallas kernels, start_call(): pl.pallas_call(start_kernel, out_shape=[jax.ShapeDtypeStruct((n_ctx, *x.s...  142 us
    all_gather x4, waiting for transfers between devices, per_device(): lax.all_gather(own_w[e], 'ctx', axis=0, tiled=True)  123 us
    dot_general x11, matrix products, contract_cols(): lax.dot_general(a, b, (((1,), (1,)), ((), ())), preferred_element_type=f32)  120 us
    dot_general x11, matrix products, dot(): return jnp.dot(a, b, preferred_element_type=f32)  108 us
    dot_general x11, matrix products, contract_rows(): lax.dot_general(a, b, (((0,), (0,)), ((), ())), preferred_element_type=f32)  98.3 us
    pallas_call x2, Pallas kernels, exchange(): pl.pallas_call(functools.partial(exchange_kernel, to_rows), out_shape=[ja...  75.1 us
  transfers between devices with their start and end apart: 13, of which 6 were waited for; matrix products, arithmetic and copies ran while one was open for 27% of the time, Pallas kernels for 30%

profile of v7, /device:TPU:0, one launch (start us, length us, event | category | flops | bytes accessed | tf_op | source)
XLA Modules:
  0.0 1473.5 jit_solution(13850809385258271052)
XLA Ops:
  26.7 142.3 %shard_map.296 = (bf16[8,256,2048]{2,1,0:T(8,128)(2,1)S(1)}, bf16[8,4,64,2048]{3,2,1,0:T(8,128)(2,1)S(1)}, bf16[8,4,64,768]{3,2,1,0:T(8,128)(2,1)S(1)}, bf16[8,4...) custom-call(bf16[256,2048]{1,0:T(8,128)(2,1)S(1)} %bitcast.162, bf16[64,2048]{1,0:T(8,128)(2,1)S(1)} %copy-done.27, ...), custom_call_target="tpu_custom_call" | custom-call | tf_op jit(solution)/shard_map/pallas_call | solution.py:746
  237.9 23.0 %shard_map.298 = (bf16[2048,256]{1,0:T(8,128)(2,1)S(1)}, f32[2,2048,1]{2,1,0:T(8,128)}, f32[2,8,128]{2,1,0:T(8,128)S(1)}) custom-call(bf16[2048,256]{1,0:T(8,128)(2,1)S(1)} %pad_maximum_fusion.21.q_ref, bf16[2048,256]{1,0:T(8,128)(2,1)S(1)} %pad_maximum_fusion.22.k_ref, bf16[2048,256]{1,0:T(8,128)(2,1)S(1)} %copy-done.20, s32[2048,1]{1,0:T(8,128)S(1)} %copy-done.19, ...), custom_call_target="tpu_custom_call" | custom-call | flops 4294967296 | bytes 4194304 | tf_op jit(solution)/shard_map/pallas_call | solution.py:111
  260.9 39.1 %shard_map.299 = bf16[256,2048]{1,0:T(8,128)(2,1)S(1)} custom-call(bf16[2048,256]{1,0:T(8,128)(2,1)S(1)} %get-tuple-element.74.refs_0_), custom_call_target="tpu_custom_call" | custom-call | tf_op jit(solution)/shard_map/pallas_call | solution.py:776
  309.7 49.9 %shard_map.300 = (bf16[4,256,2048]{2,1,0:T(8,128)(2,1)S(1)}, f32[4,2,8,128]{3,2,1,0:T(8,128)S(1)}) custom-call(bf16[256,2048]{1,0:T(8,128)(2,1)S(1)} %multiply_convert_fusion.14.refs_0_, f32[2,8,128]{2,1,0:T(8,128)S(1)} %get-tuple-element.77.refs_1_), custom_call_target="tpu_custom_call" | custom-call | tf_op jit(solution)/shard_map/pallas_call | solution.py:790
  371.0 12.7 fusion.31
  400.9 14.4 convert_convert_fusion
  427.7 15.9 %all-gather.14.cloned.1.call-done = bf16[1,2048,3072]{1,2,0:T(8,128)(2,1)} async-done(((bf16[1,256,3072]{1,2,0:T(8,128)(2,1)}), bf16[1,2048,3072]{1,2,0:T(8,128)(2,1)}) %all-gather.14.cloned.1.call-update) | async-done | bytes 12582928 | tf_op jit(solution)/shard_map/all_gather | solution.py:923
  443.6 12.9 fusion.27
  480.2 16.6 %convert_add_fusion.2 = f32[1024,2048]{1,0:T(8,128)} fusion(f32[1024,2048]{1,0:T(8,128)} %convert_convert_fusion, bf16[2048,3072]{0,1:T(8,128)(2,1)} %bitcast.259, bf16[1024,1024]{0,1:T(8,128)(2,1)} %copy-done.101, bf16[1024,1024]{0,1:T(8,128)(2,1)S(1)} %get-tuple-element.250), kind=kOutput, calls=%fused_computation.33 | convolution fusion | flops 8604614656 | bytes 29360128 | tf_op jit(solution)/shard_map/dot_general | solution.py:31
  506.9 53.7 %all-gather.16.cloned.1.call-done = bf16[1,2048,3072]{1,2,0:T(8,128)(2,1)} async-done(((bf16[1,256,3072]{1,2,0:T(8,128)(2,1)}), bf16[1,2048,3072]{1,2,0:T(8,128)(2,1)}) %all-gather.16.cloned.1.call-update) | async-done | bytes 12582928 | tf_op jit(solution)/shard_map/all_gather | solution.py:923
  560.6 12.7 fusion.23
  597.2 16.2 %convert_add_fusion.1 = f32[1024,2048]{1,0:T(8,128)} fusion(f32[1024,2048]{1,0:T(8,128)} %convert_add_fusion.2, bf16[2048,3072]{0,1:T(8,128)(2,1)} %bitcast.263, bf16[1024,1024]{0,1:T(8,128)(2,1)} %copy-done.102, bf16[1024,1024]{0,1:T(8,128)(2,1)S(1)} %get-tuple-element.248), kind=kOutput, calls=%fused_computation.32 | convolution fusion | flops 8604614656 | bytes 29360128 | tf_op jit(solution)/shard_map/dot_general | solution.py:31
  623.6 53.8 %all-gather.18.cloned.1.call-done = bf16[1,2048,3072]{1,2,0:T(8,128)(2,1)} async-done(((bf16[1,256,3072]{1,2,0:T(8,128)(2,1)}), bf16[1,2048,3072]{1,2,0:T(8,128)(2,1)}) %all-gather.18.cloned.1.call-update) | async-done | bytes 12582928 | tf_op jit(solution)/shard_map/all_gather | solution.py:923
  707.3 14.4 convolution_convert_fusion
  721.7 14.4 convert_add_fusion
  760.7 15.0 %fusion.13 = (f32[1024]{0:T(1024)S(1)}, f32[1024]{0:T(1024)S(1)}, f32[1024]{0:T(1024)S(1)}, f32[1024]{0:T(1024)S(1)}, bf16[1024,2048]{1,0:T(8,128)(2,1)}) fusion(bf16[4,256,2048]{2,1,0:T(8,128)(2,1)S(1)} %copy-done.16, bf16[1024,2048]{1,0:T(8,128)(2,1)} %convolution_convert_fusion.4, bf16[1024,2048]{1,0:T(8,128)(2,1)} %convolution_convert_fusion.5, ...), kind=kOutput, calls=%fused_computation.27 | convolution fusion | flops 4341100544 | bytes 27295744 | tf_op jit(solution)/shard_map/dot_general | solution.py:31
  775.9 49.8 %shard_map.301 = (f32[256,2048]{1,0:T(8,128)S(1)}, f32[16,256]{1,0:T(8,128)S(1)}) custom-call(bf16[4,256,2048]{2,1,0:T(8,128)(2,1)S(1)} %bitcast.177, f32[4,16,256]{2,1,0:T(8,128)S(1)} %fusion.136.refs_1_), custom_call_target="tpu_custom_call" | custom-call | tf_op jit(solution)/shard_map/pallas_call | solution.py:803
  837.4 36.0 %shard_map.302.do_ref = bf16[2048,256]{1,0:T(8,128)(2,1)S(1)} custom-call(bf16[256,2048]{1,0:T(8,128)(2,1)S(1)} %convolution_convert_fusion.14.refs_0_), custom_call_target="tpu_custom_call" | custom-call | tf_op jit(solution)/shard_map/pallas_call | solution.py:776
  878.5 37.5 %shard_map.303 = (f32[2048,256]{1,0:T(8,128)}, f32[2048,256]{1,0:T(8,128)}, f32[2048,256]{1,0:T(8,128)}) custom-call(bf16[2048,256]{1,0:T(8,128)(2,1)} %copy-done.18, bf16[2048,256]{1,0:T(8,128)(2,1)} %copy-done.17, bf16[2048,256]{1,0:T(8,128)(2,1)} %slice.494.v_ref, s32[2048,1]{1,0:T(8,128)} %broadcast_in_dim_reshape.6.doc_q_ref, s32[1,2048]{1,0:T(1,128)} %copy-done.29, ...), custom_call_target="tpu_custom_call" | custom-call | flops 10737418240 | bytes 10485760 | tf_op jit(solution)/shard_map/pallas_call | solution.py:134
  933.5 29.4 %shard_map.304 = f32[3,2048]{1,0:T(4,128)S(1)} custom-call(f32[3,2048]{1,0:T(4,128)S(1)} %pad_maximum_fusion.24.x), custom_call_target="tpu_custom_call" | custom-call | tf_op jit(solution)/shard_map/pallas_call | solution.py:817
  1004.6 175.1 %shard_map.305 = (f32[256,2048]{1,0:T(8,128)}, bf16[8,64,896]{2,1,0:T(8,128)(2,1)}, f32[64,2176]{1,0:T(8,128)}, f32[256,2048]{1,0:T(8,128)}) custom-call(bf16[8,256,2048]{2,1,0:T(8,128)(2,1)} %bitcast.183, bf16[4,512,896]{2,1,0:T(8,128)(2,1)} %bitcast.182, bf16[4,64,2176]{2,1,0:T(8,128)(2,1)} %pad_maximum_fusion.20.out, bf16[4,256,2048]{2,1,0:T(8,128)(2,1)} %bitcast.187), custom_call_target="tpu_custom_call" | custom-call | tf_op jit(solution)/shard_map/pallas_call | solution.py:833
  1185.8 54.3 %reduce-scatter.13.cloned.1.call-done = bf16[256,2048]{1,0:T(8,128)(2,1)} async-done(((bf16[2048,2048]{1,0:T(8,128)(2,1)}), bf16[256,2048]{1,0:T(8,128)(2,1)}) %reduce-scatter.13.cloned.1.call-update) | async-done | bytes 1048592 | tf_op jit(solution)/shard_map/reduce_scatter | solution.py:965
  1240.1 101.0 %reduce-scatter.17.cloned.1.call-done = bf16[256,2048]{1,0:T(8,128)(2,1)} async-done(((bf16[2048,2048]{1,0:T(8,128)(2,1)}), bf16[256,2048]{1,0:T(8,128)(2,1)}) %reduce-scatter.17.cloned.1.call-update) | async-done | bytes 1048592 | tf_op jit(solution)/shard_map/reduce_scatter | solution.py:965
  1341.1 90.3 %reduce-scatter.21.cloned.1.call-done = bf16[256,2048]{1,0:T(8,128)(2,1)} async-done(((bf16[2048,2048]{1,0:T(8,128)(2,1)}), bf16[256,2048]{1,0:T(8,128)(2,1)}) %reduce-scatter.21.cloned.1.call-update) | async-done | bytes 1048592 | tf_op jit(solution)/shard_map/reduce_scatter | solution.py:965
  (397 shorter events, 376.7 us)
Async XLA Ops:
  7.2 363.8 %all-gather.12.cloned.1.call-start = ((), (), s32[]{:S(2)}) async-start(), calls=%async_computation.17 | async-start | bytes 14155776 | tf_op jit(solution)/shard_map/all_gather | solution.py:923
  179.2 180.4 %copy-start = (bf16[8,4,64,128]{3,2,1,0:T(8,128)(2,1)}, bf16[8,4,64,128]{3,2,1,0:T(8,128)(2,1)S(1)}, u32[]{:S(2)}) copy-start(bf16[8,4,64,128]{3,2,1,0:T(8,128)(2,1)S(1)} %get-tuple-element.72) | copy-start | bytes 1572868
  185.0 258.6 %all-gather.14.cloned.1.call-start = ((), (), s32[]{:S(2)}) async-start(), calls=%async_computation.18 | async-start | bytes 14155776 | tf_op jit(solution)/shard_map/all_gather | solution.py:923
  185.8 374.8 %all-gather.16.cloned.1.call-start = ((), (), s32[]{:S(2)}) async-start(), calls=%async_computation.19 | async-start | bytes 14155776 | tf_op jit(solution)/shard_map/all_gather | solution.py:923
  186.5 490.9 %all-gather.18.cloned.1.call-start = ((), (), s32[]{:S(2)}) async-start(), calls=%async_computation.20 | async-start | bytes 14155776 | tf_op jit(solution)/shard_map/all_gather | solution.py:923
  187.1 643.4 %reduce-scatter.11.cloned.1.call-start = ((), (), s32[]{:S(2)}) async-start(), calls=%async_computation.9 | async-start | bytes 4718592 | tf_op jit(solution)/shard_map/reduce_scatter | solution.py:965
  219.5 89.0 %copy-start.66 = (f32[2048,1]{0,1:T(1,128)}, f32[2048,1]{0,1:T(1,128)S(1)}, u32[]{:S(2)}) copy-start(f32[2048,1]{0,1:T(1,128)S(1)} %copy.245) | copy-start | bytes 24580
  308.4 52.5 %copy-start.77 = (f32[256]{0:T(256)}, f32[256]{0:T(256)S(1)}, u32[]{:S(2)}) copy-start(f32[256]{0:T(256)S(1)} %add_rsqrt_fusion.3) | copy-start | bytes 3076
  309.7 51.2 %copy-start.9 = (bf16[256,2048]{1,0:T(8,128)(2,1)}, bf16[256,2048]{1,0:T(8,128)(2,1)S(1)}, u32[]{:S(2)}) copy-start(bf16[256,2048]{1,0:T(8,128)(2,1)S(1)} %multiply_convert_fusion.14.refs_0_) | copy-start | bytes 3145732
  496.9 333.6 %reduce-scatter.9.cloned.1.call-start = ((), (), s32[]{:S(2)}) async-start(), calls=%async_computation.8 | async-start | bytes 9437184 | tf_op jit(solution)/shard_map/reduce_scatter | solution.py:965
  613.4 384.3 %all-gather.10.cloned.1.call-start = ((), (), s32[]{:S(2)}) async-start(), calls=%async_computation.10 | async-start | bytes 9437184 | tf_op jit(solution)/shard_map/all_gather | solution.py:1024
  775.7 50.8 %copy-start.63 = (f32[1024,16]{0,1:T(8,128)S(1)}, f32[1024,16]{0,1:T(8,128)}, u32[]{:S(2)}) copy-start(f32[1024,16]{0,1:T(8,128)} %copy-done.62) | copy-start | bytes 196612
  775.7 50.8 %copy-start.65 = (pred[1024,16]{0,1:T(8,128)(4,1)S(1)}, pred[1024,16]{0,1:T(8,128)(4,1)}, u32[]{:S(2)}) copy-start(pred[1024,16]{0,1:T(8,128)(4,1)} %copy-done.64) | copy-start | bytes 49156
  775.7 50.8 %copy-start.95 = (f32[256]{0:T(256)S(1)}, f32[256]{0:T(256)}, u32[]{:S(2)}) copy-start(f32[256]{0:T(256)} %dynamic-slice.5) | copy-start | bytes 3076
  775.7 50.8 %copy-start.1 = (bf16[8,4,64,128]{3,2,1,0:T(8,128)(2,1)S(1)}, bf16[8,4,64,128]{3,2,1,0:T(8,128)(2,1)}, u32[]{:S(2)}) copy-start(bf16[8,4,64,128]{3,2,1,0:T(8,128)(2,1)} %copy-done) | copy-start | bytes 1572868
  775.7 50.8 %copy-start.35 = (f32[256,2048]{1,0:T(8,128)S(1)}, f32[256,2048]{1,0:T(8,128)}, u32[]{:S(2)}) copy-start(f32[256,2048]{1,0:T(8,128)} %copy-done.34) | copy-start | bytes 6291460
  775.7 50.8 %copy-start.67 = (f32[2048,1]{0,1:T(1,128)S(1)}, f32[2048,1]{0,1:T(1,128)}, u32[]{:S(2)}) copy-start(f32[2048,1]{0,1:T(1,128)} %copy-done.66) | copy-start | bytes 24580
  775.7 50.8 %copy-start.78 = (f32[256]{0:T(256)S(1)}, f32[256]{0:T(256)}, u32[]{:S(2)}) copy-start(f32[256]{0:T(256)} %copy-done.77) | copy-start | bytes 3076
  830.5 355.3 %reduce-scatter.15.cloned.1.call-start = ((), (), s32[]{:S(2)}) async-start(), calls=%async_computation.12 | async-start | bytes 4718592 | tf_op jit(solution)/shard_map/reduce_scatter | solution.py:965
  831.2 354.6 %reduce-scatter.19.cloned.1.call-start = ((), (), s32[]{:S(2)}) async-start(), calls=%async_computation.14 | async-start | bytes 4718592 | tf_op jit(solution)/shard_map/reduce_scatter | solution.py:965
  874.6 311.2 %reduce-scatter.23.cloned.1.call-start = ((), (), s32[]{:S(2)}) async-start(), calls=%async_computation.16 | async-start | bytes 4718592 | tf_op jit(solution)/shard_map/reduce_scatter | solution.py:965
  875.1 364.9 %reduce-scatter.13.cloned.1.call-start = ((), (), s32[]{:S(2)}) async-start(), calls=%async_computation.11 | async-start | bytes 9437184 | tf_op jit(solution)/shard_map/reduce_scatter | solution.py:965
  875.9 465.2 %reduce-scatter.17.cloned.1.call-start = ((), (), s32[]{:S(2)}) async-start(), calls=%async_computation.13 | async-start | bytes 9437184 | tf_op jit(solution)/shard_map/reduce_scatter | solution.py:965
  876.5 554.9 %reduce-scatter.21.cloned.1.call-start = ((), (), s32[]{:S(2)}) async-start(), calls=%async_computation.15 | async-start | bytes 9437184 | tf_op jit(solution)/shard_map/reduce_scatter | solution.py:965
  (101 other events, 784.7 us)
Sparse Core Ops, SparseCore 0:
  185.2 140.3 all-gather.11
  327.1 116.4 all-gather.13
  445.2 115.3 all-gather.15
  562.0 115.3 all-gather.17
  679.5 48.1 reduce-scatter.10
  729.9 87.7 reduce-scatter.8
  830.6 102.4 all-gather.9
  935.4 53.2 reduce-scatter.14
  991.0 66.1 reduce-scatter.18
  1059.3 88.6 reduce-scatter.22
  1150.4 89.6 reduce-scatter.12
  1242.2 98.7 reduce-scatter.16
  1343.3 87.9 reduce-scatter.20

commit v8 on v7

--- a/solution.py
+++ b/solution.py
@@ -729,6 +729,39 @@
         direct.wait_send()
 
 
+def line_reduce_kernel(count, *refs):
+    ins, outs, rest = refs[:count], refs[count : 2 * count], refs[2 * count :]
+    Greeting().line().wait()
+    all_of = [
+        LineReduce(LINE_CHUNKS, ins[i], outs[i], *rest[8 * i : 8 * i + 8]) for i in range(count)
+    ]
+    for one in all_of:
+        one.start()
+    for one in all_of:
+        one.pass_on()
+    for one in all_of:
+        one.finish()
+
+
+def line_reduce_scratch(x):
+    n_ctx, rows, width = x.shape
+    n = n_ctx // 2
+    return [pltpu.VMEM((n, rows, width), bf16)] * 3 + [
+        pltpu.SemaphoreType.DMA((n, LINE_CHUNKS))
+    ] * 5
+
+
+def line_reduce(collective_id, *arrays):
+    return pl.pallas_call(
+        functools.partial(line_reduce_kernel, len(arrays)),
+        out_shape=[jax.ShapeDtypeStruct(x.shape[1:], f32) for x in arrays],
+        in_specs=[VMEM] * len(arrays),
+        out_specs=[VMEM] * len(arrays),
+        scratch_shapes=sum((line_reduce_scratch(x) for x in arrays), []),
+        compiler_params=remote_params(collective_id, 48),
+    )(*arrays)
+
+
 def remote_params(collective_id, megabytes):
     return pltpu.CompilerParams(
         collective_id=collective_id, has_side_effects=True, vmem_limit_bytes=megabytes << 20
@@ -919,8 +952,10 @@
 
     ff = w_gate.shape[2]
     own_w = jnp.concatenate([w_gate, w_up, w_down.transpose(0, 2, 1)], axis=2)
+    first_w = own_w[0]
     x_all, own_w = lax.optimization_barrier((x_all, own_w))
-    expert_w = [lax.all_gather(own_w[e], "ctx", axis=0, tiled=True) for e in range(local)]
+    own_w = [first_w] + [own_w[e] for e in range(1, local)]
+    expert_w = [lax.all_gather(u, "ctx", axis=0, tiled=True) for u in own_w]
 
     x_wide = x_all.astype(f32)
     inverse_one = inverse_rms(x_wide)
@@ -1023,6 +1058,7 @@
     to_gather, expert_grads[0] = lax.optimization_barrier((grad_attn_own, expert_grads[0]))
     grad_attn = lax.all_gather(to_gather, "ctx", axis=0, tiled=True)
     (grad_mixed,) = exchange(5, contract_cols(grad_attn_own, out_w).astype(bf16), True)
+    last_grad = expert_grads.pop()
     grad_mixed, late = lax.optimization_barrier((grad_mixed, expert_grads[early:]))
     expert_grads[early:] = [to_owners(grad_w) for grad_w in late]
     grad_query_rot, grad_key_rot, grad_value = attend_backward(
@@ -1080,7 +1116,10 @@
         moe_part.astype(bf16).reshape(n_shard, rows, width),
     )
     output = (after + moe_sum).astype(bf16)
-    grad_hidden_one, expert_grads = lax.optimization_barrier((grad_hidden_one, expert_grads))
+    grad_hidden_one, last_grad = lax.optimization_barrier((grad_hidden_one, last_grad))
+    last_grad = line_reduce(9, *(u.reshape(n_ctx, width // n_ctx, -1) for u in last_grad))
+    last_grad, expert_grads = lax.optimization_barrier((last_grad, expert_grads))
+    expert_grads = [[u.astype(f32) for u in sums] for sums in expert_grads] + [last_grad]
     grad_weights = grad_weights.astype(f32)
     grad_small = jnp.sum(grad_weights[..., 3 * cols :], axis=0)
     grad_weights = (
@@ -1114,9 +1153,9 @@
         grad_out_w[:, :width],
         grad_small[:, 1],
         grad_small[:, 2 : 2 + experts],
-        wide_grads[..., :ff].astype(f32),
-        wide_grads[..., ff:].astype(f32),
-        down_grads.transpose(0, 2, 1).astype(f32),
+        wide_grads[..., :ff],
+        wide_grads[..., ff:],
+        down_grads.transpose(0, 2, 1),
         query_clipped,
         key_clipped,
         factors,

time: 1480 us -> 1420 us (0.959)
  waiting for transfers between devices: 374 us -> 9.36 us
  Pallas kernels: 590 us -> 887 us
    reduce_scatter x8 -> x6, waiting for transfers between devices: 246 us -> 0.01 us  [to_owners(): lax.psum_scatter(u, 'ctx', scatter_dimension=0, tiled=True)]
    pallas_call x0 -> x1, Pallas kernels: none -> 207 us  [line_reduce(): pl.pallas_call(functools.partial(line_reduce_kernel, len(arrays)), out_sh...]
    all_gather x4, waiting for transfers between devices: 123 us -> 6.14 us  [per_device(): expert_w = [lax.all_gather(u, 'ctx', axis=0, tiled=True) for u in own_w]]
    pallas_call x1, Pallas kernels: 142 us -> 220 us  [start_call(): pl.pallas_call(start_kernel, out_shape=[jax.ShapeDtypeStruct((n_ctx, *x.s...]
    unnamed x238 -> x260, local copies, waits for them, and re-layouts: 49.3 us -> 54.1 us
  transfers between devices with their start and end apart: 13 -> 11, of which waited for: 6 -> 1; matrix products, arithmetic and copies ran while one was open for 27% -> 29% of each run, Pallas kernels for 30% -> 63%
where the time goes in v8:
time: 1420 us; the launch traced here: 1400 us
  Pallas kernels  887 us (62%)
  matrix products  323 us (23%)
  local copies, waits for them, and re-layouts  91.4 us (6%)
  other arithmetic  75.7 us (5%)
  between operations  16.7 us (1%)
    pallas_call x1, Pallas kernels, start_call(): pl.pallas_call(start_kernel, out_shape=[jax.ShapeDtypeStruct((n_ctx, *x.s...  220 us
    pallas_call x1, Pallas kernels, line_reduce(): pl.pallas_call(functools.partial(line_reduce_kernel, len(arrays)), out_sh...  207 us
    pallas_call x1, Pallas kernels, end_call(): pl.pallas_call(end_kernel, out_shape=[jax.ShapeDtypeStruct((rows, width),...  179 us
    dot_general x11, matrix products, contract_cols(): lax.dot_general(a, b, (((1,), (1,)), ((), ())), preferred_element_type=f32)  119 us
    dot_general x11, matrix products, dot(): return jnp.dot(a, b, preferred_element_type=f32)  107 us
    dot_general x11, matrix products, contract_rows(): lax.dot_general(a, b, (((0,), (0,)), ((), ())), preferred_element_type=f32)  96.7 us
    pallas_call x2, Pallas kernels, exchange(): pl.pallas_call(functools.partial(exchange_kernel, to_rows), out_shape=[ja...  82.8 us
    unnamed x260, local copies, waits for them, and re-layouts  54.1 us
  transfers between devices with their start and end apart: 11, of which 1 were waited for; matrix products, arithmetic and copies ran while one was open for 29% of the time, Pallas kernels for 63%

profile of v8, /device:TPU:0, one launch (start us, length us, event | category | flops | bytes accessed | tf_op | source)
XLA Modules:
  0.0 1403.1 jit_solution(3427004939591503609)
XLA Ops:
  23.2 219.9 %shard_map.296 = (bf16[8,256,2048]{2,1,0:T(8,128)(2,1)S(1)}, bf16[8,4,64,2048]{3,2,1,0:T(8,128)(2,1)S(1)}, bf16[8,4,64,768]{3,2,1,0:T(8,128)(2,1)S(1)}, bf16[8,4...) custom-call(bf16[256,2048]{1,0:T(8,128)(2,1)S(1)} %bitcast.176, bf16[64,2048]{1,0:T(8,128)(2,1)S(1)} %copy-done.30, ...), custom_call_target="tpu_custom_call" | custom-call | tf_op jit(solution)/shard_map/pallas_call | solution.py:779
  311.9 23.0 %shard_map.298 = (bf16[2048,256]{1,0:T(8,128)(2,1)S(1)}, f32[2,2048,1]{2,1,0:T(8,128)}, f32[2,8,128]{2,1,0:T(8,128)S(1)}) custom-call(bf16[2048,256]{1,0:T(8,128)(2,1)S(1)} %pad_maximum_fusion.21.q_ref, bf16[2048,256]{1,0:T(8,128)(2,1)S(1)} %pad_maximum_fusion.22.k_ref, bf16[2048,256]{1,0:T(8,128)(2,1)S(1)} %copy-done.23, s32[2048,1]{1,0:T(8,128)S(1)} %copy-done.22, ...), custom_call_target="tpu_custom_call" | custom-call | flops 4294967296 | bytes 4194304 | tf_op jit(solution)/shard_map/pallas_call | solution.py:111
  335.0 38.6 %shard_map.299 = bf16[256,2048]{1,0:T(8,128)(2,1)S(1)} custom-call(bf16[2048,256]{1,0:T(8,128)(2,1)S(1)} %get-tuple-element.76.refs_0_), custom_call_target="tpu_custom_call" | custom-call | tf_op jit(solution)/shard_map/pallas_call | solution.py:809
  383.0 49.8 %shard_map.300 = (bf16[4,256,2048]{2,1,0:T(8,128)(2,1)S(1)}, f32[4,2,8,128]{3,2,1,0:T(8,128)S(1)}) custom-call(bf16[256,2048]{1,0:T(8,128)(2,1)S(1)} %multiply_convert_fusion.14.refs_0_, f32[2,8,128]{2,1,0:T(8,128)S(1)} %get-tuple-element.79.refs_1_), custom_call_target="tpu_custom_call" | custom-call | tf_op jit(solution)/shard_map/pallas_call | solution.py:823
  444.9 12.7 fusion.31
  474.8 14.7 %convert_convert_fusion = f32[1024,2048]{1,0:T(8,128)} fusion(bf16[2048,3072]{0,1:T(8,128)(2,1)} %bitcast.265, bf16[1024,1024]{0,1:T(8,128)(2,1)} %get-tuple-element.257, bf16[1024,1024]{0,1:T(8,128)(2,1)S(1)} %get-tuple-element.256), kind=kOutput, calls=%fused_computation.77 | convolution fusion | flops 8602517504 | bytes 20971520 | tf_op jit(solution)/shard_map/dot_general | solution.py:31
  489.6 12.4 convolution_convert_fusion.3
  502.0 13.0 fusion.27
  526.3 12.4 convolution_convert_fusion.2
  538.7 16.4 %convert_add_fusion.2 = f32[1024,2048]{1,0:T(8,128)} fusion(f32[1024,2048]{1,0:T(8,128)} %convert_convert_fusion, bf16[2048,3072]{0,1:T(8,128)(2,1)} %bitcast.269, bf16[1024,1024]{0,1:T(8,128)(2,1)} %copy-done.113, bf16[1024,1024]{0,1:T(8,128)(2,1)S(1)} %get-tuple-element.254), kind=kOutput, calls=%fused_computation.34 | convolution fusion | flops 8604614656 | bytes 29360128 | tf_op jit(solution)/shard_map/dot_general | solution.py:31
  565.1 13.0 fusion.23
  589.4 12.8 convolution_convert_fusion.1
  602.2 16.5 %convert_add_fusion.1 = f32[1024,2048]{1,0:T(8,128)} fusion(f32[1024,2048]{1,0:T(8,128)} %convert_add_fusion.2, bf16[2048,3072]{0,1:T(8,128)(2,1)} %bitcast.273, bf16[1024,1024]{0,1:T(8,128)(2,1)} %copy-done.114, bf16[1024,1024]{0,1:T(8,128)(2,1)S(1)} %get-tuple-element.252), kind=kOutput, calls=%fused_computation.33 | convolution fusion | flops 8604614656 | bytes 29360128 | tf_op jit(solution)/shard_map/dot_general | solution.py:31
  635.1 12.7 fusion.19
  662.5 12.4 convolution_convert_fusion
  674.9 12.9 convert_add_fusion
  712.5 15.0 %fusion.13 = (f32[1024]{0:T(1024)S(1)}, f32[1024]{0:T(1024)S(1)}, f32[1024]{0:T(1024)S(1)}, f32[1024]{0:T(1024)S(1)}, bf16[1024,2048]{1,0:T(8,128)(2,1)}) fusion(bf16[4,256,2048]{2,1,0:T(8,128)(2,1)S(1)} %copy-done.17, bf16[1024,2048]{1,0:T(8,128)(2,1)} %convolution_convert_fusion.4, bf16[1024,2048]{1,0:T(8,128)(2,1)} %convolution_convert_fusion.5, ...), kind=kOutput, calls=%fused_computation.27 | convolution fusion | flops 4341100544 | bytes 27295744 | tf_op jit(solution)/shard_map/dot_general | solution.py:31
  727.7 50.0 %shard_map.301 = (f32[256,2048]{1,0:T(8,128)S(1)}, f32[16,256]{1,0:T(8,128)S(1)}) custom-call(bf16[4,256,2048]{2,1,0:T(8,128)(2,1)S(1)} %bitcast.191, f32[4,16,256]{2,1,0:T(8,128)S(1)} %fusion.136.refs_1_), custom_call_target="tpu_custom_call" | custom-call | tf_op jit(solution)/shard_map/pallas_call | solution.py:836
  789.4 44.2 %shard_map.302.do_ref = bf16[2048,256]{1,0:T(8,128)(2,1)S(1)} custom-call(bf16[256,2048]{1,0:T(8,128)(2,1)S(1)} %convolution_convert_fusion.14.refs_0_), custom_call_target="tpu_custom_call" | custom-call | tf_op jit(solution)/shard_map/pallas_call | solution.py:809
  837.3 37.5 %shard_map.303 = (f32[2048,256]{1,0:T(8,128)}, f32[2048,256]{1,0:T(8,128)}, f32[2048,256]{1,0:T(8,128)}) custom-call(bf16[2048,256]{1,0:T(8,128)(2,1)} %copy-done.21, bf16[2048,256]{1,0:T(8,128)(2,1)} %copy-done.20, bf16[2048,256]{1,0:T(8,128)(2,1)} %slice.493.v_ref, s32[2048,1]{1,0:T(8,128)} %broadcast_in_dim_reshape.6.doc_q_ref, s32[1,2048]{1,0:T(1,128)} %copy-done.32, ...), custom_call_target="tpu_custom_call" | custom-call | flops 10737418240 | bytes 10485760 | tf_op jit(solution)/shard_map/pallas_call | solution.py:134
  892.3 29.0 %shard_map.304 = f32[3,2048]{1,0:T(4,128)S(1)} custom-call(f32[3,2048]{1,0:T(4,128)S(1)} %pad_maximum_fusion.24.x), custom_call_target="tpu_custom_call" | custom-call | tf_op jit(solution)/shard_map/pallas_call | solution.py:850
  928.6 12.1 fusion.3
  963.3 179.5 %shard_map.305 = (f32[256,2048]{1,0:T(8,128)}, bf16[8,64,896]{2,1,0:T(8,128)(2,1)}, f32[64,2176]{1,0:T(8,128)}, f32[256,2048]{1,0:T(8,128)}) custom-call(bf16[8,256,2048]{2,1,0:T(8,128)(2,1)} %bitcast.200, bf16[4,512,896]{2,1,0:T(8,128)(2,1)} %bitcast.198, bf16[4,64,2176]{2,1,0:T(8,128)(2,1)} %pad_maximum_fusion.20.out, bf16[4,256,2048]{2,1,0:T(8,128)(2,1)} %bitcast.205), custom_call_target="tpu_custom_call" | custom-call | tf_op jit(solution)/shard_map/pallas_call | solution.py:866
  1147.5 207.3 %shard_map.306 = (f32[256,2048]{1,0:T(8,128)S(1)}, f32[256,1024]{1,0:T(8,128)S(1)}) custom-call(bf16[8,256,2048]{2,1,0:T(8,128)(2,1)} %bitcast.199, bf16[8,256,1024]{2,1,0:T(8,128)(2,1)} %bitcast.203), custom_call_target="tpu_custom_call" | custom-call | tf_op jit(solution)/shard_map/pallas_call | solution.py:755
  (421 shorter events, 318.7 us)
Async XLA Ops:
  7.2 437.8 %all-gather.12.cloned.1.call-start = ((), (), s32[]{:S(2)}) async-start(), calls=%async_computation.13 | async-start | bytes 14155776 | tf_op jit(solution)/shard_map/all_gather | solution.py:958
  21.0 480.9 %all-gather.14.cloned.1.call-start = ((), (), s32[]{:S(2)}) async-start(), calls=%async_computation.14 | async-start | bytes 14155776 | tf_op jit(solution)/shard_map/all_gather | solution.py:958
  253.3 180.5 %copy-start = (bf16[8,4,64,128]{3,2,1,0:T(8,128)(2,1)}, bf16[8,4,64,128]{3,2,1,0:T(8,128)(2,1)S(1)}, u32[]{:S(2)}) copy-start(bf16[8,4,64,128]{3,2,1,0:T(8,128)(2,1)S(1)} %get-tuple-element.74) | copy-start | bytes 1572868
  258.1 307.0 %all-gather.16.cloned.1.call-start = ((), (), s32[]{:S(2)}) async-start(), calls=%async_computation.15 | async-start | bytes 14155776 | tf_op jit(solution)/shard_map/all_gather | solution.py:958
  258.9 376.3 %all-gather.18.cloned.1.call-start = ((), (), s32[]{:S(2)}) async-start(), calls=%async_computation.16 | async-start | bytes 14155776 | tf_op jit(solution)/shard_map/all_gather | solution.py:958
  259.5 522.9 %reduce-scatter.9.cloned.1.call-start = ((), (), s32[]{:S(2)}) async-start(), calls=%async_computation.7 | async-start | bytes 4718592 | tf_op jit(solution)/shard_map/reduce_scatter | solution.py:1000
  261.9 49.9 %copy-start.32 = (s32[1,2048]{1,0:T(1,128)}, s32[1,2048]{1,0:T(1,128)S(1)}, u32[]{:S(2)}) copy-start(s32[1,2048]{1,0:T(1,128)S(1)} %broadcast_in_dim_reshape.5.doc_k_ref) | copy-start | bytes 24580
  292.7 89.0 %copy-start.71 = (f32[2048,1]{0,1:T(1,128)}, f32[2048,1]{0,1:T(1,128)S(1)}, u32[]{:S(2)}) copy-start(f32[2048,1]{0,1:T(1,128)S(1)} %copy.245) | copy-start | bytes 24580
  381.7 52.1 %copy-start.82 = (f32[256]{0:T(256)}, f32[256]{0:T(256)S(1)}, u32[]{:S(2)}) copy-start(f32[256]{0:T(256)S(1)} %add_rsqrt_fusion.3) | copy-start | bytes 3076
  555.1 227.3 %reduce-scatter.7.cloned.1.call-start = ((), (), s32[]{:S(2)}) async-start(), calls=%async_computation.6 | async-start | bytes 9437184 | tf_op jit(solution)/shard_map/reduce_scatter | solution.py:1000
  618.7 337.8 %all-gather.10.cloned.1.call-start = ((), (), s32[]{:S(2)}) async-start(), calls=%async_computation.8 | async-start | bytes 9437184 | tf_op jit(solution)/shard_map/all_gather | solution.py:1059
  727.5 51.0 %copy-start.68 = (f32[1024,16]{0,1:T(8,128)S(1)}, f32[1024,16]{0,1:T(8,128)}, u32[]{:S(2)}) copy-start(f32[1024,16]{0,1:T(8,128)} %copy-done.67) | copy-start | bytes 196612
  727.5 51.0 %copy-start.70 = (pred[1024,16]{0,1:T(8,128)(4,1)S(1)}, pred[1024,16]{0,1:T(8,128)(4,1)}, u32[]{:S(2)}) copy-start(pred[1024,16]{0,1:T(8,128)(4,1)} %copy-done.69) | copy-start | bytes 49156
  727.5 51.0 %copy-start.100 = (f32[256]{0:T(256)S(1)}, f32[256]{0:T(256)}, u32[]{:S(2)}) copy-start(f32[256]{0:T(256)} %dynamic-slice.5) | copy-start | bytes 3076
  727.5 51.0 %copy-start.1 = (bf16[8,4,64,128]{3,2,1,0:T(8,128)(2,1)S(1)}, bf16[8,4,64,128]{3,2,1,0:T(8,128)(2,1)}, u32[]{:S(2)}) copy-start(bf16[8,4,64,128]{3,2,1,0:T(8,128)(2,1)} %copy-done) | copy-start | bytes 1572868
  727.5 51.0 %copy-start.38 = (f32[256,2048]{1,0:T(8,128)S(1)}, f32[256,2048]{1,0:T(8,128)}, u32[]{:S(2)}) copy-start(f32[256,2048]{1,0:T(8,128)} %copy-done.37) | copy-start | bytes 6291460
  727.5 51.0 %copy-start.72 = (f32[2048,1]{0,1:T(1,128)S(1)}, f32[2048,1]{0,1:T(1,128)}, u32[]{:S(2)}) copy-start(f32[2048,1]{0,1:T(1,128)} %copy-done.71) | copy-start | bytes 24580
  727.5 51.0 %copy-start.83 = (f32[256]{0:T(256)S(1)}, f32[256]{0:T(256)}, u32[]{:S(2)}) copy-start(f32[256]{0:T(256)} %copy-done.82) | copy-start | bytes 3076
  782.4 575.1 %reduce-scatter.13.cloned.1.call-start = ((), (), s32[]{:S(2)}) async-start(), calls=%async_computation.10 | async-start | bytes 4718592 | tf_op jit(solution)/shard_map/reduce_scatter | solution.py:1000
  783.2 574.3 %reduce-scatter.17.cloned.1.call-start = ((), (), s32[]{:S(2)}) async-start(), calls=%async_computation.12 | async-start | bytes 4718592 | tf_op jit(solution)/shard_map/reduce_scatter | solution.py:1000
  834.7 522.8 %reduce-scatter.11.cloned.1.call-start = ((), (), s32[]{:S(2)}) async-start(), calls=%async_computation.9 | async-start | bytes 9437184 | tf_op jit(solution)/shard_map/reduce_scatter | solution.py:1000
  835.3 522.2 %reduce-scatter.15.cloned.1.call-start = ((), (), s32[]{:S(2)}) async-start(), calls=%async_computation.11 | async-start | bytes 9437184 | tf_op jit(solution)/shard_map/reduce_scatter | solution.py:1000
  837.3 40.4 %copy-start.81 = (f32[2048]{0:T(1024)S(1)}, f32[2048]{0:T(1024)}, u32[]{:S(2)}) copy-start(f32[2048]{0:T(1024)} %copy-done.80) | copy-start | bytes 24580
  837.3 40.4 %copy-start.106 = (f32[64]{0:T(128)S(1)}, f32[64]{0:T(128)}, u32[]{:S(2)}) copy-start(f32[64]{0:T(128)} %copy-done.105) | copy-start | bytes 772
  (110 other events, 654.3 us)
Sparse Core Ops, SparseCore 0:
  21.2 184.5 all-gather.11
  258.3 143.0 all-gather.13
  403.0 115.2 all-gather.15
  519.8 115.3 all-gather.17
  637.3 48.1 reduce-scatter.8
  687.7 87.7 reduce-scatter.6
  782.6 109.3 all-gather.9
  894.3 53.8 reduce-scatter.12
  950.5 67.0 reduce-scatter.16
  1019.8 140.8 reduce-scatter.10
  1163.0 178.4 reduce-scatter.14

commit v9 on v8

--- a/solution.py
+++ b/solution.py
@@ -758,7 +758,7 @@
         in_specs=[VMEM] * len(arrays),
         out_specs=[VMEM] * len(arrays),
         scratch_shapes=sum((line_reduce_scratch(x) for x in arrays), []),
-        compiler_params=remote_params(collective_id, 48),
+        compiler_params=remote_params(collective_id, 54),
     )(*arrays)
 
 
@@ -1058,9 +1058,10 @@
     to_gather, expert_grads[0] = lax.optimization_barrier((grad_attn_own, expert_grads[0]))
     grad_attn = lax.all_gather(to_gather, "ctx", axis=0, tiled=True)
     (grad_mixed,) = exchange(5, contract_cols(grad_attn_own, out_w).astype(bf16), True)
-    last_grad = expert_grads.pop()
-    grad_mixed, late = lax.optimization_barrier((grad_mixed, expert_grads[early:]))
-    expert_grads[early:] = [to_owners(grad_w) for grad_w in late]
+    *late, last_grad = expert_grads[early:]
+    wide_late = [wide for wide, _ in late]
+    grad_mixed, wide_late = lax.optimization_barrier((grad_mixed, wide_late))
+    wide_late = to_owners(wide_late)
     grad_query_rot, grad_key_rot, grad_value = attend_backward(
         query, key, value, docs, log_total, grad_mixed
     )
@@ -1116,10 +1117,17 @@
         moe_part.astype(bf16).reshape(n_shard, rows, width),
     )
     output = (after + moe_sum).astype(bf16)
-    grad_hidden_one, last_grad = lax.optimization_barrier((grad_hidden_one, last_grad))
-    last_grad = line_reduce(9, *(u.reshape(n_ctx, width // n_ctx, -1) for u in last_grad))
-    last_grad, expert_grads = lax.optimization_barrier((last_grad, expert_grads))
-    expert_grads = [[u.astype(f32) for u in sums] for sums in expert_grads] + [last_grad]
+    by_line = [down for _, down in late] + last_grad
+    grad_hidden_one, by_line = lax.optimization_barrier((grad_hidden_one, by_line))
+    by_line = line_reduce(9, *(u.reshape(n_ctx, width // n_ctx, -1) for u in by_line))
+    by_line, queued, wide_late = lax.optimization_barrier(
+        (by_line, expert_grads[:early], wide_late)
+    )
+    by_line = list(by_line)
+    wide_grads = [wide for wide, _ in queued] + list(wide_late) + by_line[-2:-1]
+    down_grads = [down for _, down in queued] + by_line[:-2] + by_line[-1:]
+    wide_grads = jnp.stack([u.astype(f32) for u in wide_grads])
+    down_grads = jnp.stack([u.astype(f32) for u in down_grads])
     grad_weights = grad_weights.astype(f32)
     grad_small = jnp.sum(grad_weights[..., 3 * cols :], axis=0)
     grad_weights = (
@@ -1135,8 +1143,6 @@
         scaled_one - normed_own * jnp.mean(scaled_one * normed_own, axis=1, keepdims=True)
     )
 
-    wide_grads = jnp.stack([u for u, _ in expert_grads])
-    down_grads = jnp.stack([u for _, u in expert_grads])
     factors = jnp.sqrt(clip_threshold / jnp.maximum(peak_all, clip_threshold))
     col_scale = jnp.repeat(factors, HEAD)
     query_clipped = (w_query.astype(f32) * col_scale[None, :]).astype(bf16)

time: 1420 us -> 1390 us (0.979)
  Pallas kernels: 887 us -> 869 us
    pallas_call x1, Pallas kernels: 207 us -> 187 us  [line_reduce(): pl.pallas_call(functools.partial(line_reduce_kernel, len(arrays)), out_sh...]
    unnamed x260 -> x262, local copies, waits for them, and re-layouts: 54.1 us -> 52.9 us
  transfers between devices with their start and end apart: 11 -> 10, of which waited for: 1 -> 1; matrix products, arithmetic and copies ran while one was open for 29% -> 29% of each run, Pallas kernels for 63% -> 63%
where the time goes in v9:
time: 1390 us; the launch traced here: 1380 us
  Pallas kernels  869 us (63%)
  matrix products  323 us (23%)
  local copies, waits for them, and re-layouts  90.2 us (6%)
  other arithmetic  74.6 us (5%)
  between operations  17 us (1%)
    pallas_call x1, Pallas kernels, start_call(): pl.pallas_call(start_kernel, out_shape=[jax.ShapeDtypeStruct((n_ctx, *x.s...  220 us
    pallas_call x1, Pallas kernels, line_reduce(): pl.pallas_call(functools.partial(line_reduce_kernel, len(arrays)), out_sh...  187 us
    pallas_call x1, Pallas kernels, end_call(): pl.pallas_call(end_kernel, out_shape=[jax.ShapeDtypeStruct((rows, width),...  183 us
    dot_general x11, matrix products, contract_cols(): lax.dot_general(a, b, (((1,), (1,)), ((), ())), preferred_element_type=f32)  118 us
    dot_general x11, matrix products, dot(): return jnp.dot(a, b, preferred_element_type=f32)  107 us
    dot_general x11, matrix products, contract_rows(): lax.dot_general(a, b, (((0,), (0,)), ((), ())), preferred_element_type=f32)  97.1 us
    pallas_call x2, Pallas kernels, exchange(): pl.pallas_call(functools.partial(exchange_kernel, to_rows), out_shape=[ja...  82.9 us
    unnamed x262, local copies, waits for them, and re-layouts  52.9 us
  transfers between devices with their start and end apart: 10, of which 1 were waited for; matrix products, arithmetic and copies ran while one was open for 29% of the time, Pallas kernels for 63%

profile of v9, /device:TPU:0, one launch (start us, length us, event | category | flops | bytes accessed | tf_op | source)
XLA Modules:
  0.0 1382.3 jit_solution(13568109682367755628)
XLA Ops:
  23.2 219.9 %shard_map.296 = (bf16[8,256,2048]{2,1,0:T(8,128)(2,1)S(1)}, bf16[8,4,64,2048]{3,2,1,0:T(8,128)(2,1)S(1)}, bf16[8,4,64,768]{3,2,1,0:T(8,128)(2,1)S(1)}, bf16[8,4...) custom-call(bf16[256,2048]{1,0:T(8,128)(2,1)S(1)} %bitcast.175, bf16[64,2048]{1,0:T(8,128)(2,1)S(1)} %copy-done.28, ...), custom_call_target="tpu_custom_call" | custom-call | tf_op jit(solution)/shard_map/pallas_call | solution.py:779
  311.9 23.0 %shard_map.298 = (bf16[2048,256]{1,0:T(8,128)(2,1)S(1)}, f32[2,2048,1]{2,1,0:T(8,128)}, f32[2,8,128]{2,1,0:T(8,128)S(1)}) custom-call(bf16[2048,256]{1,0:T(8,128)(2,1)S(1)} %pad_maximum_fusion.21.q_ref, bf16[2048,256]{1,0:T(8,128)(2,1)S(1)} %pad_maximum_fusion.22.k_ref, bf16[2048,256]{1,0:T(8,128)(2,1)S(1)} %copy-done.21, s32[2048,1]{1,0:T(8,128)S(1)} %copy-done.20, ...), custom_call_target="tpu_custom_call" | custom-call | flops 4294967296 | bytes 4194304 | tf_op jit(solution)/shard_map/pallas_call | solution.py:111
  334.9 38.6 %shard_map.299 = bf16[256,2048]{1,0:T(8,128)(2,1)S(1)} custom-call(bf16[2048,256]{1,0:T(8,128)(2,1)S(1)} %get-tuple-element.77.refs_0_), custom_call_target="tpu_custom_call" | custom-call | tf_op jit(solution)/shard_map/pallas_call | solution.py:809
  383.0 49.8 %shard_map.300 = (bf16[4,256,2048]{2,1,0:T(8,128)(2,1)S(1)}, f32[4,2,8,128]{3,2,1,0:T(8,128)S(1)}) custom-call(bf16[256,2048]{1,0:T(8,128)(2,1)S(1)} %multiply_convert_fusion.14.refs_0_, f32[2,8,128]{2,1,0:T(8,128)S(1)} %get-tuple-element.80.refs_1_), custom_call_target="tpu_custom_call" | custom-call | tf_op jit(solution)/shard_map/pallas_call | solution.py:823
  445.1 12.7 fusion.31
  475.0 14.4 %convert_convert_fusion = f32[1024,2048]{1,0:T(8,128)} fusion(bf16[2048,3072]{0,1:T(8,128)(2,1)} %bitcast.266, bf16[1024,1024]{0,1:T(8,128)(2,1)} %get-tuple-element.259, bf16[1024,1024]{0,1:T(8,128)(2,1)S(1)} %get-tuple-element.258), kind=kOutput, calls=%fused_computation.77 | convolution fusion | flops 8602517504 | bytes 20971520 | tf_op jit(solution)/shard_map/dot_general | solution.py:31
  489.4 12.4 convolution_convert_fusion.3
  501.8 13.1 fusion.27
  526.2 12.4 convolution_convert_fusion.2
  538.6 16.6 %convert_add_fusion.2 = f32[1024,2048]{1,0:T(8,128)} fusion(f32[1024,2048]{1,0:T(8,128)} %convert_convert_fusion, bf16[2048,3072]{0,1:T(8,128)(2,1)} %bitcast.270, bf16[1024,1024]{0,1:T(8,128)(2,1)} %copy-done.114, bf16[1024,1024]{0,1:T(8,128)(2,1)S(1)} %get-tuple-element.256), kind=kOutput, calls=%fused_computation.34 | convolution fusion | flops 8604614656 | bytes 29360128 | tf_op jit(solution)/shard_map/dot_general | solution.py:31
  565.2 13.0 fusion.23
  589.5 12.6 convolution_convert_fusion.1
  602.1 16.5 %convert_add_fusion.1 = f32[1024,2048]{1,0:T(8,128)} fusion(f32[1024,2048]{1,0:T(8,128)} %convert_add_fusion.2, bf16[2048,3072]{0,1:T(8,128)(2,1)} %bitcast.274, bf16[1024,1024]{0,1:T(8,128)(2,1)} %copy-done.115, bf16[1024,1024]{0,1:T(8,128)(2,1)S(1)} %get-tuple-element.254), kind=kOutput, calls=%fused_computation.33 | convolution fusion | flops 8604614656 | bytes 29360128 | tf_op jit(solution)/shard_map/dot_general | solution.py:31
  635.1 12.7 fusion.19
  662.7 12.4 convolution_convert_fusion
  675.1 12.9 convert_add_fusion
  712.4 15.0 %fusion.13 = (f32[1024]{0:T(1024)S(1)}, f32[1024]{0:T(1024)S(1)}, f32[1024]{0:T(1024)S(1)}, f32[1024]{0:T(1024)S(1)}, bf16[1024,2048]{1,0:T(8,128)(2,1)}) fusion(bf16[4,256,2048]{2,1,0:T(8,128)(2,1)S(1)} %copy-done.17, bf16[1024,2048]{1,0:T(8,128)(2,1)} %convolution_convert_fusion.4, bf16[1024,2048]{1,0:T(8,128)(2,1)} %convolution_convert_fusion.5, ...), kind=kOutput, calls=%fused_computation.27 | convolution fusion | flops 4341100544 | bytes 27295744 | tf_op jit(solution)/shard_map/dot_general | solution.py:31
  727.6 50.2 %shard_map.301 = (f32[256,2048]{1,0:T(8,128)S(1)}, f32[16,256]{1,0:T(8,128)S(1)}) custom-call(bf16[4,256,2048]{2,1,0:T(8,128)(2,1)S(1)} %bitcast.190, f32[4,16,256]{2,1,0:T(8,128)S(1)} %fusion.136.refs_1_), custom_call_target="tpu_custom_call" | custom-call | tf_op jit(solution)/shard_map/pallas_call | solution.py:836
  790.3 44.3 %shard_map.302.do_ref = bf16[2048,256]{1,0:T(8,128)(2,1)S(1)} custom-call(bf16[256,2048]{1,0:T(8,128)(2,1)S(1)} %convolution_convert_fusion.14.refs_0_), custom_call_target="tpu_custom_call" | custom-call | tf_op jit(solution)/shard_map/pallas_call | solution.py:809
  837.1 37.5 %shard_map.303 = (f32[2048,256]{1,0:T(8,128)}, f32[2048,256]{1,0:T(8,128)}, f32[2048,256]{1,0:T(8,128)}) custom-call(bf16[2048,256]{1,0:T(8,128)(2,1)} %copy-done.19, bf16[2048,256]{1,0:T(8,128)(2,1)} %copy-done.18, bf16[2048,256]{1,0:T(8,128)(2,1)} %slice.493.v_ref, s32[2048,1]{1,0:T(8,128)} %broadcast_in_dim_reshape.6.doc_q_ref, s32[1,2048]{1,0:T(1,128)} %copy-done.30, ...), custom_call_target="tpu_custom_call" | custom-call | flops 10737418240 | bytes 10485760 | tf_op jit(solution)/shard_map/pallas_call | solution.py:134
  892.1 27.9 %shard_map.304 = f32[3,2048]{1,0:T(4,128)S(1)} custom-call(f32[3,2048]{1,0:T(4,128)S(1)} %pad_maximum_fusion.24.x), custom_call_target="tpu_custom_call" | custom-call | tf_op jit(solution)/shard_map/pallas_call | solution.py:850
  927.3 12.1 fusion.3
  962.2 182.6 %shard_map.305 = (f32[256,2048]{1,0:T(8,128)}, bf16[8,64,896]{2,1,0:T(8,128)(2,1)}, f32[64,2176]{1,0:T(8,128)}, f32[256,2048]{1,0:T(8,128)}) custom-call(bf16[8,256,2048]{2,1,0:T(8,128)(2,1)} %bitcast.197, bf16[4,512,896]{2,1,0:T(8,128)(2,1)} %bitcast.195, bf16[4,64,2176]{2,1,0:T(8,128)(2,1)} %pad_maximum_fusion.20.out, bf16[4,256,2048]{2,1,0:T(8,128)(2,1)} %bitcast.203), custom_call_target="tpu_custom_call" | custom-call | tf_op jit(solution)/shard_map/pallas_call | solution.py:866
  1149.6 186.8 %shard_map.306 = (f32[256,1024]{1,0:T(8,128)}, f32[256,2048]{1,0:T(8,128)}, f32[256,1024]{1,0:T(8,128)}) custom-call(bf16[8,256,1024]{2,1,0:T(8,128)(2,1)} %bitcast.201, bf16[8,256,2048]{2,1,0:T(8,128)(2,1)} %bitcast.196, bf16[8,256,1024]{2,1,0:T(8,128)(2,1)} %bitcast.202), custom_call_target="tpu_custom_call" | custom-call | tf_op jit(solution)/shard_map/pallas_call | solution.py:755
  (419 shorter events, 316.1 us)
Async XLA Ops:
  7.2 437.9 %all-gather.12.cloned.1.call-start = ((), (), s32[]{:S(2)}) async-start(), calls=%async_computation.11 | async-start | bytes 14155776 | tf_op jit(solution)/shard_map/all_gather | solution.py:958
  21.0 480.8 %all-gather.14.cloned.1.call-start = ((), (), s32[]{:S(2)}) async-start(), calls=%async_computation.12 | async-start | bytes 14155776 | tf_op jit(solution)/shard_map/all_gather | solution.py:958
  253.3 180.5 %copy-start = (bf16[8,4,64,128]{3,2,1,0:T(8,128)(2,1)}, bf16[8,4,64,128]{3,2,1,0:T(8,128)(2,1)S(1)}, u32[]{:S(2)}) copy-start(bf16[8,4,64,128]{3,2,1,0:T(8,128)(2,1)S(1)} %get-tuple-element.75) | copy-start | bytes 1572868
  258.1 307.1 %all-gather.16.cloned.1.call-start = ((), (), s32[]{:S(2)}) async-start(), calls=%async_computation.13 | async-start | bytes 14155776 | tf_op jit(solution)/shard_map/all_gather | solution.py:958
  258.9 376.3 %all-gather.18.cloned.1.call-start = ((), (), s32[]{:S(2)}) async-start(), calls=%async_computation.14 | async-start | bytes 14155776 | tf_op jit(solution)/shard_map/all_gather | solution.py:958
  259.4 523.1 %reduce-scatter.8.cloned.1.call-start = ((), (), s32[]{:S(2)}) async-start(), calls=%async_computation.6 | async-start | bytes 4718592 | tf_op jit(solution)/shard_map/reduce_scatter | solution.py:1000
  261.9 49.9 %copy-start.30 = (s32[1,2048]{1,0:T(1,128)}, s32[1,2048]{1,0:T(1,128)S(1)}, u32[]{:S(2)}) copy-start(s32[1,2048]{1,0:T(1,128)S(1)} %broadcast_in_dim_reshape.5.doc_k_ref) | copy-start | bytes 24580
  292.7 89.0 %copy-start.72 = (f32[2048,1]{0,1:T(1,128)}, f32[2048,1]{0,1:T(1,128)S(1)}, u32[]{:S(2)}) copy-start(f32[2048,1]{0,1:T(1,128)S(1)} %copy.245) | copy-start | bytes 24580
  381.7 52.1 %copy-start.83 = (f32[256]{0:T(256)}, f32[256]{0:T(256)S(1)}, u32[]{:S(2)}) copy-start(f32[256]{0:T(256)S(1)} %add_rsqrt_fusion.3) | copy-start | bytes 3076
  555.2 227.3 %reduce-scatter.6.cloned.1.call-start = ((), (), s32[]{:S(2)}) async-start(), calls=%async_computation.5 | async-start | bytes 9437184 | tf_op jit(solution)/shard_map/reduce_scatter | solution.py:1000
  618.6 336.4 %all-gather.10.cloned.1.call-start = ((), (), s32[]{:S(2)}) async-start(), calls=%async_computation.7 | async-start | bytes 9437184 | tf_op jit(solution)/shard_map/all_gather | solution.py:1059
  727.4 51.1 %copy-start.69 = (f32[1024,16]{0,1:T(8,128)S(1)}, f32[1024,16]{0,1:T(8,128)}, u32[]{:S(2)}) copy-start(f32[1024,16]{0,1:T(8,128)} %copy-done.68) | copy-start | bytes 196612
  727.4 51.1 %copy-start.71 = (pred[1024,16]{0,1:T(8,128)(4,1)S(1)}, pred[1024,16]{0,1:T(8,128)(4,1)}, u32[]{:S(2)}) copy-start(pred[1024,16]{0,1:T(8,128)(4,1)} %copy-done.70) | copy-start | bytes 49156
  727.4 51.1 %copy-start.101 = (f32[256]{0:T(256)S(1)}, f32[256]{0:T(256)}, u32[]{:S(2)}) copy-start(f32[256]{0:T(256)} %dynamic-slice.5) | copy-start | bytes 3076
  727.4 51.2 %copy-start.1 = (bf16[8,4,64,128]{3,2,1,0:T(8,128)(2,1)S(1)}, bf16[8,4,64,128]{3,2,1,0:T(8,128)(2,1)}, u32[]{:S(2)}) copy-start(bf16[8,4,64,128]{3,2,1,0:T(8,128)(2,1)} %copy-done) | copy-start | bytes 1572868
  727.4 51.2 %copy-start.36 = (f32[256,2048]{1,0:T(8,128)S(1)}, f32[256,2048]{1,0:T(8,128)}, u32[]{:S(2)}) copy-start(f32[256,2048]{1,0:T(8,128)} %copy-done.35) | copy-start | bytes 6291460
  727.4 51.2 %copy-start.73 = (f32[2048,1]{0,1:T(1,128)S(1)}, f32[2048,1]{0,1:T(1,128)}, u32[]{:S(2)}) copy-start(f32[2048,1]{0,1:T(1,128)} %copy-done.72) | copy-start | bytes 24580
  727.4 51.2 %copy-start.84 = (f32[256]{0:T(256)S(1)}, f32[256]{0:T(256)}, u32[]{:S(2)}) copy-start(f32[256]{0:T(256)} %copy-done.83) | copy-start | bytes 3076
  782.5 555.3 %reduce-scatter.12.cloned.1.call-start = ((), (), s32[]{:S(2)}) async-start(), calls=%async_computation.9 | async-start | bytes 4718592 | tf_op jit(solution)/shard_map/reduce_scatter | solution.py:1000
  783.3 554.5 %reduce-scatter.10.cloned.1.call-start = ((), (), s32[]{:S(2)}) async-start(), calls=%async_computation.8 | async-start | bytes 9437184 | tf_op jit(solution)/shard_map/reduce_scatter | solution.py:1000
  784.0 553.8 %reduce-scatter.14.cloned.1.call-start = ((), (), s32[]{:S(2)}) async-start(), calls=%async_computation.10 | async-start | bytes 9437184 | tf_op jit(solution)/shard_map/reduce_scatter | solution.py:1000
  837.1 40.4 %copy-start.82 = (f32[2048]{0:T(1024)S(1)}, f32[2048]{0:T(1024)}, u32[]{:S(2)}) copy-start(f32[2048]{0:T(1024)} %copy-done.81) | copy-start | bytes 24580
  837.1 40.4 %copy-start.107 = (f32[64]{0:T(128)S(1)}, f32[64]{0:T(128)}, u32[]{:S(2)}) copy-start(f32[64]{0:T(128)} %copy-done.106) | copy-start | bytes 772
  1149.6 190.5 %copy-start.58 = (bf16[256,2048]{1,0:T(8,128)(2,1)S(1)}, bf16[256,2048]{1,0:T(8,128)(2,1)}, u32[]{:S(2)}) copy-start(bf16[256,2048]{1,0:T(8,128)(2,1)} %reduce-scatter.6.cloned.1.call-done) | copy-start | bytes 3145732
  (110 other events, 652.9 us)
Sparse Core Ops, SparseCore 0:
  21.2 184.5 all-gather.11
  258.2 143.0 all-gather.13
  402.9 115.2 all-gather.15
  519.7 115.3 all-gather.17
  637.3 48.1 reduce-scatter.7
  687.6 87.7 reduce-scatter.5
  782.7 110.0 all-gather.9
  895.1 53.3 reduce-scatter.11
  950.7 147.2 reduce-scatter.9
  1100.2 110.4 reduce-scatter.13

commit v10 on v8

--- a/solution.py
+++ b/solution.py
@@ -758,7 +758,7 @@
         in_specs=[VMEM] * len(arrays),
         out_specs=[VMEM] * len(arrays),
         scratch_shapes=sum((line_reduce_scratch(x) for x in arrays), []),
-        compiler_params=remote_params(collective_id, 48),
+        compiler_params=remote_params(collective_id, 54),
     )(*arrays)
 
 
@@ -1058,9 +1058,6 @@
     to_gather, expert_grads[0] = lax.optimization_barrier((grad_attn_own, expert_grads[0]))
     grad_attn = lax.all_gather(to_gather, "ctx", axis=0, tiled=True)
     (grad_mixed,) = exchange(5, contract_cols(grad_attn_own, out_w).astype(bf16), True)
-    last_grad = expert_grads.pop()
-    grad_mixed, late = lax.optimization_barrier((grad_mixed, expert_grads[early:]))
-    expert_grads[early:] = [to_owners(grad_w) for grad_w in late]
     grad_query_rot, grad_key_rot, grad_value = attend_backward(
         query, key, value, docs, log_total, grad_mixed
     )
@@ -1116,10 +1113,14 @@
         moe_part.astype(bf16).reshape(n_shard, rows, width),
     )
     output = (after + moe_sum).astype(bf16)
-    grad_hidden_one, last_grad = lax.optimization_barrier((grad_hidden_one, last_grad))
-    last_grad = line_reduce(9, *(u.reshape(n_ctx, width // n_ctx, -1) for u in last_grad))
-    last_grad, expert_grads = lax.optimization_barrier((last_grad, expert_grads))
-    expert_grads = [[u.astype(f32) for u in sums] for sums in expert_grads] + [last_grad]
+    last = grad_hidden_one
+    for e in range(early, local):
+        last, grad_w = lax.optimization_barrier((last, expert_grads[e]))
+        expert_grads[e] = list(line_reduce(9, *(u.reshape(n_ctx, width // n_ctx, -1) for u in grad_w)))
+        last = expert_grads[e][0]
+    grad_hidden_one, expert_grads = lax.optimization_barrier((grad_hidden_one, expert_grads))
+    wide_grads = jnp.stack([wide.astype(f32) for wide, _ in expert_grads])
+    down_grads = jnp.stack([down.astype(f32) for _, down in expert_grads])
     grad_weights = grad_weights.astype(f32)
     grad_small = jnp.sum(grad_weights[..., 3 * cols :], axis=0)
     grad_weights = (
@@ -1135,8 +1136,6 @@
         scaled_one - normed_own * jnp.mean(scaled_one * normed_own, axis=1, keepdims=True)
     )
 
-    wide_grads = jnp.stack([u for u, _ in expert_grads])
-    down_grads = jnp.stack([u for _, u in expert_grads])
     factors = jnp.sqrt(clip_threshold / jnp.maximum(peak_all, clip_threshold))
     col_scale = jnp.repeat(factors, HEAD)
     query_clipped = (w_query.astype(f32) * col_scale[None, :]).astype(bf16)

time: 1420 us -> 1430 us (level)
  Pallas kernels: 887 us -> 906 us
    pallas_call x1 -> x2, Pallas kernels: 207 us -> 240 us  [line_reduce(): pl.pallas_call(functools.partial(line_reduce_kernel, len(arrays)), out_sh...]
    unnamed x260 -> x262, local copies, waits for them, and re-layouts: 54.1 us -> 51.4 us
  transfers between devices with their start and end apart: 11 -> 9, of which waited for: 1 -> 1; matrix products, arithmetic and copies ran while one was open for 29% -> 29% of each run, Pallas kernels for 63% -> 64%
where the time goes in v10:
time: 1430 us; the launch traced here: 1420 us
  Pallas kernels  906 us (63%)
  matrix products  324 us (23%)
  local copies, waits for them, and re-layouts  88.6 us (6%)
  other arithmetic  74.3 us (5%)
  between operations  16.6 us (1%)
    pallas_call x2, Pallas kernels, line_reduce(): pl.pallas_call(functools.partial(line_reduce_kernel, len(arrays)), out_sh...  240 us
    pallas_call x1, Pallas kernels, start_call(): pl.pallas_call(start_kernel, out_shape=[jax.ShapeDtypeStruct((n_ctx, *x.s...  220 us
    pallas_call x1, Pallas kernels, end_call(): pl.pallas_call(end_kernel, out_shape=[jax.ShapeDtypeStruct((rows, width),...  168 us
    dot_general x11, matrix products, contract_cols(): lax.dot_general(a, b, (((1,), (1,)), ((), ())), preferred_element_type=f32)  116 us
    dot_general x11, matrix products, dot(): return jnp.dot(a, b, preferred_element_type=f32)  111 us
    dot_general x11, matrix products, contract_rows(): lax.dot_general(a, b, (((0,), (0,)), ((), ())), preferred_element_type=f32)  97.1 us
    pallas_call x2, Pallas kernels, exchange(): pl.pallas_call(functools.partial(exchange_kernel, to_rows), out_shape=[ja...  82.4 us
    unnamed x262, local copies, waits for them, and re-layouts  51.4 us
  transfers between devices with their start and end apart: 9, of which 1 were waited for; matrix products, arithmetic and copies ran while one was open for 29% of the time, Pallas kernels for 64%

profile of v10, /device:TPU:0, one launch (start us, length us, event | category | flops | bytes accessed | tf_op | source)
XLA Modules:
  0.0 1419.8 jit_solution(15797518227689373635)
XLA Ops:
  23.2 219.9 %shard_map.296 = (bf16[8,256,2048]{2,1,0:T(8,128)(2,1)S(1)}, bf16[8,4,64,2048]{3,2,1,0:T(8,128)(2,1)S(1)}, bf16[8,4,64,768]{3,2,1,0:T(8,128)(2,1)S(1)}, bf16[8,4...) custom-call(bf16[256,2048]{1,0:T(8,128)(2,1)S(1)} %bitcast.174, bf16[64,2048]{1,0:T(8,128)(2,1)S(1)} %copy-done.28, ...), custom_call_target="tpu_custom_call" | custom-call | tf_op jit(solution)/shard_map/pallas_call | solution.py:779
  312.2 23.0 %shard_map.298 = (bf16[2048,256]{1,0:T(8,128)(2,1)S(1)}, f32[2,2048,1]{2,1,0:T(8,128)}, f32[2,8,128]{2,1,0:T(8,128)S(1)}) custom-call(bf16[2048,256]{1,0:T(8,128)(2,1)S(1)} %pad_maximum_fusion.21.q_ref, bf16[2048,256]{1,0:T(8,128)(2,1)S(1)} %pad_maximum_fusion.22.k_ref, bf16[2048,256]{1,0:T(8,128)(2,1)S(1)} %copy-done.21, s32[2048,1]{1,0:T(8,128)S(1)} %copy-done.20, ...), custom_call_target="tpu_custom_call" | custom-call | flops 4294967296 | bytes 4194304 | tf_op jit(solution)/shard_map/pallas_call | solution.py:111
  335.2 38.6 %shard_map.299 = bf16[256,2048]{1,0:T(8,128)(2,1)S(1)} custom-call(bf16[2048,256]{1,0:T(8,128)(2,1)S(1)} %get-tuple-element.77.refs_0_), custom_call_target="tpu_custom_call" | custom-call | tf_op jit(solution)/shard_map/pallas_call | solution.py:809
  383.3 49.8 %shard_map.300 = (bf16[4,256,2048]{2,1,0:T(8,128)(2,1)S(1)}, f32[4,2,8,128]{3,2,1,0:T(8,128)S(1)}) custom-call(bf16[256,2048]{1,0:T(8,128)(2,1)S(1)} %multiply_convert_fusion.14.refs_0_, f32[2,8,128]{2,1,0:T(8,128)S(1)} %get-tuple-element.80.refs_1_), custom_call_target="tpu_custom_call" | custom-call | tf_op jit(solution)/shard_map/pallas_call | solution.py:823
  445.1 12.7 fusion.31
  475.0 14.5 %convert_convert_fusion = f32[1024,2048]{1,0:T(8,128)} fusion(bf16[2048,3072]{0,1:T(8,128)(2,1)} %bitcast.267, bf16[1024,1024]{0,1:T(8,128)(2,1)} %get-tuple-element.259, bf16[1024,1024]{0,1:T(8,128)(2,1)S(1)} %get-tuple-element.258), kind=kOutput, calls=%fused_computation.77 | convolution fusion | flops 8602517504 | bytes 20971520 | tf_op jit(solution)/shard_map/dot_general | solution.py:31
  489.5 12.4 convolution_convert_fusion.3
  501.9 13.3 fusion.27
  526.6 12.4 convolution_convert_fusion.2
  539.0 16.4 %convert_add_fusion.2 = f32[1024,2048]{1,0:T(8,128)} fusion(f32[1024,2048]{1,0:T(8,128)} %convert_convert_fusion, bf16[2048,3072]{0,1:T(8,128)(2,1)} %bitcast.271, bf16[1024,1024]{0,1:T(8,128)(2,1)} %copy-done.113, bf16[1024,1024]{0,1:T(8,128)(2,1)S(1)} %get-tuple-element.256), kind=kOutput, calls=%fused_computation.34 | convolution fusion | flops 8604614656 | bytes 29360128 | tf_op jit(solution)/shard_map/dot_general | solution.py:31
  565.4 15.0 %fusion.23 = f32[1024,2048]{0,1:T(8,128)} fusion(bf16[1024,2048]{1,0:T(8,128)(2,1)} %bitcast.178, bf16[2048,3072]{0,1:T(8,128)(2,1)} %bitcast.273), kind=kOutput, calls=%fused_computation.45 | convolution fusion | flops 8589934592 | bytes 20971520 | tf_op jit(solution)/shard_map/dot_general | solution.py:23
  591.5 12.5 convolution_convert_fusion.1
  604.0 13.5 convert_add_fusion.1
  635.1 12.7 fusion.19
  674.8 12.9 convert_add_fusion
  712.3 15.0 %fusion.13 = (f32[1024]{0:T(1024)S(1)}, f32[1024]{0:T(1024)S(1)}, f32[1024]{0:T(1024)S(1)}, f32[1024]{0:T(1024)S(1)}, bf16[1024,2048]{1,0:T(8,128)(2,1)}) fusion(bf16[4,256,2048]{2,1,0:T(8,128)(2,1)S(1)} %copy-done.17, bf16[1024,2048]{1,0:T(8,128)(2,1)} %convolution_convert_fusion.4, bf16[1024,2048]{1,0:T(8,128)(2,1)} %convolution_convert_fusion.5, ...), kind=kOutput, calls=%fused_computation.27 | convolution fusion | flops 4341100544 | bytes 27295744 | tf_op jit(solution)/shard_map/dot_general | solution.py:31
  727.5 50.0 %shard_map.301 = (f32[256,2048]{1,0:T(8,128)S(1)}, f32[16,256]{1,0:T(8,128)S(1)}) custom-call(bf16[4,256,2048]{2,1,0:T(8,128)(2,1)S(1)} %bitcast.189, f32[4,16,256]{2,1,0:T(8,128)S(1)} %fusion.136.refs_1_), custom_call_target="tpu_custom_call" | custom-call | tf_op jit(solution)/shard_map/pallas_call | solution.py:836
  790.8 43.8 %shard_map.302.do_ref = bf16[2048,256]{1,0:T(8,128)(2,1)S(1)} custom-call(bf16[256,2048]{1,0:T(8,128)(2,1)S(1)} %convolution_convert_fusion.14.refs_0_), custom_call_target="tpu_custom_call" | custom-call | tf_op jit(solution)/shard_map/pallas_call | solution.py:809
  835.7 37.5 %shard_map.303 = (f32[2048,256]{1,0:T(8,128)}, f32[2048,256]{1,0:T(8,128)}, f32[2048,256]{1,0:T(8,128)}) custom-call(bf16[2048,256]{1,0:T(8,128)(2,1)} %copy-done.19, bf16[2048,256]{1,0:T(8,128)(2,1)} %copy-done.18, bf16[2048,256]{1,0:T(8,128)(2,1)} %slice.493.v_ref, s32[2048,1]{1,0:T(8,128)} %broadcast_in_dim_reshape.6.doc_q_ref, s32[1,2048]{1,0:T(1,128)} %copy-done.30, ...), custom_call_target="tpu_custom_call" | custom-call | flops 10737418240 | bytes 10485760 | tf_op jit(solution)/shard_map/pallas_call | solution.py:134
  890.6 27.2 %shard_map.304 = f32[3,2048]{1,0:T(4,128)S(1)} custom-call(f32[3,2048]{1,0:T(4,128)S(1)} %pad_maximum_fusion.24.x), custom_call_target="tpu_custom_call" | custom-call | tf_op jit(solution)/shard_map/pallas_call | solution.py:850
  924.9 12.5 fusion.3
  960.4 168.0 %shard_map.305 = (f32[256,2048]{1,0:T(8,128)}, bf16[8,64,896]{2,1,0:T(8,128)(2,1)}, f32[64,2176]{1,0:T(8,128)}, f32[256,2048]{1,0:T(8,128)}) custom-call(bf16[8,256,2048]{2,1,0:T(8,128)(2,1)} %bitcast.197, bf16[4,512,896]{2,1,0:T(8,128)(2,1)} %bitcast.194, bf16[4,64,2176]{2,1,0:T(8,128)(2,1)} %pad_maximum_fusion.20.out, bf16[4,256,2048]{2,1,0:T(8,128)(2,1)} %bitcast.203), custom_call_target="tpu_custom_call" | custom-call | tf_op jit(solution)/shard_map/pallas_call | solution.py:866
  1132.2 117.1 %shard_map.306 = (f32[256,2048]{1,0:T(8,128)}, f32[256,1024]{1,0:T(8,128)}) custom-call(bf16[8,256,2048]{2,1,0:T(8,128)(2,1)} %bitcast.195, bf16[8,256,1024]{2,1,0:T(8,128)(2,1)} %bitcast.200), custom_call_target="tpu_custom_call" | custom-call | tf_op jit(solution)/shard_map/pallas_call | solution.py:755
  1250.3 123.3 %shard_map.307 = (f32[256,2048]{1,0:T(8,128)}, f32[256,1024]{1,0:T(8,128)}) custom-call(bf16[8,256,2048]{2,1,0:T(8,128)(2,1)} %bitcast.196, bf16[8,256,1024]{2,1,0:T(8,128)(2,1)} %bitcast.201), custom_call_target="tpu_custom_call" | custom-call | tf_op jit(solution)/shard_map/pallas_call | solution.py:755
  (417 shorter events, 329.4 us)
Async XLA Ops:
  7.2 437.9 %all-gather.12.cloned.1.call-start = ((), (), s32[]{:S(2)}) async-start(), calls=%async_computation.9 | async-start | bytes 14155776 | tf_op jit(solution)/shard_map/all_gather | solution.py:958
  21.1 480.8 %all-gather.14.cloned.1.call-start = ((), (), s32[]{:S(2)}) async-start(), calls=%async_computation.10 | async-start | bytes 14155776 | tf_op jit(solution)/shard_map/all_gather | solution.py:958
  253.3 180.7 %copy-start = (bf16[8,4,64,128]{3,2,1,0:T(8,128)(2,1)}, bf16[8,4,64,128]{3,2,1,0:T(8,128)(2,1)S(1)}, u32[]{:S(2)}) copy-start(bf16[8,4,64,128]{3,2,1,0:T(8,128)(2,1)S(1)} %get-tuple-element.75) | copy-start | bytes 1572868
  258.1 307.3 %all-gather.16.cloned.1.call-start = ((), (), s32[]{:S(2)}) async-start(), calls=%async_computation.11 | async-start | bytes 14155776 | tf_op jit(solution)/shard_map/all_gather | solution.py:958
  258.8 376.3 %all-gather.18.cloned.1.call-start = ((), (), s32[]{:S(2)}) async-start(), calls=%async_computation.12 | async-start | bytes 14155776 | tf_op jit(solution)/shard_map/all_gather | solution.py:958
  259.4 522.9 %reduce-scatter.7.cloned.1.call-start = ((), (), s32[]{:S(2)}) async-start(), calls=%async_computation.5 | async-start | bytes 4718592 | tf_op jit(solution)/shard_map/reduce_scatter | solution.py:1000
  261.8 50.2 %copy-start.30 = (s32[1,2048]{1,0:T(1,128)}, s32[1,2048]{1,0:T(1,128)S(1)}, u32[]{:S(2)}) copy-start(s32[1,2048]{1,0:T(1,128)S(1)} %broadcast_in_dim_reshape.5.doc_k_ref) | copy-start | bytes 24580
  293.0 89.0 %copy-start.71 = (f32[2048,1]{0,1:T(1,128)}, f32[2048,1]{0,1:T(1,128)S(1)}, u32[]{:S(2)}) copy-start(f32[2048,1]{0,1:T(1,128)S(1)} %copy.245) | copy-start | bytes 24580
  382.0 52.1 %copy-start.82 = (f32[256]{0:T(256)}, f32[256]{0:T(256)S(1)}, u32[]{:S(2)}) copy-start(f32[256]{0:T(256)S(1)} %add_rsqrt_fusion.3) | copy-start | bytes 3076
  555.4 226.9 %reduce-scatter.5.cloned.1.call-start = ((), (), s32[]{:S(2)}) async-start(), calls=%async_computation.4 | async-start | bytes 9437184 | tf_op jit(solution)/shard_map/reduce_scatter | solution.py:1000
  617.5 335.3 %all-gather.10.cloned.1.call-start = ((), (), s32[]{:S(2)}) async-start(), calls=%async_computation.6 | async-start | bytes 9437184 | tf_op jit(solution)/shard_map/all_gather | solution.py:1059
  727.3 50.9 %copy-start.68 = (f32[1024,16]{0,1:T(8,128)S(1)}, f32[1024,16]{0,1:T(8,128)}, u32[]{:S(2)}) copy-start(f32[1024,16]{0,1:T(8,128)} %copy-done.67) | copy-start | bytes 196612
  727.3 50.9 %copy-start.70 = (pred[1024,16]{0,1:T(8,128)(4,1)S(1)}, pred[1024,16]{0,1:T(8,128)(4,1)}, u32[]{:S(2)}) copy-start(pred[1024,16]{0,1:T(8,128)(4,1)} %copy-done.69) | copy-start | bytes 49156
  727.3 50.9 %copy-start.100 = (f32[256]{0:T(256)S(1)}, f32[256]{0:T(256)}, u32[]{:S(2)}) copy-start(f32[256]{0:T(256)} %dynamic-slice.5) | copy-start | bytes 3076
  727.3 51.0 %copy-start.1 = (bf16[8,4,64,128]{3,2,1,0:T(8,128)(2,1)S(1)}, bf16[8,4,64,128]{3,2,1,0:T(8,128)(2,1)}, u32[]{:S(2)}) copy-start(bf16[8,4,64,128]{3,2,1,0:T(8,128)(2,1)} %copy-done) | copy-start | bytes 1572868
  727.3 51.0 %copy-start.36 = (f32[256,2048]{1,0:T(8,128)S(1)}, f32[256,2048]{1,0:T(8,128)}, u32[]{:S(2)}) copy-start(f32[256,2048]{1,0:T(8,128)} %copy-done.35) | copy-start | bytes 6291460
  727.4 51.0 %copy-start.72 = (f32[2048,1]{0,1:T(1,128)S(1)}, f32[2048,1]{0,1:T(1,128)}, u32[]{:S(2)}) copy-start(f32[2048,1]{0,1:T(1,128)} %copy-done.71) | copy-start | bytes 24580
  727.4 51.0 %copy-start.83 = (f32[256]{0:T(256)S(1)}, f32[256]{0:T(256)}, u32[]{:S(2)}) copy-start(f32[256]{0:T(256)} %copy-done.82) | copy-start | bytes 3076
  782.3 592.7 %reduce-scatter.11.cloned.1.call-start = ((), (), s32[]{:S(2)}) async-start(), calls=%async_computation.8 | async-start | bytes 4718592 | tf_op jit(solution)/shard_map/reduce_scatter | solution.py:1000
  783.1 591.9 %reduce-scatter.9.cloned.1.call-start = ((), (), s32[]{:S(2)}) async-start(), calls=%async_computation.7 | async-start | bytes 9437184 | tf_op jit(solution)/shard_map/reduce_scatter | solution.py:1000
  835.6 40.3 %copy-start.81 = (f32[2048]{0:T(1024)S(1)}, f32[2048]{0:T(1024)}, u32[]{:S(2)}) copy-start(f32[2048]{0:T(1024)} %copy-done.80) | copy-start | bytes 24580
  835.6 40.3 %copy-start.106 = (f32[64]{0:T(128)S(1)}, f32[64]{0:T(128)}, u32[]{:S(2)}) copy-start(f32[64]{0:T(128)} %copy-done.105) | copy-start | bytes 772
  1132.2 117.1 %copy-start.64 = (f32[64,2176]{1,0:T(8,128)S(1)}, f32[64,2176]{1,0:T(8,128)}, u32[]{:S(2)}) copy-start(f32[64,2176]{1,0:T(8,128)} %get-tuple-element.120) | copy-start | bytes 1671172
  1250.3 127.0 %copy-start.57 = (bf16[256,2048]{1,0:T(8,128)(2,1)S(1)}, bf16[256,2048]{1,0:T(8,128)(2,1)}, u32[]{:S(2)}) copy-start(bf16[256,2048]{1,0:T(8,128)(2,1)} %reduce-scatter.5.cloned.1.call-done) | copy-start | bytes 3145732
  (109 other events, 686.8 us)
Sparse Core Ops, SparseCore 0:
  21.2 184.5 all-gather.11
  258.2 143.0 all-gather.13
  402.9 115.2 all-gather.15
  519.7 115.3 all-gather.17
  637.2 48.1 reduce-scatter.6
  687.6 87.7 reduce-scatter.4
  782.4 110.0 all-gather.9
  894.8 52.7 reduce-scatter.10
  949.8 148.3 reduce-scatter.8
